TPU v7x, 512 devices: a whole 4x8x8 slice. The times are simulated.
512 devices in a mesh: dp: 16 (over z_lo, y), mp: 8 (over z_hi, core), section: 4 (over x).
Axes of the slice: x: 4, y: 8, z: 8 (z_hi: 4, z_lo: 2; z = z_hi * 2 + z_lo), core: 2. Of those that a mesh axis runs over, the one named last changes fastest.
Arguments:
- states: bfloat16 [16384, 8192], P(('dp', 'section'), 'mp'), may hold values from -6 to 6
- direction: bfloat16 [16384, 1024], P(('dp', 'section'), 'mp'), may hold values from -0.09375 to 0.09375
- old_logp: bfloat16 [16384], P(('dp', 'section')), may hold values from -4 to -0.049804688
- lengths: int32 [128], P(('dp', 'section')), may hold values from 1 to 128, as said below
- group_ids: int32 [128], P(('dp', 'section')), may hold values from 0 to 15, as said below
- routes: int32 [16384, 1], P(('dp', 'section')), may hold values from 0 to 15; in each aligned block of 256 rows (0 to 255, 256 to 511, ...) at most 20 rows name the same one
- reward_head: bfloat16 [8192], P('mp'), may hold values from -0.0625 to 0.0625
- policy_k: bfloat16 [8192, 1024], P(('dp', 'section'), 'mp'), may hold values from -0.0625 to 0.0625
- reference_k: bfloat16 [8192, 1024], P(('dp', 'section'), 'mp'), may hold values from -0.0625 to 0.0625
Outputs:
- grad_k: float32 [8192, 1024], P(('dp', 'section'), 'mp')
- packed_logp: float32 [16, 4, 320], P('dp', 'section')
Inputs may be any that keep to these rules, and one draw needn't show every extreme that they name: `lengths`: some response has all 128 tokens valid. `group_ids`: each prompt id is held by exactly 8 responses. `routes`: among the rows of one rollout device at most 20 name the same learner shard, a bound that some block reaches of them.
All inputs are finite; a program needn't handle non-finite values.
Results may differ from a plain program's by a relative error of at most 0.004.
Values may be sent and summed in bfloat16 or wider, within the bound.
No kernel may reach another device: no remote copies, remote signals or barrier semaphores. Data moves between devices by JAX's collectives and lax.ppermute only.
A program may use at most 64 MiB of HBM per device.

v0:
```python
import jax
import jax.numpy as jnp
from jax import lax
from jax.sharding import PartitionSpec as P

GROUP = 8


kl_weight = 0.4
var_offset = 0.25


def row_slots(routes, shards, capacity):
    target = routes[:, 0]
    choose = (target[:, None] == jnp.arange(shards, dtype=jnp.int32)[None, :]).astype(jnp.int32)
    ranked = jnp.cumsum(choose, axis=0) - 1
    within = jnp.sum(ranked * choose, axis=1)
    places = target * capacity + within
    row_count = routes.shape[0]
    source = jnp.full((shards * capacity,), row_count, jnp.int32)
    return source.at[places].set(jnp.arange(row_count, dtype=jnp.int32))


def pick_rows(values, source):
    return jnp.take(values, source, axis=0, mode="fill", fill_value=0)


def advantages(scores, lengths, group_ids):
    seq_count = lengths.shape[0]
    seq_len = scores.shape[0] // seq_count
    groups = seq_count * lax.axis_size("dp") * lax.axis_size("section") // GROUP
    valid = (jnp.arange(seq_len, dtype=jnp.int32)[None, :] < lengths[:, None]).astype(jnp.float32)
    reward = jnp.sum(scores.reshape(seq_count, seq_len) * valid, axis=1) / jnp.sqrt(
        lengths.astype(jnp.float32)
    )
    member = (group_ids[:, None] == jnp.arange(groups, dtype=jnp.int32)[None, :]).astype(
        jnp.float32
    )
    totals, squares = lax.psum(
        (
            jnp.sum(member * reward[:, None], axis=0),
            jnp.sum(member * (reward * reward)[:, None], axis=0),
        ),
        ("dp", "section"),
    )
    center = totals / GROUP
    spread = squares / GROUP - center * center
    own_center = jnp.sum(member * center[None, :], axis=1)
    own_spread = jnp.sum(member * spread[None, :], axis=1)
    advantage = ((reward - own_center) / jnp.sqrt(own_spread + var_offset)).astype(jnp.bfloat16)
    return (jnp.repeat(advantage, seq_len), valid.reshape(-1))


def project(whole, policy_k, reference_k):
    return (
        jnp.dot(
            whole,
            lax.all_gather(policy_k, ("dp", "section"), axis=0, tiled=True),
            preferred_element_type=jnp.float32,
        ),
        jnp.dot(
            whole,
            lax.all_gather(reference_k, ("dp", "section"), axis=0, tiled=True),
            preferred_element_type=jnp.float32,
        ),
    )


def token_coef(dir_rows, old_rows, adv_rows, valid_rows, term_policy, term_reference):
    logp = old_rows.astype(jnp.float32) + term_policy
    coef = valid_rows * (
        -adv_rows * jnp.exp(term_policy) + kl_weight * (1.0 - jnp.exp(term_reference - term_policy))
    )
    change = (coef[:, None] * dir_rows.astype(jnp.float32)).astype(jnp.bfloat16)
    return (logp, change)


def weight_grads(whole, change):
    return lax.psum_scatter(
        lax.dot_general(
            whole, change, (((0,), (0,)), ((), ())), preferred_element_type=jnp.float32
        ),
        ("dp", "section"),
        scatter_dimension=0,
        tiled=True,
    )


def body(
    states, direction, old_logp, lengths, group_ids, routes, reward_head, policy_k, reference_k
):
    row_count = states.shape[0]
    score_part = jnp.dot(states, reward_head, preferred_element_type=jnp.float32)
    shards = lax.axis_size("dp")
    capacity = max(2, 5 * row_count // (4 * shards))
    source = row_slots(routes, shards, capacity)
    scores = lax.psum(score_part, "mp")
    adv_rows, valid_rows = advantages(scores, lengths, group_ids)
    extras = jnp.stack([old_logp, adv_rows, valid_rows.astype(jnp.bfloat16)], axis=1)
    send_states = pick_rows(states, source).reshape(shards, capacity, states.shape[1])
    send_dir = pick_rows(direction, source).reshape(shards, capacity, direction.shape[1])
    send_extras = pick_rows(extras, source).reshape(shards, capacity, 3)
    got_states, got_dir, got_extras = (
        lax.all_to_all(send_states, "dp", split_axis=0, concat_axis=0, tiled=True),
        lax.all_to_all(send_dir, "dp", split_axis=0, concat_axis=0, tiled=True),
        lax.all_to_all(send_extras, "dp", split_axis=0, concat_axis=0, tiled=True),
    )
    slot_count = shards * capacity
    learn_states = got_states.reshape(slot_count, states.shape[1])
    learn_dir = got_dir.reshape(slot_count, direction.shape[1])
    learn_extras = got_extras.reshape(slot_count, 3)
    whole = lax.all_gather(learn_states, "mp", axis=1, tiled=True)
    key_policy, key_reference = project(whole, policy_k, reference_k)
    dir_wide = learn_dir.astype(jnp.float32)
    term_policy, term_reference = lax.psum(
        (jnp.sum(dir_wide * key_policy, axis=1), jnp.sum(dir_wide * key_reference, axis=1)), "mp"
    )
    logp, change = token_coef(
        learn_dir,
        learn_extras[:, 0],
        learn_extras[:, 1].astype(jnp.float32),
        learn_extras[:, 2].astype(jnp.float32),
        term_policy,
        term_reference,
    )
    grad_k = weight_grads(whole, change)
    packed_logp = logp.reshape(1, 1, slot_count)
    return (grad_k, packed_logp)


def solution(mesh):
    return jax.shard_map(
        body,
        mesh=mesh,
        in_specs=(
            P(("dp", "section"), "mp"),
            P(("dp", "section"), "mp"),
            P(("dp", "section")),
            P(("dp", "section")),
            P(("dp", "section")),
            P(("dp", "section"), None),
            P("mp"),
            P(("dp", "section"), "mp"),
            P(("dp", "section"), "mp"),
        ),
        out_specs=(P(("dp", "section"), "mp"), P("dp", "section", None)),
        check_vma=False,
    )
```

profile of v0, /device:TPU:64, one launch (start us, length us, event | category | flops | bytes accessed | tf_op | source)
XLA Modules:
  0.0 1203.8 jit_solution(4523003245266882236)
XLA Ops:
  7.2 0.0 copy-start
  7.2 0.0 all-gather.6.cloned.1.call-start
  7.2 0.7 all-gather.6.cloned.1.call-update
  7.9 0.0 all-gather.4.cloned.1.call-start
  8.0 0.7 fusion.6
  8.6 0.6 reduce-window.6
  9.2 0.2 slice_reduce_fusion
  9.4 0.8 fusion.5
  10.2 0.7 compare_select_fusion
  10.9 1.4 scatter_custom_fusion
  12.3 0.0 copy-done
  12.3 0.0 copy-start.1
  12.4 2.1 gather_fusion
  14.5 0.0 copy-start.2
  14.5 0.0 copy-start.5
  14.5 0.0 copy-start.4
  14.5 0.1 gather.19
  14.6 0.1 broadcast_in_dim.52
  14.7 0.1 broadcast_select_fusion
  14.9 29.1 %all_to_all.15 = bf16[16,20,1024]{2,1,0:T(8,128)(2,1)S(1)} all-to-all(bf16[16,20,1024]{2,1,0:T(8,128)(2,1)S(1)} %broadcast_select_fusion), channel_id=1, replica_groups=mesh['dp'=16,'mp'=8,'section'=4] {'dp'}, dimensions={0} | all-to-all | bytes 1310720 | tf_op jit(solution)/shard_map/all_to_all | solution.py:104
  44.0 1.0 reshape.105
  45.0 0.0 all-gather.4.cloned.1.call-update
  45.0 0.0 all-gather.8.cloned.1.call-start
  45.0 0.7 all-gather.8.cloned.1.call-update
  45.7 0.0 copy-done.1
  45.7 1.4 gather_fusion.2
  47.2 0.8 broadcast_select_fusion.1
  47.9 6.3 all-to-all-start.2
  54.3 0.0 reduce-scatter.2.cloned.1.call-start
  54.3 0.0 copy-done.2
  54.3 0.0 copy-done.5
  54.4 0.2 fusion.16
  54.6 0.0 copy-done.4
  54.6 0.1 fusion.13
  54.7 7.0 all-to-all-done.2
  61.7 253.6 %all-gather.6.cloned.1.call-done = bf16[8192,128]{1,0:T(8,128)(2,1)} async-done(((bf16[128,128]{1,0:T(8,128)(2,1)}), bf16[8192,128]{1,0:T(8,128)(2,1)}) %all-gather.6.cloned.1.call-update) | async-done | bytes 2097168 | tf_op jit(solution)/shard_map/all_gather | solution.py:58
  315.3 65.4 %all-gather.4.cloned.1.call-done = bf16[320,8192]{1,0:T(8,128)(2,1)} async-done(((bf16[320,1024]{1,0:T(8,128)(2,1)}), bf16[320,8192]{1,0:T(8,128)(2,1)}) %all-gather.4.cloned.1.call-update) | async-done | bytes 5242896 | tf_op jit(solution)/shard_map/all_gather | solution.py:112
  380.7 4.8 fusion
  385.5 0.0 copy-start.3
  385.5 297.1 %all-gather.8.cloned.1.call-done = bf16[8192,128]{1,0:T(8,128)(2,1)} async-done(((bf16[128,128]{1,0:T(8,128)(2,1)}), bf16[8192,128]{1,0:T(8,128)(2,1)}) %all-gather.8.cloned.1.call-update) | async-done | bytes 2097168 | tf_op jit(solution)/shard_map/all_gather | solution.py:63
  682.6 4.8 fusion.1
  687.4 14.7 %all-reduce.1 = (f32[2,128]{1,0:T(2,128)S(1)}, f32[320]{0:T(512)S(1)}, f32[320]{0:T(512)S(1)}) all-reduce(f32[2,128]{1,0:T(2,128)S(1)} %bitcast.47, f32[320]{0:T(512)S(1)} %fusion.1, f32[320]{0:T(512)S(1)} %fusion), channel_id=1, replica_groups=mesh['dp'=16,'mp'=8,'section'=4] {'mp'}, use_global_device_ids=true, to_apply=%region_4.5 | all-reduce | flops 896 | bytes 7168 | tf_op jit(solution)/shard_map/psum | solution.py:97
  702.1 0.2 select_reduce_fusion.4
  702.3 0.0 copy-done.3
  702.3 0.1 select_reduce_fusion.3
  702.4 157.2 %all-reduce = (f32[16]{0:T(128)S(1)}, f32[16]{0:T(128)S(1)}) all-reduce(f32[16]{0:T(128)S(1)} %get-tuple-element.7, f32[16]{0:T(128)S(1)} %get-tuple-element.8), channel_id=1, replica_groups=mesh['dp'=16,'mp'=8,'section'=4] {'dp','section'}, use_global_device_ids=true, to_apply=%region_7.8 | all-reduce | flops 32 | bytes 256 | tf_op jit(solution)/shard_map/psum | solution.py:39
  859.6 0.2 select_reduce_fusion.2
  859.8 0.1 broadcast_bitcast_fusion
  859.9 0.1 copy.22
  860.1 1.4 gather_fusion.1
  861.5 0.1 copy.23
  861.6 0.1 gather.21
  861.7 10.8 all_to_all.16
  872.5 0.1 reshape.107
  872.7 6.5 fusion.2
  879.1 0.0 reduce-scatter.2.cloned.1.call-update
  879.1 0.6 reshape.108
  879.7 317.5 %reduce-scatter.2.cloned.1.call-done = f32[128,128]{1,0:T(8,128)} async-done(((f32[8192,128]{1,0:T(8,128)}), f32[128,128]{1,0:T(8,128)}) %reduce-scatter.2.cloned.1.call-update) | async-done | bytes 65552 | tf_op jit(solution)/shard_map/reduce_scatter | solution.py:79
  (20 shorter events, 0.2 us)
Async XLA Ops:
  7.2 5.2 copy-start
  7.2 308.1 %all-gather.6.cloned.1.call-start = ((), (), s32[]{:S(2)}) async-start(), calls=%async_computation.5 | async-start | bytes 2129920 | tf_op jit(solution)/shard_map/all_gather | solution.py:58
  7.9 372.8 %all-gather.4.cloned.1.call-start = ((), (), s32[]{:S(2)}) async-start(), calls=%async_computation.4 | async-start | bytes 5898240 | tf_op jit(solution)/shard_map/all_gather | solution.py:112
  12.3 33.4 %copy-start.1 = (bf16[256,128]{1,0:T(8,128)(2,1)S(1)}, bf16[256,128]{1,0:T(8,128)(2,1)}, u32[]{:S(2)}) copy-start(bf16[256,128]{1,0:T(8,128)(2,1)} %param.10) | copy-start | bytes 196612
  14.5 39.9 %copy-start.2 = (bf16[1024]{0:T(1024)(128)(2,1)S(1)}, bf16[1024]{0:T(1024)(128)(2,1)}, u32[]{:S(2)}) copy-start(bf16[1024]{0:T(1024)(128)(2,1)} %param.15) | copy-start | bytes 6148
  14.5 39.9 %copy-start.5 = (bf16[256]{0:T(256)(128)(2,1)S(1)}, bf16[256]{0:T(256)(128)(2,1)}, u32[]{:S(2)}) copy-start(bf16[256]{0:T(256)(128)(2,1)} %param.11) | copy-start | bytes 1540
  14.5 40.1 %copy-start.4 = (s32[2]{0:T(128)S(1)}, s32[2]{0:T(128)}, u32[]{:S(2)}) copy-start(s32[2]{0:T(128)} %param.12) | copy-start | bytes 28
  45.0 637.6 %all-gather.8.cloned.1.call-start = ((), (), s32[]{:S(2)}) async-start(), calls=%async_computation.6 | async-start | bytes 2129920 | tf_op jit(solution)/shard_map/all_gather | solution.py:63
  47.9 13.8 %all-to-all-start.2 = ((bf16[16,20,128]{2,1,0:T(8,128)(2,1)}), bf16[16,20,128]{2,1,0:T(8,128)(2,1)S(1)}, u32[]{:S(2)}, u32[]{:S(2)}) async-start(bf16[16,20,128]{2,1,0:T(8,128)(2,1)} %broadcast_select_fusion.1), calls=%async_computation.2 | async-start | bytes 196608 | tf_op jit(solution)/shard_map/all_to_all | solution.py:105
  54.3 1143.0 %reduce-scatter.2.cloned.1.call-start = ((), (), s32[]{:S(2)}) async-start(), calls=%async_computation.7 | async-start | bytes 4259840 | tf_op jit(solution)/shard_map/reduce_scatter | solution.py:79
  385.5 316.8 %copy-start.3 = (s32[2]{0:T(128)S(1)}, s32[2]{0:T(128)}, u32[]{:S(2)}) copy-start(s32[2]{0:T(128)} %param.13) | copy-start | bytes 28
Sparse Core Ops, SparseCore 0:
  10.1 305.1 all-gather.5
  317.4 63.2 all-gather.3
  382.8 299.7 all-gather.7
  879.3 317.9 reduce-scatter.1
where the time goes:
time: 1200 us
  waiting for transfers between devices  942 us (78%)
  blocking collectives  212 us (18%)
  matrix products  16.2 us (1%)
  between operations  14 us (1%)
    reduce_scatter x1, waiting for transfers between devices, weight_grads(): lax.psum_scatter(lax.dot_general(whole, change, (((0,), (0,)), ((), ())),...  318 us
    all_gather x1, waiting for transfers between devices, project(): lax.all_gather(reference_k, ('dp', 'section'), axis=0, tiled=True)  297 us
    all_gather x1, waiting for transfers between devices, project(): lax.all_gather(policy_k, ('dp', 'section'), axis=0, tiled=True)  254 us
    psum x1, blocking collectives, advantages(): lax.psum((jnp.sum(member * reward[:, None], axis=0), jnp.sum(member * (re...  157 us
    all_gather x1, waiting for transfers between devices, body(): whole = lax.all_gather(learn_states, 'mp', axis=1, tiled=True)  65.4 us
    all_to_all x1, blocking collectives, body(): lax.all_to_all(send_states, 'dp', split_axis=0, concat_axis=0, tiled=True)  29.1 us
  transfers between devices with their start and end apart: 5, of which 5 were waited for; matrix products, arithmetic and copies ran while one was open for 1% of the time, Pallas kernels for 0%

commit v1 on v0

v1 whole, which is shorter than its diff:
```python
import jax
import jax.numpy as jnp
from jax import lax
from jax.experimental import pallas as pl
from jax.experimental.pallas import tpu as pltpu
from jax.sharding import Mesh
from jax.sharding import PartitionSpec as P

GROUP = 8
NGROUPS = 16
CAP = 20
SLOT = 32

kl_weight = 0.4
var_offset = 0.25

DP = ("zl", "y")
ALL = ("zl", "y", "zh", "core", "sec")
BF = jnp.bfloat16
F32 = jnp.float32
NT = (((1,), (1,)), ((), ()))


def split3(x):
    hi = x.astype(BF).astype(F32)
    rest = x - hi
    mid = rest.astype(BF).astype(F32)
    return hi, mid, rest - mid


def dp_index():
    return lax.axis_index("zl") * 8 + lax.axis_index("y")


def prepare_kernel(
    lengths, group_ids, states, direction, head, routes, wp, wr,
    quarters, dir_t, w_t, extra, slots,
):
    for k in range(4):
        quarters[k] = states[:, 256 * k : 256 * (k + 1)]
    dir_t[...] = direction[...].astype(F32).T.astype(BF)
    w_t[0:128, :] = wp[...].astype(F32).T.astype(BF)
    w_t[128:256, :] = wr[...].astype(F32).T.astype(BF)
    score = lax.dot_general(
        jnp.broadcast_to(head[...], (8, 1024)), states[...], NT, preferred_element_type=F32
    )
    lane = lax.broadcasted_iota(jnp.int32, (1, 128), 1)
    rows = []
    for q in range(2):
        valid = (lane < lengths[q]).astype(F32)
        part = jnp.sum(score[0:1, 128 * q : 128 * (q + 1)] * valid, axis=1, keepdims=True)
        rows.extend(split3(part))
    for values in (group_ids, lengths):
        for q in range(2):
            rows.append(jnp.full((1, 1), values[q], jnp.int32).astype(F32))
    at = lax.broadcasted_iota(jnp.int32, (16, 128), 0)
    block = jnp.zeros((16, 128), F32)
    for n, row in enumerate(rows):
        block = jnp.where(at == n, row, block)
    extra[...] = block.astype(BF)
    target = routes[...]
    choose = (lax.broadcasted_iota(jnp.int32, (16, 256), 0) == target).astype(F32)
    before = (
        lax.broadcasted_iota(jnp.int32, (256, 256), 0)
        < lax.broadcasted_iota(jnp.int32, (256, 256), 1)
    ).astype(F32)
    ranked = jnp.dot(choose.astype(BF), before.astype(BF), preferred_element_type=F32)
    rank = jnp.sum(choose * ranked, axis=0, keepdims=True)
    slots[...] = target * SLOT + rank.astype(jnp.int32)


def terms_kernel(own, other, weights, dir_t, out, pay):
    core = lax.axis_index("core")
    acc = [jnp.zeros((2, 256), F32) for _ in range(4)]
    for z in range(4):
        mats = []
        for u in (core, 1 - core):
            mats.append(
                jnp.concatenate(
                    [weights[u * 8 + z, 0:256, :], weights[u * 8 + 4 + z, 0:256, :]], axis=1
                )
            )
        for s in range(4):
            key = lax.dot_general(mats[0], own[s], NT, preferred_element_type=F32)
            key += lax.dot_general(mats[1], other[s], NT, preferred_element_type=F32)
            wide = dir_t[z, s].astype(F32)
            acc[s] += jnp.concatenate(
                [
                    jnp.sum(wide * key[0:128], axis=0, keepdims=True),
                    jnp.sum(wide * key[128:256], axis=0, keepdims=True),
                ],
                axis=0,
            )
    for s in range(4):
        for p in range(2):
            for q in range(2):
                n = 8 * p + 2 * s + q
                pay[n : n + 1, :] = acc[s][p : p + 1, 128 * q : 128 * (q + 1)]
    lane = lax.broadcasted_iota(jnp.int32, (16, 128), 1)
    block = jnp.zeros((16, 128), F32)
    for i in range(16):
        block = jnp.where(lane == i, weights[i, 256:272, :].astype(F32), block)
    pay[16:17, :] = block[0:1] + block[1:2] + block[2:3]
    pay[17:18, :] = block[3:4] + block[4:5] + block[5:6]
    pay[18:22, :] = block[6:10]
    pay[22:24, :] = jnp.zeros((2, 128), F32)
    whole = pay[...]
    for d in range(32):
        out[d] = whole


def grads_kernel(pays, own, other, dir_t, old_logp, slots, out, change):
    core, dp, sec = lax.axis_index("core"), dp_index(), lax.axis_index("sec")
    terms = pays[0, 0:16, :]
    for d in range(1, 32):
        terms = terms + pays[d, 0:16, :]
    tp, tr = terms[0:8], terms[8:16]
    facts = []
    for s in range(4):
        fact = pays[s, 16:24, :]
        for d in range(1, 8):
            fact = fact + pays[4 * d + s, 16:24, :]
        facts.append(fact)
    lane = lax.broadcasted_iota(jnp.int32, (8, 128), 1)
    used = lane < 16
    sums = jnp.concatenate([f[0:2] for f in facts], axis=0)
    ids = jnp.concatenate([f[2:4] for f in facts], axis=0) * 0.125
    lens = jnp.where(used, jnp.concatenate([f[4:6] for f in facts], axis=0) * 0.125, 1.0)
    reward = sums / jnp.sqrt(lens)
    center = jnp.zeros((8, 128), F32)
    spread = jnp.zeros((8, 128), F32)
    for g in range(NGROUPS):
        member = used & (ids == float(g))
        mine = jnp.where(member, reward, 0.0)
        total = jnp.sum(jnp.sum(mine, axis=0, keepdims=True), axis=1, keepdims=True)
        square = jnp.sum(jnp.sum(mine * mine, axis=0, keepdims=True), axis=1, keepdims=True)
        mid = total / GROUP
        center = jnp.where(member, mid, center)
        spread = jnp.where(member, square / GROUP - mid * mid, spread)
    advantage = ((reward - center) / jnp.sqrt(spread + var_offset)).astype(BF).astype(F32)
    here = lane == dp
    adv = jnp.sum(jnp.where(here, advantage, 0.0), axis=1, keepdims=True)
    length = jnp.sum(jnp.where(here, lens, 0.0), axis=1, keepdims=True)
    valid = (lane.astype(F32) < length).astype(F32)
    coef = valid * (-adv * jnp.exp(tp) + kl_weight * (1.0 - jnp.exp(tr - tp)))
    for z in range(4):
        for s in range(4):
            row = jnp.concatenate([coef[2 * s : 2 * s + 1], coef[2 * s + 1 : 2 * s + 2]], axis=1)
            change[128 * z : 128 * (z + 1), 256 * s : 256 * (s + 1)] = (
                dir_t[z, s].astype(F32) * row
            ).astype(BF)
    for u, part in ((core, own), (1 - core, other)):
        grad = jnp.dot(
            change[...], part[...].reshape(1024, 256), preferred_element_type=F32
        ).astype(BF)
        for v in range(2):
            for z in range(4):
                out[u * 8 + v * 4 + z, 0:128, :] = grad[
                    128 * z : 128 * (z + 1), 128 * v : 128 * (v + 1)
                ]
    at = lax.broadcasted_iota(jnp.int32, (8, 128), 0)
    halves = [
        jnp.sum(jnp.where(at == 2 * sec + q, tp, 0.0), axis=0, keepdims=True) for q in range(2)
    ]
    logp = old_logp[...].astype(F32) + jnp.concatenate(halves, axis=1)
    hi, mid, lo = split3(logp)
    rows = jnp.concatenate([hi, mid, lo, jnp.zeros((5, 256), F32)], axis=0).astype(BF)
    place = (lax.broadcasted_iota(jnp.int32, (16 * SLOT, 256), 0) == slots[...]).astype(F32)
    placed = lax.dot_general(rows, place.astype(BF), NT, preferred_element_type=F32)
    tail = jnp.concatenate(
        [placed[h : h + 1, 128 * a : 128 * (a + 1)] for h in range(3) for a in range(4)]
        + [jnp.zeros((4, 128), F32)],
        axis=0,
    ).astype(BF)
    for k in range(16):
        out[k, 128:144, :] = tail


def finish_kernel(parts, grad, packed):
    dp = dp_index()
    total = parts[0, 0:128, :].astype(F32)
    for i in range(1, 16):
        total = total + parts[i, 0:128, :].astype(F32)
    grad[...] = total.T
    at = lax.broadcasted_iota(jnp.int32, (16, 128), 0)
    mine = (at < 12) & (lax.rem(at, 4) == dp // 4)
    rows = []
    for i in range(16):
        tail = jnp.where(mine, parts[i, 128:144, :].astype(F32), 0.0)
        rows.append(jnp.sum(tail, axis=0, keepdims=True))
    table = jnp.concatenate(rows, axis=0)
    pick = jnp.zeros((16, SLOT), F32)
    for a in range(4):
        pick = jnp.where(lax.rem(dp, 4) == a, table[:, SLOT * a : SLOT * (a + 1)], pick)
    packed[...] = jnp.concatenate([pick[i : i + 1, 0:CAP] for i in range(16)], axis=1)


def cost(flops, size):
    return pl.CostEstimate(flops=flops, bytes_accessed=size, transcendentals=0)


def shape(dims, dtype):
    return jax.ShapeDtypeStruct(dims, dtype)


def call(kernel, outs, scratch=(), smem=0, inputs=0, flops=0, size=0):
    vmem = pl.BlockSpec(memory_space=pltpu.VMEM)
    scalar = pl.BlockSpec(memory_space=pltpu.SMEM)
    return pl.pallas_call(
        kernel,
        out_shape=outs,
        in_specs=[scalar] * smem + [vmem] * inputs,
        out_specs=jax.tree.map(lambda _: vmem, outs),
        scratch_shapes=list(scratch),
        cost_estimate=cost(flops, size),
    )


def flat(i, zh, core, sec):
    return ((i * 4 + zh) * 2 + core) * 4 + sec


TO_HANDLER = [
    (
        flat(i, zh, core, sec),
        flat(((i >> 1) & 1) * 8 + (sec & 1) * 4 + zh, i >> 2, core, 2 * (i & 1) + (sec >> 1)),
    )
    for i in range(16)
    for zh in range(4)
    for core in range(2)
    for sec in range(4)
]
TO_OWNER = [(b, a) for a, b in TO_HANDLER]


def body(
    states, direction, old_logp, lengths, group_ids, routes, reward_head, policy_k, reference_k
):
    quarters, dir_t, w_t, extra, slots = call(
        prepare_kernel,
        (
            shape((4, 256, 256), BF),
            shape((128, 256), BF),
            shape((256, 128), BF),
            shape((16, 128), BF),
            shape((1, 256), jnp.int32),
        ),
        smem=2,
        inputs=6,
        flops=8 * 256 * 1024 * 2,
        size=1 << 20,
    )(
        lengths,
        group_ids,
        states,
        direction,
        reward_head.reshape(1, 1024),
        routes.reshape(1, 256),
        policy_k,
        reference_k,
    )
    w_here = lax.ppermute(w_t, ALL, TO_HANDLER)
    own = lax.all_to_all(quarters, "sec", 0, 0, tiled=True)
    other = lax.ppermute(own, "core", [(0, 1), (1, 0)])
    dirs = lax.all_to_all(
        jnp.broadcast_to(dir_t[None], (16, 128, 256)), ("zh", "sec"), 0, 0, tiled=True
    ).reshape(4, 4, 128, 256)
    w_pack = jnp.concatenate([w_here, extra], axis=0)
    weights = lax.all_to_all(
        jnp.broadcast_to(w_pack[None], (16, 272, 128)), DP, 0, 0, tiled=True
    )
    pays = call(
        terms_kernel,
        shape((32, 24, 128), F32),
        scratch=[pltpu.VMEM((24, 128), F32)],
        inputs=4,
        flops=1 << 30,
        size=4 << 20,
    )(own, other, weights, dirs)
    pays = lax.all_to_all(pays, ("zh", "core", "sec"), 0, 0, tiled=True)
    parts = call(
        grads_kernel,
        shape((16, 144, 128), BF),
        scratch=[pltpu.VMEM((512, 1024), BF)],
        inputs=6,
        flops=1 << 29,
        size=4 << 20,
    )(pays, own, other, dirs, old_logp.reshape(1, 256), slots)
    parts = lax.all_to_all(parts, DP, 0, 0, tiled=True)
    grad, packed = call(
        finish_kernel,
        (shape((128, 128), F32), shape((1, 320), F32)),
        inputs=1,
        flops=1 << 20,
        size=1 << 20,
    )(parts)
    return lax.ppermute(grad, ALL, TO_OWNER), packed.reshape(1, 1, 320)


def solution(mesh):
    fine = Mesh(mesh.devices.reshape(2, 8, 4, 2, 4), ALL)
    rows, cols = ("zl", "y", "sec"), ("zh", "core")
    return jax.shard_map(
        body,
        mesh=fine,
        in_specs=(
            P(rows, cols),
            P(rows, cols),
            P(rows),
            P(rows),
            P(rows),
            P(rows, None),
            P(cols),
            P(rows, cols),
            P(rows, cols),
        ),
        out_specs=(P(rows, cols), P(DP, "sec", None)),
        check_vma=False,
    )
```

time: 1200 us -> 174 us (0.14)
  the two profiles are of different devices: /device:TPU:64 before, /device:TPU:70 now
where the time goes in v1:
time: 174 us; the launch traced here: 173 us
  waiting for transfers between devices  64 us (37%)
  starting transfers between devices  52.2 us (30%)
  blocking collectives  37.3 us (21%)
  Pallas kernels  11.6 us (7%)
  local copies, waits for them, and re-layouts  7.59 us (4%)
    all_to_all x1, blocking collectives, body(): parts = lax.all_to_all(parts, DP, 0, 0, tiled=True)  25.1 us
    all_to_all x1, waiting for transfers between devices, body(): lax.all_to_all(jnp.broadcast_to(w_pack[None], (16, 272, 128)), DP, 0, 0,...  20.5 us
    all_to_all x1, waiting for transfers between devices, body(): lax.all_to_all(jnp.broadcast_to(dir_t[None], (16, 128, 256)), ('zh', 'sec...  13.7 us
    ppermute x1, waiting for transfers between devices, body(): return (lax.ppermute(grad, ALL, TO_OWNER), packed.reshape(1, 1, 320))  13.4 us
    all_to_all x1, waiting for transfers between devices, body(): pays = lax.all_to_all(pays, ('zh', 'core', 'sec'), 0, 0, tiled=True)  12.7 us
    ppermute x1, starting transfers between devices, body(): w_here = lax.ppermute(w_t, ALL, TO_HANDLER)  12.5 us
    all_to_all x1, starting transfers between devices, body(): lax.all_to_all(jnp.broadcast_to(dir_t[None], (16, 128, 256)), ('zh', 'sec...  12.2 us
    all_to_all x1, starting transfers between devices, body(): lax.all_to_all(jnp.broadcast_to(w_pack[None], (16, 272, 128)), DP, 0, 0,...  12.2 us
  transfers between devices with their start and end apart: 6, of which 6 were waited for; matrix products, arithmetic and copies ran while one was open for 0% of the time, Pallas kernels for 0%

profile of v1, /device:TPU:70, one launch (start us, length us, event | category | flops | bytes accessed | tf_op | source)
XLA Modules:
  0.0 173.4 jit_solution(4406646480553861768)
XLA Ops:
  0.6 1.3 reshape.21.head
  1.9 2.3 %shard_map.104 = (bf16[4,256,256]{2,1,0:T(8,128)(2,1)}, bf16[128,256]{1,0:T(8,128)(2,1)}, bf16[256,128]{1,0:T(8,128)(2,1)}, bf16[16,128]{1,0:T(8,128)(2,1)}, s32[1,256]{1,0:T(1,128)}) custom-call(s32[2]{0:T(128)} %lengths.1, s32[2]{0:T(128)} %group_ids.1, bf16[256,1024]{1,0:T(8,128)(2,1)} %states.1, bf16[256,128]{1,0:T(8,128)(2,1)} %direction.1, ...), custom_call_target="tpu_custom_call" | custom-call | flops 4194304 | bytes 1048576 | tf_op jit(solution)/shard_map/pallas_call | solution.py:239
  4.2 12.2 %all_to_all.25.own = bf16[4,256,256]{2,1,0:T(8,128)(2,1)S(1)} all-to-all(bf16[4,256,256]{2,1,0:T(8,128)(2,1)} %get-tuple-element.9), channel_id=1, replica_groups=mesh['zl'=2,'y'=8,'zh'=4,'core'=2,'sec'=4] {'sec'}, dimensions={0} | all-to-all | bytes 1048576 | tf_op jit(solution)/shard_map/all_to_all | solution.py:263
  16.3 0.0 copy-start.1
  16.3 2.0 %broadcast_in_dim.5 = bf16[16,128,256]{2,1,0:T(8,128)(2,1)} broadcast(bf16[128,256]{1,0:T(8,128)(2,1)} %get-tuple-element.12), dimensions={1,2} | broadcast | bytes 1114112 | tf_op jit(solution)/shard_map/broadcast_in_dim | solution.py:266
  18.3 0.0 copy-start.6
  18.3 0.0 copy-start.5
  18.3 12.2 %all-to-all-start.2 = ((bf16[16,128,256]{2,1,0:T(8,128)(2,1)}), bf16[16,128,256]{2,1,0:T(8,128)(2,1)S(1)}, u32[]{:S(2)}, u32[]{:S(2)}) async-start(bf16[16,128,256]{2,1,0:T(8,128)(2,1)} %broadcast_in_dim.5), calls=%async_computation.2 | async-start | bytes 2097152 | tf_op jit(solution)/shard_map/all_to_all | solution.py:265
  30.5 0.0 copy-done.6
  30.5 12.5 %collective-permute-start.1 = (bf16[256,128]{1,0:T(8,128)(2,1)S(1)}, bf16[256,128]{1,0:T(8,128)(2,1)S(1)}, u32[]{:S(2)}, u32[]{:S(2)}) collective-permute-start(bf16[256,128]{1,0:T(8,128)(2,1)S(1)} %copy-done.6), channel_id=1, source_target_pairs={{0,0},{1,128},{2,1},{3,129},{4,4},{5,132},{6,5},{7,133},{8,32},{9,... | collective-permute-start | bytes 196616 | tf_op jit(solution)/shard_map/ppermute | solution.py:262
  43.1 1.9 %collective-permute-done.1 = bf16[256,128]{1,0:T(8,128)(2,1)S(1)} collective-permute-done((bf16[256,128]{1,0:T(8,128)(2,1)S(1)}, bf16[256,128]{1,0:T(8,128)(2,1)S(1)}, u32[]{:S(2)}, u32[]{:S(2)}) %collective-permute-start.1) | collective-permute-done | bytes 65568 | tf_op jit(solution)/shard_map/ppermute | solution.py:262
  45.0 0.0 copy-done.5
  45.0 13.7 %all-to-all-done.2 = bf16[16,128,256]{2,1,0:T(8,128)(2,1)S(1)} async-done(((bf16[16,128,256]{2,1,0:T(8,128)(2,1)}), bf16[16,128,256]{2,1,0:T(8,128)(2,1)S(1)}, u32[]{:S(2)}, u32[]{:S(2)}) %all-to-all-start.2) | async-done | bytes 1048608 | tf_op jit(solution)/shard_map/all_to_all | solution.py:265
  58.7 0.0 copy-start
  58.7 1.3 broadcast_in_dim.4
  59.9 0.1 copy-done
  60.0 12.2 %all-to-all-start.1 = ((bf16[16,272,128]{2,1,0:T(8,128)(2,1)}), bf16[16,272,128]{2,1,0:T(8,128)(2,1)S(1)}, u32[]{:S(2)}, u32[]{:S(2)}) async-start(bf16[16,272,128]{2,1,0:T(8,128)(2,1)} %broadcast_in_dim.4), calls=%async_computation.1 | async-start | bytes 2228224 | tf_op jit(solution)/shard_map/all_to_all | solution.py:269
  72.2 0.0 copy-done.1
  72.2 1.9 %collective-permute-start = (bf16[4,256,256]{2,1,0:T(8,128)(2,1)S(1)}, bf16[4,256,256]{2,1,0:T(8,128)(2,1)S(1)}, u32[]{:S(2)}, u32[]{:S(2)}) collective-permute-start(bf16[4,256,256]{2,1,0:T(8,128)(2,1)S(1)} %all_to_all.25.own), channel_id=1, source_target_pairs={{0,4},{4,0},{1,5},{5,1},{2,6},{6,2},{3,7},{7,3},{8,12},{12,8},{9,1... | collective-permute-start | bytes 1572872 | tf_op jit(solution)/shard_map/ppermute | solution.py:264
  74.1 1.9 %collective-permute-done.other = bf16[4,256,256]{2,1,0:T(8,128)(2,1)S(1)} collective-permute-done((bf16[4,256,256]{2,1,0:T(8,128)(2,1)S(1)}, bf16[4,256,256]{2,1,0:T(8,128)(2,1)S(1)}, u32[]{:S(2)}, u32[]{:S(2)}) %collective-permute-start) | collective-permute-done | bytes 524320 | tf_op jit(solution)/shard_map/ppermute | solution.py:264
  76.0 0.0 copy-start.4
  76.0 20.5 %all-to-all-done.1.weights = bf16[16,272,128]{2,1,0:T(8,128)(2,1)S(1)} async-done(((bf16[16,272,128]{2,1,0:T(8,128)(2,1)}), bf16[16,272,128]{2,1,0:T(8,128)(2,1)S(1)}, u32[]{:S(2)}, u32[]{:S(2)}) %all-to-all-start.1) | async-done | bytes 1114144 | tf_op jit(solution)/shard_map/all_to_all | solution.py:269
  96.5 0.0 copy-start.3
  96.5 0.0 copy-done.4
  96.5 1.0 copy-done.3
  97.5 0.0 copy-start.7
  97.5 4.0 %shard_map.105 = f32[32,24,128]{2,1,0:T(8,128)} custom-call(bf16[4,256,256]{2,1,0:T(8,128)(2,1)} %copy-done.1, bf16[4,256,256]{2,1,0:T(8,128)(2,1)} %copy-done.4, bf16[16,272,128]{2,1,0:T(8,128)(2,1)} %copy-done.3, bf16[4,4,128,256]{3,2,1,0:T(8,128)(2,1)} %bitcast.3), custom_call_target="tpu_custom_call" | custom-call | flops 1073741824 | bytes 4194304 | tf_op jit(solution)/shard_map/pallas_call | solution.py:272
  101.5 10.1 %all-to-all-start.3 = ((f32[32,24,128]{2,1,0:T(8,128)}), f32[32,24,128]{2,1,0:T(8,128)S(1)}, u32[]{:S(2)}, u32[]{:S(2)}) async-start(f32[32,24,128]{2,1,0:T(8,128)} %shard_map.105), calls=%async_computation.3 | async-start | bytes 786432 | tf_op jit(solution)/shard_map/all_to_all | solution.py:280
  111.6 0.0 copy-done.7
  111.6 0.6 reshape.24.old_logp
  112.2 12.7 %all-to-all-done.3.pays = f32[32,24,128]{2,1,0:T(8,128)S(1)} async-done(((f32[32,24,128]{2,1,0:T(8,128)}), f32[32,24,128]{2,1,0:T(8,128)S(1)}, u32[]{:S(2)}, u32[]{:S(2)}) %all-to-all-start.3) | async-done | bytes 393248 | tf_op jit(solution)/shard_map/all_to_all | solution.py:280
  124.9 0.0 copy-start.2
  124.9 0.8 copy-done.2
  125.7 3.4 %shard_map.106 = bf16[16,144,128]{2,1,0:T(8,128)(2,1)} custom-call(f32[32,24,128]{2,1,0:T(8,128)} %copy-done.2, bf16[4,256,256]{2,1,0:T(8,128)(2,1)} %copy-done.1, bf16[4,256,256]{2,1,0:T(8,128)(2,1)} %copy-done.4, bf16[4,4,128,256]{3,2,1,0:T(8,128)(2,1)} %bitcast.4, bf16[1,256]{1,0:T(2,128)(2,1)} %reshape.24.old_logp, s32[1,256]{1,0:T(1,128)} %get-tuple-element.13.slots), custom_call_target="tpu_custom_call" | custom-call | flops 536870912 | bytes 4194304 | tf_op jit(solution)/shard_map/pallas_call | solution.py:281
  129.1 25.1 %all_to_all.26.parts = bf16[16,144,128]{2,1,0:T(8,128)(2,1)} all-to-all(bf16[16,144,128]{2,1,0:T(8,128)(2,1)} %shard_map.106), channel_id=1, replica_groups=mesh['zl'=2,'y'=8,'zh'=4,'core'=2,'sec'=4] {'zl','y'}, dimensions={0} | all-to-all | bytes 1179648 | tf_op jit(solution)/shard_map/all_to_all | solution.py:289
  154.2 2.0 %shard_map.107 = (f32[128,128]{1,0:T(8,128)}, f32[1,320]{1,0:T(1,128)}) custom-call(bf16[16,144,128]{2,1,0:T(8,128)(2,1)} %all_to_all.26.parts), custom_call_target="tpu_custom_call" | custom-call | flops 1048576 | bytes 1048576 | tf_op jit(solution)/shard_map/pallas_call | solution.py:290
  156.2 3.2 %collective-permute-start.2 = (f32[128,128]{1,0:T(8,128)}, f32[128,128]{1,0:T(8,128)S(1)}, u32[]{:S(2)}, u32[]{:S(2)}) collective-permute-start(f32[128,128]{1,0:T(8,128)} %get-tuple-element.14), channel_id=1, source_target_pairs={{0,0},{128,1},{1,2},{129,3},{4,4},{132,5},{5,6},{133,7},{32,8},{16... | collective-permute-start | bytes 196616 | tf_op jit(solution)/shard_map/ppermute | solution.py:297
  159.4 13.4 %collective-permute-done.2 = f32[128,128]{1,0:T(8,128)S(1)} collective-permute-done((f32[128,128]{1,0:T(8,128)}, f32[128,128]{1,0:T(8,128)S(1)}, u32[]{:S(2)}, u32[]{:S(2)}) %collective-permute-start.2) | collective-permute-done | bytes 65568 | tf_op jit(solution)/shard_map/ppermute | solution.py:297
  172.7 0.6 copy.12
  (1 shorter events, 0.0 us)
Async XLA Ops:
  16.3 55.9 %copy-start.1 = (bf16[4,256,256]{2,1,0:T(8,128)(2,1)}, bf16[4,256,256]{2,1,0:T(8,128)(2,1)S(1)}, u32[]{:S(2)}) copy-start(bf16[4,256,256]{2,1,0:T(8,128)(2,1)S(1)} %all_to_all.25.own) | copy-start | bytes 1572868
  18.3 12.2 %copy-start.6 = (bf16[256,128]{1,0:T(8,128)(2,1)S(1)}, bf16[256,128]{1,0:T(8,128)(2,1)}, u32[]{:S(2)}) copy-start(bf16[256,128]{1,0:T(8,128)(2,1)} %get-tuple-element.10) | copy-start | bytes 196612
  18.3 26.7 %copy-start.5 = (bf16[16,128]{1,0:T(8,128)(2,1)S(1)}, bf16[16,128]{1,0:T(8,128)(2,1)}, u32[]{:S(2)}) copy-start(bf16[16,128]{1,0:T(8,128)(2,1)} %get-tuple-element.11) | copy-start | bytes 12292
  18.3 40.3 %all-to-all-start.2 = ((bf16[16,128,256]{2,1,0:T(8,128)(2,1)}), bf16[16,128,256]{2,1,0:T(8,128)(2,1)S(1)}, u32[]{:S(2)}, u32[]{:S(2)}) async-start(bf16[16,128,256]{2,1,0:T(8,128)(2,1)} %broadcast_in_dim.5), calls=%async_computation.2 | async-start | bytes 2097152 | tf_op jit(solution)/shard_map/all_to_all | solution.py:265
  30.5 14.4 %collective-permute-start.1 = (bf16[256,128]{1,0:T(8,128)(2,1)S(1)}, bf16[256,128]{1,0:T(8,128)(2,1)S(1)}, u32[]{:S(2)}, u32[]{:S(2)}) collective-permute-start(bf16[256,128]{1,0:T(8,128)(2,1)S(1)} %copy-done.6), channel_id=1, source_target_pairs={{0,0},{1,128},{2,1},{3,129},{4,4},{5,132},{6,5},{7,133},{8,32},{9,... | collective-permute-start | bytes 196616 | tf_op jit(solution)/shard_map/ppermute | solution.py:262
  58.7 1.4 copy-start
  60.0 36.5 %all-to-all-start.1 = ((bf16[16,272,128]{2,1,0:T(8,128)(2,1)}), bf16[16,272,128]{2,1,0:T(8,128)(2,1)S(1)}, u32[]{:S(2)}, u32[]{:S(2)}) async-start(bf16[16,272,128]{2,1,0:T(8,128)(2,1)} %broadcast_in_dim.4), calls=%async_computation.1 | async-start | bytes 2228224 | tf_op jit(solution)/shard_map/all_to_all | solution.py:269
  72.2 3.8 %collective-permute-start = (bf16[4,256,256]{2,1,0:T(8,128)(2,1)S(1)}, bf16[4,256,256]{2,1,0:T(8,128)(2,1)S(1)}, u32[]{:S(2)}, u32[]{:S(2)}) collective-permute-start(bf16[4,256,256]{2,1,0:T(8,128)(2,1)S(1)} %all_to_all.25.own), channel_id=1, source_target_pairs={{0,4},{4,0},{1,5},{5,1},{2,6},{6,2},{3,7},{7,3},{8,12},{12,8},{9,1... | collective-permute-start | bytes 1572872 | tf_op jit(solution)/shard_map/ppermute | solution.py:264
  76.0 20.5 %copy-start.4 = (bf16[4,256,256]{2,1,0:T(8,128)(2,1)}, bf16[4,256,256]{2,1,0:T(8,128)(2,1)S(1)}, u32[]{:S(2)}) copy-start(bf16[4,256,256]{2,1,0:T(8,128)(2,1)S(1)} %collective-permute-done.other) | copy-start | bytes 1572868
  96.5 1.0 copy-start.3
  97.5 14.1 %copy-start.7 = (bf16[256]{0:T(256)(128)(2,1)S(1)}, bf16[256]{0:T(256)(128)(2,1)}, u32[]{:S(2)}) copy-start(bf16[256]{0:T(256)(128)(2,1)} %param.11) | copy-start | bytes 1540
  101.5 23.5 %all-to-all-start.3 = ((f32[32,24,128]{2,1,0:T(8,128)}), f32[32,24,128]{2,1,0:T(8,128)S(1)}, u32[]{:S(2)}, u32[]{:S(2)}) async-start(f32[32,24,128]{2,1,0:T(8,128)} %shard_map.105), calls=%async_computation.3 | async-start | bytes 786432 | tf_op jit(solution)/shard_map/all_to_all | solution.py:280
  124.9 0.8 copy-start.2
  156.2 16.6 %collective-permute-start.2 = (f32[128,128]{1,0:T(8,128)}, f32[128,128]{1,0:T(8,128)S(1)}, u32[]{:S(2)}, u32[]{:S(2)}) collective-permute-start(f32[128,128]{1,0:T(8,128)} %get-tuple-element.14), channel_id=1, source_target_pairs={{0,0},{128,1},{1,2},{129,3},{4,4},{132,5},{5,6},{133,7},{32,8},{16... | collective-permute-start | bytes 196616 | tf_op jit(solution)/shard_map/ppermute | solution.py:297

commit v2 on v1

--- a/solution.py
+++ b/solution.py
@@ -36,13 +36,19 @@
     lengths, group_ids, states, direction, head, routes, wp, wr,
     quarters, dir_t, w_t, extra, slots,
 ):
+    sec = lax.axis_index("sec")
     for k in range(4):
-        quarters[k] = states[:, 256 * k : 256 * (k + 1)]
-    dir_t[...] = direction[...].astype(F32).T.astype(BF)
+        whole = states[:, 256 * k : 256 * (k + 1)]
+        quarters[lax.rem(k - sec + 4, 4)] = whole
+    turned = direction[...].astype(F32).T.astype(BF)
+    for k in range(4):
+        dir_t[k] = turned
     w_t[0:128, :] = wp[...].astype(F32).T.astype(BF)
     w_t[128:256, :] = wr[...].astype(F32).T.astype(BF)
+    head_rows = head[...].astype(F32)
+    wide_head = jnp.concatenate([head_rows[k : k + 1] for k in range(8)], axis=1).astype(BF)
     score = lax.dot_general(
-        jnp.broadcast_to(head[...], (8, 1024)), states[...], NT, preferred_element_type=F32
+        jnp.broadcast_to(wide_head, (8, 1024)), states[...], NT, preferred_element_type=F32
     )
     lane = lax.broadcasted_iota(jnp.int32, (1, 128), 1)
     rows = []
@@ -70,7 +76,7 @@
 
 
 def terms_kernel(own, other, weights, dir_t, out, pay):
-    core = lax.axis_index("core")
+    core, sec = lax.axis_index("core"), lax.axis_index("sec")
     acc = [jnp.zeros((2, 256), F32) for _ in range(4)]
     for z in range(4):
         mats = []
@@ -83,7 +89,7 @@
         for s in range(4):
             key = lax.dot_general(mats[0], own[s], NT, preferred_element_type=F32)
             key += lax.dot_general(mats[1], other[s], NT, preferred_element_type=F32)
-            wide = dir_t[z, s].astype(F32)
+            wide = dir_t[lax.rem(sec - s + 4, 4), z].astype(F32)
             acc[s] += jnp.concatenate(
                 [
                     jnp.sum(wide * key[0:128], axis=0, keepdims=True),
@@ -94,8 +100,8 @@
     for s in range(4):
         for p in range(2):
             for q in range(2):
-                n = 8 * p + 2 * s + q
-                pay[n : n + 1, :] = acc[s][p : p + 1, 128 * q : 128 * (q + 1)]
+                n = 8 * p + 2 * lax.rem(sec - s + 4, 4) + q
+                pay[pl.ds(n, 1), :] = acc[s][p : p + 1, 128 * q : 128 * (q + 1)]
     lane = lax.broadcasted_iota(jnp.int32, (16, 128), 1)
     block = jnp.zeros((16, 128), F32)
     for i in range(16):
@@ -109,7 +115,7 @@
         out[d] = whole
 
 
-def grads_kernel(pays, own, other, dir_t, old_logp, slots, out, change):
+def grads_kernel(pays, own, other, dir_t, old_logp, slots, out, change, coefs):
     core, dp, sec = lax.axis_index("core"), dp_index(), lax.axis_index("sec")
     terms = pays[0, 0:16, :]
     for d in range(1, 32):
@@ -143,11 +149,15 @@
     length = jnp.sum(jnp.where(here, lens, 0.0), axis=1, keepdims=True)
     valid = (lane.astype(F32) < length).astype(F32)
     coef = valid * (-adv * jnp.exp(tp) + kl_weight * (1.0 - jnp.exp(tr - tp)))
-    for z in range(4):
-        for s in range(4):
-            row = jnp.concatenate([coef[2 * s : 2 * s + 1], coef[2 * s + 1 : 2 * s + 2]], axis=1)
+    coefs[...] = coef
+    for s in range(4):
+        at = lax.rem(sec - s + 4, 4)
+        row = jnp.concatenate(
+            [coefs[pl.ds(2 * at, 1), :], coefs[pl.ds(2 * at + 1, 1), :]], axis=1
+        )
+        for z in range(4):
             change[128 * z : 128 * (z + 1), 256 * s : 256 * (s + 1)] = (
-                dir_t[z, s].astype(F32) * row
+                dir_t[at, z].astype(F32) * row
             ).astype(BF)
     for u, part in ((core, own), (1 - core, other)):
         grad = jnp.dot(
@@ -159,10 +169,14 @@
                     128 * z : 128 * (z + 1), 128 * v : 128 * (v + 1)
                 ]
     at = lax.broadcasted_iota(jnp.int32, (8, 128), 0)
-    halves = [
-        jnp.sum(jnp.where(at == 2 * sec + q, tp, 0.0), axis=0, keepdims=True) for q in range(2)
-    ]
-    logp = old_logp[...].astype(F32) + jnp.concatenate(halves, axis=1)
+    old = old_logp[...].astype(F32)
+    logp = jnp.concatenate(
+        [
+            old[q : q + 1] + jnp.sum(jnp.where(at == 2 * sec + q, tp, 0.0), axis=0, keepdims=True)
+            for q in range(2)
+        ],
+        axis=1,
+    )
     hi, mid, lo = split3(logp)
     rows = jnp.concatenate([hi, mid, lo, jnp.zeros((5, 256), F32)], axis=0).astype(BF)
     place = (lax.broadcasted_iota(jnp.int32, (16 * SLOT, 256), 0) == slots[...]).astype(F32)
@@ -203,7 +217,7 @@
     return jax.ShapeDtypeStruct(dims, dtype)
 
 
-def call(kernel, outs, scratch=(), smem=0, inputs=0, flops=0, size=0):
+def call(kernel, outs, scratch=(), smem=0, inputs=0, flops=0, size=0, vmem_mib=16):
     vmem = pl.BlockSpec(memory_space=pltpu.VMEM)
     scalar = pl.BlockSpec(memory_space=pltpu.SMEM)
     return pl.pallas_call(
@@ -213,6 +227,7 @@
         out_specs=jax.tree.map(lambda _: vmem, outs),
         scratch_shapes=list(scratch),
         cost_estimate=cost(flops, size),
+        compiler_params=pltpu.CompilerParams(vmem_limit_bytes=vmem_mib << 20),
     )
 
 
@@ -240,7 +255,7 @@
         prepare_kernel,
         (
             shape((4, 256, 256), BF),
-            shape((128, 256), BF),
+            shape((4, 128, 256), BF),
             shape((256, 128), BF),
             shape((16, 128), BF),
             shape((1, 256), jnp.int32),
@@ -249,22 +264,25 @@
         inputs=6,
         flops=8 * 256 * 1024 * 2,
         size=1 << 20,
+        vmem_mib=60,
     )(
         lengths,
         group_ids,
         states,
         direction,
-        reward_head.reshape(1, 1024),
+        reward_head.reshape(8, 128),
         routes.reshape(1, 256),
         policy_k,
         reference_k,
     )
     w_here = lax.ppermute(w_t, ALL, TO_HANDLER)
-    own = lax.all_to_all(quarters, "sec", 0, 0, tiled=True)
+    dirs = lax.all_to_all(dir_t, "zh", 0, 0, tiled=True)
+    dirs = lax.all_gather(dirs, "sec", axis=0, tiled=True).reshape(4, 4, 128, 256)
+    own = [quarters[0]] + [
+        lax.ppermute(quarters[k], "sec", [(j, (j + k) % 4) for j in range(4)]) for k in (1, 2, 3)
+    ]
+    own = jnp.stack(own)
     other = lax.ppermute(own, "core", [(0, 1), (1, 0)])
-    dirs = lax.all_to_all(
-        jnp.broadcast_to(dir_t[None], (16, 128, 256)), ("zh", "sec"), 0, 0, tiled=True
-    ).reshape(4, 4, 128, 256)
     w_pack = jnp.concatenate([w_here, extra], axis=0)
     weights = lax.all_to_all(
         jnp.broadcast_to(w_pack[None], (16, 272, 128)), DP, 0, 0, tiled=True
@@ -281,11 +299,11 @@
     parts = call(
         grads_kernel,
         shape((16, 144, 128), BF),
-        scratch=[pltpu.VMEM((512, 1024), BF)],
+        scratch=[pltpu.VMEM((512, 1024), BF), pltpu.VMEM((8, 128), F32)],
         inputs=6,
         flops=1 << 29,
         size=4 << 20,
-    )(pays, own, other, dirs, old_logp.reshape(1, 256), slots)
+    )(pays, own, other, dirs, old_logp.reshape(2, 128), slots)
     parts = lax.all_to_all(parts, DP, 0, 0, tiled=True)
     grad, packed = call(
         finish_kernel,

time: 174 us -> 157 us (0.902)
  waiting for transfers between devices: 64 us -> 35.1 us
  between operations: 0.69 us -> 14.1 us
  blocking collectives: 37.3 us -> 49.8 us
  Pallas kernels: 11.6 us -> 5.59 us
  local copies, waits for them, and re-layouts: 7.59 us -> 3.08 us
  starting transfers between devices: 52.2 us -> 47.8 us
    all_to_all x2 -> x1, waiting for transfers between devices: 26.4 us -> 0.01 us  [body(): dirs = lax.all_to_all(dir_t, 'zh', 0, 0, tiled=True)]
    all_to_all x1, waiting for transfers between devices: 20.5 us -> 0.01 us  [body(): lax.all_to_all(jnp.broadcast_to(w_pack[None], (16, 272, 128)), DP, 0, 0,...]
    all_to_all x2 -> x1, starting transfers between devices: 22.3 us -> 9.4 us  [body(): dirs = lax.all_to_all(dir_t, 'zh', 0, 0, tiled=True)]
    all_gather x0 -> x1, waiting for transfers between devices: none -> 12.5 us  [body(): lax.all_gather(dirs, 'sec', axis=0, tiled=True).reshape(4, 4, 128, 256)]
    all_to_all x1, blocking collectives: 12.2 us -> 24.5 us  [body(): pays = lax.all_to_all(pays, ('zh', 'core', 'sec'), 0, 0, tiled=True)]
    ppermute x0 -> x3, starting transfers between devices: none -> 10.2 us  [body(): lax.ppermute(quarters[k], 'sec', [(j, (j + k) % 4) for j in range(4)])]
    ppermute x0 -> x3, waiting for transfers between devices: none -> 4.74 us  [body(): lax.ppermute(quarters[k], 'sec', [(j, (j + k) % 4) for j in range(4)])]
    pallas_call x1, Pallas kernels: 3.99 us -> 1.34 us  [body(): call(terms_kernel, shape((32, 24, 128), F32), scratch=[pltpu.VMEM((24, 12...]
  transfers between devices with their start and end apart: 6 -> 9, of which waited for: 6 -> 6; matrix products, arithmetic and copies ran while one was open for 0% -> 0% of each run, Pallas kernels for 0% -> 0%
where the time goes in v2:
time: 157 us; the launch traced here: 156 us
  blocking collectives  49.8 us (32%)
  starting transfers between devices  47.8 us (30%)
  waiting for transfers between devices  35.1 us (22%)
  between operations  14.1 us (9%)
  Pallas kernels  5.59 us (4%)
  local copies, waits for them, and re-layouts  3.08 us (2%)
    all_to_all x1, blocking collectives, body(): parts = lax.all_to_all(parts, DP, 0, 0, tiled=True)  25.2 us
    all_to_all x1, blocking collectives, body(): pays = lax.all_to_all(pays, ('zh', 'core', 'sec'), 0, 0, tiled=True)  24.5 us
    ppermute x1, waiting for transfers between devices, body(): return (lax.ppermute(grad, ALL, TO_OWNER), packed.reshape(1, 1, 320))  13.1 us
    ppermute x1, starting transfers between devices, body(): w_here = lax.ppermute(w_t, ALL, TO_HANDLER)  13 us
    all_gather x1, waiting for transfers between devices, body(): lax.all_gather(dirs, 'sec', axis=0, tiled=True).reshape(4, 4, 128, 256)  12.5 us
    ppermute x3, starting transfers between devices, body(): lax.ppermute(quarters[k], 'sec', [(j, (j + k) % 4) for j in range(4)])  10.2 us
    all_to_all x1, starting transfers between devices, body(): lax.all_to_all(jnp.broadcast_to(w_pack[None], (16, 272, 128)), DP, 0, 0,...  10.1 us
    all_to_all x1, starting transfers between devices, body(): dirs = lax.all_to_all(dir_t, 'zh', 0, 0, tiled=True)  9.4 us
  transfers between devices with their start and end apart: 9, of which 6 were waited for; matrix products, arithmetic and copies ran while one was open for 0% of the time, Pallas kernels for 0%

profile of v2, /device:TPU:70, one launch (start us, length us, event | category | flops | bytes accessed | tf_op | source)
XLA Modules:
  0.0 156.2 jit_solution(17136893720023710230)
XLA Ops:
  7.2 2.3 %shard_map.104 = (bf16[4,256,256]{2,1,0:T(8,128)(2,1)}, bf16[4,128,256]{2,1,0:T(8,128)(2,1)}, bf16[256,128]{1,0:T(8,128)(2,1)}, bf16[16,128]{1,0:T(8,128)(2,1)}, s32[1,256]{1,0:T(1,128)}) custom-call(s32[2]{0:T(128)} %lengths.1, s32[2]{0:T(128)} %group_ids.1, bf16[256,1024]{1,0:T(8,128)(2,1)} %states.1, bf16[256,128]{1,0:T(8,128)(2,1)} %direction.1, ...), custom_call_target="tpu_custom_call" | custom-call | flops 4194304 | bytes 1048576 | tf_op jit(solution)/shard_map/pallas_call | solution.py:254
  9.5 9.4 %all-to-all-start.1 = ((bf16[4,128,256]{2,1,0:T(8,128)(2,1)}), bf16[4,128,256]{2,1,0:T(8,128)(2,1)S(1)}, u32[]{:S(2)}, u32[]{:S(2)}) async-start(bf16[4,128,256]{2,1,0:T(8,128)(2,1)} %get-tuple-element.12), calls=%async_computation.1 | async-start | bytes 524288 | tf_op jit(solution)/shard_map/all_to_all | solution.py:279
  18.9 13.0 %collective-permute-start.4 = (bf16[256,128]{1,0:T(8,128)(2,1)}, bf16[256,128]{1,0:T(8,128)(2,1)S(1)}, u32[]{:S(2)}, u32[]{:S(2)}) collective-permute-start(bf16[256,128]{1,0:T(8,128)(2,1)} %get-tuple-element.10), channel_id=1, source_target_pairs={{0,0},{1,128},{2,1},{3,129},{4,4},{5,132},{6,5},{7,133},{8,32},{9,... | collective-permute-start | bytes 196616 | tf_op jit(solution)/shard_map/ppermute | solution.py:278
  31.9 2.2 %collective-permute-done.4 = bf16[256,128]{1,0:T(8,128)(2,1)S(1)} collective-permute-done((bf16[256,128]{1,0:T(8,128)(2,1)}, bf16[256,128]{1,0:T(8,128)(2,1)S(1)}, u32[]{:S(2)}, u32[]{:S(2)}) %collective-permute-start.4) | collective-permute-done | bytes 65568 | tf_op jit(solution)/shard_map/ppermute | solution.py:278
  34.1 0.7 pad_maximum_fusion.1
  34.8 0.0 all-to-all-done.1
  34.8 0.0 copy-start.4
  34.8 1.2 broadcast_in_dim.2
  36.0 0.0 copy-start.5
  36.0 0.0 copy-done.4
  36.0 10.1 %all-to-all-start = ((bf16[16,272,128]{2,1,0:T(8,128)(2,1)}), bf16[16,272,128]{2,1,0:T(8,128)(2,1)S(1)}, u32[]{:S(2)}, u32[]{:S(2)}) async-start(bf16[16,272,128]{2,1,0:T(8,128)(2,1)} %broadcast_in_dim.2), calls=%async_computation | async-start | bytes 2228224 | tf_op jit(solution)/shard_map/all_to_all | solution.py:287
  46.0 0.0 all-gather.2.cloned.1.call-start
  46.1 0.7 all-gather.2.cloned.1.call-update
  46.8 0.0 copy-done.5
  46.8 2.7 %collective-permute-start = (bf16[256,256]{1,0:T(8,128)(2,1)S(1)}, bf16[256,256]{1,0:T(8,128)(2,1)S(1)}, u32[]{:S(2)}, u32[]{:S(2)}) collective-permute-start(bf16[256,256]{1,0:T(8,128)(2,1)S(1)} %get-tuple-element.19), channel_id=1, source_target_pairs={{0,1},{1,2},{2,3},{3,0},{4,5},{5,6},{6,7},{7,4},{8,9},{9,10},{10,1... | collective-permute-start | bytes 393224 | tf_op jit(solution)/shard_map/ppermute | solution.py:282
  49.5 4.2 %collective-permute-start.1 = (bf16[256,256]{1,0:T(8,128)(2,1)S(1)}, bf16[256,256]{1,0:T(8,128)(2,1)S(1)}, u32[]{:S(2)}, u32[]{:S(2)}) collective-permute-start(bf16[256,256]{1,0:T(8,128)(2,1)S(1)} %get-tuple-element.18), channel_id=1, source_target_pairs={{0,2},{1,3},{2,0},{3,1},{4,6},{5,7},{6,4},{7,5},{8,10},{9,11},{10,... | collective-permute-start | bytes 393224 | tf_op jit(solution)/shard_map/ppermute | solution.py:282
  53.7 3.3 %collective-permute-start.2 = (bf16[256,256]{1,0:T(8,128)(2,1)S(1)}, bf16[256,256]{1,0:T(8,128)(2,1)S(1)}, u32[]{:S(2)}, u32[]{:S(2)}) collective-permute-start(bf16[256,256]{1,0:T(8,128)(2,1)S(1)} %get-tuple-element.17), channel_id=1, source_target_pairs={{0,3},{1,0},{2,1},{3,2},{4,7},{5,4},{6,5},{7,6},{8,11},{9,8},{10,9... | collective-permute-start | bytes 393224 | tf_op jit(solution)/shard_map/ppermute | solution.py:282
  57.0 0.0 collective-permute-done
  57.0 0.8 collective-permute-done.1
  57.9 3.9 %collective-permute-done.2 = bf16[256,256]{1,0:T(8,128)(2,1)S(1)} collective-permute-done((bf16[256,256]{1,0:T(8,128)(2,1)S(1)}, bf16[256,256]{1,0:T(8,128)(2,1)S(1)}, u32[]{:S(2)}, u32[]{:S(2)}) %collective-permute-start.2) | collective-permute-done | bytes 131104 | tf_op jit(solution)/shard_map/ppermute | solution.py:282
  61.8 0.1 pad_maximum_fusion.own
  61.8 1.9 %collective-permute-start.3 = (bf16[4,256,256]{2,1,0:T(8,128)(2,1)S(1)}, bf16[4,256,256]{2,1,0:T(8,128)(2,1)S(1)}, u32[]{:S(2)}, u32[]{:S(2)}) collective-permute-start(bf16[4,256,256]{2,1,0:T(8,128)(2,1)S(1)} %pad_maximum_fusion.own), channel_id=1, source_target_pairs={{0,4},{4,0},{1,5},{5,1},{2,6},{6,2},{3,7},{7,3},{8,12},{12,8},{9,1... | collective-permute-start | bytes 1572872 | tf_op jit(solution)/shard_map/ppermute | solution.py:285
  63.8 1.9 %collective-permute-done.3.other = bf16[4,256,256]{2,1,0:T(8,128)(2,1)S(1)} collective-permute-done((bf16[4,256,256]{2,1,0:T(8,128)(2,1)S(1)}, bf16[4,256,256]{2,1,0:T(8,128)(2,1)S(1)}, u32[]{:S(2)}, u32[]{:S(2)}) %collective-permute-start.3) | collective-permute-done | bytes 524320 | tf_op jit(solution)/shard_map/ppermute | solution.py:285
  65.6 12.5 %all-gather.2.cloned.1.call-done = bf16[16,128,256]{2,1,0:T(8,128)(2,1)} async-done(((bf16[4,128,256]{2,1,0:T(8,128)(2,1)}), bf16[16,128,256]{2,1,0:T(8,128)(2,1)}) %all-gather.2.cloned.1.call-update) | async-done | bytes 1048592 | tf_op jit(solution)/shard_map/all_gather | solution.py:280
  78.1 0.0 all-to-all-done.weights
  78.1 0.0 copy-start
  78.1 1.2 copy-done
  79.3 0.0 copy-start.1
  79.3 0.0 copy-start.2
  79.3 0.0 copy-start.3
  79.3 1.3 shard_map.105
  80.7 24.5 %all_to_all.20.pays = f32[32,24,128]{2,1,0:T(8,128)S(1)} all-to-all(f32[32,24,128]{2,1,0:T(8,128)S(1)} %shard_map.105), channel_id=1, replica_groups=mesh['zl'=2,'y'=8,'zh'=4,'core'=2,'sec'=4] {'zh','core','sec'}, dimensions={0} | all-to-all | bytes 786432 | tf_op jit(solution)/shard_map/all_to_all | solution.py:298
  105.2 0.0 copy-done.1
  105.2 0.0 copy-done.2
  105.2 0.0 copy-done.3
  105.2 1.0 shard_map.106
  106.2 25.2 %all_to_all.21.parts = bf16[16,144,128]{2,1,0:T(8,128)(2,1)S(1)} all-to-all(bf16[16,144,128]{2,1,0:T(8,128)(2,1)S(1)} %shard_map.106), channel_id=1, replica_groups=mesh['zl'=2,'y'=8,'zh'=4,'core'=2,'sec'=4] {'zl','y'}, dimensions={0} | all-to-all | bytes 1179648 | tf_op jit(solution)/shard_map/all_to_all | solution.py:307
  131.5 0.9 shard_map.107
  132.4 3.2 %collective-permute-start.5 = (f32[128,128]{1,0:T(8,128)S(1)}, f32[128,128]{1,0:T(8,128)S(1)}, u32[]{:S(2)}, u32[]{:S(2)}) collective-permute-start(f32[128,128]{1,0:T(8,128)S(1)} %get-tuple-element.14), channel_id=1, source_target_pairs={{0,0},{128,1},{1,2},{129,3},{4,4},{132,5},{5,6},{133,7},{32,8},{16... | collective-permute-start | bytes 196616 | tf_op jit(solution)/shard_map/ppermute | solution.py:315
  135.6 13.1 %collective-permute-done.5 = f32[128,128]{1,0:T(8,128)S(1)} collective-permute-done((f32[128,128]{1,0:T(8,128)S(1)}, f32[128,128]{1,0:T(8,128)S(1)}, u32[]{:S(2)}, u32[]{:S(2)}) %collective-permute-start.5) | collective-permute-done | bytes 65568 | tf_op jit(solution)/shard_map/ppermute | solution.py:315
  148.8 0.6 copy.12
  (1 shorter events, 0.0 us)
Async XLA Ops:
  9.5 25.3 %all-to-all-start.1 = ((bf16[4,128,256]{2,1,0:T(8,128)(2,1)}), bf16[4,128,256]{2,1,0:T(8,128)(2,1)S(1)}, u32[]{:S(2)}, u32[]{:S(2)}) async-start(bf16[4,128,256]{2,1,0:T(8,128)(2,1)} %get-tuple-element.12), calls=%async_computation.1 | async-start | bytes 524288 | tf_op jit(solution)/shard_map/all_to_all | solution.py:279
  18.9 15.2 %collective-permute-start.4 = (bf16[256,128]{1,0:T(8,128)(2,1)}, bf16[256,128]{1,0:T(8,128)(2,1)S(1)}, u32[]{:S(2)}, u32[]{:S(2)}) collective-permute-start(bf16[256,128]{1,0:T(8,128)(2,1)} %get-tuple-element.10), channel_id=1, source_target_pairs={{0,0},{1,128},{2,1},{3,129},{4,4},{5,132},{6,5},{7,133},{8,32},{9,... | collective-permute-start | bytes 196616 | tf_op jit(solution)/shard_map/ppermute | solution.py:278
  34.8 1.2 copy-start.4
  36.0 10.8 %copy-start.5 = (bf16[4,256,256]{2,1,0:T(8,128)(2,1)S(1)}, bf16[4,256,256]{2,1,0:T(8,128)(2,1)}, u32[]{:S(2)}) copy-start(bf16[4,256,256]{2,1,0:T(8,128)(2,1)} %get-tuple-element.9) | copy-start | bytes 1572868
  36.0 42.1 %all-to-all-start = ((bf16[16,272,128]{2,1,0:T(8,128)(2,1)}), bf16[16,272,128]{2,1,0:T(8,128)(2,1)S(1)}, u32[]{:S(2)}, u32[]{:S(2)}) async-start(bf16[16,272,128]{2,1,0:T(8,128)(2,1)} %broadcast_in_dim.2), calls=%async_computation | async-start | bytes 2228224 | tf_op jit(solution)/shard_map/all_to_all | solution.py:287
  46.0 32.1 %all-gather.2.cloned.1.call-start = ((), (), s32[]{:S(2)}) async-start(), calls=%async_computation.4 | async-start | bytes 1310720 | tf_op jit(solution)/shard_map/all_gather | solution.py:280
  46.8 10.2 %collective-permute-start = (bf16[256,256]{1,0:T(8,128)(2,1)S(1)}, bf16[256,256]{1,0:T(8,128)(2,1)S(1)}, u32[]{:S(2)}, u32[]{:S(2)}) collective-permute-start(bf16[256,256]{1,0:T(8,128)(2,1)S(1)} %get-tuple-element.19), channel_id=1, source_target_pairs={{0,1},{1,2},{2,3},{3,0},{4,5},{5,6},{6,7},{7,4},{8,9},{9,10},{10,1... | collective-permute-start | bytes 393224 | tf_op jit(solution)/shard_map/ppermute | solution.py:282
  49.5 8.4 %collective-permute-start.1 = (bf16[256,256]{1,0:T(8,128)(2,1)S(1)}, bf16[256,256]{1,0:T(8,128)(2,1)S(1)}, u32[]{:S(2)}, u32[]{:S(2)}) collective-permute-start(bf16[256,256]{1,0:T(8,128)(2,1)S(1)} %get-tuple-element.18), channel_id=1, source_target_pairs={{0,2},{1,3},{2,0},{3,1},{4,6},{5,7},{6,4},{7,5},{8,10},{9,11},{10,... | collective-permute-start | bytes 393224 | tf_op jit(solution)/shard_map/ppermute | solution.py:282
  53.7 8.1 %collective-permute-start.2 = (bf16[256,256]{1,0:T(8,128)(2,1)S(1)}, bf16[256,256]{1,0:T(8,128)(2,1)S(1)}, u32[]{:S(2)}, u32[]{:S(2)}) collective-permute-start(bf16[256,256]{1,0:T(8,128)(2,1)S(1)} %get-tuple-element.17), channel_id=1, source_target_pairs={{0,3},{1,0},{2,1},{3,2},{4,7},{5,4},{6,5},{7,6},{8,11},{9,8},{10,9... | collective-permute-start | bytes 393224 | tf_op jit(solution)/shard_map/ppermute | solution.py:282
  61.8 3.8 %collective-permute-start.3 = (bf16[4,256,256]{2,1,0:T(8,128)(2,1)S(1)}, bf16[4,256,256]{2,1,0:T(8,128)(2,1)S(1)}, u32[]{:S(2)}, u32[]{:S(2)}) collective-permute-start(bf16[4,256,256]{2,1,0:T(8,128)(2,1)S(1)} %pad_maximum_fusion.own), channel_id=1, source_target_pairs={{0,4},{4,0},{1,5},{5,1},{2,6},{6,2},{3,7},{7,3},{8,12},{12,8},{9,1... | collective-permute-start | bytes 1572872 | tf_op jit(solution)/shard_map/ppermute | solution.py:285
  78.1 1.2 copy-start
  79.3 25.9 %copy-start.1 = (bf16[16,128,256]{2,1,0:T(8,128)(2,1)S(1)}, bf16[16,128,256]{2,1,0:T(8,128)(2,1)}, u32[]{:S(2)}) copy-start(bf16[16,128,256]{2,1,0:T(8,128)(2,1)} %all-gather.2.cloned.1.call-done) | copy-start | bytes 3145732
  79.3 25.9 %copy-start.2 = (s32[1,256]{1,0:T(1,128)S(1)}, s32[1,256]{1,0:T(1,128)}, u32[]{:S(2)}) copy-start(s32[1,256]{1,0:T(1,128)} %get-tuple-element.13.slots) | copy-start | bytes 3076
  79.3 25.9 %copy-start.3 = (bf16[256]{0:T(256)(128)(2,1)S(1)}, bf16[256]{0:T(256)(128)(2,1)}, u32[]{:S(2)}) copy-start(bf16[256]{0:T(256)(128)(2,1)} %param.11) | copy-start | bytes 1540
  132.4 16.4 %collective-permute-start.5 = (f32[128,128]{1,0:T(8,128)S(1)}, f32[128,128]{1,0:T(8,128)S(1)}, u32[]{:S(2)}, u32[]{:S(2)}) collective-permute-start(f32[128,128]{1,0:T(8,128)S(1)} %get-tuple-element.14), channel_id=1, source_target_pairs={{0,0},{128,1},{1,2},{129,3},{4,4},{132,5},{5,6},{133,7},{32,8},{16... | collective-permute-start | bytes 196616 | tf_op jit(solution)/shard_map/ppermute | solution.py:315
Sparse Core Ops, SparseCore 0:
  49.0 29.1 all-gather.1

commit v3 on v2

--- a/solution.py
+++ b/solution.py
@@ -32,19 +32,26 @@
     return lax.axis_index("zl") * 8 + lax.axis_index("y")
 
 
-def prepare_kernel(
-    lengths, group_ids, states, direction, head, routes, wp, wr,
-    quarters, dir_t, w_t, extra, slots,
-):
+def handler(zh, block, zz):
+    turn = (zz - zh + (zh >> 1)) & 3
+    zl = (turn & 1) ^ (turn >> 1)
+    near = 4 * (zh & 1)
+    y = near + block + (turn >> 1) * (7 - 2 * block)
+    return zl * 8 + (y & 7)
+
+
+def turn_kernel(direction, wp, wr, dir_t, w_t):
+    dir_t[...] = direction[...].astype(F32).T.astype(BF)
+    w_t[0:128, :] = wp[...].astype(F32).T.astype(BF)
+    w_t[128:256, :] = wr[...].astype(F32).T.astype(BF)
+
+
+def prepare_kernel(lengths, group_ids, states, head, routes, quarters, extra, slots):
     sec = lax.axis_index("sec")
     for k in range(4):
-        whole = states[:, 256 * k : 256 * (k + 1)]
-        quarters[lax.rem(k - sec + 4, 4)] = whole
-    turned = direction[...].astype(F32).T.astype(BF)
-    for k in range(4):
-        dir_t[k] = turned
-    w_t[0:128, :] = wp[...].astype(F32).T.astype(BF)
-    w_t[128:256, :] = wr[...].astype(F32).T.astype(BF)
+        to = lax.rem(k - sec + 4, 4)
+        quarters[to, :, 0:128] = states[:, 128 * k : 128 * (k + 1)]
+        quarters[to, :, 128:256] = states[:, 512 + 128 * k : 512 + 128 * (k + 1)]
     head_rows = head[...].astype(F32)
     wide_head = jnp.concatenate([head_rows[k : k + 1] for k in range(8)], axis=1).astype(BF)
     score = lax.dot_general(
@@ -75,21 +82,31 @@
     slots[...] = target * SLOT + rank.astype(jnp.int32)
 
 
-def terms_kernel(own, other, weights, dir_t, out, pay):
-    core, sec = lax.axis_index("core"), lax.axis_index("sec")
+def pack_kernel(quarters, d0, d1, d2, d3, *outs):
+    for k in range(4):
+        outs[k][0:256, :] = quarters[k]
+        for q, block in enumerate((d0, d1, d2, d3)):
+            outs[k][256 + 128 * q : 384 + 128 * q, :] = block[...]
+
+
+def terms_kernel(s0, s1, s2, s3, other, weights, out, pay):
+    shares = (s0, s1, s2, s3)
+    zh, core, sec = (lax.axis_index(name) for name in ("zh", "core", "sec"))
     acc = [jnp.zeros((2, 256), F32) for _ in range(4)]
-    for z in range(4):
-        mats = []
-        for u in (core, 1 - core):
-            mats.append(
-                jnp.concatenate(
-                    [weights[u * 8 + z, 0:256, :], weights[u * 8 + 4 + z, 0:256, :]], axis=1
-                )
+    for q in range(4):
+        zz = (zh - q) & 3
+        mats = [
+            jnp.concatenate(
+                [weights[handler(zh, 2 * u + h, zz), 0:256, :] for h in range(2)], axis=1
             )
-        for s in range(4):
-            key = lax.dot_general(mats[0], own[s], NT, preferred_element_type=F32)
-            key += lax.dot_general(mats[1], other[s], NT, preferred_element_type=F32)
-            wide = dir_t[lax.rem(sec - s + 4, 4), z].astype(F32)
+            for u in (core, 1 - core)
+        ]
+        for s, share in enumerate(shares):
+            key = lax.dot_general(mats[0], share[0:256, :], NT, preferred_element_type=F32)
+            key += lax.dot_general(
+                mats[1], other[256 * s : 256 * (s + 1), :], NT, preferred_element_type=F32
+            )
+            wide = share[256 + 128 * q : 384 + 128 * q, :].astype(F32)
             acc[s] += jnp.concatenate(
                 [
                     jnp.sum(wide * key[0:128], axis=0, keepdims=True),
@@ -115,8 +132,10 @@
         out[d] = whole
 
 
-def grads_kernel(pays, own, other, dir_t, old_logp, slots, out, change, coefs):
-    core, dp, sec = lax.axis_index("core"), dp_index(), lax.axis_index("sec")
+def grads_kernel(pays, s0, s1, s2, s3, other, old_logp, slots, out, change, coefs):
+    shares = (s0, s1, s2, s3)
+    zh, core, sec = (lax.axis_index(name) for name in ("zh", "core", "sec"))
+    dp = dp_index()
     terms = pays[0, 0:16, :]
     for d in range(1, 32):
         terms = terms + pays[d, 0:16, :]
@@ -155,18 +174,24 @@
         row = jnp.concatenate(
             [coefs[pl.ds(2 * at, 1), :], coefs[pl.ds(2 * at + 1, 1), :]], axis=1
         )
-        for z in range(4):
-            change[128 * z : 128 * (z + 1), 256 * s : 256 * (s + 1)] = (
-                dir_t[at, z].astype(F32) * row
+        for q in range(4):
+            change[128 * q : 128 * (q + 1), 256 * s : 256 * (s + 1)] = (
+                shares[s][256 + 128 * q : 384 + 128 * q, :].astype(F32) * row
             ).astype(BF)
-    for u, part in ((core, own), (1 - core, other)):
-        grad = jnp.dot(
-            change[...], part[...].reshape(1024, 256), preferred_element_type=F32
-        ).astype(BF)
-        for v in range(2):
-            for z in range(4):
-                out[u * 8 + v * 4 + z, 0:128, :] = grad[
-                    128 * z : 128 * (z + 1), 128 * v : 128 * (v + 1)
+    grads = [
+        jnp.dot(change[:, 0:256], s0[0:256, :], preferred_element_type=F32),
+        jnp.dot(change[...], other[...], preferred_element_type=F32),
+    ]
+    for s in range(1, 4):
+        grads[0] += jnp.dot(
+            change[:, 256 * s : 256 * (s + 1)], shares[s][0:256, :], preferred_element_type=F32
+        )
+    for u, grad in ((core, grads[0]), (1 - core, grads[1])):
+        grad = grad.astype(BF)
+        for h in range(2):
+            for q in range(4):
+                out[handler(zh, 2 * u + h, (zh - q) & 3), 0:128, :] = grad[
+                    128 * q : 128 * (q + 1), 128 * h : 128 * (h + 1)
                 ]
     at = lax.broadcasted_iota(jnp.int32, (8, 128), 0)
     old = old_logp[...].astype(F32)
@@ -236,74 +261,72 @@
 
 
 TO_HANDLER = [
-    (
-        flat(i, zh, core, sec),
-        flat(((i >> 1) & 1) * 8 + (sec & 1) * 4 + zh, i >> 2, core, 2 * (i & 1) + (sec >> 1)),
-    )
+    (flat(i, zz, core, sec), flat(handler(i >> 2, i & 3, zz), i >> 2, core, sec))
     for i in range(16)
-    for zh in range(4)
+    for zz in range(4)
     for core in range(2)
     for sec in range(4)
 ]
 TO_OWNER = [(b, a) for a, b in TO_HANDLER]
 
 
+def ring(step):
+    return [(j, (j + step) % 4) for j in range(4)]
+
+
 def body(
     states, direction, old_logp, lengths, group_ids, routes, reward_head, policy_k, reference_k
 ):
-    quarters, dir_t, w_t, extra, slots = call(
+    dir_t, w_t = call(
+        turn_kernel,
+        (shape((128, 256), BF), shape((256, 128), BF)),
+        inputs=3,
+        flops=1 << 16,
+        size=1 << 18,
+        vmem_mib=60,
+    )(direction, policy_k, reference_k)
+    w_here = lax.ppermute(w_t, ALL, TO_HANDLER)
+    quarters, extra, slots = call(
         prepare_kernel,
-        (
-            shape((4, 256, 256), BF),
-            shape((4, 128, 256), BF),
-            shape((256, 128), BF),
-            shape((16, 128), BF),
-            shape((1, 256), jnp.int32),
-        ),
+        (shape((4, 256, 256), BF), shape((16, 128), BF), shape((1, 256), jnp.int32)),
         smem=2,
-        inputs=6,
+        inputs=3,
         flops=8 * 256 * 1024 * 2,
         size=1 << 20,
         vmem_mib=60,
-    )(
-        lengths,
-        group_ids,
-        states,
-        direction,
-        reward_head.reshape(8, 128),
-        routes.reshape(1, 256),
-        policy_k,
-        reference_k,
-    )
-    w_here = lax.ppermute(w_t, ALL, TO_HANDLER)
-    dirs = lax.all_to_all(dir_t, "zh", 0, 0, tiled=True)
-    dirs = lax.all_gather(dirs, "sec", axis=0, tiled=True).reshape(4, 4, 128, 256)
-    own = [quarters[0]] + [
-        lax.ppermute(quarters[k], "sec", [(j, (j + k) % 4) for j in range(4)]) for k in (1, 2, 3)
-    ]
-    own = jnp.stack(own)
-    other = lax.ppermute(own, "core", [(0, 1), (1, 0)])
-    w_pack = jnp.concatenate([w_here, extra], axis=0)
+    )(lengths, group_ids, states, reward_head.reshape(8, 128), routes.reshape(1, 256))
     weights = lax.all_to_all(
-        jnp.broadcast_to(w_pack[None], (16, 272, 128)), DP, 0, 0, tiled=True
+        jnp.broadcast_to(jnp.concatenate([w_here, extra], axis=0)[None], (16, 272, 128)),
+        DP,
+        0,
+        0,
+        tiled=True,
+    )
+    blocks = [dir_t] + [lax.ppermute(dir_t, "zh", ring(k)) for k in (1, 2, 3)]
+    packs = call(
+        pack_kernel, (shape((768, 256), BF),) * 4, inputs=5, flops=1 << 10, size=3 << 20
+    )(quarters, *blocks)
+    shares = [packs[0]] + [lax.ppermute(packs[k], "sec", ring(k)) for k in (1, 2, 3)]
+    other = lax.ppermute(
+        jnp.concatenate([share[0:256] for share in shares], axis=0), "core", [(0, 1), (1, 0)]
     )
     pays = call(
         terms_kernel,
         shape((32, 24, 128), F32),
         scratch=[pltpu.VMEM((24, 128), F32)],
-        inputs=4,
+        inputs=6,
         flops=1 << 30,
         size=4 << 20,
-    )(own, other, weights, dirs)
+    )(*shares, other, weights)
     pays = lax.all_to_all(pays, ("zh", "core", "sec"), 0, 0, tiled=True)
     parts = call(
         grads_kernel,
         shape((16, 144, 128), BF),
         scratch=[pltpu.VMEM((512, 1024), BF), pltpu.VMEM((8, 128), F32)],
-        inputs=6,
+        inputs=8,
         flops=1 << 29,
         size=4 << 20,
-    )(pays, own, other, dirs, old_logp.reshape(2, 128), slots)
+    )(pays, *shares, other, old_logp.reshape(2, 128), slots)
     parts = lax.all_to_all(parts, DP, 0, 0, tiled=True)
     grad, packed = call(
         finish_kernel,

time: 157 us -> 142 us (0.904)
  the two profiles are of different devices: /device:TPU:70 before, /device:TPU:72 now
where the time goes in v3:
time: 142 us; the launch traced here: 141 us
  blocking collectives  52.3 us (37%)
  starting transfers between devices  50.2 us (35%)
  waiting for transfers between devices  27.9 us (20%)
  Pallas kernels  7.16 us (5%)
  local copies, waits for them, and re-layouts  1.85 us (1%)
    all_to_all x1, blocking collectives, body(): parts = lax.all_to_all(parts, DP, 0, 0, tiled=True)  31.1 us
    all_to_all x1, blocking collectives, body(): pays = lax.all_to_all(pays, ('zh', 'core', 'sec'), 0, 0, tiled=True)  21.2 us
    ppermute x3, starting transfers between devices, body(): blocks = [dir_t] + [lax.ppermute(dir_t, 'zh', ring(k)) for k in (1, 2, 3)]  15.5 us
    ppermute x1, starting transfers between devices, body(): w_here = lax.ppermute(w_t, ALL, TO_HANDLER)  12.7 us
    ppermute x3, starting transfers between devices, body(): lax.ppermute(packs[k], 'sec', ring(k))  11.4 us
    ppermute x1, waiting for transfers between devices, body(): return (lax.ppermute(grad, ALL, TO_OWNER), packed.reshape(1, 1, 320))  11.1 us
    ppermute x3, waiting for transfers between devices, body(): lax.ppermute(packs[k], 'sec', ring(k))  10.5 us
    all_to_all x1, starting transfers between devices, body(): lax.all_to_all(jnp.broadcast_to(jnp.concatenate([w_here, extra], axis=0)[...  6.8 us
  transfers between devices with their start and end apart: 10, of which 7 were waited for; matrix products, arithmetic and copies ran while one was open for 0% of the time, Pallas kernels for 2%

profile of v3, /device:TPU:72, one launch (start us, length us, event | category | flops | bytes accessed | tf_op | source)
XLA Modules:
  0.0 141.0 jit_solution(6944922944857941542)
XLA Ops:
  0.6 1.6 %shard_map.105 = (bf16[128,256]{1,0:T(8,128)(2,1)}, bf16[256,128]{1,0:T(8,128)(2,1)}) custom-call(bf16[256,128]{1,0:T(8,128)(2,1)} %direction.1, bf16[128,128]{1,0:T(8,128)(2,1)} %wp.1, bf16[128,128]{1,0:T(8,128)(2,1)} %wr.1), custom_call_target="tpu_custom_call" | custom-call | flops 65536 | bytes 262144 | tf_op jit(solution)/shard_map/pallas_call | solution.py:280
  2.2 12.7 %collective-permute-start.7 = (bf16[256,128]{1,0:T(8,128)(2,1)}, bf16[256,128]{1,0:T(8,128)(2,1)S(1)}, u32[]{:S(2)}, u32[]{:S(2)}) collective-permute-start(bf16[256,128]{1,0:T(8,128)(2,1)} %get-tuple-element.19), channel_id=1, source_target_pairs={{0,0},{1,1},{2,2},{3,3},{4,4},{5,5},{6,6},{7,7},{8,256},{9,257},{1... | collective-permute-start | bytes 196616 | tf_op jit(solution)/shard_map/ppermute | solution.py:288
  14.9 2.2 %shard_map.104 = (bf16[4,256,256]{2,1,0:T(8,128)(2,1)}, bf16[16,128]{1,0:T(8,128)(2,1)}, s32[1,256]{1,0:T(1,128)}) custom-call(s32[2]{0:T(128)} %lengths.1, s32[2]{0:T(128)} %group_ids.1, bf16[256,1024]{1,0:T(8,128)(2,1)} %states.1, bf16[8,128]{1,0:T(8,128)(2,1)} %bitcast.5, s32[1,256]{1,0:T(1,128)} %bitcast.6), custom_call_target="tpu_custom_call" | custom-call | flops 4194304 | bytes 1048576 | tf_op jit(solution)/shard_map/pallas_call | solution.py:289
  17.1 0.0 collective-permute-done.7
  17.1 0.7 pad_maximum_fusion.1
  17.8 1.2 broadcast_in_dim.2
  19.0 0.0 copy-start.1
  19.0 0.0 copy-start
  19.0 6.8 %all-to-all-start = ((bf16[16,272,128]{2,1,0:T(8,128)(2,1)}), bf16[16,272,128]{2,1,0:T(8,128)(2,1)S(1)}, u32[]{:S(2)}, u32[]{:S(2)}) async-start(bf16[16,272,128]{2,1,0:T(8,128)(2,1)} %broadcast_in_dim.2), calls=%async_computation | async-start | bytes 2228224 | tf_op jit(solution)/shard_map/all_to_all | solution.py:298
  25.8 0.0 copy-done.1
  25.8 6.4 %collective-permute-start.2 = (bf16[128,256]{1,0:T(8,128)(2,1)S(1)}, bf16[128,256]{1,0:T(8,128)(2,1)S(1)}, u32[]{:S(2)}, u32[]{:S(2)}) collective-permute-start(bf16[128,256]{1,0:T(8,128)(2,1)S(1)} %copy-done.1), channel_id=1, source_target_pairs={{0,24},{8,0},{16,8},{24,16},{1,25},{9,1},{17,9},{25,17},{2,26},{10... | collective-permute-start | bytes 196616 | tf_op jit(solution)/shard_map/ppermute | solution.py:305
  32.2 4.3 %collective-permute-start.1 = (bf16[128,256]{1,0:T(8,128)(2,1)S(1)}, bf16[128,256]{1,0:T(8,128)(2,1)S(1)}, u32[]{:S(2)}, u32[]{:S(2)}) collective-permute-start(bf16[128,256]{1,0:T(8,128)(2,1)S(1)} %copy-done.1), channel_id=1, source_target_pairs={{0,16},{8,24},{16,0},{24,8},{1,17},{9,25},{17,1},{25,9},{2,18},{10... | collective-permute-start | bytes 196616 | tf_op jit(solution)/shard_map/ppermute | solution.py:305
  36.5 4.8 %collective-permute-start = (bf16[128,256]{1,0:T(8,128)(2,1)S(1)}, bf16[128,256]{1,0:T(8,128)(2,1)S(1)}, u32[]{:S(2)}, u32[]{:S(2)}) collective-permute-start(bf16[128,256]{1,0:T(8,128)(2,1)S(1)} %copy-done.1), channel_id=1, source_target_pairs={{0,8},{8,16},{16,24},{24,0},{1,9},{9,17},{17,25},{25,1},{2,10},{10... | collective-permute-start | bytes 196616 | tf_op jit(solution)/shard_map/ppermute | solution.py:305
  41.3 0.0 collective-permute-done.2.d3
  41.3 3.0 %collective-permute-done.1.d2 = bf16[128,256]{1,0:T(8,128)(2,1)S(1)} collective-permute-done((bf16[128,256]{1,0:T(8,128)(2,1)S(1)}, bf16[128,256]{1,0:T(8,128)(2,1)S(1)}, u32[]{:S(2)}, u32[]{:S(2)}) %collective-permute-start.1) | collective-permute-done | bytes 65568 | tf_op jit(solution)/shard_map/ppermute | solution.py:305
  44.4 1.4 collective-permute-done.d1
  45.8 0.0 copy-done
  45.8 0.1 shard_map.106
  45.9 3.4 %collective-permute-start.3 = (bf16[768,256]{1,0:T(8,128)(2,1)S(1)}, bf16[768,256]{1,0:T(8,128)(2,1)S(1)}, u32[]{:S(2)}, u32[]{:S(2)}) collective-permute-start(bf16[768,256]{1,0:T(8,128)(2,1)S(1)} %get-tuple-element.16), channel_id=1, source_target_pairs={{0,1},{1,2},{2,3},{3,0},{4,5},{5,6},{6,7},{7,4},{8,9},{9,10},{10,1... | collective-permute-start | bytes 1179656 | tf_op jit(solution)/shard_map/ppermute | solution.py:309
  49.3 4.6 %collective-permute-start.4 = (bf16[768,256]{1,0:T(8,128)(2,1)S(1)}, bf16[768,256]{1,0:T(8,128)(2,1)S(1)}, u32[]{:S(2)}, u32[]{:S(2)}) collective-permute-start(bf16[768,256]{1,0:T(8,128)(2,1)S(1)} %get-tuple-element.17), channel_id=1, source_target_pairs={{0,2},{1,3},{2,0},{3,1},{4,6},{5,7},{6,4},{7,5},{8,10},{9,11},{10,... | collective-permute-start | bytes 1179656 | tf_op jit(solution)/shard_map/ppermute | solution.py:309
  53.9 3.3 %collective-permute-start.5 = (bf16[768,256]{1,0:T(8,128)(2,1)S(1)}, bf16[768,256]{1,0:T(8,128)(2,1)S(1)}, u32[]{:S(2)}, u32[]{:S(2)}) collective-permute-start(bf16[768,256]{1,0:T(8,128)(2,1)S(1)} %get-tuple-element.18), channel_id=1, source_target_pairs={{0,3},{1,0},{2,1},{3,2},{4,7},{5,4},{6,5},{7,6},{8,11},{9,8},{10,9... | collective-permute-start | bytes 1179656 | tf_op jit(solution)/shard_map/ppermute | solution.py:309
  57.3 2.7 %collective-permute-done.3.s1 = bf16[768,256]{1,0:T(8,128)(2,1)S(1)} collective-permute-done((bf16[768,256]{1,0:T(8,128)(2,1)S(1)}, bf16[768,256]{1,0:T(8,128)(2,1)S(1)}, u32[]{:S(2)}, u32[]{:S(2)}) %collective-permute-start.3) | collective-permute-done | bytes 393248 | tf_op jit(solution)/shard_map/ppermute | solution.py:309
  60.1 6.2 %collective-permute-done.4.s2 = bf16[768,256]{1,0:T(8,128)(2,1)S(1)} collective-permute-done((bf16[768,256]{1,0:T(8,128)(2,1)S(1)}, bf16[768,256]{1,0:T(8,128)(2,1)S(1)}, u32[]{:S(2)}, u32[]{:S(2)}) %collective-permute-start.4) | collective-permute-done | bytes 393248 | tf_op jit(solution)/shard_map/ppermute | solution.py:309
  66.3 1.5 %collective-permute-done.5.s3 = bf16[768,256]{1,0:T(8,128)(2,1)S(1)} collective-permute-done((bf16[768,256]{1,0:T(8,128)(2,1)S(1)}, bf16[768,256]{1,0:T(8,128)(2,1)S(1)}, u32[]{:S(2)}, u32[]{:S(2)}) %collective-permute-start.5) | collective-permute-done | bytes 393248 | tf_op jit(solution)/shard_map/ppermute | solution.py:309
  67.9 0.0 copy-start.2
  67.9 0.0 copy-start.3
  67.9 1.9 %collective-permute-start.6 = (bf16[1024,256]{1,0:T(8,128)(2,1)S(1)}, bf16[1024,256]{1,0:T(8,128)(2,1)S(1)}, u32[]{:S(2)}, u32[]{:S(2)}) collective-permute-start(bf16[1024,256]{1,0:T(8,128)(2,1)S(1)} %pad_maximum_fusion), channel_id=1, source_target_pairs={{0,4},{4,0},{1,5},{5,1},{2,6},{6,2},{3,7},{7,3},{8,12},{12,8},{9,1... | collective-permute-start | bytes 1572872 | tf_op jit(solution)/shard_map/ppermute | solution.py:310
  69.8 1.9 %collective-permute-done.6.other = bf16[1024,256]{1,0:T(8,128)(2,1)S(1)} collective-permute-done((bf16[1024,256]{1,0:T(8,128)(2,1)S(1)}, bf16[1024,256]{1,0:T(8,128)(2,1)S(1)}, u32[]{:S(2)}, u32[]{:S(2)}) %collective-permute-start.6) | collective-permute-done | bytes 524320 | tf_op jit(solution)/shard_map/ppermute | solution.py:310
  71.7 0.0 all-to-all-done.weights
  71.7 1.4 shard_map.107
  73.1 21.2 %all_to_all.15.pays = f32[32,24,128]{2,1,0:T(8,128)S(1)} all-to-all(f32[32,24,128]{2,1,0:T(8,128)S(1)} %shard_map.107), channel_id=1, replica_groups=mesh['zl'=2,'y'=8,'zh'=4,'core'=2,'sec'=4] {'zh','core','sec'}, dimensions={0} | all-to-all | bytes 786432 | tf_op jit(solution)/shard_map/all_to_all | solution.py:321
  94.3 0.0 copy-done.2
  94.3 0.0 copy-done.3
  94.3 1.0 shard_map.108
  95.3 31.1 %all_to_all.16.parts = bf16[16,144,128]{2,1,0:T(8,128)(2,1)S(1)} all-to-all(bf16[16,144,128]{2,1,0:T(8,128)(2,1)S(1)} %shard_map.108), channel_id=1, replica_groups=mesh['zl'=2,'y'=8,'zh'=4,'core'=2,'sec'=4] {'zl','y'}, dimensions={0} | all-to-all | bytes 1179648 | tf_op jit(solution)/shard_map/all_to_all | solution.py:330
  126.4 0.9 shard_map.109
  127.3 1.9 %collective-permute-start.8 = (f32[128,128]{1,0:T(8,128)S(1)}, f32[128,128]{1,0:T(8,128)S(1)}, u32[]{:S(2)}, u32[]{:S(2)}) collective-permute-start(f32[128,128]{1,0:T(8,128)S(1)} %get-tuple-element.22), channel_id=1, source_target_pairs={{0,0},{1,1},{2,2},{3,3},{4,4},{5,5},{6,6},{7,7},{256,8},{257,9},{2... | collective-permute-start | bytes 196616 | tf_op jit(solution)/shard_map/ppermute | solution.py:338
  129.2 11.1 %collective-permute-done.8 = f32[128,128]{1,0:T(8,128)S(1)} collective-permute-done((f32[128,128]{1,0:T(8,128)S(1)}, f32[128,128]{1,0:T(8,128)S(1)}, u32[]{:S(2)}, u32[]{:S(2)}) %collective-permute-start.8) | collective-permute-done | bytes 65568 | tf_op jit(solution)/shard_map/ppermute | solution.py:338
  140.4 0.6 copy.12
  (5 shorter events, 0.1 us)
Async XLA Ops:
  2.2 14.9 %collective-permute-start.7 = (bf16[256,128]{1,0:T(8,128)(2,1)}, bf16[256,128]{1,0:T(8,128)(2,1)S(1)}, u32[]{:S(2)}, u32[]{:S(2)}) collective-permute-start(bf16[256,128]{1,0:T(8,128)(2,1)} %get-tuple-element.19), channel_id=1, source_target_pairs={{0,0},{1,1},{2,2},{3,3},{4,4},{5,5},{6,6},{7,7},{8,256},{9,257},{1... | collective-permute-start | bytes 196616 | tf_op jit(solution)/shard_map/ppermute | solution.py:288
  19.0 6.8 %copy-start.1 = (bf16[128,256]{1,0:T(8,128)(2,1)S(1)}, bf16[128,256]{1,0:T(8,128)(2,1)}, u32[]{:S(2)}) copy-start(bf16[128,256]{1,0:T(8,128)(2,1)} %get-tuple-element.14.d0) | copy-start | bytes 196612
  19.0 26.8 %copy-start = (bf16[4,256,256]{2,1,0:T(8,128)(2,1)S(1)}, bf16[4,256,256]{2,1,0:T(8,128)(2,1)}, u32[]{:S(2)}) copy-start(bf16[4,256,256]{2,1,0:T(8,128)(2,1)} %get-tuple-element.13.quarters) | copy-start | bytes 1572868
  19.0 52.7 %all-to-all-start = ((bf16[16,272,128]{2,1,0:T(8,128)(2,1)}), bf16[16,272,128]{2,1,0:T(8,128)(2,1)S(1)}, u32[]{:S(2)}, u32[]{:S(2)}) async-start(bf16[16,272,128]{2,1,0:T(8,128)(2,1)} %broadcast_in_dim.2), calls=%async_computation | async-start | bytes 2228224 | tf_op jit(solution)/shard_map/all_to_all | solution.py:298
  25.8 15.5 %collective-permute-start.2 = (bf16[128,256]{1,0:T(8,128)(2,1)S(1)}, bf16[128,256]{1,0:T(8,128)(2,1)S(1)}, u32[]{:S(2)}, u32[]{:S(2)}) collective-permute-start(bf16[128,256]{1,0:T(8,128)(2,1)S(1)} %copy-done.1), channel_id=1, source_target_pairs={{0,24},{8,0},{16,8},{24,16},{1,25},{9,1},{17,9},{25,17},{2,26},{10... | collective-permute-start | bytes 196616 | tf_op jit(solution)/shard_map/ppermute | solution.py:305
  32.2 12.2 %collective-permute-start.1 = (bf16[128,256]{1,0:T(8,128)(2,1)S(1)}, bf16[128,256]{1,0:T(8,128)(2,1)S(1)}, u32[]{:S(2)}, u32[]{:S(2)}) collective-permute-start(bf16[128,256]{1,0:T(8,128)(2,1)S(1)} %copy-done.1), channel_id=1, source_target_pairs={{0,16},{8,24},{16,0},{24,8},{1,17},{9,25},{17,1},{25,9},{2,18},{10... | collective-permute-start | bytes 196616 | tf_op jit(solution)/shard_map/ppermute | solution.py:305
  36.5 9.3 %collective-permute-start = (bf16[128,256]{1,0:T(8,128)(2,1)S(1)}, bf16[128,256]{1,0:T(8,128)(2,1)S(1)}, u32[]{:S(2)}, u32[]{:S(2)}) collective-permute-start(bf16[128,256]{1,0:T(8,128)(2,1)S(1)} %copy-done.1), channel_id=1, source_target_pairs={{0,8},{8,16},{16,24},{24,0},{1,9},{9,17},{17,25},{25,1},{2,10},{10... | collective-permute-start | bytes 196616 | tf_op jit(solution)/shard_map/ppermute | solution.py:305
  45.9 14.2 %collective-permute-start.3 = (bf16[768,256]{1,0:T(8,128)(2,1)S(1)}, bf16[768,256]{1,0:T(8,128)(2,1)S(1)}, u32[]{:S(2)}, u32[]{:S(2)}) collective-permute-start(bf16[768,256]{1,0:T(8,128)(2,1)S(1)} %get-tuple-element.16), channel_id=1, source_target_pairs={{0,1},{1,2},{2,3},{3,0},{4,5},{5,6},{6,7},{7,4},{8,9},{9,10},{10,1... | collective-permute-start | bytes 1179656 | tf_op jit(solution)/shard_map/ppermute | solution.py:309
  49.3 17.0 %collective-permute-start.4 = (bf16[768,256]{1,0:T(8,128)(2,1)S(1)}, bf16[768,256]{1,0:T(8,128)(2,1)S(1)}, u32[]{:S(2)}, u32[]{:S(2)}) collective-permute-start(bf16[768,256]{1,0:T(8,128)(2,1)S(1)} %get-tuple-element.17), channel_id=1, source_target_pairs={{0,2},{1,3},{2,0},{3,1},{4,6},{5,7},{6,4},{7,5},{8,10},{9,11},{10,... | collective-permute-start | bytes 1179656 | tf_op jit(solution)/shard_map/ppermute | solution.py:309
  53.9 13.9 %collective-permute-start.5 = (bf16[768,256]{1,0:T(8,128)(2,1)S(1)}, bf16[768,256]{1,0:T(8,128)(2,1)S(1)}, u32[]{:S(2)}, u32[]{:S(2)}) collective-permute-start(bf16[768,256]{1,0:T(8,128)(2,1)S(1)} %get-tuple-element.18), channel_id=1, source_target_pairs={{0,3},{1,0},{2,1},{3,2},{4,7},{5,4},{6,5},{7,6},{8,11},{9,8},{10,9... | collective-permute-start | bytes 1179656 | tf_op jit(solution)/shard_map/ppermute | solution.py:309
  67.9 26.4 %copy-start.2 = (s32[1,256]{1,0:T(1,128)S(1)}, s32[1,256]{1,0:T(1,128)}, u32[]{:S(2)}) copy-start(s32[1,256]{1,0:T(1,128)} %get-tuple-element.21.slots) | copy-start | bytes 3076
  67.9 26.4 %copy-start.3 = (bf16[256]{0:T(256)(128)(2,1)S(1)}, bf16[256]{0:T(256)(128)(2,1)}, u32[]{:S(2)}) copy-start(bf16[256]{0:T(256)(128)(2,1)} %param.11) | copy-start | bytes 1540
  67.9 3.8 %collective-permute-start.6 = (bf16[1024,256]{1,0:T(8,128)(2,1)S(1)}, bf16[1024,256]{1,0:T(8,128)(2,1)S(1)}, u32[]{:S(2)}, u32[]{:S(2)}) collective-permute-start(bf16[1024,256]{1,0:T(8,128)(2,1)S(1)} %pad_maximum_fusion), channel_id=1, source_target_pairs={{0,4},{4,0},{1,5},{5,1},{2,6},{6,2},{3,7},{7,3},{8,12},{12,8},{9,1... | collective-permute-start | bytes 1572872 | tf_op jit(solution)/shard_map/ppermute | solution.py:310
  127.3 13.1 %collective-permute-start.8 = (f32[128,128]{1,0:T(8,128)S(1)}, f32[128,128]{1,0:T(8,128)S(1)}, u32[]{:S(2)}, u32[]{:S(2)}) collective-permute-start(f32[128,128]{1,0:T(8,128)S(1)} %get-tuple-element.22), channel_id=1, source_target_pairs={{0,0},{1,1},{2,2},{3,3},{4,4},{5,5},{6,6},{7,7},{256,8},{257,9},{2... | collective-permute-start | bytes 196616 | tf_op jit(solution)/shard_map/ppermute | solution.py:338

commit v4 on v3

--- a/solution.py
+++ b/solution.py
@@ -87,6 +87,12 @@
         outs[k][0:256, :] = quarters[k]
         for q, block in enumerate((d0, d1, d2, d3)):
             outs[k][256 + 128 * q : 384 + 128 * q, :] = block[...]
+
+
+def spread_kernel(w, extra, out):
+    for k in range(16):
+        out[k, 0:256, :] = w[...]
+        out[k, 256:272, :] = extra[...]
 
 
 def terms_kernel(s0, s1, s2, s3, other, weights, out, pay):
@@ -116,42 +122,50 @@
             )
     for s in range(4):
         for p in range(2):
-            for q in range(2):
-                n = 8 * p + 2 * lax.rem(sec - s + 4, 4) + q
-                pay[pl.ds(n, 1), :] = acc[s][p : p + 1, 128 * q : 128 * (q + 1)]
+            pay[0:1, 1024 * p + 256 * s : 1024 * p + 256 * (s + 1)] = acc[s][p : p + 1]
     lane = lax.broadcasted_iota(jnp.int32, (16, 128), 1)
     block = jnp.zeros((16, 128), F32)
     for i in range(16):
-        block = jnp.where(lane == i, weights[i, 256:272, :].astype(F32), block)
-    pay[16:17, :] = block[0:1] + block[1:2] + block[2:3]
-    pay[17:18, :] = block[3:4] + block[4:5] + block[5:6]
-    pay[18:22, :] = block[6:10]
-    pay[22:24, :] = jnp.zeros((2, 128), F32)
+        block = jnp.where((lane & 15) == i, weights[i, 256:272, :].astype(F32), block)
+    fields = [block[0:1] + block[1:2] + block[2:3], block[3:4] + block[4:5] + block[5:6]]
+    fields.extend(block[n : n + 1] for n in range(6, 10))
+    facts = jnp.zeros((1, 128), F32)
+    for n, field in enumerate(fields):
+        facts = jnp.where((lane[0:1] >> 4) == n, field, facts)
+    pay[0:1, 2048:2176] = facts
     whole = pay[...]
     for d in range(32):
         out[d] = whole
 
 
-def grads_kernel(pays, s0, s1, s2, s3, other, old_logp, slots, out, change, coefs):
+def grads_kernel(pays, s0, s1, s2, s3, other, old_logp, slots, out, sums, change, coefs):
     shares = (s0, s1, s2, s3)
     zh, core, sec = (lax.axis_index(name) for name in ("zh", "core", "sec"))
     dp = dp_index()
-    terms = pays[0, 0:16, :]
-    for d in range(1, 32):
-        terms = terms + pays[d, 0:16, :]
-    tp, tr = terms[0:8], terms[8:16]
+    for s in range(4):
+        for p in range(2):
+            total = jnp.zeros((1, 256), F32)
+            for d in range(32):
+                k = (d - s) & 3
+                total += pays[d, 0:1, 1024 * p + 256 * k : 1024 * p + 256 * (k + 1)]
+            for q in range(2):
+                n = 8 * p + 4 * q + s
+                sums[n : n + 1, :] = total[:, 128 * q : 128 * (q + 1)]
+    tp, tr = sums[0:8, :], sums[8:16, :]
     facts = []
     for s in range(4):
-        fact = pays[s, 16:24, :]
+        fact = pays[s, 0:1, 2048:2176]
         for d in range(1, 8):
-            fact = fact + pays[4 * d + s, 16:24, :]
+            fact = fact + pays[4 * d + s, 0:1, 2048:2176]
         facts.append(fact)
+    facts = jnp.concatenate(facts + facts, axis=0)
     lane = lax.broadcasted_iota(jnp.int32, (8, 128), 1)
+    at = lax.broadcasted_iota(jnp.int32, (8, 128), 0)
+    facts = jnp.where(at < 4, facts, pltpu.roll(facts, 112, 1))
     used = lane < 16
-    sums = jnp.concatenate([f[0:2] for f in facts], axis=0)
-    ids = jnp.concatenate([f[2:4] for f in facts], axis=0) * 0.125
-    lens = jnp.where(used, jnp.concatenate([f[4:6] for f in facts], axis=0) * 0.125, 1.0)
-    reward = sums / jnp.sqrt(lens)
+    ids = pltpu.roll(facts, 96, 1) * 0.125
+    lens = jnp.where(used, pltpu.roll(facts, 64, 1) * 0.125, 1.0)
+    reward = facts / jnp.sqrt(lens)
     center = jnp.zeros((8, 128), F32)
     spread = jnp.zeros((8, 128), F32)
     for g in range(NGROUPS):
@@ -170,9 +184,9 @@
     coef = valid * (-adv * jnp.exp(tp) + kl_weight * (1.0 - jnp.exp(tr - tp)))
     coefs[...] = coef
     for s in range(4):
-        at = lax.rem(sec - s + 4, 4)
+        from_sec = (sec - s) & 3
         row = jnp.concatenate(
-            [coefs[pl.ds(2 * at, 1), :], coefs[pl.ds(2 * at + 1, 1), :]], axis=1
+            [coefs[pl.ds(from_sec, 1), :], coefs[pl.ds(4 + from_sec, 1), :]], axis=1
         )
         for q in range(4):
             change[128 * q : 128 * (q + 1), 256 * s : 256 * (s + 1)] = (
@@ -193,11 +207,10 @@
                 out[handler(zh, 2 * u + h, (zh - q) & 3), 0:128, :] = grad[
                     128 * q : 128 * (q + 1), 128 * h : 128 * (h + 1)
                 ]
-    at = lax.broadcasted_iota(jnp.int32, (8, 128), 0)
     old = old_logp[...].astype(F32)
     logp = jnp.concatenate(
         [
-            old[q : q + 1] + jnp.sum(jnp.where(at == 2 * sec + q, tp, 0.0), axis=0, keepdims=True)
+            old[q : q + 1] + jnp.sum(jnp.where(at == 4 * q + sec, tp, 0.0), axis=0, keepdims=True)
             for q in range(2)
         ],
         axis=1,
@@ -206,13 +219,10 @@
     rows = jnp.concatenate([hi, mid, lo, jnp.zeros((5, 256), F32)], axis=0).astype(BF)
     place = (lax.broadcasted_iota(jnp.int32, (16 * SLOT, 256), 0) == slots[...]).astype(F32)
     placed = lax.dot_general(rows, place.astype(BF), NT, preferred_element_type=F32)
-    tail = jnp.concatenate(
-        [placed[h : h + 1, 128 * a : 128 * (a + 1)] for h in range(3) for a in range(4)]
-        + [jnp.zeros((4, 128), F32)],
-        axis=0,
-    ).astype(BF)
-    for k in range(16):
-        out[k, 128:144, :] = tail
+    for a in range(4):
+        tail = placed[:, 128 * a : 128 * (a + 1)].astype(BF)
+        for k in range(4):
+            out[4 * a + k, 128:136, :] = tail
 
 
 def finish_kernel(parts, grad, packed):
@@ -221,12 +231,9 @@
     for i in range(1, 16):
         total = total + parts[i, 0:128, :].astype(F32)
     grad[...] = total.T
-    at = lax.broadcasted_iota(jnp.int32, (16, 128), 0)
-    mine = (at < 12) & (lax.rem(at, 4) == dp // 4)
-    rows = []
-    for i in range(16):
-        tail = jnp.where(mine, parts[i, 128:144, :].astype(F32), 0.0)
-        rows.append(jnp.sum(tail, axis=0, keepdims=True))
+    rows = [
+        jnp.sum(parts[i, 128:136, :].astype(F32), axis=0, keepdims=True) for i in range(16)
+    ]
     table = jnp.concatenate(rows, axis=0)
     pick = jnp.zeros((16, SLOT), F32)
     for a in range(4):
@@ -295,14 +302,12 @@
         size=1 << 20,
         vmem_mib=60,
     )(lengths, group_ids, states, reward_head.reshape(8, 128), routes.reshape(1, 256))
-    weights = lax.all_to_all(
-        jnp.broadcast_to(jnp.concatenate([w_here, extra], axis=0)[None], (16, 272, 128)),
-        DP,
-        0,
-        0,
-        tiled=True,
-    )
     blocks = [dir_t] + [lax.ppermute(dir_t, "zh", ring(k)) for k in (1, 2, 3)]
+    w_here, *blocks = lax.optimization_barrier((w_here, *blocks))
+    weights = call(
+        spread_kernel, shape((16, 272, 128), BF), inputs=2, flops=1 << 10, size=1 << 20
+    )(w_here, extra)
+    weights = lax.all_to_all(weights, DP, 0, 0, tiled=True)
     packs = call(
         pack_kernel, (shape((768, 256), BF),) * 4, inputs=5, flops=1 << 10, size=3 << 20
     )(quarters, *blocks)
@@ -312,8 +317,8 @@
     )
     pays = call(
         terms_kernel,
-        shape((32, 24, 128), F32),
-        scratch=[pltpu.VMEM((24, 128), F32)],
+        shape((32, 1, 2176), F32),
+        scratch=[pltpu.VMEM((1, 2176), F32)],
         inputs=6,
         flops=1 << 30,
         size=4 << 20,
@@ -321,8 +326,12 @@
     pays = lax.all_to_all(pays, ("zh", "core", "sec"), 0, 0, tiled=True)
     parts = call(
         grads_kernel,
-        shape((16, 144, 128), BF),
-        scratch=[pltpu.VMEM((512, 1024), BF), pltpu.VMEM((8, 128), F32)],
+        shape((16, 136, 128), BF),
+        scratch=[
+            pltpu.VMEM((16, 128), F32),
+            pltpu.VMEM((512, 1024), BF),
+            pltpu.VMEM((8, 128), F32),
+        ],
         inputs=8,
         flops=1 << 29,
         size=4 << 20,

time: 142 us -> 129 us (0.908)
  blocking collectives: 52.3 us -> 44.8 us
  starting transfers between devices: 50.2 us -> 46.4 us
  waiting for transfers between devices: 27.9 us -> 26.3 us
    all_to_all x1, blocking collectives: 31.1 us -> 24.9 us  [body(): parts = lax.all_to_all(parts, DP, 0, 0, tiled=True)]
    ppermute x3, starting transfers between devices: 15.5 us -> 9.57 us  [body(): blocks = [dir_t] + [lax.ppermute(dir_t, 'zh', ring(k)) for k in (1, 2, 3)]]
    all_to_all x1, starting transfers between devices: 6.8 us -> 8.45 us  [body(): weights = lax.all_to_all(weights, DP, 0, 0, tiled=True)]
    ppermute x3, waiting for transfers between devices: 4.42 us -> 2.91 us  [body(): blocks = [dir_t] + [lax.ppermute(dir_t, 'zh', ring(k)) for k in (1, 2, 3)]]
    pallas_call x2 -> x3, Pallas kernels: 2.34 us -> 3.63 us  [the longest x1 1.37 us: body(): call(terms_kernel, shape((32, 1, 2176), F32), scratch=[pltpu.VMEM((1, 217...]
  transfers between devices with their start and end apart: 10 -> 10, of which waited for: 7 -> 6; matrix products, arithmetic and copies ran while one was open for 0% -> 0% of each run, Pallas kernels for 2% -> 2%
where the time goes in v4:
time: 129 us; the launch traced here: 128 us
  starting transfers between devices  46.4 us (36%)
  blocking collectives  44.8 us (35%)
  waiting for transfers between devices  26.3 us (20%)
  Pallas kernels  8.45 us (7%)
  local copies, waits for them, and re-layouts  1.36 us (1%)
    all_to_all x1, blocking collectives, body(): parts = lax.all_to_all(parts, DP, 0, 0, tiled=True)  24.9 us
    all_to_all x1, blocking collectives, body(): pays = lax.all_to_all(pays, ('zh', 'core', 'sec'), 0, 0, tiled=True)  19.9 us
    ppermute x1, starting transfers between devices, body(): w_here = lax.ppermute(w_t, ALL, TO_HANDLER)  12.7 us
    ppermute x3, starting transfers between devices, body(): lax.ppermute(packs[k], 'sec', ring(k))  11.4 us
    ppermute x3, waiting for transfers between devices, body(): lax.ppermute(packs[k], 'sec', ring(k))  10.9 us
    ppermute x1, waiting for transfers between devices, body(): return (lax.ppermute(grad, ALL, TO_OWNER), packed.reshape(1, 1, 320))  10.6 us
    ppermute x3, starting transfers between devices, body(): blocks = [dir_t] + [lax.ppermute(dir_t, 'zh', ring(k)) for k in (1, 2, 3)]  9.57 us
    all_to_all x1, starting transfers between devices, body(): weights = lax.all_to_all(weights, DP, 0, 0, tiled=True)  8.45 us
  transfers between devices with their start and end apart: 10, of which 6 were waited for; matrix products, arithmetic and copies ran while one was open for 0% of the time, Pallas kernels for 2%

profile of v4, /device:TPU:72, one launch (start us, length us, event | category | flops | bytes accessed | tf_op | source)
XLA Modules:
  0.0 128.2 jit_solution(1728677834400817491)
XLA Ops:
  0.6 1.6 %shard_map.105 = (bf16[128,256]{1,0:T(8,128)(2,1)}, bf16[256,128]{1,0:T(8,128)(2,1)}) custom-call(bf16[256,128]{1,0:T(8,128)(2,1)} %direction.1, bf16[128,128]{1,0:T(8,128)(2,1)} %wp.1, bf16[128,128]{1,0:T(8,128)(2,1)} %wr.1), custom_call_target="tpu_custom_call" | custom-call | flops 65536 | bytes 262144 | tf_op jit(solution)/shard_map/pallas_call | solution.py:287
  2.2 12.7 %collective-permute-start = (bf16[256,128]{1,0:T(8,128)(2,1)}, bf16[256,128]{1,0:T(8,128)(2,1)S(1)}, u32[]{:S(2)}, u32[]{:S(2)}) collective-permute-start(bf16[256,128]{1,0:T(8,128)(2,1)} %get-tuple-element.19), channel_id=1, source_target_pairs={{0,0},{1,1},{2,2},{3,3},{4,4},{5,5},{6,6},{7,7},{8,256},{9,257},{1... | collective-permute-start | bytes 196616 | tf_op jit(solution)/shard_map/ppermute | solution.py:295
  14.9 3.4 %collective-permute-start.3 = (bf16[128,256]{1,0:T(8,128)(2,1)}, bf16[128,256]{1,0:T(8,128)(2,1)S(1)}, u32[]{:S(2)}, u32[]{:S(2)}) collective-permute-start(bf16[128,256]{1,0:T(8,128)(2,1)} %get-tuple-element.21.d0), channel_id=1, source_target_pairs={{0,24},{8,0},{16,8},{24,16},{1,25},{9,1},{17,9},{25,17},{2,26},{10... | collective-permute-start | bytes 196616 | tf_op jit(solution)/shard_map/ppermute | solution.py:305
  18.3 1.9 %collective-permute-start.2 = (bf16[128,256]{1,0:T(8,128)(2,1)}, bf16[128,256]{1,0:T(8,128)(2,1)S(1)}, u32[]{:S(2)}, u32[]{:S(2)}) collective-permute-start(bf16[128,256]{1,0:T(8,128)(2,1)} %get-tuple-element.21.d0), channel_id=1, source_target_pairs={{0,16},{8,24},{16,0},{24,8},{1,17},{9,25},{17,1},{25,9},{2,18},{10... | collective-permute-start | bytes 196616 | tf_op jit(solution)/shard_map/ppermute | solution.py:305
  20.2 4.3 %collective-permute-start.1 = (bf16[128,256]{1,0:T(8,128)(2,1)}, bf16[128,256]{1,0:T(8,128)(2,1)S(1)}, u32[]{:S(2)}, u32[]{:S(2)}) collective-permute-start(bf16[128,256]{1,0:T(8,128)(2,1)} %get-tuple-element.21.d0), channel_id=1, source_target_pairs={{0,8},{8,16},{16,24},{24,0},{1,9},{9,17},{17,25},{25,1},{2,10},{10... | collective-permute-start | bytes 196616 | tf_op jit(solution)/shard_map/ppermute | solution.py:305
  24.5 2.2 %shard_map.104 = (bf16[4,256,256]{2,1,0:T(8,128)(2,1)}, bf16[16,128]{1,0:T(8,128)(2,1)}, s32[1,256]{1,0:T(1,128)}) custom-call(s32[2]{0:T(128)} %lengths.1, s32[2]{0:T(128)} %group_ids.1, bf16[256,1024]{1,0:T(8,128)(2,1)} %states.1, bf16[8,128]{1,0:T(8,128)(2,1)} %bitcast.5, s32[1,256]{1,0:T(1,128)} %bitcast.6), custom_call_target="tpu_custom_call" | custom-call | flops 4194304 | bytes 1048576 | tf_op jit(solution)/shard_map/pallas_call | solution.py:296
  26.7 0.0 collective-permute-done.w
  26.7 0.0 collective-permute-done.3.d3
  26.7 2.9 %collective-permute-done.2.d2 = bf16[128,256]{1,0:T(8,128)(2,1)S(1)} collective-permute-done((bf16[128,256]{1,0:T(8,128)(2,1)}, bf16[128,256]{1,0:T(8,128)(2,1)S(1)}, u32[]{:S(2)}, u32[]{:S(2)}) %collective-permute-start.2) | collective-permute-done | bytes 65568 | tf_op jit(solution)/shard_map/ppermute | solution.py:305
  29.6 0.0 collective-permute-done.1.d1
  29.6 0.0 copy-start.2
  29.6 0.7 copy-done.2
  30.3 1.2 shard_map.107
  31.5 0.0 copy-start
  31.5 0.0 copy-start.1
  31.5 8.5 %all-to-all-start = ((bf16[16,272,128]{2,1,0:T(8,128)(2,1)}), bf16[16,272,128]{2,1,0:T(8,128)(2,1)S(1)}, u32[]{:S(2)}, u32[]{:S(2)}) async-start(bf16[16,272,128]{2,1,0:T(8,128)(2,1)} %shard_map.107), calls=%async_computation | async-start | bytes 2228224 | tf_op jit(solution)/shard_map/all_to_all | solution.py:310
  39.9 0.0 copy-done
  39.9 0.0 copy-done.1
  40.0 0.1 shard_map.106
  40.1 3.4 %collective-permute-start.4 = (bf16[768,256]{1,0:T(8,128)(2,1)S(1)}, bf16[768,256]{1,0:T(8,128)(2,1)S(1)}, u32[]{:S(2)}, u32[]{:S(2)}) collective-permute-start(bf16[768,256]{1,0:T(8,128)(2,1)S(1)} %get-tuple-element.26), channel_id=1, source_target_pairs={{0,1},{1,2},{2,3},{3,0},{4,5},{5,6},{6,7},{7,4},{8,9},{9,10},{10,1... | collective-permute-start | bytes 1179656 | tf_op jit(solution)/shard_map/ppermute | solution.py:314
  43.5 4.6 %collective-permute-start.5 = (bf16[768,256]{1,0:T(8,128)(2,1)S(1)}, bf16[768,256]{1,0:T(8,128)(2,1)S(1)}, u32[]{:S(2)}, u32[]{:S(2)}) collective-permute-start(bf16[768,256]{1,0:T(8,128)(2,1)S(1)} %get-tuple-element.27), channel_id=1, source_target_pairs={{0,2},{1,3},{2,0},{3,1},{4,6},{5,7},{6,4},{7,5},{8,10},{9,11},{10,... | collective-permute-start | bytes 1179656 | tf_op jit(solution)/shard_map/ppermute | solution.py:314
  48.1 3.3 %collective-permute-start.6 = (bf16[768,256]{1,0:T(8,128)(2,1)S(1)}, bf16[768,256]{1,0:T(8,128)(2,1)S(1)}, u32[]{:S(2)}, u32[]{:S(2)}) collective-permute-start(bf16[768,256]{1,0:T(8,128)(2,1)S(1)} %get-tuple-element.28), channel_id=1, source_target_pairs={{0,3},{1,0},{2,1},{3,2},{4,7},{5,4},{6,5},{7,6},{8,11},{9,8},{10,9... | collective-permute-start | bytes 1179656 | tf_op jit(solution)/shard_map/ppermute | solution.py:314
  51.5 2.7 %collective-permute-done.4.s1 = bf16[768,256]{1,0:T(8,128)(2,1)S(1)} collective-permute-done((bf16[768,256]{1,0:T(8,128)(2,1)S(1)}, bf16[768,256]{1,0:T(8,128)(2,1)S(1)}, u32[]{:S(2)}, u32[]{:S(2)}) %collective-permute-start.4) | collective-permute-done | bytes 393248 | tf_op jit(solution)/shard_map/ppermute | solution.py:314
  54.3 6.6 %collective-permute-done.5.s2 = bf16[768,256]{1,0:T(8,128)(2,1)S(1)} collective-permute-done((bf16[768,256]{1,0:T(8,128)(2,1)S(1)}, bf16[768,256]{1,0:T(8,128)(2,1)S(1)}, u32[]{:S(2)}, u32[]{:S(2)}) %collective-permute-start.5) | collective-permute-done | bytes 393248 | tf_op jit(solution)/shard_map/ppermute | solution.py:314
  60.9 1.5 %collective-permute-done.6.s3 = bf16[768,256]{1,0:T(8,128)(2,1)S(1)} collective-permute-done((bf16[768,256]{1,0:T(8,128)(2,1)S(1)}, bf16[768,256]{1,0:T(8,128)(2,1)S(1)}, u32[]{:S(2)}, u32[]{:S(2)}) %collective-permute-start.6) | collective-permute-done | bytes 393248 | tf_op jit(solution)/shard_map/ppermute | solution.py:314
  62.5 0.0 copy-start.3
  62.5 0.0 copy-start.4
  62.5 1.9 %collective-permute-start.7 = (bf16[1024,256]{1,0:T(8,128)(2,1)S(1)}, bf16[1024,256]{1,0:T(8,128)(2,1)S(1)}, u32[]{:S(2)}, u32[]{:S(2)}) collective-permute-start(bf16[1024,256]{1,0:T(8,128)(2,1)S(1)} %pad_maximum_fusion), channel_id=1, source_target_pairs={{0,4},{4,0},{1,5},{5,1},{2,6},{6,2},{3,7},{7,3},{8,12},{12,8},{9,1... | collective-permute-start | bytes 1572872 | tf_op jit(solution)/shard_map/ppermute | solution.py:315
  64.4 1.9 %collective-permute-done.7.other = bf16[1024,256]{1,0:T(8,128)(2,1)S(1)} collective-permute-done((bf16[1024,256]{1,0:T(8,128)(2,1)S(1)}, bf16[1024,256]{1,0:T(8,128)(2,1)S(1)}, u32[]{:S(2)}, u32[]{:S(2)}) %collective-permute-start.7) | collective-permute-done | bytes 524320 | tf_op jit(solution)/shard_map/ppermute | solution.py:315
  66.3 0.0 all-to-all-done.weights
  66.3 1.4 %shard_map.108 = f32[32,1,2176]{2,1,0:T(1,128)S(1)} custom-call(bf16[768,256]{1,0:T(8,128)(2,1)S(1)} %get-tuple-element.25.s0, bf16[768,256]{1,0:T(8,128)(2,1)S(1)} %collective-permute-done.4.s1, bf16[768,256]{1,0:T(8,128)(2,1)S(1)} %collective-permute-done.5.s2, bf16[768,256]{1,0:T(8,128)(2,1)S(1)} %collective-permute-done.6.s3, ...), custom_call_target="tpu_custom_call" | custom-call | flops 1073741824 | bytes 4194304 | tf_op jit(solution)/shard_map/pallas_call | solution.py:318
  67.7 19.9 %all_to_all.15.pays = f32[32,1,2176]{2,1,0:T(1,128)S(1)} all-to-all(f32[32,1,2176]{2,1,0:T(1,128)S(1)} %shard_map.108), channel_id=1, replica_groups=mesh['zl'=2,'y'=8,'zh'=4,'core'=2,'sec'=4] {'zh','core','sec'}, dimensions={0} | all-to-all | bytes 557056 | tf_op jit(solution)/shard_map/all_to_all | solution.py:326
  87.6 0.0 copy-done.3
  87.6 0.0 copy-done.4
  87.6 1.1 shard_map.109
  88.7 24.9 %all_to_all.16.parts = bf16[16,136,128]{2,1,0:T(8,128)(2,1)S(1)} all-to-all(bf16[16,136,128]{2,1,0:T(8,128)(2,1)S(1)} %shard_map.109), channel_id=1, replica_groups=mesh['zl'=2,'y'=8,'zh'=4,'core'=2,'sec'=4] {'zl','y'}, dimensions={0} | all-to-all | bytes 1114112 | tf_op jit(solution)/shard_map/all_to_all | solution.py:339
  113.6 0.9 shard_map.110
  114.5 2.4 %collective-permute-start.8 = (f32[128,128]{1,0:T(8,128)S(1)}, f32[128,128]{1,0:T(8,128)S(1)}, u32[]{:S(2)}, u32[]{:S(2)}) collective-permute-start(f32[128,128]{1,0:T(8,128)S(1)} %get-tuple-element.32), channel_id=1, source_target_pairs={{0,0},{1,1},{2,2},{3,3},{4,4},{5,5},{6,6},{7,7},{256,8},{257,9},{2... | collective-permute-start | bytes 196616 | tf_op jit(solution)/shard_map/ppermute | solution.py:347
  116.9 10.6 %collective-permute-done.8 = f32[128,128]{1,0:T(8,128)S(1)} collective-permute-done((f32[128,128]{1,0:T(8,128)S(1)}, f32[128,128]{1,0:T(8,128)S(1)}, u32[]{:S(2)}, u32[]{:S(2)}) %collective-permute-start.8) | collective-permute-done | bytes 65568 | tf_op jit(solution)/shard_map/ppermute | solution.py:347
  127.5 0.6 copy.12
  (5 shorter events, 0.1 us)
Async XLA Ops:
  2.2 24.5 %collective-permute-start = (bf16[256,128]{1,0:T(8,128)(2,1)}, bf16[256,128]{1,0:T(8,128)(2,1)S(1)}, u32[]{:S(2)}, u32[]{:S(2)}) collective-permute-start(bf16[256,128]{1,0:T(8,128)(2,1)} %get-tuple-element.19), channel_id=1, source_target_pairs={{0,0},{1,1},{2,2},{3,3},{4,4},{5,5},{6,6},{7,7},{8,256},{9,257},{1... | collective-permute-start | bytes 196616 | tf_op jit(solution)/shard_map/ppermute | solution.py:295
  14.9 11.8 %collective-permute-start.3 = (bf16[128,256]{1,0:T(8,128)(2,1)}, bf16[128,256]{1,0:T(8,128)(2,1)S(1)}, u32[]{:S(2)}, u32[]{:S(2)}) collective-permute-start(bf16[128,256]{1,0:T(8,128)(2,1)} %get-tuple-element.21.d0), channel_id=1, source_target_pairs={{0,24},{8,0},{16,8},{24,16},{1,25},{9,1},{17,9},{25,17},{2,26},{10... | collective-permute-start | bytes 196616 | tf_op jit(solution)/shard_map/ppermute | solution.py:305
  18.3 11.3 %collective-permute-start.2 = (bf16[128,256]{1,0:T(8,128)(2,1)}, bf16[128,256]{1,0:T(8,128)(2,1)S(1)}, u32[]{:S(2)}, u32[]{:S(2)}) collective-permute-start(bf16[128,256]{1,0:T(8,128)(2,1)} %get-tuple-element.21.d0), channel_id=1, source_target_pairs={{0,16},{8,24},{16,0},{24,8},{1,17},{9,25},{17,1},{25,9},{2,18},{10... | collective-permute-start | bytes 196616 | tf_op jit(solution)/shard_map/ppermute | solution.py:305
  20.2 9.4 %collective-permute-start.1 = (bf16[128,256]{1,0:T(8,128)(2,1)}, bf16[128,256]{1,0:T(8,128)(2,1)S(1)}, u32[]{:S(2)}, u32[]{:S(2)}) collective-permute-start(bf16[128,256]{1,0:T(8,128)(2,1)} %get-tuple-element.21.d0), channel_id=1, source_target_pairs={{0,8},{8,16},{16,24},{24,0},{1,9},{9,17},{17,25},{25,1},{2,10},{10... | collective-permute-start | bytes 196616 | tf_op jit(solution)/shard_map/ppermute | solution.py:305
  29.6 0.7 copy-start.2
  31.5 8.5 %copy-start = (bf16[4,256,256]{2,1,0:T(8,128)(2,1)S(1)}, bf16[4,256,256]{2,1,0:T(8,128)(2,1)}, u32[]{:S(2)}) copy-start(bf16[4,256,256]{2,1,0:T(8,128)(2,1)} %get-tuple-element.18.quarters) | copy-start | bytes 1572868
  31.5 8.5 %copy-start.1 = (bf16[128,256]{1,0:T(8,128)(2,1)S(1)}, bf16[128,256]{1,0:T(8,128)(2,1)}, u32[]{:S(2)}) copy-start(bf16[128,256]{1,0:T(8,128)(2,1)} %get-tuple-element.21.d0) | copy-start | bytes 196612
  31.5 34.8 %all-to-all-start = ((bf16[16,272,128]{2,1,0:T(8,128)(2,1)}), bf16[16,272,128]{2,1,0:T(8,128)(2,1)S(1)}, u32[]{:S(2)}, u32[]{:S(2)}) async-start(bf16[16,272,128]{2,1,0:T(8,128)(2,1)} %shard_map.107), calls=%async_computation | async-start | bytes 2228224 | tf_op jit(solution)/shard_map/all_to_all | solution.py:310
  40.1 14.2 %collective-permute-start.4 = (bf16[768,256]{1,0:T(8,128)(2,1)S(1)}, bf16[768,256]{1,0:T(8,128)(2,1)S(1)}, u32[]{:S(2)}, u32[]{:S(2)}) collective-permute-start(bf16[768,256]{1,0:T(8,128)(2,1)S(1)} %get-tuple-element.26), channel_id=1, source_target_pairs={{0,1},{1,2},{2,3},{3,0},{4,5},{5,6},{6,7},{7,4},{8,9},{9,10},{10,1... | collective-permute-start | bytes 1179656 | tf_op jit(solution)/shard_map/ppermute | solution.py:314
  43.5 17.4 %collective-permute-start.5 = (bf16[768,256]{1,0:T(8,128)(2,1)S(1)}, bf16[768,256]{1,0:T(8,128)(2,1)S(1)}, u32[]{:S(2)}, u32[]{:S(2)}) collective-permute-start(bf16[768,256]{1,0:T(8,128)(2,1)S(1)} %get-tuple-element.27), channel_id=1, source_target_pairs={{0,2},{1,3},{2,0},{3,1},{4,6},{5,7},{6,4},{7,5},{8,10},{9,11},{10,... | collective-permute-start | bytes 1179656 | tf_op jit(solution)/shard_map/ppermute | solution.py:314
  48.1 14.3 %collective-permute-start.6 = (bf16[768,256]{1,0:T(8,128)(2,1)S(1)}, bf16[768,256]{1,0:T(8,128)(2,1)S(1)}, u32[]{:S(2)}, u32[]{:S(2)}) collective-permute-start(bf16[768,256]{1,0:T(8,128)(2,1)S(1)} %get-tuple-element.28), channel_id=1, source_target_pairs={{0,3},{1,0},{2,1},{3,2},{4,7},{5,4},{6,5},{7,6},{8,11},{9,8},{10,9... | collective-permute-start | bytes 1179656 | tf_op jit(solution)/shard_map/ppermute | solution.py:314
  62.5 25.1 %copy-start.3 = (s32[1,256]{1,0:T(1,128)S(1)}, s32[1,256]{1,0:T(1,128)}, u32[]{:S(2)}) copy-start(s32[1,256]{1,0:T(1,128)} %get-tuple-element.31.slots) | copy-start | bytes 3076
  62.5 25.1 %copy-start.4 = (bf16[256]{0:T(256)(128)(2,1)S(1)}, bf16[256]{0:T(256)(128)(2,1)}, u32[]{:S(2)}) copy-start(bf16[256]{0:T(256)(128)(2,1)} %param.11) | copy-start | bytes 1540
  62.5 3.8 %collective-permute-start.7 = (bf16[1024,256]{1,0:T(8,128)(2,1)S(1)}, bf16[1024,256]{1,0:T(8,128)(2,1)S(1)}, u32[]{:S(2)}, u32[]{:S(2)}) collective-permute-start(bf16[1024,256]{1,0:T(8,128)(2,1)S(1)} %pad_maximum_fusion), channel_id=1, source_target_pairs={{0,4},{4,0},{1,5},{5,1},{2,6},{6,2},{3,7},{7,3},{8,12},{12,8},{9,1... | collective-permute-start | bytes 1572872 | tf_op jit(solution)/shard_map/ppermute | solution.py:315
  114.5 13.1 %collective-permute-start.8 = (f32[128,128]{1,0:T(8,128)S(1)}, f32[128,128]{1,0:T(8,128)S(1)}, u32[]{:S(2)}, u32[]{:S(2)}) collective-permute-start(f32[128,128]{1,0:T(8,128)S(1)} %get-tuple-element.32), channel_id=1, source_target_pairs={{0,0},{1,1},{2,2},{3,3},{4,4},{5,5},{6,6},{7,7},{256,8},{257,9},{2... | collective-permute-start | bytes 196616 | tf_op jit(solution)/shard_map/ppermute | solution.py:347

commit v5 on v4

--- a/solution.py
+++ b/solution.py
@@ -41,7 +41,9 @@
 
 
 def turn_kernel(direction, wp, wr, dir_t, w_t):
-    dir_t[...] = direction[...].astype(F32).T.astype(BF)
+    turned = direction[...].astype(F32).T.astype(BF)
+    for k in range(4):
+        dir_t[k] = turned
     w_t[0:128, :] = wp[...].astype(F32).T.astype(BF)
     w_t[128:256, :] = wr[...].astype(F32).T.astype(BF)
 
@@ -82,11 +84,11 @@
     slots[...] = target * SLOT + rank.astype(jnp.int32)
 
 
-def pack_kernel(quarters, d0, d1, d2, d3, *outs):
+def pack_kernel(quarters, dirs, *outs):
     for k in range(4):
         outs[k][0:256, :] = quarters[k]
-        for q, block in enumerate((d0, d1, d2, d3)):
-            outs[k][256 + 128 * q : 384 + 128 * q, :] = block[...]
+        for q in range(4):
+            outs[k][256 + 128 * q : 384 + 128 * q, :] = dirs[q]
 
 
 def spread_kernel(w, extra, out):
@@ -95,15 +97,14 @@
         out[k, 256:272, :] = extra[...]
 
 
-def terms_kernel(s0, s1, s2, s3, other, weights, out, pay):
+def terms_kernel(s0, s1, s2, s3, other, weights, pay):
     shares = (s0, s1, s2, s3)
     zh, core, sec = (lax.axis_index(name) for name in ("zh", "core", "sec"))
     acc = [jnp.zeros((2, 256), F32) for _ in range(4)]
     for q in range(4):
-        zz = (zh - q) & 3
         mats = [
             jnp.concatenate(
-                [weights[handler(zh, 2 * u + h, zz), 0:256, :] for h in range(2)], axis=1
+                [weights[handler(zh, 2 * u + h, q), 0:256, :] for h in range(2)], axis=1
             )
             for u in (core, 1 - core)
         ]
@@ -133,8 +134,11 @@
     for n, field in enumerate(fields):
         facts = jnp.where((lane[0:1] >> 4) == n, field, facts)
     pay[0:1, 2048:2176] = facts
-    whole = pay[...]
-    for d in range(32):
+
+
+def join_kernel(mine, partner, out):
+    whole = mine[...] + partner[...]
+    for d in range(16):
         out[d] = whole
 
 
@@ -145,7 +149,7 @@
     for s in range(4):
         for p in range(2):
             total = jnp.zeros((1, 256), F32)
-            for d in range(32):
+            for d in range(16):
                 k = (d - s) & 3
                 total += pays[d, 0:1, 1024 * p + 256 * k : 1024 * p + 256 * (k + 1)]
             for q in range(2):
@@ -155,7 +159,7 @@
     facts = []
     for s in range(4):
         fact = pays[s, 0:1, 2048:2176]
-        for d in range(1, 8):
+        for d in range(1, 4):
             fact = fact + pays[4 * d + s, 0:1, 2048:2176]
         facts.append(fact)
     facts = jnp.concatenate(facts + facts, axis=0)
@@ -204,7 +208,7 @@
         grad = grad.astype(BF)
         for h in range(2):
             for q in range(4):
-                out[handler(zh, 2 * u + h, (zh - q) & 3), 0:128, :] = grad[
+                out[handler(zh, 2 * u + h, q), 0:128, :] = grad[
                     128 * q : 128 * (q + 1), 128 * h : 128 * (h + 1)
                 ]
     old = old_logp[...].astype(F32)
@@ -286,7 +290,7 @@
 ):
     dir_t, w_t = call(
         turn_kernel,
-        (shape((128, 256), BF), shape((256, 128), BF)),
+        (shape((4, 128, 256), BF), shape((256, 128), BF)),
         inputs=3,
         flops=1 << 16,
         size=1 << 18,
@@ -300,30 +304,27 @@
         inputs=3,
         flops=8 * 256 * 1024 * 2,
         size=1 << 20,
-        vmem_mib=60,
     )(lengths, group_ids, states, reward_head.reshape(8, 128), routes.reshape(1, 256))
-    blocks = [dir_t] + [lax.ppermute(dir_t, "zh", ring(k)) for k in (1, 2, 3)]
-    w_here, *blocks = lax.optimization_barrier((w_here, *blocks))
+    dirs = lax.all_to_all(dir_t, "zh", 0, 0, tiled=True)
+    w_here, dirs = lax.optimization_barrier((w_here, dirs))
     weights = call(
         spread_kernel, shape((16, 272, 128), BF), inputs=2, flops=1 << 10, size=1 << 20
     )(w_here, extra)
     weights = lax.all_to_all(weights, DP, 0, 0, tiled=True)
     packs = call(
-        pack_kernel, (shape((768, 256), BF),) * 4, inputs=5, flops=1 << 10, size=3 << 20
-    )(quarters, *blocks)
+        pack_kernel, (shape((768, 256), BF),) * 4, inputs=2, flops=1 << 10, size=3 << 20
+    )(quarters, dirs)
     shares = [packs[0]] + [lax.ppermute(packs[k], "sec", ring(k)) for k in (1, 2, 3)]
     other = lax.ppermute(
         jnp.concatenate([share[0:256] for share in shares], axis=0), "core", [(0, 1), (1, 0)]
     )
-    pays = call(
-        terms_kernel,
-        shape((32, 1, 2176), F32),
-        scratch=[pltpu.VMEM((1, 2176), F32)],
-        inputs=6,
-        flops=1 << 30,
-        size=4 << 20,
+    pay = call(
+        terms_kernel, shape((1, 2176), F32), inputs=6, flops=1 << 30, size=4 << 20
     )(*shares, other, weights)
-    pays = lax.all_to_all(pays, ("zh", "core", "sec"), 0, 0, tiled=True)
+    pays = call(join_kernel, shape((16, 1, 2176), F32), inputs=2, flops=1 << 12, size=1 << 18)(
+        pay, lax.ppermute(pay, "core", [(0, 1), (1, 0)])
+    )
+    pays = lax.all_to_all(pays, ("zh", "sec"), 0, 0, tiled=True)
     parts = call(
         grads_kernel,
         shape((16, 136, 128), BF),

time: 129 us -> 124 us (0.961)
  local copies, waits for them, and re-layouts: 1.36 us -> 4.38 us
  blocking collectives: 44.8 us -> 42.3 us
  waiting for transfers between devices: 26.3 us -> 23.9 us
  starting transfers between devices: 46.4 us -> 44.5 us
    all_to_all x0 -> x1, starting transfers between devices: none -> 9.4 us  [body(): dirs = lax.all_to_all(dir_t, 'zh', 0, 0, tiled=True)]
    ppermute x3 -> x1, starting transfers between devices: 9.57 us -> 2.06 us  [body(): lax.ppermute(pay, 'core', [(0, 1), (1, 0)])]
    unnamed x11 -> x13, local copies, waits for them, and re-layouts: 1.33 us -> 4.34 us
    all_to_all x1, starting transfers between devices: 8.45 us -> 5.85 us  [body(): weights = lax.all_to_all(weights, DP, 0, 0, tiled=True)]
    ppermute x1, starting transfers between devices: 12.7 us -> 10.5 us  [body(): w_here = lax.ppermute(w_t, ALL, TO_HANDLER)]
    ppermute x3 -> x1, waiting for transfers between devices: 2.91 us -> 1 us  [body(): lax.ppermute(pay, 'core', [(0, 1), (1, 0)])]
    all_to_all x1, blocking collectives: 24.9 us -> 23.2 us  [body(): parts = lax.all_to_all(parts, DP, 0, 0, tiled=True)]
    pallas_call x3 -> x4, Pallas kernels: 3.09 us -> 3.15 us  [the longest x1 1.69 us: body(): call(turn_kernel, (shape((4, 128, 256), BF), shape((256, 128), BF)), inpu...]
  transfers between devices with their start and end apart: 10 -> 9, of which waited for: 6 -> 6; matrix products, arithmetic and copies ran while one was open for 0% -> 0% of each run, Pallas kernels for 2% -> 1%
where the time goes in v5:
time: 124 us; the launch traced here: 123 us
  starting transfers between devices  44.5 us (36%)
  blocking collectives  42.3 us (34%)
  waiting for transfers between devices  23.9 us (19%)
  Pallas kernels  7.25 us (6%)
  local copies, waits for them, and re-layouts  4.38 us (4%)
    all_to_all x1, blocking collectives, body(): parts = lax.all_to_all(parts, DP, 0, 0, tiled=True)  23.2 us
    all_to_all x1, blocking collectives, body(): pays = lax.all_to_all(pays, ('zh', 'sec'), 0, 0, tiled=True)  19.1 us
    ppermute x3, waiting for transfers between devices, body(): lax.ppermute(packs[k], 'sec', ring(k))  11.4 us
    ppermute x3, starting transfers between devices, body(): lax.ppermute(packs[k], 'sec', ring(k))  11.4 us
    ppermute x1, starting transfers between devices, body(): w_here = lax.ppermute(w_t, ALL, TO_HANDLER)  10.5 us
    ppermute x1, waiting for transfers between devices, body(): return (lax.ppermute(grad, ALL, TO_OWNER), packed.reshape(1, 1, 320))  9.63 us
    all_to_all x1, starting transfers between devices, body(): dirs = lax.all_to_all(dir_t, 'zh', 0, 0, tiled=True)  9.4 us
    all_to_all x1, starting transfers between devices, body(): weights = lax.all_to_all(weights, DP, 0, 0, tiled=True)  5.85 us
  transfers between devices with their start and end apart: 9, of which 6 were waited for; matrix products, arithmetic and copies ran while one was open for 0% of the time, Pallas kernels for 1%

profile of v5, /device:TPU:72, one launch (start us, length us, event | category | flops | bytes accessed | tf_op | source)
XLA Modules:
  0.0 123.2 jit_solution(4992582865270181264)
XLA Ops:
  0.6 1.7 %shard_map.105 = (bf16[4,128,256]{2,1,0:T(8,128)(2,1)}, bf16[256,128]{1,0:T(8,128)(2,1)}) custom-call(bf16[256,128]{1,0:T(8,128)(2,1)} %direction.1, bf16[128,128]{1,0:T(8,128)(2,1)} %wp.1, bf16[128,128]{1,0:T(8,128)(2,1)} %wr.1), custom_call_target="tpu_custom_call" | custom-call | flops 65536 | bytes 262144 | tf_op jit(solution)/shard_map/pallas_call | solution.py:291
  2.3 9.4 %all-to-all-start = ((bf16[4,128,256]{2,1,0:T(8,128)(2,1)}), bf16[4,128,256]{2,1,0:T(8,128)(2,1)S(1)}, u32[]{:S(2)}, u32[]{:S(2)}) async-start(bf16[4,128,256]{2,1,0:T(8,128)(2,1)} %get-tuple-element.17), calls=%async_computation | async-start | bytes 524288 | tf_op jit(solution)/shard_map/all_to_all | solution.py:308
  11.7 10.5 %collective-permute-start = (bf16[256,128]{1,0:T(8,128)(2,1)}, bf16[256,128]{1,0:T(8,128)(2,1)S(1)}, u32[]{:S(2)}, u32[]{:S(2)}) collective-permute-start(bf16[256,128]{1,0:T(8,128)(2,1)} %get-tuple-element.16), channel_id=1, source_target_pairs={{0,0},{1,1},{2,2},{3,3},{4,4},{5,5},{6,6},{7,7},{8,256},{9,257},{1... | collective-permute-start | bytes 196616 | tf_op jit(solution)/shard_map/ppermute | solution.py:299
  22.2 0.0 copy-start
  22.2 1.0 copy-done
  23.3 0.0 copy-start.1
  23.3 0.7 copy-done.1
  24.0 0.0 copy-start.2
  24.0 0.7 copy-done.2
  24.6 0.0 copy-start.3
  24.6 0.7 copy-done.3
  25.3 0.0 copy-start.4
  25.3 0.7 copy-done.4
  25.9 1.0 shard_map.104
  26.9 0.0 collective-permute-done.w
  26.9 0.0 all-to-all-done.dirs
  26.9 1.2 shard_map.107
  28.1 5.8 %all-to-all-start.1 = ((bf16[16,272,128]{2,1,0:T(8,128)(2,1)}), bf16[16,272,128]{2,1,0:T(8,128)(2,1)S(1)}, u32[]{:S(2)}, u32[]{:S(2)}) async-start(bf16[16,272,128]{2,1,0:T(8,128)(2,1)} %shard_map.107), calls=%async_computation.1 | async-start | bytes 2228224 | tf_op jit(solution)/shard_map/all_to_all | solution.py:313
  33.9 0.1 shard_map.106
  34.0 3.4 %collective-permute-start.1 = (bf16[768,256]{1,0:T(8,128)(2,1)S(1)}, bf16[768,256]{1,0:T(8,128)(2,1)S(1)}, u32[]{:S(2)}, u32[]{:S(2)}) collective-permute-start(bf16[768,256]{1,0:T(8,128)(2,1)S(1)} %get-tuple-element.20), channel_id=1, source_target_pairs={{0,1},{1,2},{2,3},{3,0},{4,5},{5,6},{6,7},{7,4},{8,9},{9,10},{10,1... | collective-permute-start | bytes 1179656 | tf_op jit(solution)/shard_map/ppermute | solution.py:317
  37.4 4.6 %collective-permute-start.2 = (bf16[768,256]{1,0:T(8,128)(2,1)S(1)}, bf16[768,256]{1,0:T(8,128)(2,1)S(1)}, u32[]{:S(2)}, u32[]{:S(2)}) collective-permute-start(bf16[768,256]{1,0:T(8,128)(2,1)S(1)} %get-tuple-element.21), channel_id=1, source_target_pairs={{0,2},{1,3},{2,0},{3,1},{4,6},{5,7},{6,4},{7,5},{8,10},{9,11},{10,... | collective-permute-start | bytes 1179656 | tf_op jit(solution)/shard_map/ppermute | solution.py:317
  42.1 3.3 %collective-permute-start.3 = (bf16[768,256]{1,0:T(8,128)(2,1)S(1)}, bf16[768,256]{1,0:T(8,128)(2,1)S(1)}, u32[]{:S(2)}, u32[]{:S(2)}) collective-permute-start(bf16[768,256]{1,0:T(8,128)(2,1)S(1)} %get-tuple-element.22), channel_id=1, source_target_pairs={{0,3},{1,0},{2,1},{3,2},{4,7},{5,4},{6,5},{7,6},{8,11},{9,8},{10,9... | collective-permute-start | bytes 1179656 | tf_op jit(solution)/shard_map/ppermute | solution.py:317
  45.5 2.7 %collective-permute-done.1.s1 = bf16[768,256]{1,0:T(8,128)(2,1)S(1)} collective-permute-done((bf16[768,256]{1,0:T(8,128)(2,1)S(1)}, bf16[768,256]{1,0:T(8,128)(2,1)S(1)}, u32[]{:S(2)}, u32[]{:S(2)}) %collective-permute-start.1) | collective-permute-done | bytes 393248 | tf_op jit(solution)/shard_map/ppermute | solution.py:317
  48.2 7.2 %collective-permute-done.2.s2 = bf16[768,256]{1,0:T(8,128)(2,1)S(1)} collective-permute-done((bf16[768,256]{1,0:T(8,128)(2,1)S(1)}, bf16[768,256]{1,0:T(8,128)(2,1)S(1)}, u32[]{:S(2)}, u32[]{:S(2)}) %collective-permute-start.2) | collective-permute-done | bytes 393248 | tf_op jit(solution)/shard_map/ppermute | solution.py:317
  55.4 1.5 %collective-permute-done.3.s3 = bf16[768,256]{1,0:T(8,128)(2,1)S(1)} collective-permute-done((bf16[768,256]{1,0:T(8,128)(2,1)S(1)}, bf16[768,256]{1,0:T(8,128)(2,1)S(1)}, u32[]{:S(2)}, u32[]{:S(2)}) %collective-permute-start.3) | collective-permute-done | bytes 393248 | tf_op jit(solution)/shard_map/ppermute | solution.py:317
  57.0 0.0 copy-start.5
  57.0 1.9 %collective-permute-start.4 = (bf16[1024,256]{1,0:T(8,128)(2,1)S(1)}, bf16[1024,256]{1,0:T(8,128)(2,1)S(1)}, u32[]{:S(2)}, u32[]{:S(2)}) collective-permute-start(bf16[1024,256]{1,0:T(8,128)(2,1)S(1)} %pad_maximum_fusion), channel_id=1, source_target_pairs={{0,4},{4,0},{1,5},{5,1},{2,6},{6,2},{3,7},{7,3},{8,12},{12,8},{9,1... | collective-permute-start | bytes 1572872 | tf_op jit(solution)/shard_map/ppermute | solution.py:318
  58.9 1.9 %collective-permute-done.4.other = bf16[1024,256]{1,0:T(8,128)(2,1)S(1)} collective-permute-done((bf16[1024,256]{1,0:T(8,128)(2,1)S(1)}, bf16[1024,256]{1,0:T(8,128)(2,1)S(1)}, u32[]{:S(2)}, u32[]{:S(2)}) %collective-permute-start.4) | collective-permute-done | bytes 524320 | tf_op jit(solution)/shard_map/ppermute | solution.py:318
  60.8 0.0 all-to-all-done.1.weights
  60.8 1.3 %shard_map.108.mine = f32[1,2176]{1,0:T(1,128)S(1)} custom-call(bf16[768,256]{1,0:T(8,128)(2,1)S(1)} %get-tuple-element.19.s0, bf16[768,256]{1,0:T(8,128)(2,1)S(1)} %collective-permute-done.1.s1, bf16[768,256]{1,0:T(8,128)(2,1)S(1)} %collective-permute-done.2.s2, bf16[768,256]{1,0:T(8,128)(2,1)S(1)} %collective-permute-done.3.s3, ...), custom_call_target="tpu_custom_call" | custom-call | flops 1073741824 | bytes 4194304 | tf_op jit(solution)/shard_map/pallas_call | solution.py:321
  62.1 2.1 %collective-permute-start.5 = (f32[1,2176]{1,0:T(1,128)S(1)}, f32[1,2176]{1,0:T(1,128)S(1)}, u32[]{:S(2)}, u32[]{:S(2)}) collective-permute-start(f32[1,2176]{1,0:T(1,128)S(1)} %shard_map.108.mine), channel_id=1, source_target_pairs={{0,4},{4,0},{1,5},{5,1},{2,6},{6,2},{3,7},{7,3},{8,12},{12,8},{9,1... | collective-permute-start | bytes 26120 | tf_op jit(solution)/shard_map/ppermute | solution.py:325
  64.2 1.0 collective-permute-done.5.partner
  65.2 19.1 %all_to_all.20.pays = f32[16,1,2176]{2,1,0:T(1,128)S(1)} all-to-all(f32[16,1,2176]{2,1,0:T(1,128)S(1)} %shard_map.109), channel_id=1, replica_groups=mesh['zl'=2,'y'=8,'zh'=4,'core'=2,'sec'=4] {'zh','sec'}, dimensions={0} | all-to-all | bytes 278528 | tf_op jit(solution)/shard_map/all_to_all | solution.py:327
  84.3 0.0 copy-done.5
  84.3 1.1 shard_map.110
  85.4 23.2 %all_to_all.21.parts = bf16[16,136,128]{2,1,0:T(8,128)(2,1)S(1)} all-to-all(bf16[16,136,128]{2,1,0:T(8,128)(2,1)S(1)} %shard_map.110), channel_id=1, replica_groups=mesh['zl'=2,'y'=8,'zh'=4,'core'=2,'sec'=4] {'zl','y'}, dimensions={0} | all-to-all | bytes 1114112 | tf_op jit(solution)/shard_map/all_to_all | solution.py:340
  108.6 0.9 shard_map.111
  109.5 3.4 %collective-permute-start.6 = (f32[128,128]{1,0:T(8,128)S(1)}, f32[128,128]{1,0:T(8,128)S(1)}, u32[]{:S(2)}, u32[]{:S(2)}) collective-permute-start(f32[128,128]{1,0:T(8,128)S(1)} %get-tuple-element.26), channel_id=1, source_target_pairs={{0,0},{1,1},{2,2},{3,3},{4,4},{5,5},{6,6},{7,7},{256,8},{257,9},{2... | collective-permute-start | bytes 196616 | tf_op jit(solution)/shard_map/ppermute | solution.py:348
  112.9 9.6 %collective-permute-done.6 = f32[128,128]{1,0:T(8,128)S(1)} collective-permute-done((f32[128,128]{1,0:T(8,128)S(1)}, f32[128,128]{1,0:T(8,128)S(1)}, u32[]{:S(2)}, u32[]{:S(2)}) %collective-permute-start.6) | collective-permute-done | bytes 65568 | tf_op jit(solution)/shard_map/ppermute | solution.py:348
  122.5 0.6 copy.12
  (6 shorter events, 0.1 us)
Async XLA Ops:
  2.3 24.6 %all-to-all-start = ((bf16[4,128,256]{2,1,0:T(8,128)(2,1)}), bf16[4,128,256]{2,1,0:T(8,128)(2,1)S(1)}, u32[]{:S(2)}, u32[]{:S(2)}) async-start(bf16[4,128,256]{2,1,0:T(8,128)(2,1)} %get-tuple-element.17), calls=%async_computation | async-start | bytes 524288 | tf_op jit(solution)/shard_map/all_to_all | solution.py:308
  11.7 15.2 %collective-permute-start = (bf16[256,128]{1,0:T(8,128)(2,1)}, bf16[256,128]{1,0:T(8,128)(2,1)S(1)}, u32[]{:S(2)}, u32[]{:S(2)}) collective-permute-start(bf16[256,128]{1,0:T(8,128)(2,1)} %get-tuple-element.16), channel_id=1, source_target_pairs={{0,0},{1,1},{2,2},{3,3},{4,4},{5,5},{6,6},{7,7},{8,256},{9,257},{1... | collective-permute-start | bytes 196616 | tf_op jit(solution)/shard_map/ppermute | solution.py:299
  22.2 1.0 copy-start
  23.3 0.7 copy-start.1
  24.0 0.7 copy-start.2
  24.6 0.7 copy-start.3
  25.3 0.7 copy-start.4
  28.1 32.7 %all-to-all-start.1 = ((bf16[16,272,128]{2,1,0:T(8,128)(2,1)}), bf16[16,272,128]{2,1,0:T(8,128)(2,1)S(1)}, u32[]{:S(2)}, u32[]{:S(2)}) async-start(bf16[16,272,128]{2,1,0:T(8,128)(2,1)} %shard_map.107), calls=%async_computation.1 | async-start | bytes 2228224 | tf_op jit(solution)/shard_map/all_to_all | solution.py:313
  34.0 14.2 %collective-permute-start.1 = (bf16[768,256]{1,0:T(8,128)(2,1)S(1)}, bf16[768,256]{1,0:T(8,128)(2,1)S(1)}, u32[]{:S(2)}, u32[]{:S(2)}) collective-permute-start(bf16[768,256]{1,0:T(8,128)(2,1)S(1)} %get-tuple-element.20), channel_id=1, source_target_pairs={{0,1},{1,2},{2,3},{3,0},{4,5},{5,6},{6,7},{7,4},{8,9},{9,10},{10,1... | collective-permute-start | bytes 1179656 | tf_op jit(solution)/shard_map/ppermute | solution.py:317
  37.4 18.0 %collective-permute-start.2 = (bf16[768,256]{1,0:T(8,128)(2,1)S(1)}, bf16[768,256]{1,0:T(8,128)(2,1)S(1)}, u32[]{:S(2)}, u32[]{:S(2)}) collective-permute-start(bf16[768,256]{1,0:T(8,128)(2,1)S(1)} %get-tuple-element.21), channel_id=1, source_target_pairs={{0,2},{1,3},{2,0},{3,1},{4,6},{5,7},{6,4},{7,5},{8,10},{9,11},{10,... | collective-permute-start | bytes 1179656 | tf_op jit(solution)/shard_map/ppermute | solution.py:317
  42.1 14.8 %collective-permute-start.3 = (bf16[768,256]{1,0:T(8,128)(2,1)S(1)}, bf16[768,256]{1,0:T(8,128)(2,1)S(1)}, u32[]{:S(2)}, u32[]{:S(2)}) collective-permute-start(bf16[768,256]{1,0:T(8,128)(2,1)S(1)} %get-tuple-element.22), channel_id=1, source_target_pairs={{0,3},{1,0},{2,1},{3,2},{4,7},{5,4},{6,5},{7,6},{8,11},{9,8},{10,9... | collective-permute-start | bytes 1179656 | tf_op jit(solution)/shard_map/ppermute | solution.py:317
  57.0 27.4 %copy-start.5 = (bf16[256]{0:T(256)(128)(2,1)S(1)}, bf16[256]{0:T(256)(128)(2,1)}, u32[]{:S(2)}) copy-start(bf16[256]{0:T(256)(128)(2,1)} %param.11) | copy-start | bytes 1540
  57.0 3.8 %collective-permute-start.4 = (bf16[1024,256]{1,0:T(8,128)(2,1)S(1)}, bf16[1024,256]{1,0:T(8,128)(2,1)S(1)}, u32[]{:S(2)}, u32[]{:S(2)}) collective-permute-start(bf16[1024,256]{1,0:T(8,128)(2,1)S(1)} %pad_maximum_fusion), channel_id=1, source_target_pairs={{0,4},{4,0},{1,5},{5,1},{2,6},{6,2},{3,7},{7,3},{8,12},{12,8},{9,1... | collective-permute-start | bytes 1572872 | tf_op jit(solution)/shard_map/ppermute | solution.py:318
  62.1 3.1 %collective-permute-start.5 = (f32[1,2176]{1,0:T(1,128)S(1)}, f32[1,2176]{1,0:T(1,128)S(1)}, u32[]{:S(2)}, u32[]{:S(2)}) collective-permute-start(f32[1,2176]{1,0:T(1,128)S(1)} %shard_map.108.mine), channel_id=1, source_target_pairs={{0,4},{4,0},{1,5},{5,1},{2,6},{6,2},{3,7},{7,3},{8,12},{12,8},{9,1... | collective-permute-start | bytes 26120 | tf_op jit(solution)/shard_map/ppermute | solution.py:325
  109.5 13.1 %collective-permute-start.6 = (f32[128,128]{1,0:T(8,128)S(1)}, f32[128,128]{1,0:T(8,128)S(1)}, u32[]{:S(2)}, u32[]{:S(2)}) collective-permute-start(f32[128,128]{1,0:T(8,128)S(1)} %get-tuple-element.26), channel_id=1, source_target_pairs={{0,0},{1,1},{2,2},{3,3},{4,4},{5,5},{6,6},{7,7},{256,8},{257,9},{2... | collective-permute-start | bytes 196616 | tf_op jit(solution)/shard_map/ppermute | solution.py:348

commit v6 on v5

--- a/solution.py
+++ b/solution.py
@@ -123,7 +123,10 @@
             )
     for s in range(4):
         for p in range(2):
-            pay[0:1, 1024 * p + 256 * s : 1024 * p + 256 * (s + 1)] = acc[s][p : p + 1]
+            for q in range(2):
+                pay[pl.ds(8 * p + 4 * q + ((sec - s) & 3), 1), :] = acc[s][
+                    p : p + 1, 128 * q : 128 * (q + 1)
+                ]
     lane = lax.broadcasted_iota(jnp.int32, (16, 128), 1)
     block = jnp.zeros((16, 128), F32)
     for i in range(16):
@@ -133,7 +136,7 @@
     facts = jnp.zeros((1, 128), F32)
     for n, field in enumerate(fields):
         facts = jnp.where((lane[0:1] >> 4) == n, field, facts)
-    pay[0:1, 2048:2176] = facts
+    pay[16:24, :] = jnp.broadcast_to(facts, (8, 128))
 
 
 def join_kernel(mine, partner, out):
@@ -142,25 +145,19 @@
         out[d] = whole
 
 
-def grads_kernel(pays, s0, s1, s2, s3, other, old_logp, slots, out, sums, change, coefs):
+def grads_kernel(pays, s0, s1, s2, s3, other, old_logp, slots, out, change, coefs):
     shares = (s0, s1, s2, s3)
     zh, core, sec = (lax.axis_index(name) for name in ("zh", "core", "sec"))
     dp = dp_index()
-    for s in range(4):
-        for p in range(2):
-            total = jnp.zeros((1, 256), F32)
-            for d in range(16):
-                k = (d - s) & 3
-                total += pays[d, 0:1, 1024 * p + 256 * k : 1024 * p + 256 * (k + 1)]
-            for q in range(2):
-                n = 8 * p + 4 * q + s
-                sums[n : n + 1, :] = total[:, 128 * q : 128 * (q + 1)]
-    tp, tr = sums[0:8, :], sums[8:16, :]
+    sums = pays[0, 0:16, :]
+    for d in range(1, 16):
+        sums = sums + pays[d, 0:16, :]
+    tp, tr = sums[0:8], sums[8:16]
     facts = []
     for s in range(4):
-        fact = pays[s, 0:1, 2048:2176]
+        fact = pays[s, 16:17, :]
         for d in range(1, 4):
-            fact = fact + pays[4 * d + s, 0:1, 2048:2176]
+            fact = fact + pays[4 * d + s, 16:17, :]
         facts.append(fact)
     facts = jnp.concatenate(facts + facts, axis=0)
     lane = lax.broadcasted_iota(jnp.int32, (8, 128), 1)
@@ -304,6 +301,7 @@
         inputs=3,
         flops=8 * 256 * 1024 * 2,
         size=1 << 20,
+        vmem_mib=60,
     )(lengths, group_ids, states, reward_head.reshape(8, 128), routes.reshape(1, 256))
     dirs = lax.all_to_all(dir_t, "zh", 0, 0, tiled=True)
     w_here, dirs = lax.optimization_barrier((w_here, dirs))
@@ -319,9 +317,9 @@
         jnp.concatenate([share[0:256] for share in shares], axis=0), "core", [(0, 1), (1, 0)]
     )
     pay = call(
-        terms_kernel, shape((1, 2176), F32), inputs=6, flops=1 << 30, size=4 << 20
+        terms_kernel, shape((24, 128), F32), inputs=6, flops=1 << 30, size=4 << 20
     )(*shares, other, weights)
-    pays = call(join_kernel, shape((16, 1, 2176), F32), inputs=2, flops=1 << 12, size=1 << 18)(
+    pays = call(join_kernel, shape((16, 24, 128), F32), inputs=2, flops=1 << 12, size=1 << 18)(
         pay, lax.ppermute(pay, "core", [(0, 1), (1, 0)])
     )
     pays = lax.all_to_all(pays, ("zh", "sec"), 0, 0, tiled=True)
@@ -329,7 +327,6 @@
         grads_kernel,
         shape((16, 136, 128), BF),
         scratch=[
-            pltpu.VMEM((16, 128), F32),
             pltpu.VMEM((512, 1024), BF),
             pltpu.VMEM((8, 128), F32),
         ],

time: 124 us -> 127 us (1.024)
  local copies, waits for them, and re-layouts: 4.38 us -> 1.35 us
  blocking collectives: 42.3 us -> 44.2 us
  starting transfers between devices: 44.5 us -> 46.1 us
    unnamed x13 -> x9, local copies, waits for them, and re-layouts: 4.34 us -> 1.31 us
    all_to_all x1, starting transfers between devices: 5.85 us -> 8.47 us  [body(): weights = lax.all_to_all(weights, DP, 0, 0, tiled=True)]
  transfers between devices with their start and end apart: 9 -> 9, of which waited for: 6 -> 6; matrix products, arithmetic and copies ran while one was open for 0% -> 0% of each run, Pallas kernels for 1% -> 2%
where the time goes in v6:
time: 127 us; the launch traced here: 126 us
  starting transfers between devices  46.1 us (36%)
  blocking collectives  44.2 us (35%)
  waiting for transfers between devices  24.9 us (20%)
  Pallas kernels  8.5 us (7%)
  local copies, waits for them, and re-layouts  1.35 us (1%)
    all_to_all x1, blocking collectives, body(): parts = lax.all_to_all(parts, DP, 0, 0, tiled=True)  24.2 us
    all_to_all x1, blocking collectives, body(): pays = lax.all_to_all(pays, ('zh', 'sec'), 0, 0, tiled=True)  20 us
    ppermute x3, waiting for transfers between devices, body(): lax.ppermute(packs[k], 'sec', ring(k))  11.4 us
    ppermute x3, starting transfers between devices, body(): lax.ppermute(packs[k], 'sec', ring(k))  11.4 us
    ppermute x1, waiting for transfers between devices, body(): return (lax.ppermute(grad, ALL, TO_OWNER), packed.reshape(1, 1, 320))  10.6 us
    ppermute x1, starting transfers between devices, body(): w_here = lax.ppermute(w_t, ALL, TO_HANDLER)  10.5 us
    all_to_all x1, starting transfers between devices, body(): dirs = lax.all_to_all(dir_t, 'zh', 0, 0, tiled=True)  9.4 us
    all_to_all x1, starting transfers between devices, body(): weights = lax.all_to_all(weights, DP, 0, 0, tiled=True)  8.47 us
  transfers between devices with their start and end apart: 9, of which 6 were waited for; matrix products, arithmetic and copies ran while one was open for 0% of the time, Pallas kernels for 2%

profile of v6, /device:TPU:72, one launch (start us, length us, event | category | flops | bytes accessed | tf_op | source)
XLA Modules:
  0.0 126.0 jit_solution(580046179031678950)
XLA Ops:
  0.6 1.7 %shard_map.105 = (bf16[4,128,256]{2,1,0:T(8,128)(2,1)}, bf16[256,128]{1,0:T(8,128)(2,1)}) custom-call(bf16[256,128]{1,0:T(8,128)(2,1)} %direction.1, bf16[128,128]{1,0:T(8,128)(2,1)} %wp.1, bf16[128,128]{1,0:T(8,128)(2,1)} %wr.1), custom_call_target="tpu_custom_call" | custom-call | flops 65536 | bytes 262144 | tf_op jit(solution)/shard_map/pallas_call | solution.py:288
  2.3 9.4 %all-to-all-start = ((bf16[4,128,256]{2,1,0:T(8,128)(2,1)}), bf16[4,128,256]{2,1,0:T(8,128)(2,1)S(1)}, u32[]{:S(2)}, u32[]{:S(2)}) async-start(bf16[4,128,256]{2,1,0:T(8,128)(2,1)} %get-tuple-element.17), calls=%async_computation | async-start | bytes 524288 | tf_op jit(solution)/shard_map/all_to_all | solution.py:306
  11.7 10.5 %collective-permute-start = (bf16[256,128]{1,0:T(8,128)(2,1)}, bf16[256,128]{1,0:T(8,128)(2,1)S(1)}, u32[]{:S(2)}, u32[]{:S(2)}) collective-permute-start(bf16[256,128]{1,0:T(8,128)(2,1)} %get-tuple-element.16), channel_id=1, source_target_pairs={{0,0},{1,1},{2,2},{3,3},{4,4},{5,5},{6,6},{7,7},{8,256},{9,257},{1... | collective-permute-start | bytes 196616 | tf_op jit(solution)/shard_map/ppermute | solution.py:296
  22.2 2.2 %shard_map.104 = (bf16[4,256,256]{2,1,0:T(8,128)(2,1)}, bf16[16,128]{1,0:T(8,128)(2,1)}, s32[1,256]{1,0:T(1,128)}) custom-call(s32[2]{0:T(128)} %lengths.1, s32[2]{0:T(128)} %group_ids.1, bf16[256,1024]{1,0:T(8,128)(2,1)} %states.1, bf16[8,128]{1,0:T(8,128)(2,1)} %bitcast.5, s32[1,256]{1,0:T(1,128)} %bitcast.6), custom_call_target="tpu_custom_call" | custom-call | flops 4194304 | bytes 1048576 | tf_op jit(solution)/shard_map/pallas_call | solution.py:297
  24.4 0.0 collective-permute-done.w
  24.4 0.0 all-to-all-done.dirs
  24.4 0.0 copy-start.1
  24.4 0.7 copy-done.1
  25.1 1.2 shard_map.107
  26.3 0.0 copy-start
  26.3 8.5 %all-to-all-start.1 = ((bf16[16,272,128]{2,1,0:T(8,128)(2,1)}), bf16[16,272,128]{2,1,0:T(8,128)(2,1)S(1)}, u32[]{:S(2)}, u32[]{:S(2)}) async-start(bf16[16,272,128]{2,1,0:T(8,128)(2,1)} %shard_map.107), calls=%async_computation.1 | async-start | bytes 2228224 | tf_op jit(solution)/shard_map/all_to_all | solution.py:311
  34.8 0.0 copy-done
  34.8 0.1 shard_map.106
  34.9 3.4 %collective-permute-start.1 = (bf16[768,256]{1,0:T(8,128)(2,1)S(1)}, bf16[768,256]{1,0:T(8,128)(2,1)S(1)}, u32[]{:S(2)}, u32[]{:S(2)}) collective-permute-start(bf16[768,256]{1,0:T(8,128)(2,1)S(1)} %get-tuple-element.20), channel_id=1, source_target_pairs={{0,1},{1,2},{2,3},{3,0},{4,5},{5,6},{6,7},{7,4},{8,9},{9,10},{10,1... | collective-permute-start | bytes 1179656 | tf_op jit(solution)/shard_map/ppermute | solution.py:315
  38.3 4.6 %collective-permute-start.2 = (bf16[768,256]{1,0:T(8,128)(2,1)S(1)}, bf16[768,256]{1,0:T(8,128)(2,1)S(1)}, u32[]{:S(2)}, u32[]{:S(2)}) collective-permute-start(bf16[768,256]{1,0:T(8,128)(2,1)S(1)} %get-tuple-element.21), channel_id=1, source_target_pairs={{0,2},{1,3},{2,0},{3,1},{4,6},{5,7},{6,4},{7,5},{8,10},{9,11},{10,... | collective-permute-start | bytes 1179656 | tf_op jit(solution)/shard_map/ppermute | solution.py:315
  42.9 3.3 %collective-permute-start.3 = (bf16[768,256]{1,0:T(8,128)(2,1)S(1)}, bf16[768,256]{1,0:T(8,128)(2,1)S(1)}, u32[]{:S(2)}, u32[]{:S(2)}) collective-permute-start(bf16[768,256]{1,0:T(8,128)(2,1)S(1)} %get-tuple-element.22), channel_id=1, source_target_pairs={{0,3},{1,0},{2,1},{3,2},{4,7},{5,4},{6,5},{7,6},{8,11},{9,8},{10,9... | collective-permute-start | bytes 1179656 | tf_op jit(solution)/shard_map/ppermute | solution.py:315
  46.3 2.7 %collective-permute-done.1.s1 = bf16[768,256]{1,0:T(8,128)(2,1)S(1)} collective-permute-done((bf16[768,256]{1,0:T(8,128)(2,1)S(1)}, bf16[768,256]{1,0:T(8,128)(2,1)S(1)}, u32[]{:S(2)}, u32[]{:S(2)}) %collective-permute-start.1) | collective-permute-done | bytes 393248 | tf_op jit(solution)/shard_map/ppermute | solution.py:315
  49.1 7.2 %collective-permute-done.2.s2 = bf16[768,256]{1,0:T(8,128)(2,1)S(1)} collective-permute-done((bf16[768,256]{1,0:T(8,128)(2,1)S(1)}, bf16[768,256]{1,0:T(8,128)(2,1)S(1)}, u32[]{:S(2)}, u32[]{:S(2)}) %collective-permute-start.2) | collective-permute-done | bytes 393248 | tf_op jit(solution)/shard_map/ppermute | solution.py:315
  56.2 1.5 %collective-permute-done.3.s3 = bf16[768,256]{1,0:T(8,128)(2,1)S(1)} collective-permute-done((bf16[768,256]{1,0:T(8,128)(2,1)S(1)}, bf16[768,256]{1,0:T(8,128)(2,1)S(1)}, u32[]{:S(2)}, u32[]{:S(2)}) %collective-permute-start.3) | collective-permute-done | bytes 393248 | tf_op jit(solution)/shard_map/ppermute | solution.py:315
  57.8 0.0 copy-start.2
  57.8 0.0 copy-start.3
  57.8 1.9 %collective-permute-start.4 = (bf16[1024,256]{1,0:T(8,128)(2,1)S(1)}, bf16[1024,256]{1,0:T(8,128)(2,1)S(1)}, u32[]{:S(2)}, u32[]{:S(2)}) collective-permute-start(bf16[1024,256]{1,0:T(8,128)(2,1)S(1)} %pad_maximum_fusion), channel_id=1, source_target_pairs={{0,4},{4,0},{1,5},{5,1},{2,6},{6,2},{3,7},{7,3},{8,12},{12,8},{9,1... | collective-permute-start | bytes 1572872 | tf_op jit(solution)/shard_map/ppermute | solution.py:316
  59.8 1.9 %collective-permute-done.4.other = bf16[1024,256]{1,0:T(8,128)(2,1)S(1)} collective-permute-done((bf16[1024,256]{1,0:T(8,128)(2,1)S(1)}, bf16[1024,256]{1,0:T(8,128)(2,1)S(1)}, u32[]{:S(2)}, u32[]{:S(2)}) %collective-permute-start.4) | collective-permute-done | bytes 524320 | tf_op jit(solution)/shard_map/ppermute | solution.py:316
  61.6 0.0 all-to-all-done.1.weights
  61.6 1.3 %shard_map.108.mine = f32[24,128]{1,0:T(8,128)S(1)} custom-call(bf16[768,256]{1,0:T(8,128)(2,1)S(1)} %get-tuple-element.19.s0, bf16[768,256]{1,0:T(8,128)(2,1)S(1)} %collective-permute-done.1.s1, bf16[768,256]{1,0:T(8,128)(2,1)S(1)} %collective-permute-done.2.s2, bf16[768,256]{1,0:T(8,128)(2,1)S(1)} %collective-permute-done.3.s3, ...), custom_call_target="tpu_custom_call" | custom-call | flops 1073741824 | bytes 4194304 | tf_op jit(solution)/shard_map/pallas_call | solution.py:319
  63.0 2.1 %collective-permute-start.5 = (f32[24,128]{1,0:T(8,128)S(1)}, f32[24,128]{1,0:T(8,128)S(1)}, u32[]{:S(2)}, u32[]{:S(2)}) collective-permute-start(f32[24,128]{1,0:T(8,128)S(1)} %shard_map.108.mine), channel_id=1, source_target_pairs={{0,4},{4,0},{1,5},{5,1},{2,6},{6,2},{3,7},{7,3},{8,12},{12,8},{9,1... | collective-permute-start | bytes 36872 | tf_op jit(solution)/shard_map/ppermute | solution.py:323
  65.0 1.0 collective-permute-done.5.partner
  66.1 20.0 %all_to_all.20.pays = f32[16,24,128]{2,1,0:T(8,128)S(1)} all-to-all(f32[16,24,128]{2,1,0:T(8,128)S(1)} %shard_map.109), channel_id=1, replica_groups=mesh['zl'=2,'y'=8,'zh'=4,'core'=2,'sec'=4] {'zh','sec'}, dimensions={0} | all-to-all | bytes 393216 | tf_op jit(solution)/shard_map/all_to_all | solution.py:325
  86.1 0.0 copy-done.2
  86.1 0.0 copy-done.3
  86.1 1.1 shard_map.110
  87.2 24.2 %all_to_all.21.parts = bf16[16,136,128]{2,1,0:T(8,128)(2,1)S(1)} all-to-all(bf16[16,136,128]{2,1,0:T(8,128)(2,1)S(1)} %shard_map.110), channel_id=1, replica_groups=mesh['zl'=2,'y'=8,'zh'=4,'core'=2,'sec'=4] {'zl','y'}, dimensions={0} | all-to-all | bytes 1114112 | tf_op jit(solution)/shard_map/all_to_all | solution.py:337
  111.4 0.9 shard_map.111
  112.3 2.4 %collective-permute-start.6 = (f32[128,128]{1,0:T(8,128)S(1)}, f32[128,128]{1,0:T(8,128)S(1)}, u32[]{:S(2)}, u32[]{:S(2)}) collective-permute-start(f32[128,128]{1,0:T(8,128)S(1)} %get-tuple-element.26), channel_id=1, source_target_pairs={{0,0},{1,1},{2,2},{3,3},{4,4},{5,5},{6,6},{7,7},{256,8},{257,9},{2... | collective-permute-start | bytes 196616 | tf_op jit(solution)/shard_map/ppermute | solution.py:345
  114.7 10.6 %collective-permute-done.6 = f32[128,128]{1,0:T(8,128)S(1)} collective-permute-done((f32[128,128]{1,0:T(8,128)S(1)}, f32[128,128]{1,0:T(8,128)S(1)}, u32[]{:S(2)}, u32[]{:S(2)}) %collective-permute-start.6) | collective-permute-done | bytes 65568 | tf_op jit(solution)/shard_map/ppermute | solution.py:345
  125.3 0.6 copy.12
  (6 shorter events, 0.1 us)
Async XLA Ops:
  2.3 22.1 %all-to-all-start = ((bf16[4,128,256]{2,1,0:T(8,128)(2,1)}), bf16[4,128,256]{2,1,0:T(8,128)(2,1)S(1)}, u32[]{:S(2)}, u32[]{:S(2)}) async-start(bf16[4,128,256]{2,1,0:T(8,128)(2,1)} %get-tuple-element.17), calls=%async_computation | async-start | bytes 524288 | tf_op jit(solution)/shard_map/all_to_all | solution.py:306
  11.7 12.7 %collective-permute-start = (bf16[256,128]{1,0:T(8,128)(2,1)}, bf16[256,128]{1,0:T(8,128)(2,1)S(1)}, u32[]{:S(2)}, u32[]{:S(2)}) collective-permute-start(bf16[256,128]{1,0:T(8,128)(2,1)} %get-tuple-element.16), channel_id=1, source_target_pairs={{0,0},{1,1},{2,2},{3,3},{4,4},{5,5},{6,6},{7,7},{8,256},{9,257},{1... | collective-permute-start | bytes 196616 | tf_op jit(solution)/shard_map/ppermute | solution.py:296
  24.4 0.7 copy-start.1
  26.3 8.5 %copy-start = (bf16[4,256,256]{2,1,0:T(8,128)(2,1)S(1)}, bf16[4,256,256]{2,1,0:T(8,128)(2,1)}, u32[]{:S(2)}) copy-start(bf16[4,256,256]{2,1,0:T(8,128)(2,1)} %get-tuple-element.15.quarters) | copy-start | bytes 1572868
  26.3 35.4 %all-to-all-start.1 = ((bf16[16,272,128]{2,1,0:T(8,128)(2,1)}), bf16[16,272,128]{2,1,0:T(8,128)(2,1)S(1)}, u32[]{:S(2)}, u32[]{:S(2)}) async-start(bf16[16,272,128]{2,1,0:T(8,128)(2,1)} %shard_map.107), calls=%async_computation.1 | async-start | bytes 2228224 | tf_op jit(solution)/shard_map/all_to_all | solution.py:311
  34.9 14.2 %collective-permute-start.1 = (bf16[768,256]{1,0:T(8,128)(2,1)S(1)}, bf16[768,256]{1,0:T(8,128)(2,1)S(1)}, u32[]{:S(2)}, u32[]{:S(2)}) collective-permute-start(bf16[768,256]{1,0:T(8,128)(2,1)S(1)} %get-tuple-element.20), channel_id=1, source_target_pairs={{0,1},{1,2},{2,3},{3,0},{4,5},{5,6},{6,7},{7,4},{8,9},{9,10},{10,1... | collective-permute-start | bytes 1179656 | tf_op jit(solution)/shard_map/ppermute | solution.py:315
  38.3 18.0 %collective-permute-start.2 = (bf16[768,256]{1,0:T(8,128)(2,1)S(1)}, bf16[768,256]{1,0:T(8,128)(2,1)S(1)}, u32[]{:S(2)}, u32[]{:S(2)}) collective-permute-start(bf16[768,256]{1,0:T(8,128)(2,1)S(1)} %get-tuple-element.21), channel_id=1, source_target_pairs={{0,2},{1,3},{2,0},{3,1},{4,6},{5,7},{6,4},{7,5},{8,10},{9,11},{10,... | collective-permute-start | bytes 1179656 | tf_op jit(solution)/shard_map/ppermute | solution.py:315
  42.9 14.8 %collective-permute-start.3 = (bf16[768,256]{1,0:T(8,128)(2,1)S(1)}, bf16[768,256]{1,0:T(8,128)(2,1)S(1)}, u32[]{:S(2)}, u32[]{:S(2)}) collective-permute-start(bf16[768,256]{1,0:T(8,128)(2,1)S(1)} %get-tuple-element.22), channel_id=1, source_target_pairs={{0,3},{1,0},{2,1},{3,2},{4,7},{5,4},{6,5},{7,6},{8,11},{9,8},{10,9... | collective-permute-start | bytes 1179656 | tf_op jit(solution)/shard_map/ppermute | solution.py:315
  57.8 28.3 %copy-start.2 = (s32[1,256]{1,0:T(1,128)S(1)}, s32[1,256]{1,0:T(1,128)}, u32[]{:S(2)}) copy-start(s32[1,256]{1,0:T(1,128)} %get-tuple-element.25.slots) | copy-start | bytes 3076
  57.8 28.3 %copy-start.3 = (bf16[256]{0:T(256)(128)(2,1)S(1)}, bf16[256]{0:T(256)(128)(2,1)}, u32[]{:S(2)}) copy-start(bf16[256]{0:T(256)(128)(2,1)} %param.11) | copy-start | bytes 1540
  57.8 3.8 %collective-permute-start.4 = (bf16[1024,256]{1,0:T(8,128)(2,1)S(1)}, bf16[1024,256]{1,0:T(8,128)(2,1)S(1)}, u32[]{:S(2)}, u32[]{:S(2)}) collective-permute-start(bf16[1024,256]{1,0:T(8,128)(2,1)S(1)} %pad_maximum_fusion), channel_id=1, source_target_pairs={{0,4},{4,0},{1,5},{5,1},{2,6},{6,2},{3,7},{7,3},{8,12},{12,8},{9,1... | collective-permute-start | bytes 1572872 | tf_op jit(solution)/shard_map/ppermute | solution.py:316
  63.0 3.1 %collective-permute-start.5 = (f32[24,128]{1,0:T(8,128)S(1)}, f32[24,128]{1,0:T(8,128)S(1)}, u32[]{:S(2)}, u32[]{:S(2)}) collective-permute-start(f32[24,128]{1,0:T(8,128)S(1)} %shard_map.108.mine), channel_id=1, source_target_pairs={{0,4},{4,0},{1,5},{5,1},{2,6},{6,2},{3,7},{7,3},{8,12},{12,8},{9,1... | collective-permute-start | bytes 36872 | tf_op jit(solution)/shard_map/ppermute | solution.py:323
  112.3 13.1 %collective-permute-start.6 = (f32[128,128]{1,0:T(8,128)S(1)}, f32[128,128]{1,0:T(8,128)S(1)}, u32[]{:S(2)}, u32[]{:S(2)}) collective-permute-start(f32[128,128]{1,0:T(8,128)S(1)} %get-tuple-element.26), channel_id=1, source_target_pairs={{0,0},{1,1},{2,2},{3,3},{4,4},{5,5},{6,6},{7,7},{256,8},{257,9},{2... | collective-permute-start | bytes 196616 | tf_op jit(solution)/shard_map/ppermute | solution.py:345

commit v7 on v6

v7 whole, which is shorter than its diff:
```python
import jax
import jax.numpy as jnp
from jax import lax
from jax.experimental import pallas as pl
from jax.experimental.pallas import tpu as pltpu
from jax.sharding import Mesh
from jax.sharding import PartitionSpec as P

GROUP = 8
NGROUPS = 16
CAP = 20
SLOT = 32

kl_weight = 0.4
var_offset = 0.25

DP = ("zl", "y")
ALL = ("zl", "y", "zh", "core", "sec")
BF = jnp.bfloat16
F32 = jnp.float32
NT = (((1,), (1,)), ((), ()))


def split3(x):
    hi = x.astype(BF).astype(F32)
    rest = x - hi
    mid = rest.astype(BF).astype(F32)
    return hi, mid, rest - mid


def dp_index():
    return lax.axis_index("zl") * 8 + lax.axis_index("y")


def handler(zh, block, zz):
    turn = (zz - zh + (zh >> 1)) & 3
    zl = (turn & 1) ^ (turn >> 1)
    near = 4 * (zh & 1)
    y = near + block + (turn >> 1) * (7 - 2 * block)
    return zl * 8 + (y & 7)


def turn_kernel(direction, routes, old_logp, wp, wr, dir_t, w_t):
    dir_t[0:128, :] = direction[...].astype(F32).T.astype(BF)
    at = lax.broadcasted_iota(jnp.int32, (8, 256), 0)
    old = old_logp[...].astype(F32)
    old = jnp.concatenate([old[0:1], old[1:2]], axis=1)
    rows = jnp.where(at == 0, routes[...].astype(F32), jnp.where(at == 1, old, 0.0))
    dir_t[128:136, :] = rows.astype(BF)
    w_t[0:128, :] = wp[...].astype(F32).T.astype(BF)
    w_t[128:256, :] = wr[...].astype(F32).T.astype(BF)


def prepare_kernel(lengths, group_ids, states, head, w_t, w_pack, half0, half1):
    sec, odd = lax.axis_index("sec"), lax.axis_index("y") & 1
    for b, half in enumerate((half0, half1)):
        for k in range(4):
            start = 512 * (b ^ odd) + 128 * ((sec - k) & 3)
            half[:, 128 * k : 128 * (k + 1)] = states[:, pl.ds(pl.multiple_of(start, 128), 128)]
    head_rows = head[...].astype(F32)
    wide_head = jnp.concatenate([head_rows[k : k + 1] for k in range(8)], axis=1).astype(BF)
    score = lax.dot_general(
        jnp.broadcast_to(wide_head, (8, 1024)), states[...], NT, preferred_element_type=F32
    )
    lane = lax.broadcasted_iota(jnp.int32, (1, 128), 1)
    rows = []
    for q in range(2):
        valid = (lane < lengths[q]).astype(F32)
        part = jnp.sum(score[0:1, 128 * q : 128 * (q + 1)] * valid, axis=1, keepdims=True)
        rows.extend(split3(part))
    for values in (group_ids, lengths):
        for q in range(2):
            rows.append(jnp.full((1, 1), values[q], jnp.int32).astype(F32))
    at = lax.broadcasted_iota(jnp.int32, (16, 128), 0)
    block = jnp.zeros((16, 128), F32)
    for n, row in enumerate(rows):
        block = jnp.where(at == n, row, block)
    for z in range(4):
        w_pack[z, 0:256, :] = w_t[...]
        w_pack[z, 256:272, :] = block.astype(BF)


def spread_kernel(block, out):
    for k in range(16):
        out[k] = block[...]


def row_block(n):
    core, odd = lax.axis_index("core"), lax.axis_index("y") & 1
    return 2 * (core ^ (n >> 1)) + ((n & 1) ^ odd)


def terms_kernel(own, other, w0, w1, w2, w3, dirs, pay):
    weights = (w0, w1, w2, w3)
    zh, sec = lax.axis_index("zh"), lax.axis_index("sec")
    acc = [jnp.zeros((2, 256), F32) for _ in range(4)]
    for z in range(4):
        mat = jnp.concatenate([w[z, 0:256, :] for w in weights], axis=1)
        for n in range(4):
            part = (own, other)[n >> 1][256 * (n & 1) : 256 * (n & 1) + 256, :]
            key = lax.dot_general(mat, part, NT, preferred_element_type=F32)
            wide = dirs[handler(zh, row_block(n), z), 0:128, :].astype(F32)
            acc[n] += jnp.concatenate(
                [
                    jnp.sum(wide * key[0:128], axis=0, keepdims=True),
                    jnp.sum(wide * key[128:256], axis=0, keepdims=True),
                ],
                axis=0,
            )
    for n in range(4):
        for p in range(2):
            for q in range(2):
                pay[pl.ds(8 * p + 4 * q + row_block(n), 1), :] = acc[n][
                    p : p + 1, 128 * q : 128 * (q + 1)
                ]
    lane = lax.broadcasted_iota(jnp.int32, (16, 128), 1)
    block = jnp.zeros((16, 128), F32)
    for k, w in enumerate(weights):
        tail = w[0, 256:272, :].astype(F32)
        for z in range(1, 4):
            tail = tail + w[z, 256:272, :].astype(F32)
        block = jnp.where((lane & 15) == ((sec - k) & 3), tail, block)
    fields = [block[0:1] + block[1:2] + block[2:3], block[3:4] + block[4:5] + block[5:6]]
    fields.extend(block[n : n + 1] for n in range(6, 10))
    facts = jnp.zeros((1, 128), F32)
    for n, field in enumerate(fields):
        facts = jnp.where((lane[0:1] >> 4) == n, field, facts)
    pay[16:24, :] = jnp.broadcast_to(facts, (8, 128))


def join_kernel(mine, partner, out):
    whole = mine[...] + partner[...]
    for d in range(16):
        out[d] = whole


def grads_kernel(pays, own, other, dirs, out, change, table, coefs):
    zh, sec, dp = lax.axis_index("zh"), lax.axis_index("sec"), dp_index()
    sums = pays[0, 0:16, :]
    for d in range(1, 16):
        sums = sums + pays[d, 0:16, :]
    tp, tr = sums[0:8], sums[8:16]
    facts = jnp.concatenate([pays[d, 16:17, :] for d in range(16)], axis=0)
    facts = jnp.concatenate([facts, pltpu.roll(facts, 112, 1)], axis=0)
    lane = lax.broadcasted_iota(jnp.int32, (32, 128), 1)
    used = lane < 4
    ids = pltpu.roll(facts, 96, 1) * 0.125
    lens = jnp.where(used, pltpu.roll(facts, 64, 1) * 0.125, 1.0)
    reward = facts / jnp.sqrt(lens)
    center = jnp.zeros((32, 128), F32)
    spread = jnp.zeros((32, 128), F32)
    for g in range(NGROUPS):
        member = used & (ids == float(g))
        mine = jnp.where(member, reward, 0.0)
        total = jnp.sum(jnp.sum(mine, axis=0, keepdims=True), axis=1, keepdims=True)
        square = jnp.sum(jnp.sum(mine * mine, axis=0, keepdims=True), axis=1, keepdims=True)
        mid = total / GROUP
        center = jnp.where(member, mid, center)
        spread = jnp.where(member, square / GROUP - mid * mid, spread)
    advantage = ((reward - center) / jnp.sqrt(spread + var_offset)).astype(BF).astype(F32)
    here = lane == sec
    picked = []
    for values in (advantage, lens):
        column = jnp.sum(jnp.where(here, values, 0.0), axis=1, keepdims=True)
        table[...] = jnp.broadcast_to(column, (32, 128))
        picked.append(
            jnp.concatenate(
                [table[pl.ds(16 * q + 4 * zh + a, 1), :] for q in range(2) for a in range(4)],
                axis=0,
            )
        )
    adv, length = picked
    valid = (lane[0:8].astype(F32) < length).astype(F32)
    coefs[...] = valid * (-adv * jnp.exp(tp) + kl_weight * (1.0 - jnp.exp(tr - tp)))
    for n in range(4):
        a = row_block(n)
        row = jnp.concatenate([coefs[pl.ds(a, 1), :], coefs[pl.ds(4 + a, 1), :]], axis=1)
        for z in range(4):
            change[128 * z : 128 * (z + 1), 256 * n : 256 * (n + 1)] = (
                dirs[handler(zh, a, z), 0:128, :].astype(F32) * row
            ).astype(BF)
    grad = jnp.dot(change[:, 0:512], own[...], preferred_element_type=F32)
    grad += jnp.dot(change[:, 512:1024], other[...], preferred_element_type=F32)
    grad = grad.astype(BF)
    for z in range(4):
        for k in range(4):
            out[4 * z + ((sec - k) & 3), 0:128, :] = grad[
                128 * z : 128 * (z + 1), 128 * k : 128 * (k + 1)
            ]
    marks, logps = [], []
    for a in range(4):
        facts = dirs[handler(zh, a, 0), 128:136, :].astype(F32)
        marks.append((facts[0:1] == dp.astype(F32)).astype(F32))
        logps.append(facts[1:2] + jnp.concatenate([tp[a : a + 1], tp[4 + a : 5 + a]], axis=1))
    zeros = jnp.zeros((4, 256), F32)
    before = (
        lax.broadcasted_iota(jnp.int32, (256, 256), 0)
        < lax.broadcasted_iota(jnp.int32, (256, 256), 1)
    ).astype(F32)
    ranks = jnp.dot(
        jnp.concatenate(marks + [zeros], axis=0).astype(BF),
        before.astype(BF),
        preferred_element_type=F32,
    )
    slot = lax.broadcasted_iota(jnp.int32, (SLOT, 256), 0).astype(F32)
    tails = []
    for a in range(4):
        place = jnp.where(slot == ranks[a : a + 1], marks[a], 0.0).astype(BF)
        hi, mid, lo = split3(logps[a])
        rows = jnp.concatenate([hi, mid, lo, zeros, zeros[0:1]], axis=0).astype(BF)
        tails.append(lax.dot_general(rows, place, NT, preferred_element_type=F32))
    tail = jnp.concatenate(tails, axis=1).astype(BF)
    for d in range(16):
        out[d, 128:136, :] = tail


def finish_kernel(parts, grad, packed):
    sec = lax.axis_index("sec")
    total = parts[0, 0:128, :].astype(F32)
    for d in range(1, 16):
        total = total + parts[d, 0:128, :].astype(F32)
    grad[...] = total.T
    pieces = []
    for z in range(4):
        row = jnp.sum(parts[4 * z + sec, 128:136, :].astype(F32), axis=0, keepdims=True)
        pieces.extend(row[:, SLOT * a : SLOT * a + CAP] for a in range(4))
    packed[...] = jnp.concatenate(pieces, axis=1)


def cost(flops, size):
    return pl.CostEstimate(flops=flops, bytes_accessed=size, transcendentals=0)


def shape(dims, dtype):
    return jax.ShapeDtypeStruct(dims, dtype)


def call(kernel, outs, scratch=(), smem=0, inputs=0, flops=0, size=0, vmem_mib=16):
    vmem = pl.BlockSpec(memory_space=pltpu.VMEM)
    scalar = pl.BlockSpec(memory_space=pltpu.SMEM)
    return pl.pallas_call(
        kernel,
        out_shape=outs,
        in_specs=[scalar] * smem + [vmem] * inputs,
        out_specs=jax.tree.map(lambda _: vmem, outs),
        scratch_shapes=list(scratch),
        cost_estimate=cost(flops, size),
        compiler_params=pltpu.CompilerParams(vmem_limit_bytes=vmem_mib << 20),
    )


def flat(i, zh, core, sec):
    return ((i * 4 + zh) * 2 + core) * 4 + sec


PLACES = [
    (i, zh, core, sec)
    for i in range(16)
    for zh in range(4)
    for core in range(2)
    for sec in range(4)
]
TO_HANDLER = [
    (flat(i, zz, core, sec), flat(handler(i >> 2, i & 3, zz), i >> 2, core, sec))
    for i, zz, core, sec in PLACES
]
TO_POOL = [
    [
        (
            flat(i, zh, core, sec),
            flat(4 * zh + 2 * core + (b ^ (i & 1)), i >> 2, (i >> 1) & 1, sec),
        )
        for i, zh, core, sec in PLACES
    ]
    for b in range(2)
]


def ring(step):
    return [(j, (j + step) % 4) for j in range(4)]


def swap(x):
    return lax.ppermute(x, "core", [(0, 1), (1, 0)])


def body(
    states, direction, old_logp, lengths, group_ids, routes, reward_head, policy_k, reference_k
):
    dir_t, w_t = call(
        turn_kernel,
        (shape((136, 256), BF), shape((256, 128), BF)),
        inputs=5,
        flops=1 << 16,
        size=1 << 18,
        vmem_mib=60,
    )(direction, routes.reshape(1, 256), old_logp.reshape(2, 128), policy_k, reference_k)
    dir_here = lax.ppermute(dir_t, ALL, TO_HANDLER)
    w_pack, half0, half1 = call(
        prepare_kernel,
        (shape((4, 272, 128), BF), shape((256, 512), BF), shape((256, 512), BF)),
        smem=2,
        inputs=3,
        flops=8 * 256 * 1024 * 2,
        size=1 << 20,
        vmem_mib=60,
    )(lengths, group_ids, states, reward_head.reshape(8, 128), w_t)
    w_cols = lax.all_to_all(w_pack, "zh", 0, 0, tiled=True)
    dir_here, w_cols = lax.optimization_barrier((dir_here, w_cols))
    dirs = call(spread_kernel, shape((16, 136, 256), BF), inputs=1, flops=1 << 10, size=1 << 20)(
        dir_here
    )
    dirs = lax.all_to_all(dirs, DP, 0, 0, tiled=True)
    weights = [w_cols] + [lax.ppermute(w_cols, "sec", ring(k)) for k in (1, 2, 3)]
    own = jnp.concatenate(
        [lax.ppermute(half0, ALL, TO_POOL[0]), lax.ppermute(half1, ALL, TO_POOL[1])], axis=0
    )
    other = swap(own)
    pay = call(terms_kernel, shape((24, 128), F32), inputs=7, flops=1 << 30, size=4 << 20)(
        own, other, *weights, dirs
    )
    pays = call(join_kernel, shape((16, 24, 128), F32), inputs=2, flops=1 << 12, size=1 << 18)(
        pay, swap(pay)
    )
    pays = lax.all_to_all(pays, DP, 0, 0, tiled=True)
    parts = call(
        grads_kernel,
        shape((16, 136, 128), BF),
        scratch=[
            pltpu.VMEM((512, 1024), BF),
            pltpu.VMEM((32, 128), F32),
            pltpu.VMEM((8, 128), F32),
        ],
        inputs=4,
        flops=1 << 29,
        size=4 << 20,
    )(pays, own, other, dirs)
    parts = lax.all_to_all(parts, ("zh", "sec"), 0, 0, tiled=True)
    grad, packed = call(
        finish_kernel,
        (shape((128, 128), F32), shape((1, 320), F32)),
        inputs=1,
        flops=1 << 20,
        size=1 << 20,
    )(parts)
    return grad, packed.reshape(1, 1, 320)


def solution(mesh):
    fine = Mesh(mesh.devices.reshape(2, 8, 4, 2, 4), ALL)
    rows, cols = ("zl", "y", "sec"), ("zh", "core")
    return jax.shard_map(
        body,
        mesh=fine,
        in_specs=(
            P(rows, cols),
            P(rows, cols),
            P(rows),
            P(rows),
            P(rows),
            P(rows, None),
            P(cols),
            P(rows, cols),
            P(rows, cols),
        ),
        out_specs=(P(rows, cols), P(DP, "sec", None)),
        check_vma=False,
    )
```

time: 127 us -> 157 us (1.24)
  the two profiles are of different devices: /device:TPU:72 before, /device:TPU:8 now
where the time goes in v7:
time: 157 us; the launch traced here: 156 us
  waiting for transfers between devices  56.4 us (36%)
  blocking collectives  49.1 us (31%)
  starting transfers between devices  41.2 us (26%)
  Pallas kernels  8.36 us (5%)
    ppermute x1, waiting for transfers between devices, body(): lax.ppermute(half1, ALL, TO_POOL[1])  32.4 us
    all_to_all x1, blocking collectives, body(): pays = lax.all_to_all(pays, DP, 0, 0, tiled=True)  26.5 us
    all_to_all x1, blocking collectives, body(): parts = lax.all_to_all(parts, ('zh', 'sec'), 0, 0, tiled=True)  22.7 us
    ppermute x3, waiting for transfers between devices, body(): lax.ppermute(w_cols, 'sec', ring(k))  12.1 us
    all_to_all x1, waiting for transfers between devices, body(): w_cols = lax.all_to_all(w_pack, 'zh', 0, 0, tiled=True)  10.7 us
    all_to_all x1, starting transfers between devices, body(): w_cols = lax.all_to_all(w_pack, 'zh', 0, 0, tiled=True)  10.3 us
    all_to_all x1, starting transfers between devices, body(): dirs = lax.all_to_all(dirs, DP, 0, 0, tiled=True)  10.2 us
    ppermute x3, starting transfers between devices, body(): lax.ppermute(w_cols, 'sec', ring(k))  10.2 us
  transfers between devices with their start and end apart: 10, of which 6 were waited for; matrix products, arithmetic and copies ran while one was open for 0% of the time, Pallas kernels for 0%

profile of v7, /device:TPU:8, one launch (start us, length us, event | category | flops | bytes accessed | tf_op | source)
XLA Modules:
  0.0 156.0 jit_solution(5764681880424603980)
XLA Ops:
  0.6 1.6 %shard_map.104 = (bf16[136,256]{1,0:T(8,128)(2,1)}, bf16[256,128]{1,0:T(8,128)(2,1)}) custom-call(bf16[256,128]{1,0:T(8,128)(2,1)} %direction.1, s32[1,256]{1,0:T(1,128)} %bitcast.5, bf16[2,128]{1,0:T(2,128)(2,1)} %bitcast.6, bf16[128,128]{1,0:T(8,128)(2,1)} %wp.1, bf16[128,128]{1,0:T(8,128)(2,1)} %wr.1), custom_call_target="tpu_custom_call" | custom-call | flops 65536 | bytes 262144 | tf_op jit(solution)/shard_map/pallas_call | solution.py:290
  2.3 0.0 copy-start.2
  2.3 2.2 %shard_map.105 = (bf16[4,272,128]{2,1,0:T(8,128)(2,1)}, bf16[256,512]{1,0:T(8,128)(2,1)}, bf16[256,512]{1,0:T(8,128)(2,1)}) custom-call(s32[2]{0:T(128)} %lengths.1, s32[2]{0:T(128)} %group_ids.1, bf16[256,1024]{1,0:T(8,128)(2,1)} %states.1, bf16[8,128]{1,0:T(8,128)(2,1)} %bitcast.4, bf16[256,128]{1,0:T(8,128)(2,1)} %get-tuple-element.11.w_t), custom_call_target="tpu_custom_call" | custom-call | flops 4194304 | bytes 1048576 | tf_op jit(solution)/shard_map/pallas_call | solution.py:299
  4.5 10.3 %all-to-all-start = ((bf16[4,272,128]{2,1,0:T(8,128)(2,1)}), bf16[4,272,128]{2,1,0:T(8,128)(2,1)S(1)}, u32[]{:S(2)}, u32[]{:S(2)}) async-start(bf16[4,272,128]{2,1,0:T(8,128)(2,1)} %get-tuple-element.15), calls=%async_computation | async-start | bytes 557056 | tf_op jit(solution)/shard_map/all_to_all | solution.py:308
  14.8 0.0 copy-done.2
  14.8 0.7 collective-permute-start.3
  15.5 0.0 collective-permute-done.3.block
  15.5 10.7 %all-to-all-done.w0 = bf16[4,272,128]{2,1,0:T(8,128)(2,1)S(1)} async-done(((bf16[4,272,128]{2,1,0:T(8,128)(2,1)}), bf16[4,272,128]{2,1,0:T(8,128)(2,1)S(1)}, u32[]{:S(2)}, u32[]{:S(2)}) %all-to-all-start) | async-done | bytes 278560 | tf_op jit(solution)/shard_map/all_to_all | solution.py:308
  26.2 1.1 shard_map.106
  27.3 0.0 copy-start.1
  27.3 0.0 copy-start
  27.3 10.2 %all-to-all-start.1 = ((bf16[16,136,256]{2,1,0:T(8,128)(2,1)}), bf16[16,136,256]{2,1,0:T(8,128)(2,1)S(1)}, u32[]{:S(2)}, u32[]{:S(2)}) async-start(bf16[16,136,256]{2,1,0:T(8,128)(2,1)} %shard_map.106), calls=%async_computation.1 | async-start | bytes 2228224 | tf_op jit(solution)/shard_map/all_to_all | solution.py:313
  37.5 0.0 copy-done.1
  37.5 0.7 collective-permute-start
  38.2 0.0 copy-done
  38.2 2.0 %collective-permute-start.1 = (bf16[256,512]{1,0:T(8,128)(2,1)S(1)}, bf16[256,512]{1,0:T(8,128)(2,1)S(1)}, u32[]{:S(2)}, u32[]{:S(2)}) collective-permute-start(bf16[256,512]{1,0:T(8,128)(2,1)S(1)} %copy-done), channel_id=1, source_target_pairs={{0,32},{1,33},{2,34},{3,35},{4,96},{5,97},{6,98},{7,99},{8,160},{9... | collective-permute-start | bytes 786440 | tf_op jit(solution)/shard_map/ppermute | solution.py:316
  40.2 0.0 collective-permute-done
  40.2 32.4 %collective-permute-done.1 = bf16[256,512]{1,0:T(8,128)(2,1)S(1)} collective-permute-done((bf16[256,512]{1,0:T(8,128)(2,1)S(1)}, bf16[256,512]{1,0:T(8,128)(2,1)S(1)}, u32[]{:S(2)}, u32[]{:S(2)}) %collective-permute-start.1) | collective-permute-done | bytes 262176 | tf_op jit(solution)/shard_map/ppermute | solution.py:316
  72.7 5.3 %collective-permute-start.2 = (bf16[512,512]{1,0:T(8,128)(2,1)S(1)}, bf16[512,512]{1,0:T(8,128)(2,1)S(1)}, u32[]{:S(2)}, u32[]{:S(2)}) collective-permute-start(bf16[512,512]{1,0:T(8,128)(2,1)S(1)} %constant_dynamic-update-slice_fusion.own), channel_id=1, source_target_pairs={{0,4},{4,0},{1,5},{5,1},{2,6},{6,2},{3,7},{7,3},{8,12},{12,8},{9,1... | collective-permute-start | bytes 1572872 | tf_op jit(solution)/shard_map/ppermute | solution.py:284
  78.0 4.7 %collective-permute-start.6 = (bf16[4,272,128]{2,1,0:T(8,128)(2,1)S(1)}, bf16[4,272,128]{2,1,0:T(8,128)(2,1)S(1)}, u32[]{:S(2)}, u32[]{:S(2)}) collective-permute-start(bf16[4,272,128]{2,1,0:T(8,128)(2,1)S(1)} %all-to-all-done.w0), channel_id=1, source_target_pairs={{0,3},{1,0},{2,1},{3,2},{4,7},{5,4},{6,5},{7,6},{8,11},{9,8},{10,9... | collective-permute-start | bytes 835592 | tf_op jit(solution)/shard_map/ppermute | solution.py:314
  82.7 2.7 %collective-permute-start.5 = (bf16[4,272,128]{2,1,0:T(8,128)(2,1)S(1)}, bf16[4,272,128]{2,1,0:T(8,128)(2,1)S(1)}, u32[]{:S(2)}, u32[]{:S(2)}) collective-permute-start(bf16[4,272,128]{2,1,0:T(8,128)(2,1)S(1)} %all-to-all-done.w0), channel_id=1, source_target_pairs={{0,2},{1,3},{2,0},{3,1},{4,6},{5,7},{6,4},{7,5},{8,10},{9,11},{10,... | collective-permute-start | bytes 835592 | tf_op jit(solution)/shard_map/ppermute | solution.py:314
  85.4 2.8 %collective-permute-start.4 = (bf16[4,272,128]{2,1,0:T(8,128)(2,1)S(1)}, bf16[4,272,128]{2,1,0:T(8,128)(2,1)S(1)}, u32[]{:S(2)}, u32[]{:S(2)}) collective-permute-start(bf16[4,272,128]{2,1,0:T(8,128)(2,1)S(1)} %all-to-all-done.w0), channel_id=1, source_target_pairs={{0,1},{1,2},{2,3},{3,0},{4,5},{5,6},{6,7},{7,4},{8,9},{9,10},{10,1... | collective-permute-start | bytes 835592 | tf_op jit(solution)/shard_map/ppermute | solution.py:314
  88.2 6.6 %collective-permute-done.6.w3 = bf16[4,272,128]{2,1,0:T(8,128)(2,1)S(1)} collective-permute-done((bf16[4,272,128]{2,1,0:T(8,128)(2,1)S(1)}, bf16[4,272,128]{2,1,0:T(8,128)(2,1)S(1)}, u32[]{:S(2)}, u32[]{:S(2)}) %collective-permute-start.6) | collective-permute-done | bytes 278560 | tf_op jit(solution)/shard_map/ppermute | solution.py:314
  94.8 0.9 collective-permute-done.5.w2
  95.7 4.7 %collective-permute-done.4.w1 = bf16[4,272,128]{2,1,0:T(8,128)(2,1)S(1)} collective-permute-done((bf16[4,272,128]{2,1,0:T(8,128)(2,1)S(1)}, bf16[4,272,128]{2,1,0:T(8,128)(2,1)S(1)}, u32[]{:S(2)}, u32[]{:S(2)}) %collective-permute-start.4) | collective-permute-done | bytes 278560 | tf_op jit(solution)/shard_map/ppermute | solution.py:314
  100.3 0.0 collective-permute-done.2.other
  100.3 0.0 all-to-all-done.1.dirs
  100.4 1.3 shard_map.107.mine
  101.7 1.9 %collective-permute-start.7 = (f32[24,128]{1,0:T(8,128)S(1)}, f32[24,128]{1,0:T(8,128)S(1)}, u32[]{:S(2)}, u32[]{:S(2)}) collective-permute-start(f32[24,128]{1,0:T(8,128)S(1)} %shard_map.107.mine), channel_id=1, source_target_pairs={{0,4},{4,0},{1,5},{5,1},{2,6},{6,2},{3,7},{7,3},{8,12},{12,8},{9,1... | collective-permute-start | bytes 36872 | tf_op jit(solution)/shard_map/ppermute | solution.py:284
  103.6 1.1 collective-permute-done.7.partner
  104.8 26.5 %all_to_all.20.pays = f32[16,24,128]{2,1,0:T(8,128)S(1)} all-to-all(f32[16,24,128]{2,1,0:T(8,128)S(1)} %shard_map.108), channel_id=1, replica_groups=mesh['zl'=2,'y'=8,'zh'=4,'core'=2,'sec'=4] {'zl','y'}, dimensions={0} | all-to-all | bytes 393216 | tf_op jit(solution)/shard_map/all_to_all | solution.py:325
  131.2 1.3 shard_map.109
  132.5 22.7 %all_to_all.21.parts = bf16[16,136,128]{2,1,0:T(8,128)(2,1)S(1)} all-to-all(bf16[16,136,128]{2,1,0:T(8,128)(2,1)S(1)} %shard_map.109), channel_id=1, replica_groups=mesh['zl'=2,'y'=8,'zh'=4,'core'=2,'sec'=4] {'zh','sec'}, dimensions={0} | all-to-all | bytes 1114112 | tf_op jit(solution)/shard_map/all_to_all | solution.py:338
  155.2 0.8 shard_map.110
  (3 shorter events, 0.1 us)
Async XLA Ops:
  2.3 12.5 %copy-start.2 = (bf16[136,256]{1,0:T(8,128)(2,1)S(1)}, bf16[136,256]{1,0:T(8,128)(2,1)}, u32[]{:S(2)}) copy-start(bf16[136,256]{1,0:T(8,128)(2,1)} %get-tuple-element.14) | copy-start | bytes 208900
  4.5 21.7 %all-to-all-start = ((bf16[4,272,128]{2,1,0:T(8,128)(2,1)}), bf16[4,272,128]{2,1,0:T(8,128)(2,1)S(1)}, u32[]{:S(2)}, u32[]{:S(2)}) async-start(bf16[4,272,128]{2,1,0:T(8,128)(2,1)} %get-tuple-element.15), calls=%async_computation | async-start | bytes 557056 | tf_op jit(solution)/shard_map/all_to_all | solution.py:308
  14.8 0.7 collective-permute-start.3
  27.3 10.2 %copy-start.1 = (bf16[256,512]{1,0:T(8,128)(2,1)S(1)}, bf16[256,512]{1,0:T(8,128)(2,1)}, u32[]{:S(2)}) copy-start(bf16[256,512]{1,0:T(8,128)(2,1)} %get-tuple-element.12) | copy-start | bytes 786436
  27.3 10.9 %copy-start = (bf16[256,512]{1,0:T(8,128)(2,1)S(1)}, bf16[256,512]{1,0:T(8,128)(2,1)}, u32[]{:S(2)}) copy-start(bf16[256,512]{1,0:T(8,128)(2,1)} %get-tuple-element.13) | copy-start | bytes 786436
  27.3 73.1 %all-to-all-start.1 = ((bf16[16,136,256]{2,1,0:T(8,128)(2,1)}), bf16[16,136,256]{2,1,0:T(8,128)(2,1)S(1)}, u32[]{:S(2)}, u32[]{:S(2)}) async-start(bf16[16,136,256]{2,1,0:T(8,128)(2,1)} %shard_map.106), calls=%async_computation.1 | async-start | bytes 2228224 | tf_op jit(solution)/shard_map/all_to_all | solution.py:313
  37.5 2.7 %collective-permute-start = (bf16[256,512]{1,0:T(8,128)(2,1)S(1)}, bf16[256,512]{1,0:T(8,128)(2,1)S(1)}, u32[]{:S(2)}, u32[]{:S(2)}) collective-permute-start(bf16[256,512]{1,0:T(8,128)(2,1)S(1)} %copy-done.1), channel_id=1, source_target_pairs={{0,0},{1,1},{2,2},{3,3},{4,64},{5,65},{6,66},{7,67},{8,128},{9,129... | collective-permute-start | bytes 786440 | tf_op jit(solution)/shard_map/ppermute | solution.py:316
  38.2 34.5 %collective-permute-start.1 = (bf16[256,512]{1,0:T(8,128)(2,1)S(1)}, bf16[256,512]{1,0:T(8,128)(2,1)S(1)}, u32[]{:S(2)}, u32[]{:S(2)}) collective-permute-start(bf16[256,512]{1,0:T(8,128)(2,1)S(1)} %copy-done), channel_id=1, source_target_pairs={{0,32},{1,33},{2,34},{3,35},{4,96},{5,97},{6,98},{7,99},{8,160},{9... | collective-permute-start | bytes 786440 | tf_op jit(solution)/shard_map/ppermute | solution.py:316
  72.7 27.7 %collective-permute-start.2 = (bf16[512,512]{1,0:T(8,128)(2,1)S(1)}, bf16[512,512]{1,0:T(8,128)(2,1)S(1)}, u32[]{:S(2)}, u32[]{:S(2)}) collective-permute-start(bf16[512,512]{1,0:T(8,128)(2,1)S(1)} %constant_dynamic-update-slice_fusion.own), channel_id=1, source_target_pairs={{0,4},{4,0},{1,5},{5,1},{2,6},{6,2},{3,7},{7,3},{8,12},{12,8},{9,1... | collective-permute-start | bytes 1572872 | tf_op jit(solution)/shard_map/ppermute | solution.py:284
  78.0 16.7 %collective-permute-start.6 = (bf16[4,272,128]{2,1,0:T(8,128)(2,1)S(1)}, bf16[4,272,128]{2,1,0:T(8,128)(2,1)S(1)}, u32[]{:S(2)}, u32[]{:S(2)}) collective-permute-start(bf16[4,272,128]{2,1,0:T(8,128)(2,1)S(1)} %all-to-all-done.w0), channel_id=1, source_target_pairs={{0,3},{1,0},{2,1},{3,2},{4,7},{5,4},{6,5},{7,6},{8,11},{9,8},{10,9... | collective-permute-start | bytes 835592 | tf_op jit(solution)/shard_map/ppermute | solution.py:314
  82.7 13.0 %collective-permute-start.5 = (bf16[4,272,128]{2,1,0:T(8,128)(2,1)S(1)}, bf16[4,272,128]{2,1,0:T(8,128)(2,1)S(1)}, u32[]{:S(2)}, u32[]{:S(2)}) collective-permute-start(bf16[4,272,128]{2,1,0:T(8,128)(2,1)S(1)} %all-to-all-done.w0), channel_id=1, source_target_pairs={{0,2},{1,3},{2,0},{3,1},{4,6},{5,7},{6,4},{7,5},{8,10},{9,11},{10,... | collective-permute-start | bytes 835592 | tf_op jit(solution)/shard_map/ppermute | solution.py:314
  85.4 14.9 %collective-permute-start.4 = (bf16[4,272,128]{2,1,0:T(8,128)(2,1)S(1)}, bf16[4,272,128]{2,1,0:T(8,128)(2,1)S(1)}, u32[]{:S(2)}, u32[]{:S(2)}) collective-permute-start(bf16[4,272,128]{2,1,0:T(8,128)(2,1)S(1)} %all-to-all-done.w0), channel_id=1, source_target_pairs={{0,1},{1,2},{2,3},{3,0},{4,5},{5,6},{6,7},{7,4},{8,9},{9,10},{10,1... | collective-permute-start | bytes 835592 | tf_op jit(solution)/shard_map/ppermute | solution.py:314
  101.7 3.1 %collective-permute-start.7 = (f32[24,128]{1,0:T(8,128)S(1)}, f32[24,128]{1,0:T(8,128)S(1)}, u32[]{:S(2)}, u32[]{:S(2)}) collective-permute-start(f32[24,128]{1,0:T(8,128)S(1)} %shard_map.107.mine), channel_id=1, source_target_pairs={{0,4},{4,0},{1,5},{5,1},{2,6},{6,2},{3,7},{7,3},{8,12},{12,8},{9,1... | collective-permute-start | bytes 36872 | tf_op jit(solution)/shard_map/ppermute | solution.py:284

commit v8 on v6

--- a/solution.py
+++ b/solution.py
@@ -36,7 +36,7 @@
     turn = (zz - zh + (zh >> 1)) & 3
     zl = (turn & 1) ^ (turn >> 1)
     near = 4 * (zh & 1)
-    y = near + block + (turn >> 1) * (7 - 2 * block)
+    y = near + block + (1 - (turn >> 1)) * (7 - 2 * block)
     return zl * 8 + (y & 7)
 
 
@@ -224,6 +224,7 @@
         tail = placed[:, 128 * a : 128 * (a + 1)].astype(BF)
         for k in range(4):
             out[4 * a + k, 128:136, :] = tail
+            out[4 * a + k, 136:144, :] = jnp.zeros((8, 128), BF)
 
 
 def finish_kernel(parts, grad, packed):
@@ -304,7 +305,6 @@
         vmem_mib=60,
     )(lengths, group_ids, states, reward_head.reshape(8, 128), routes.reshape(1, 256))
     dirs = lax.all_to_all(dir_t, "zh", 0, 0, tiled=True)
-    w_here, dirs = lax.optimization_barrier((w_here, dirs))
     weights = call(
         spread_kernel, shape((16, 272, 128), BF), inputs=2, flops=1 << 10, size=1 << 20
     )(w_here, extra)
@@ -325,7 +325,7 @@
     pays = lax.all_to_all(pays, ("zh", "sec"), 0, 0, tiled=True)
     parts = call(
         grads_kernel,
-        shape((16, 136, 128), BF),
+        shape((16, 144, 128), BF),
         scratch=[
             pltpu.VMEM((512, 1024), BF),
             pltpu.VMEM((8, 128), F32),

time: 127 us -> 123 us (0.969)
  the two profiles are of different devices: /device:TPU:72 before, /device:TPU:8 now
where the time goes in v8:
time: 123 us
  starting transfers between devices  44 us (36%)
  blocking collectives  43.5 us (35%)
  waiting for transfers between devices  24.4 us (20%)
  Pallas kernels  8.52 us (7%)
  local copies, waits for them, and re-layouts  1.36 us (1%)
    all_to_all x1, blocking collectives, body(): parts = lax.all_to_all(parts, DP, 0, 0, tiled=True)  24.9 us
    all_to_all x1, blocking collectives, body(): pays = lax.all_to_all(pays, ('zh', 'sec'), 0, 0, tiled=True)  18.6 us
    ppermute x3, waiting for transfers between devices, body(): lax.ppermute(packs[k], 'sec', ring(k))  12.5 us
    ppermute x3, starting transfers between devices, body(): lax.ppermute(packs[k], 'sec', ring(k))  11.4 us
    all_to_all x1, starting transfers between devices, body(): dirs = lax.all_to_all(dir_t, 'zh', 0, 0, tiled=True)  10.3 us
    all_to_all x1, starting transfers between devices, body(): weights = lax.all_to_all(weights, DP, 0, 0, tiled=True)  8.85 us
    ppermute x1, starting transfers between devices, body(): w_here = lax.ppermute(w_t, ALL, TO_HANDLER)  6.04 us
    ppermute x1, waiting for transfers between devices, body(): return (lax.ppermute(grad, ALL, TO_OWNER), packed.reshape(1, 1, 320))  5.71 us
  transfers between devices with their start and end apart: 9, of which 7 were waited for; matrix products, arithmetic and copies ran while one was open for 0% of the time, Pallas kernels for 3%

profile of v8, /device:TPU:8, one launch (start us, length us, event | category | flops | bytes accessed | tf_op | source)
XLA Modules:
  0.0 122.5 jit_solution(18105963538051059619)
XLA Ops:
  0.6 1.7 %shard_map.105 = (bf16[4,128,256]{2,1,0:T(8,128)(2,1)}, bf16[256,128]{1,0:T(8,128)(2,1)}) custom-call(bf16[256,128]{1,0:T(8,128)(2,1)} %direction.1, bf16[128,128]{1,0:T(8,128)(2,1)} %wp.1, bf16[128,128]{1,0:T(8,128)(2,1)} %wr.1), custom_call_target="tpu_custom_call" | custom-call | flops 65536 | bytes 262144 | tf_op jit(solution)/shard_map/pallas_call | solution.py:289
  2.3 10.3 %all-to-all-start = ((bf16[4,128,256]{2,1,0:T(8,128)(2,1)}), bf16[4,128,256]{2,1,0:T(8,128)(2,1)S(1)}, u32[]{:S(2)}, u32[]{:S(2)}) async-start(bf16[4,128,256]{2,1,0:T(8,128)(2,1)} %get-tuple-element.14), calls=%async_computation | async-start | bytes 524288 | tf_op jit(solution)/shard_map/all_to_all | solution.py:307
  12.6 6.0 %collective-permute-start.4 = (bf16[256,128]{1,0:T(8,128)(2,1)}, bf16[256,128]{1,0:T(8,128)(2,1)S(1)}, u32[]{:S(2)}, u32[]{:S(2)}) collective-permute-start(bf16[256,128]{1,0:T(8,128)(2,1)} %get-tuple-element.19), channel_id=1, source_target_pairs={{0,224},{1,225},{2,226},{3,227},{4,228},{5,229},{6,230},{7,231},{8... | collective-permute-start | bytes 196616 | tf_op jit(solution)/shard_map/ppermute | solution.py:297
  18.7 2.2 %shard_map.104 = (bf16[4,256,256]{2,1,0:T(8,128)(2,1)}, bf16[16,128]{1,0:T(8,128)(2,1)}, s32[1,256]{1,0:T(1,128)}) custom-call(s32[2]{0:T(128)} %lengths.1, s32[2]{0:T(128)} %group_ids.1, bf16[256,1024]{1,0:T(8,128)(2,1)} %states.1, bf16[8,128]{1,0:T(8,128)(2,1)} %bitcast.5, s32[1,256]{1,0:T(1,128)} %bitcast.6), custom_call_target="tpu_custom_call" | custom-call | flops 4194304 | bytes 1048576 | tf_op jit(solution)/shard_map/pallas_call | solution.py:298
  20.9 3.3 %collective-permute-done.4.w = bf16[256,128]{1,0:T(8,128)(2,1)S(1)} collective-permute-done((bf16[256,128]{1,0:T(8,128)(2,1)}, bf16[256,128]{1,0:T(8,128)(2,1)S(1)}, u32[]{:S(2)}, u32[]{:S(2)}) %collective-permute-start.4) | collective-permute-done | bytes 65568 | tf_op jit(solution)/shard_map/ppermute | solution.py:297
  24.1 0.0 copy-start.1
  24.1 0.7 copy-done.1
  24.8 1.2 shard_map.107
  26.0 0.0 copy-start
  26.0 0.0 all-to-all-done.dirs
  26.0 8.8 %all-to-all-start.1 = ((bf16[16,272,128]{2,1,0:T(8,128)(2,1)}), bf16[16,272,128]{2,1,0:T(8,128)(2,1)S(1)}, u32[]{:S(2)}, u32[]{:S(2)}) async-start(bf16[16,272,128]{2,1,0:T(8,128)(2,1)} %shard_map.107), calls=%async_computation.1 | async-start | bytes 2228224 | tf_op jit(solution)/shard_map/all_to_all | solution.py:311
  34.8 0.0 copy-done
  34.8 0.1 shard_map.106
  35.0 3.4 %collective-permute-start = (bf16[768,256]{1,0:T(8,128)(2,1)S(1)}, bf16[768,256]{1,0:T(8,128)(2,1)S(1)}, u32[]{:S(2)}, u32[]{:S(2)}) collective-permute-start(bf16[768,256]{1,0:T(8,128)(2,1)S(1)} %get-tuple-element.16), channel_id=1, source_target_pairs={{0,1},{1,2},{2,3},{3,0},{4,5},{5,6},{6,7},{7,4},{8,9},{9,10},{10,1... | collective-permute-start | bytes 1179656 | tf_op jit(solution)/shard_map/ppermute | solution.py:315
  38.4 4.6 %collective-permute-start.1 = (bf16[768,256]{1,0:T(8,128)(2,1)S(1)}, bf16[768,256]{1,0:T(8,128)(2,1)S(1)}, u32[]{:S(2)}, u32[]{:S(2)}) collective-permute-start(bf16[768,256]{1,0:T(8,128)(2,1)S(1)} %get-tuple-element.17), channel_id=1, source_target_pairs={{0,2},{1,3},{2,0},{3,1},{4,6},{5,7},{6,4},{7,5},{8,10},{9,11},{10,... | collective-permute-start | bytes 1179656 | tf_op jit(solution)/shard_map/ppermute | solution.py:315
  43.0 3.3 %collective-permute-start.2 = (bf16[768,256]{1,0:T(8,128)(2,1)S(1)}, bf16[768,256]{1,0:T(8,128)(2,1)S(1)}, u32[]{:S(2)}, u32[]{:S(2)}) collective-permute-start(bf16[768,256]{1,0:T(8,128)(2,1)S(1)} %get-tuple-element.18), channel_id=1, source_target_pairs={{0,3},{1,0},{2,1},{3,2},{4,7},{5,4},{6,5},{7,6},{8,11},{9,8},{10,9... | collective-permute-start | bytes 1179656 | tf_op jit(solution)/shard_map/ppermute | solution.py:315
  46.4 2.7 %collective-permute-done.s1 = bf16[768,256]{1,0:T(8,128)(2,1)S(1)} collective-permute-done((bf16[768,256]{1,0:T(8,128)(2,1)S(1)}, bf16[768,256]{1,0:T(8,128)(2,1)S(1)}, u32[]{:S(2)}, u32[]{:S(2)}) %collective-permute-start) | collective-permute-done | bytes 393248 | tf_op jit(solution)/shard_map/ppermute | solution.py:315
  49.1 8.2 %collective-permute-done.1.s2 = bf16[768,256]{1,0:T(8,128)(2,1)S(1)} collective-permute-done((bf16[768,256]{1,0:T(8,128)(2,1)S(1)}, bf16[768,256]{1,0:T(8,128)(2,1)S(1)}, u32[]{:S(2)}, u32[]{:S(2)}) %collective-permute-start.1) | collective-permute-done | bytes 393248 | tf_op jit(solution)/shard_map/ppermute | solution.py:315
  57.4 1.5 %collective-permute-done.2.s3 = bf16[768,256]{1,0:T(8,128)(2,1)S(1)} collective-permute-done((bf16[768,256]{1,0:T(8,128)(2,1)S(1)}, bf16[768,256]{1,0:T(8,128)(2,1)S(1)}, u32[]{:S(2)}, u32[]{:S(2)}) %collective-permute-start.2) | collective-permute-done | bytes 393248 | tf_op jit(solution)/shard_map/ppermute | solution.py:315
  59.0 0.0 copy-start.2
  59.0 0.0 copy-start.3
  59.0 1.9 %collective-permute-start.3 = (bf16[1024,256]{1,0:T(8,128)(2,1)S(1)}, bf16[1024,256]{1,0:T(8,128)(2,1)S(1)}, u32[]{:S(2)}, u32[]{:S(2)}) collective-permute-start(bf16[1024,256]{1,0:T(8,128)(2,1)S(1)} %pad_maximum_fusion), channel_id=1, source_target_pairs={{0,4},{4,0},{1,5},{5,1},{2,6},{6,2},{3,7},{7,3},{8,12},{12,8},{9,1... | collective-permute-start | bytes 1572872 | tf_op jit(solution)/shard_map/ppermute | solution.py:316
  61.0 1.9 %collective-permute-done.3.other = bf16[1024,256]{1,0:T(8,128)(2,1)S(1)} collective-permute-done((bf16[1024,256]{1,0:T(8,128)(2,1)S(1)}, bf16[1024,256]{1,0:T(8,128)(2,1)S(1)}, u32[]{:S(2)}, u32[]{:S(2)}) %collective-permute-start.3) | collective-permute-done | bytes 524320 | tf_op jit(solution)/shard_map/ppermute | solution.py:316
  62.8 0.0 all-to-all-done.1.weights
  62.8 1.3 %shard_map.108.mine = f32[24,128]{1,0:T(8,128)S(1)} custom-call(bf16[768,256]{1,0:T(8,128)(2,1)S(1)} %get-tuple-element.15.s0, bf16[768,256]{1,0:T(8,128)(2,1)S(1)} %collective-permute-done.s1, bf16[768,256]{1,0:T(8,128)(2,1)S(1)} %collective-permute-done.1.s2, bf16[768,256]{1,0:T(8,128)(2,1)S(1)} %collective-permute-done.2.s3, ...), custom_call_target="tpu_custom_call" | custom-call | flops 1073741824 | bytes 4194304 | tf_op jit(solution)/shard_map/pallas_call | solution.py:319
  64.2 2.0 %collective-permute-start.5 = (f32[24,128]{1,0:T(8,128)S(1)}, f32[24,128]{1,0:T(8,128)S(1)}, u32[]{:S(2)}, u32[]{:S(2)}) collective-permute-start(f32[24,128]{1,0:T(8,128)S(1)} %shard_map.108.mine), channel_id=1, source_target_pairs={{0,4},{4,0},{1,5},{5,1},{2,6},{6,2},{3,7},{7,3},{8,12},{12,8},{9,1... | collective-permute-start | bytes 36872 | tf_op jit(solution)/shard_map/ppermute | solution.py:323
  66.2 1.0 collective-permute-done.5.partner
  67.3 18.6 %all_to_all.20.pays = f32[16,24,128]{2,1,0:T(8,128)S(1)} all-to-all(f32[16,24,128]{2,1,0:T(8,128)S(1)} %shard_map.109), channel_id=1, replica_groups=mesh['zl'=2,'y'=8,'zh'=4,'core'=2,'sec'=4] {'zh','sec'}, dimensions={0} | all-to-all | bytes 393216 | tf_op jit(solution)/shard_map/all_to_all | solution.py:325
  85.8 0.0 copy-done.2
  85.8 0.0 copy-done.3
  85.8 1.1 shard_map.110
  86.9 24.9 %all_to_all.21.parts = bf16[16,144,128]{2,1,0:T(8,128)(2,1)S(1)} all-to-all(bf16[16,144,128]{2,1,0:T(8,128)(2,1)S(1)} %shard_map.110), channel_id=1, replica_groups=mesh['zl'=2,'y'=8,'zh'=4,'core'=2,'sec'=4] {'zl','y'}, dimensions={0} | all-to-all | bytes 1179648 | tf_op jit(solution)/shard_map/all_to_all | solution.py:337
  111.9 0.9 shard_map.111
  112.7 3.4 %collective-permute-start.6 = (f32[128,128]{1,0:T(8,128)S(1)}, f32[128,128]{1,0:T(8,128)S(1)}, u32[]{:S(2)}, u32[]{:S(2)}) collective-permute-start(f32[128,128]{1,0:T(8,128)S(1)} %get-tuple-element.22), channel_id=1, source_target_pairs={{224,0},{225,1},{226,2},{227,3},{228,4},{229,5},{230,6},{231,7},{4... | collective-permute-start | bytes 196616 | tf_op jit(solution)/shard_map/ppermute | solution.py:345
  116.2 5.7 %collective-permute-done.6 = f32[128,128]{1,0:T(8,128)S(1)} collective-permute-done((f32[128,128]{1,0:T(8,128)S(1)}, f32[128,128]{1,0:T(8,128)S(1)}, u32[]{:S(2)}, u32[]{:S(2)}) %collective-permute-start.6) | collective-permute-done | bytes 65568 | tf_op jit(solution)/shard_map/ppermute | solution.py:345
  121.9 0.6 copy.12
  (6 shorter events, 0.1 us)
Async XLA Ops:
  2.3 23.7 %all-to-all-start = ((bf16[4,128,256]{2,1,0:T(8,128)(2,1)}), bf16[4,128,256]{2,1,0:T(8,128)(2,1)S(1)}, u32[]{:S(2)}, u32[]{:S(2)}) async-start(bf16[4,128,256]{2,1,0:T(8,128)(2,1)} %get-tuple-element.14), calls=%async_computation | async-start | bytes 524288 | tf_op jit(solution)/shard_map/all_to_all | solution.py:307
  12.6 11.5 %collective-permute-start.4 = (bf16[256,128]{1,0:T(8,128)(2,1)}, bf16[256,128]{1,0:T(8,128)(2,1)S(1)}, u32[]{:S(2)}, u32[]{:S(2)}) collective-permute-start(bf16[256,128]{1,0:T(8,128)(2,1)} %get-tuple-element.19), channel_id=1, source_target_pairs={{0,224},{1,225},{2,226},{3,227},{4,228},{5,229},{6,230},{7,231},{8... | collective-permute-start | bytes 196616 | tf_op jit(solution)/shard_map/ppermute | solution.py:297
  24.1 0.7 copy-start.1
  26.0 8.9 %copy-start = (bf16[4,256,256]{2,1,0:T(8,128)(2,1)S(1)}, bf16[4,256,256]{2,1,0:T(8,128)(2,1)}, u32[]{:S(2)}) copy-start(bf16[4,256,256]{2,1,0:T(8,128)(2,1)} %get-tuple-element.13.quarters) | copy-start | bytes 1572868
  26.0 36.8 %all-to-all-start.1 = ((bf16[16,272,128]{2,1,0:T(8,128)(2,1)}), bf16[16,272,128]{2,1,0:T(8,128)(2,1)S(1)}, u32[]{:S(2)}, u32[]{:S(2)}) async-start(bf16[16,272,128]{2,1,0:T(8,128)(2,1)} %shard_map.107), calls=%async_computation.1 | async-start | bytes 2228224 | tf_op jit(solution)/shard_map/all_to_all | solution.py:311
  35.0 14.2 %collective-permute-start = (bf16[768,256]{1,0:T(8,128)(2,1)S(1)}, bf16[768,256]{1,0:T(8,128)(2,1)S(1)}, u32[]{:S(2)}, u32[]{:S(2)}) collective-permute-start(bf16[768,256]{1,0:T(8,128)(2,1)S(1)} %get-tuple-element.16), channel_id=1, source_target_pairs={{0,1},{1,2},{2,3},{3,0},{4,5},{5,6},{6,7},{7,4},{8,9},{9,10},{10,1... | collective-permute-start | bytes 1179656 | tf_op jit(solution)/shard_map/ppermute | solution.py:315
  38.4 19.0 %collective-permute-start.1 = (bf16[768,256]{1,0:T(8,128)(2,1)S(1)}, bf16[768,256]{1,0:T(8,128)(2,1)S(1)}, u32[]{:S(2)}, u32[]{:S(2)}) collective-permute-start(bf16[768,256]{1,0:T(8,128)(2,1)S(1)} %get-tuple-element.17), channel_id=1, source_target_pairs={{0,2},{1,3},{2,0},{3,1},{4,6},{5,7},{6,4},{7,5},{8,10},{9,11},{10,... | collective-permute-start | bytes 1179656 | tf_op jit(solution)/shard_map/ppermute | solution.py:315
  43.0 15.9 %collective-permute-start.2 = (bf16[768,256]{1,0:T(8,128)(2,1)S(1)}, bf16[768,256]{1,0:T(8,128)(2,1)S(1)}, u32[]{:S(2)}, u32[]{:S(2)}) collective-permute-start(bf16[768,256]{1,0:T(8,128)(2,1)S(1)} %get-tuple-element.18), channel_id=1, source_target_pairs={{0,3},{1,0},{2,1},{3,2},{4,7},{5,4},{6,5},{7,6},{8,11},{9,8},{10,9... | collective-permute-start | bytes 1179656 | tf_op jit(solution)/shard_map/ppermute | solution.py:315
  59.0 26.8 %copy-start.2 = (s32[1,256]{1,0:T(1,128)S(1)}, s32[1,256]{1,0:T(1,128)}, u32[]{:S(2)}) copy-start(s32[1,256]{1,0:T(1,128)} %get-tuple-element.21.slots) | copy-start | bytes 3076
  59.0 26.8 %copy-start.3 = (bf16[256]{0:T(256)(128)(2,1)S(1)}, bf16[256]{0:T(256)(128)(2,1)}, u32[]{:S(2)}) copy-start(bf16[256]{0:T(256)(128)(2,1)} %param.11) | copy-start | bytes 1540
  59.0 3.8 %collective-permute-start.3 = (bf16[1024,256]{1,0:T(8,128)(2,1)S(1)}, bf16[1024,256]{1,0:T(8,128)(2,1)S(1)}, u32[]{:S(2)}, u32[]{:S(2)}) collective-permute-start(bf16[1024,256]{1,0:T(8,128)(2,1)S(1)} %pad_maximum_fusion), channel_id=1, source_target_pairs={{0,4},{4,0},{1,5},{5,1},{2,6},{6,2},{3,7},{7,3},{8,12},{12,8},{9,1... | collective-permute-start | bytes 1572872 | tf_op jit(solution)/shard_map/ppermute | solution.py:316
  64.2 3.1 %collective-permute-start.5 = (f32[24,128]{1,0:T(8,128)S(1)}, f32[24,128]{1,0:T(8,128)S(1)}, u32[]{:S(2)}, u32[]{:S(2)}) collective-permute-start(f32[24,128]{1,0:T(8,128)S(1)} %shard_map.108.mine), channel_id=1, source_target_pairs={{0,4},{4,0},{1,5},{5,1},{2,6},{6,2},{3,7},{7,3},{8,12},{12,8},{9,1... | collective-permute-start | bytes 36872 | tf_op jit(solution)/shard_map/ppermute | solution.py:323
  112.7 9.2 %collective-permute-start.6 = (f32[128,128]{1,0:T(8,128)S(1)}, f32[128,128]{1,0:T(8,128)S(1)}, u32[]{:S(2)}, u32[]{:S(2)}) collective-permute-start(f32[128,128]{1,0:T(8,128)S(1)} %get-tuple-element.22), channel_id=1, source_target_pairs={{224,0},{225,1},{226,2},{227,3},{228,4},{229,5},{230,6},{231,7},{4... | collective-permute-start | bytes 196616 | tf_op jit(solution)/shard_map/ppermute | solution.py:345

commit v9 on v8

--- a/solution.py
+++ b/solution.py
@@ -91,10 +91,15 @@
             outs[k][256 + 128 * q : 384 + 128 * q, :] = dirs[q]
 
 
-def spread_kernel(w, extra, out):
+def spread_kernel(w, extra, out, sems):
+    copies = []
     for k in range(16):
-        out[k, 0:256, :] = w[...]
-        out[k, 256:272, :] = extra[...]
+        copies.append(pltpu.make_async_copy(w, out.at[k, 0:256, :], sems.at[k]))
+        copies.append(pltpu.make_async_copy(extra, out.at[k, 256:272, :], sems.at[16 + k]))
+    for copy in copies:
+        copy.start()
+    for copy in copies:
+        copy.wait()
 
 
 def terms_kernel(s0, s1, s2, s3, other, weights, pay):
@@ -224,7 +229,6 @@
         tail = placed[:, 128 * a : 128 * (a + 1)].astype(BF)
         for k in range(4):
             out[4 * a + k, 128:136, :] = tail
-            out[4 * a + k, 136:144, :] = jnp.zeros((8, 128), BF)
 
 
 def finish_kernel(parts, grad, packed):
@@ -305,8 +309,15 @@
         vmem_mib=60,
     )(lengths, group_ids, states, reward_head.reshape(8, 128), routes.reshape(1, 256))
     dirs = lax.all_to_all(dir_t, "zh", 0, 0, tiled=True)
-    weights = call(
-        spread_kernel, shape((16, 272, 128), BF), inputs=2, flops=1 << 10, size=1 << 20
+    anywhere = pl.BlockSpec(memory_space=pl.ANY)
+    weights = pl.pallas_call(
+        spread_kernel,
+        out_shape=shape((16, 272, 128), BF),
+        in_specs=[anywhere, pl.BlockSpec(memory_space=pltpu.HBM)],
+        out_specs=anywhere,
+        scratch_shapes=[pltpu.SemaphoreType.DMA((32,))],
+        cost_estimate=cost(1 << 10, 1 << 20),
+        compiler_params=pltpu.CompilerParams(vmem_limit_bytes=16 << 20),
     )(w_here, extra)
     weights = lax.all_to_all(weights, DP, 0, 0, tiled=True)
     packs = call(
@@ -325,7 +336,7 @@
     pays = lax.all_to_all(pays, ("zh", "sec"), 0, 0, tiled=True)
     parts = call(
         grads_kernel,
-        shape((16, 144, 128), BF),
+        shape((16, 136, 128), BF),
         scratch=[
             pltpu.VMEM((512, 1024), BF),
             pltpu.VMEM((8, 128), F32),

time: 123 us -> 123 us (level)
  no operation moved by 1% of the time
where the time goes in v9:
time: 123 us; the launch traced here: 122 us
  starting transfers between devices  44 us (36%)
  blocking collectives  42.9 us (35%)
  waiting for transfers between devices  24.4 us (20%)
  Pallas kernels  8.65 us (7%)
  local copies, waits for them, and re-layouts  1.36 us (1%)
    all_to_all x1, blocking collectives, body(): parts = lax.all_to_all(parts, DP, 0, 0, tiled=True)  24.4 us
    all_to_all x1, blocking collectives, body(): pays = lax.all_to_all(pays, ('zh', 'sec'), 0, 0, tiled=True)  18.5 us
    ppermute x3, waiting for transfers between devices, body(): lax.ppermute(packs[k], 'sec', ring(k))  12.5 us
    ppermute x3, starting transfers between devices, body(): lax.ppermute(packs[k], 'sec', ring(k))  11.4 us
    all_to_all x1, starting transfers between devices, body(): dirs = lax.all_to_all(dir_t, 'zh', 0, 0, tiled=True)  10.3 us
    all_to_all x1, starting transfers between devices, body(): weights = lax.all_to_all(weights, DP, 0, 0, tiled=True)  8.86 us
    ppermute x1, starting transfers between devices, body(): w_here = lax.ppermute(w_t, ALL, TO_HANDLER)  6.04 us
    ppermute x1, waiting for transfers between devices, body(): return (lax.ppermute(grad, ALL, TO_OWNER), packed.reshape(1, 1, 320))  5.68 us
  transfers between devices with their start and end apart: 9, of which 7 were waited for; matrix products, arithmetic and copies ran while one was open for 0% of the time, Pallas kernels for 3%

profile of v9, /device:TPU:8, one launch (start us, length us, event | category | flops | bytes accessed | tf_op | source)
XLA Modules:
  0.0 122.1 jit_solution(13708322273374586497)
XLA Ops:
  0.6 1.7 %shard_map.105 = (bf16[4,128,256]{2,1,0:T(8,128)(2,1)}, bf16[256,128]{1,0:T(8,128)(2,1)}) custom-call(bf16[256,128]{1,0:T(8,128)(2,1)} %direction.1, bf16[128,128]{1,0:T(8,128)(2,1)} %wp.1, bf16[128,128]{1,0:T(8,128)(2,1)} %wr.1), custom_call_target="tpu_custom_call" | custom-call | flops 65536 | bytes 262144 | tf_op jit(solution)/shard_map/pallas_call | solution.py:293
  2.3 10.3 %all-to-all-start = ((bf16[4,128,256]{2,1,0:T(8,128)(2,1)}), bf16[4,128,256]{2,1,0:T(8,128)(2,1)S(1)}, u32[]{:S(2)}, u32[]{:S(2)}) async-start(bf16[4,128,256]{2,1,0:T(8,128)(2,1)} %get-tuple-element.14), calls=%async_computation | async-start | bytes 524288 | tf_op jit(solution)/shard_map/all_to_all | solution.py:311
  12.6 6.0 %collective-permute-start.4 = (bf16[256,128]{1,0:T(8,128)(2,1)}, bf16[256,128]{1,0:T(8,128)(2,1)S(1)}, u32[]{:S(2)}, u32[]{:S(2)}) collective-permute-start(bf16[256,128]{1,0:T(8,128)(2,1)} %get-tuple-element.19), channel_id=1, source_target_pairs={{0,224},{1,225},{2,226},{3,227},{4,228},{5,229},{6,230},{7,231},{8... | collective-permute-start | bytes 196616 | tf_op jit(solution)/shard_map/ppermute | solution.py:301
  18.7 2.2 %shard_map.104 = (bf16[4,256,256]{2,1,0:T(8,128)(2,1)}, bf16[16,128]{1,0:T(8,128)(2,1)}, s32[1,256]{1,0:T(1,128)}) custom-call(s32[2]{0:T(128)} %lengths.1, s32[2]{0:T(128)} %group_ids.1, bf16[256,1024]{1,0:T(8,128)(2,1)} %states.1, bf16[8,128]{1,0:T(8,128)(2,1)} %bitcast.5, s32[1,256]{1,0:T(1,128)} %bitcast.6), custom_call_target="tpu_custom_call" | custom-call | flops 4194304 | bytes 1048576 | tf_op jit(solution)/shard_map/pallas_call | solution.py:302
  20.9 3.3 %collective-permute-done.4.w = bf16[256,128]{1,0:T(8,128)(2,1)S(1)} collective-permute-done((bf16[256,128]{1,0:T(8,128)(2,1)}, bf16[256,128]{1,0:T(8,128)(2,1)S(1)}, u32[]{:S(2)}, u32[]{:S(2)}) %collective-permute-start.4) | collective-permute-done | bytes 65568 | tf_op jit(solution)/shard_map/ppermute | solution.py:301
  24.1 0.0 copy-start.1
  24.1 0.7 copy-done.1
  24.8 1.3 %shard_map.107 = bf16[16,272,128]{2,1,0:T(8,128)(2,1)} custom-call(bf16[256,128]{1,0:T(8,128)(2,1)S(1)} %collective-permute-done.4.w, bf16[16,128]{1,0:T(8,128)(2,1)S(1)} %copy-done.1), custom_call_target="tpu_custom_call" | custom-call | flops 1024 | bytes 1048576 | tf_op jit(solution)/shard_map/pallas_call | solution.py:313
  26.1 0.0 copy-start
  26.1 0.0 all-to-all-done.dirs
  26.2 8.9 %all-to-all-start.1 = ((bf16[16,272,128]{2,1,0:T(8,128)(2,1)}), bf16[16,272,128]{2,1,0:T(8,128)(2,1)S(1)}, u32[]{:S(2)}, u32[]{:S(2)}) async-start(bf16[16,272,128]{2,1,0:T(8,128)(2,1)} %shard_map.107), calls=%async_computation.1 | async-start | bytes 2228224 | tf_op jit(solution)/shard_map/all_to_all | solution.py:322
  35.0 0.0 copy-done
  35.0 0.1 shard_map.106
  35.1 3.4 %collective-permute-start = (bf16[768,256]{1,0:T(8,128)(2,1)S(1)}, bf16[768,256]{1,0:T(8,128)(2,1)S(1)}, u32[]{:S(2)}, u32[]{:S(2)}) collective-permute-start(bf16[768,256]{1,0:T(8,128)(2,1)S(1)} %get-tuple-element.16), channel_id=1, source_target_pairs={{0,1},{1,2},{2,3},{3,0},{4,5},{5,6},{6,7},{7,4},{8,9},{9,10},{10,1... | collective-permute-start | bytes 1179656 | tf_op jit(solution)/shard_map/ppermute | solution.py:326
  38.5 4.6 %collective-permute-start.1 = (bf16[768,256]{1,0:T(8,128)(2,1)S(1)}, bf16[768,256]{1,0:T(8,128)(2,1)S(1)}, u32[]{:S(2)}, u32[]{:S(2)}) collective-permute-start(bf16[768,256]{1,0:T(8,128)(2,1)S(1)} %get-tuple-element.17), channel_id=1, source_target_pairs={{0,2},{1,3},{2,0},{3,1},{4,6},{5,7},{6,4},{7,5},{8,10},{9,11},{10,... | collective-permute-start | bytes 1179656 | tf_op jit(solution)/shard_map/ppermute | solution.py:326
  43.2 3.3 %collective-permute-start.2 = (bf16[768,256]{1,0:T(8,128)(2,1)S(1)}, bf16[768,256]{1,0:T(8,128)(2,1)S(1)}, u32[]{:S(2)}, u32[]{:S(2)}) collective-permute-start(bf16[768,256]{1,0:T(8,128)(2,1)S(1)} %get-tuple-element.18), channel_id=1, source_target_pairs={{0,3},{1,0},{2,1},{3,2},{4,7},{5,4},{6,5},{7,6},{8,11},{9,8},{10,9... | collective-permute-start | bytes 1179656 | tf_op jit(solution)/shard_map/ppermute | solution.py:326
  46.6 2.7 %collective-permute-done.s1 = bf16[768,256]{1,0:T(8,128)(2,1)S(1)} collective-permute-done((bf16[768,256]{1,0:T(8,128)(2,1)S(1)}, bf16[768,256]{1,0:T(8,128)(2,1)S(1)}, u32[]{:S(2)}, u32[]{:S(2)}) %collective-permute-start) | collective-permute-done | bytes 393248 | tf_op jit(solution)/shard_map/ppermute | solution.py:326
  49.3 8.2 %collective-permute-done.1.s2 = bf16[768,256]{1,0:T(8,128)(2,1)S(1)} collective-permute-done((bf16[768,256]{1,0:T(8,128)(2,1)S(1)}, bf16[768,256]{1,0:T(8,128)(2,1)S(1)}, u32[]{:S(2)}, u32[]{:S(2)}) %collective-permute-start.1) | collective-permute-done | bytes 393248 | tf_op jit(solution)/shard_map/ppermute | solution.py:326
  57.6 1.5 %collective-permute-done.2.s3 = bf16[768,256]{1,0:T(8,128)(2,1)S(1)} collective-permute-done((bf16[768,256]{1,0:T(8,128)(2,1)S(1)}, bf16[768,256]{1,0:T(8,128)(2,1)S(1)}, u32[]{:S(2)}, u32[]{:S(2)}) %collective-permute-start.2) | collective-permute-done | bytes 393248 | tf_op jit(solution)/shard_map/ppermute | solution.py:326
  59.2 0.0 copy-start.2
  59.2 0.0 copy-start.3
  59.2 1.9 %collective-permute-start.3 = (bf16[1024,256]{1,0:T(8,128)(2,1)S(1)}, bf16[1024,256]{1,0:T(8,128)(2,1)S(1)}, u32[]{:S(2)}, u32[]{:S(2)}) collective-permute-start(bf16[1024,256]{1,0:T(8,128)(2,1)S(1)} %pad_maximum_fusion), channel_id=1, source_target_pairs={{0,4},{4,0},{1,5},{5,1},{2,6},{6,2},{3,7},{7,3},{8,12},{12,8},{9,1... | collective-permute-start | bytes 1572872 | tf_op jit(solution)/shard_map/ppermute | solution.py:327
  61.1 1.9 %collective-permute-done.3.other = bf16[1024,256]{1,0:T(8,128)(2,1)S(1)} collective-permute-done((bf16[1024,256]{1,0:T(8,128)(2,1)S(1)}, bf16[1024,256]{1,0:T(8,128)(2,1)S(1)}, u32[]{:S(2)}, u32[]{:S(2)}) %collective-permute-start.3) | collective-permute-done | bytes 524320 | tf_op jit(solution)/shard_map/ppermute | solution.py:327
  63.0 0.0 all-to-all-done.1.weights
  63.0 1.3 %shard_map.108.mine = f32[24,128]{1,0:T(8,128)S(1)} custom-call(bf16[768,256]{1,0:T(8,128)(2,1)S(1)} %get-tuple-element.15.s0, bf16[768,256]{1,0:T(8,128)(2,1)S(1)} %collective-permute-done.s1, bf16[768,256]{1,0:T(8,128)(2,1)S(1)} %collective-permute-done.1.s2, bf16[768,256]{1,0:T(8,128)(2,1)S(1)} %collective-permute-done.2.s3, ...), custom_call_target="tpu_custom_call" | custom-call | flops 1073741824 | bytes 4194304 | tf_op jit(solution)/shard_map/pallas_call | solution.py:330
  64.4 2.0 %collective-permute-start.5 = (f32[24,128]{1,0:T(8,128)S(1)}, f32[24,128]{1,0:T(8,128)S(1)}, u32[]{:S(2)}, u32[]{:S(2)}) collective-permute-start(f32[24,128]{1,0:T(8,128)S(1)} %shard_map.108.mine), channel_id=1, source_target_pairs={{0,4},{4,0},{1,5},{5,1},{2,6},{6,2},{3,7},{7,3},{8,12},{12,8},{9,1... | collective-permute-start | bytes 36872 | tf_op jit(solution)/shard_map/ppermute | solution.py:334
  66.4 1.0 collective-permute-done.5.partner
  67.5 18.5 %all_to_all.20.pays = f32[16,24,128]{2,1,0:T(8,128)S(1)} all-to-all(f32[16,24,128]{2,1,0:T(8,128)S(1)} %shard_map.109), channel_id=1, replica_groups=mesh['zl'=2,'y'=8,'zh'=4,'core'=2,'sec'=4] {'zh','sec'}, dimensions={0} | all-to-all | bytes 393216 | tf_op jit(solution)/shard_map/all_to_all | solution.py:336
  86.0 0.0 copy-done.2
  86.0 0.0 copy-done.3
  86.0 1.1 shard_map.110
  87.1 24.4 %all_to_all.21.parts = bf16[16,136,128]{2,1,0:T(8,128)(2,1)S(1)} all-to-all(bf16[16,136,128]{2,1,0:T(8,128)(2,1)S(1)} %shard_map.110), channel_id=1, replica_groups=mesh['zl'=2,'y'=8,'zh'=4,'core'=2,'sec'=4] {'zl','y'}, dimensions={0} | all-to-all | bytes 1114112 | tf_op jit(solution)/shard_map/all_to_all | solution.py:348
  111.5 0.9 shard_map.111
  112.4 3.5 %collective-permute-start.6 = (f32[128,128]{1,0:T(8,128)S(1)}, f32[128,128]{1,0:T(8,128)S(1)}, u32[]{:S(2)}, u32[]{:S(2)}) collective-permute-start(f32[128,128]{1,0:T(8,128)S(1)} %get-tuple-element.22), channel_id=1, source_target_pairs={{224,0},{225,1},{226,2},{227,3},{228,4},{229,5},{230,6},{231,7},{4... | collective-permute-start | bytes 196616 | tf_op jit(solution)/shard_map/ppermute | solution.py:356
  115.8 5.7 %collective-permute-done.6 = f32[128,128]{1,0:T(8,128)S(1)} collective-permute-done((f32[128,128]{1,0:T(8,128)S(1)}, f32[128,128]{1,0:T(8,128)S(1)}, u32[]{:S(2)}, u32[]{:S(2)}) %collective-permute-start.6) | collective-permute-done | bytes 65568 | tf_op jit(solution)/shard_map/ppermute | solution.py:356
  121.5 0.6 copy.12
  (6 shorter events, 0.1 us)
Async XLA Ops:
  2.3 23.8 %all-to-all-start = ((bf16[4,128,256]{2,1,0:T(8,128)(2,1)}), bf16[4,128,256]{2,1,0:T(8,128)(2,1)S(1)}, u32[]{:S(2)}, u32[]{:S(2)}) async-start(bf16[4,128,256]{2,1,0:T(8,128)(2,1)} %get-tuple-element.14), calls=%async_computation | async-start | bytes 524288 | tf_op jit(solution)/shard_map/all_to_all | solution.py:311
  12.6 11.5 %collective-permute-start.4 = (bf16[256,128]{1,0:T(8,128)(2,1)}, bf16[256,128]{1,0:T(8,128)(2,1)S(1)}, u32[]{:S(2)}, u32[]{:S(2)}) collective-permute-start(bf16[256,128]{1,0:T(8,128)(2,1)} %get-tuple-element.19), channel_id=1, source_target_pairs={{0,224},{1,225},{2,226},{3,227},{4,228},{5,229},{6,230},{7,231},{8... | collective-permute-start | bytes 196616 | tf_op jit(solution)/shard_map/ppermute | solution.py:301
  24.1 0.7 copy-start.1
  26.1 8.9 %copy-start = (bf16[4,256,256]{2,1,0:T(8,128)(2,1)S(1)}, bf16[4,256,256]{2,1,0:T(8,128)(2,1)}, u32[]{:S(2)}) copy-start(bf16[4,256,256]{2,1,0:T(8,128)(2,1)} %get-tuple-element.13.quarters) | copy-start | bytes 1572868
  26.2 36.8 %all-to-all-start.1 = ((bf16[16,272,128]{2,1,0:T(8,128)(2,1)}), bf16[16,272,128]{2,1,0:T(8,128)(2,1)S(1)}, u32[]{:S(2)}, u32[]{:S(2)}) async-start(bf16[16,272,128]{2,1,0:T(8,128)(2,1)} %shard_map.107), calls=%async_computation.1 | async-start | bytes 2228224 | tf_op jit(solution)/shard_map/all_to_all | solution.py:322
  35.1 14.2 %collective-permute-start = (bf16[768,256]{1,0:T(8,128)(2,1)S(1)}, bf16[768,256]{1,0:T(8,128)(2,1)S(1)}, u32[]{:S(2)}, u32[]{:S(2)}) collective-permute-start(bf16[768,256]{1,0:T(8,128)(2,1)S(1)} %get-tuple-element.16), channel_id=1, source_target_pairs={{0,1},{1,2},{2,3},{3,0},{4,5},{5,6},{6,7},{7,4},{8,9},{9,10},{10,1... | collective-permute-start | bytes 1179656 | tf_op jit(solution)/shard_map/ppermute | solution.py:326
  38.5 19.0 %collective-permute-start.1 = (bf16[768,256]{1,0:T(8,128)(2,1)S(1)}, bf16[768,256]{1,0:T(8,128)(2,1)S(1)}, u32[]{:S(2)}, u32[]{:S(2)}) collective-permute-start(bf16[768,256]{1,0:T(8,128)(2,1)S(1)} %get-tuple-element.17), channel_id=1, source_target_pairs={{0,2},{1,3},{2,0},{3,1},{4,6},{5,7},{6,4},{7,5},{8,10},{9,11},{10,... | collective-permute-start | bytes 1179656 | tf_op jit(solution)/shard_map/ppermute | solution.py:326
  43.2 15.9 %collective-permute-start.2 = (bf16[768,256]{1,0:T(8,128)(2,1)S(1)}, bf16[768,256]{1,0:T(8,128)(2,1)S(1)}, u32[]{:S(2)}, u32[]{:S(2)}) collective-permute-start(bf16[768,256]{1,0:T(8,128)(2,1)S(1)} %get-tuple-element.18), channel_id=1, source_target_pairs={{0,3},{1,0},{2,1},{3,2},{4,7},{5,4},{6,5},{7,6},{8,11},{9,8},{10,9... | collective-permute-start | bytes 1179656 | tf_op jit(solution)/shard_map/ppermute | solution.py:326
  59.2 26.8 %copy-start.2 = (s32[1,256]{1,0:T(1,128)S(1)}, s32[1,256]{1,0:T(1,128)}, u32[]{:S(2)}) copy-start(s32[1,256]{1,0:T(1,128)} %get-tuple-element.21.slots) | copy-start | bytes 3076
  59.2 26.8 %copy-start.3 = (bf16[256]{0:T(256)(128)(2,1)S(1)}, bf16[256]{0:T(256)(128)(2,1)}, u32[]{:S(2)}) copy-start(bf16[256]{0:T(256)(128)(2,1)} %param.11) | copy-start | bytes 1540
  59.2 3.8 %collective-permute-start.3 = (bf16[1024,256]{1,0:T(8,128)(2,1)S(1)}, bf16[1024,256]{1,0:T(8,128)(2,1)S(1)}, u32[]{:S(2)}, u32[]{:S(2)}) collective-permute-start(bf16[1024,256]{1,0:T(8,128)(2,1)S(1)} %pad_maximum_fusion), channel_id=1, source_target_pairs={{0,4},{4,0},{1,5},{5,1},{2,6},{6,2},{3,7},{7,3},{8,12},{12,8},{9,1... | collective-permute-start | bytes 1572872 | tf_op jit(solution)/shard_map/ppermute | solution.py:327
  64.4 3.1 %collective-permute-start.5 = (f32[24,128]{1,0:T(8,128)S(1)}, f32[24,128]{1,0:T(8,128)S(1)}, u32[]{:S(2)}, u32[]{:S(2)}) collective-permute-start(f32[24,128]{1,0:T(8,128)S(1)} %shard_map.108.mine), channel_id=1, source_target_pairs={{0,4},{4,0},{1,5},{5,1},{2,6},{6,2},{3,7},{7,3},{8,12},{12,8},{9,1... | collective-permute-start | bytes 36872 | tf_op jit(solution)/shard_map/ppermute | solution.py:334
  112.4 9.2 %collective-permute-start.6 = (f32[128,128]{1,0:T(8,128)S(1)}, f32[128,128]{1,0:T(8,128)S(1)}, u32[]{:S(2)}, u32[]{:S(2)}) collective-permute-start(f32[128,128]{1,0:T(8,128)S(1)} %get-tuple-element.22), channel_id=1, source_target_pairs={{224,0},{225,1},{226,2},{227,3},{228,4},{229,5},{230,6},{231,7},{4... | collective-permute-start | bytes 196616 | tf_op jit(solution)/shard_map/ppermute | solution.py:356

commit v10 on v9

--- a/solution.py
+++ b/solution.py
@@ -10,6 +10,8 @@
 NGROUPS = 16
 CAP = 20
 SLOT = 32
+
+STEPS = (0, 2, 1, 3)
 
 kl_weight = 0.4
 var_offset = 0.25
@@ -86,7 +88,7 @@
 
 def pack_kernel(quarters, dirs, *outs):
     for k in range(4):
-        outs[k][0:256, :] = quarters[k]
+        outs[k][0:256, :] = quarters[STEPS[k]]
         for q in range(4):
             outs[k][256 + 128 * q : 384 + 128 * q, :] = dirs[q]
 
@@ -129,7 +131,7 @@
     for s in range(4):
         for p in range(2):
             for q in range(2):
-                pay[pl.ds(8 * p + 4 * q + ((sec - s) & 3), 1), :] = acc[s][
+                pay[pl.ds(8 * p + 4 * q + ((sec - STEPS[s]) & 3), 1), :] = acc[s][
                     p : p + 1, 128 * q : 128 * (q + 1)
                 ]
     lane = lax.broadcasted_iota(jnp.int32, (16, 128), 1)
@@ -190,7 +192,7 @@
     coef = valid * (-adv * jnp.exp(tp) + kl_weight * (1.0 - jnp.exp(tr - tp)))
     coefs[...] = coef
     for s in range(4):
-        from_sec = (sec - s) & 3
+        from_sec = (sec - STEPS[s]) & 3
         row = jnp.concatenate(
             [coefs[pl.ds(from_sec, 1), :], coefs[pl.ds(4 + from_sec, 1), :]], axis=1
         )
@@ -323,7 +325,7 @@
     packs = call(
         pack_kernel, (shape((768, 256), BF),) * 4, inputs=2, flops=1 << 10, size=3 << 20
     )(quarters, dirs)
-    shares = [packs[0]] + [lax.ppermute(packs[k], "sec", ring(k)) for k in (1, 2, 3)]
+    shares = [packs[0]] + [lax.ppermute(packs[n], "sec", ring(STEPS[n])) for n in (1, 2, 3)]
     other = lax.ppermute(
         jnp.concatenate([share[0:256] for share in shares], axis=0), "core", [(0, 1), (1, 0)]
     )

time: 123 us -> 121 us (0.984)
  blocking collectives: 42.9 us -> 41.5 us
    ppermute x3, waiting for transfers between devices: 12.5 us -> 9.77 us  [body(): lax.ppermute(packs[n], 'sec', ring(STEPS[n]))]
    all_to_all x1, waiting for transfers between devices: 0.01 us -> 1.57 us  [body(): weights = lax.all_to_all(weights, DP, 0, 0, tiled=True)]
  transfers between devices with their start and end apart: 9 -> 9, of which waited for: 7 -> 8; matrix products, arithmetic and copies ran while one was open for 0% -> 0% of each run, Pallas kernels for 3% -> 3%
where the time goes in v10:
time: 121 us; the launch traced here: 120 us
  starting transfers between devices  44.5 us (37%)
  blocking collectives  41.5 us (34%)
  waiting for transfers between devices  23.3 us (19%)
  Pallas kernels  8.65 us (7%)
  local copies, waits for them, and re-layouts  1.36 us (1%)
    all_to_all x1, blocking collectives, body(): parts = lax.all_to_all(parts, DP, 0, 0, tiled=True)  23.6 us
    all_to_all x1, blocking collectives, body(): pays = lax.all_to_all(pays, ('zh', 'sec'), 0, 0, tiled=True)  18 us
    ppermute x3, starting transfers between devices, body(): lax.ppermute(packs[n], 'sec', ring(STEPS[n]))  12 us
    all_to_all x1, starting transfers between devices, body(): dirs = lax.all_to_all(dir_t, 'zh', 0, 0, tiled=True)  10.3 us
    ppermute x3, waiting for transfers between devices, body(): lax.ppermute(packs[n], 'sec', ring(STEPS[n]))  9.77 us
    all_to_all x1, starting transfers between devices, body(): weights = lax.all_to_all(weights, DP, 0, 0, tiled=True)  8.86 us
    ppermute x1, starting transfers between devices, body(): w_here = lax.ppermute(w_t, ALL, TO_HANDLER)  6.04 us
    ppermute x1, waiting for transfers between devices, body(): return (lax.ppermute(grad, ALL, TO_OWNER), packed.reshape(1, 1, 320))  5.68 us
  transfers between devices with their start and end apart: 9, of which 8 were waited for; matrix products, arithmetic and copies ran while one was open for 0% of the time, Pallas kernels for 3%

profile of v10, /device:TPU:8, one launch (start us, length us, event | category | flops | bytes accessed | tf_op | source)
XLA Modules:
  0.0 120.2 jit_solution(16034161449408200916)
XLA Ops:
  0.6 1.7 %shard_map.105 = (bf16[4,128,256]{2,1,0:T(8,128)(2,1)}, bf16[256,128]{1,0:T(8,128)(2,1)}) custom-call(bf16[256,128]{1,0:T(8,128)(2,1)} %direction.1, bf16[128,128]{1,0:T(8,128)(2,1)} %wp.1, bf16[128,128]{1,0:T(8,128)(2,1)} %wr.1), custom_call_target="tpu_custom_call" | custom-call | flops 65536 | bytes 262144 | tf_op jit(solution)/shard_map/pallas_call | solution.py:295
  2.3 10.3 %all-to-all-start = ((bf16[4,128,256]{2,1,0:T(8,128)(2,1)}), bf16[4,128,256]{2,1,0:T(8,128)(2,1)S(1)}, u32[]{:S(2)}, u32[]{:S(2)}) async-start(bf16[4,128,256]{2,1,0:T(8,128)(2,1)} %get-tuple-element.14), calls=%async_computation | async-start | bytes 524288 | tf_op jit(solution)/shard_map/all_to_all | solution.py:313
  12.6 6.0 %collective-permute-start.4 = (bf16[256,128]{1,0:T(8,128)(2,1)}, bf16[256,128]{1,0:T(8,128)(2,1)S(1)}, u32[]{:S(2)}, u32[]{:S(2)}) collective-permute-start(bf16[256,128]{1,0:T(8,128)(2,1)} %get-tuple-element.19), channel_id=1, source_target_pairs={{0,224},{1,225},{2,226},{3,227},{4,228},{5,229},{6,230},{7,231},{8... | collective-permute-start | bytes 196616 | tf_op jit(solution)/shard_map/ppermute | solution.py:303
  18.7 2.2 %shard_map.104 = (bf16[4,256,256]{2,1,0:T(8,128)(2,1)}, bf16[16,128]{1,0:T(8,128)(2,1)}, s32[1,256]{1,0:T(1,128)}) custom-call(s32[2]{0:T(128)} %lengths.1, s32[2]{0:T(128)} %group_ids.1, bf16[256,1024]{1,0:T(8,128)(2,1)} %states.1, bf16[8,128]{1,0:T(8,128)(2,1)} %bitcast.5, s32[1,256]{1,0:T(1,128)} %bitcast.6), custom_call_target="tpu_custom_call" | custom-call | flops 4194304 | bytes 1048576 | tf_op jit(solution)/shard_map/pallas_call | solution.py:304
  20.9 3.3 %collective-permute-done.4.w = bf16[256,128]{1,0:T(8,128)(2,1)S(1)} collective-permute-done((bf16[256,128]{1,0:T(8,128)(2,1)}, bf16[256,128]{1,0:T(8,128)(2,1)S(1)}, u32[]{:S(2)}, u32[]{:S(2)}) %collective-permute-start.4) | collective-permute-done | bytes 65568 | tf_op jit(solution)/shard_map/ppermute | solution.py:303
  24.1 0.0 copy-start.1
  24.1 0.7 copy-done.1
  24.8 1.3 %shard_map.107 = bf16[16,272,128]{2,1,0:T(8,128)(2,1)} custom-call(bf16[256,128]{1,0:T(8,128)(2,1)S(1)} %collective-permute-done.4.w, bf16[16,128]{1,0:T(8,128)(2,1)S(1)} %copy-done.1), custom_call_target="tpu_custom_call" | custom-call | flops 1024 | bytes 1048576 | tf_op jit(solution)/shard_map/pallas_call | solution.py:315
  26.1 0.0 copy-start
  26.1 0.0 all-to-all-done.dirs
  26.2 8.9 %all-to-all-start.1 = ((bf16[16,272,128]{2,1,0:T(8,128)(2,1)}), bf16[16,272,128]{2,1,0:T(8,128)(2,1)S(1)}, u32[]{:S(2)}, u32[]{:S(2)}) async-start(bf16[16,272,128]{2,1,0:T(8,128)(2,1)} %shard_map.107), calls=%async_computation.1 | async-start | bytes 2228224 | tf_op jit(solution)/shard_map/all_to_all | solution.py:324
  35.0 0.0 copy-done
  35.0 0.1 shard_map.106
  35.1 4.9 %collective-permute-start = (bf16[768,256]{1,0:T(8,128)(2,1)S(1)}, bf16[768,256]{1,0:T(8,128)(2,1)S(1)}, u32[]{:S(2)}, u32[]{:S(2)}) collective-permute-start(bf16[768,256]{1,0:T(8,128)(2,1)S(1)} %get-tuple-element.16), channel_id=1, source_target_pairs={{0,2},{1,3},{2,0},{3,1},{4,6},{5,7},{6,4},{7,5},{8,10},{9,11},{10,... | collective-permute-start | bytes 1179656 | tf_op jit(solution)/shard_map/ppermute | solution.py:328
  40.1 2.5 %collective-permute-start.1 = (bf16[768,256]{1,0:T(8,128)(2,1)S(1)}, bf16[768,256]{1,0:T(8,128)(2,1)S(1)}, u32[]{:S(2)}, u32[]{:S(2)}) collective-permute-start(bf16[768,256]{1,0:T(8,128)(2,1)S(1)} %get-tuple-element.17), channel_id=1, source_target_pairs={{0,1},{1,2},{2,3},{3,0},{4,5},{5,6},{6,7},{7,4},{8,9},{9,10},{10,1... | collective-permute-start | bytes 1179656 | tf_op jit(solution)/shard_map/ppermute | solution.py:328
  42.6 4.6 %collective-permute-start.2 = (bf16[768,256]{1,0:T(8,128)(2,1)S(1)}, bf16[768,256]{1,0:T(8,128)(2,1)S(1)}, u32[]{:S(2)}, u32[]{:S(2)}) collective-permute-start(bf16[768,256]{1,0:T(8,128)(2,1)S(1)} %get-tuple-element.18), channel_id=1, source_target_pairs={{0,3},{1,0},{2,1},{3,2},{4,7},{5,4},{6,5},{7,6},{8,11},{9,8},{10,9... | collective-permute-start | bytes 1179656 | tf_op jit(solution)/shard_map/ppermute | solution.py:328
  47.2 3.5 %collective-permute-done.s1 = bf16[768,256]{1,0:T(8,128)(2,1)S(1)} collective-permute-done((bf16[768,256]{1,0:T(8,128)(2,1)S(1)}, bf16[768,256]{1,0:T(8,128)(2,1)S(1)}, u32[]{:S(2)}, u32[]{:S(2)}) %collective-permute-start) | collective-permute-done | bytes 393248 | tf_op jit(solution)/shard_map/ppermute | solution.py:328
  50.6 6.2 %collective-permute-done.1.s2 = bf16[768,256]{1,0:T(8,128)(2,1)S(1)} collective-permute-done((bf16[768,256]{1,0:T(8,128)(2,1)S(1)}, bf16[768,256]{1,0:T(8,128)(2,1)S(1)}, u32[]{:S(2)}, u32[]{:S(2)}) %collective-permute-start.1) | collective-permute-done | bytes 393248 | tf_op jit(solution)/shard_map/ppermute | solution.py:328
  56.9 0.1 collective-permute-done.2.s3
  57.0 0.0 copy-start.2
  57.0 0.0 copy-start.3
  57.0 1.9 %collective-permute-start.3 = (bf16[1024,256]{1,0:T(8,128)(2,1)S(1)}, bf16[1024,256]{1,0:T(8,128)(2,1)S(1)}, u32[]{:S(2)}, u32[]{:S(2)}) collective-permute-start(bf16[1024,256]{1,0:T(8,128)(2,1)S(1)} %pad_maximum_fusion), channel_id=1, source_target_pairs={{0,4},{4,0},{1,5},{5,1},{2,6},{6,2},{3,7},{7,3},{8,12},{12,8},{9,1... | collective-permute-start | bytes 1572872 | tf_op jit(solution)/shard_map/ppermute | solution.py:329
  59.0 1.9 %collective-permute-done.3.other = bf16[1024,256]{1,0:T(8,128)(2,1)S(1)} collective-permute-done((bf16[1024,256]{1,0:T(8,128)(2,1)S(1)}, bf16[1024,256]{1,0:T(8,128)(2,1)S(1)}, u32[]{:S(2)}, u32[]{:S(2)}) %collective-permute-start.3) | collective-permute-done | bytes 524320 | tf_op jit(solution)/shard_map/ppermute | solution.py:329
  60.8 1.6 %all-to-all-done.1.weights = bf16[16,272,128]{2,1,0:T(8,128)(2,1)S(1)} async-done(((bf16[16,272,128]{2,1,0:T(8,128)(2,1)}), bf16[16,272,128]{2,1,0:T(8,128)(2,1)S(1)}, u32[]{:S(2)}, u32[]{:S(2)}) %all-to-all-start.1) | async-done | bytes 1114144 | tf_op jit(solution)/shard_map/all_to_all | solution.py:324
  62.4 1.3 %shard_map.108.mine = f32[24,128]{1,0:T(8,128)S(1)} custom-call(bf16[768,256]{1,0:T(8,128)(2,1)S(1)} %get-tuple-element.15.s0, bf16[768,256]{1,0:T(8,128)(2,1)S(1)} %collective-permute-done.s1, bf16[768,256]{1,0:T(8,128)(2,1)S(1)} %collective-permute-done.1.s2, bf16[768,256]{1,0:T(8,128)(2,1)S(1)} %collective-permute-done.2.s3, ...), custom_call_target="tpu_custom_call" | custom-call | flops 1073741824 | bytes 4194304 | tf_op jit(solution)/shard_map/pallas_call | solution.py:332
  63.8 1.9 %collective-permute-start.5 = (f32[24,128]{1,0:T(8,128)S(1)}, f32[24,128]{1,0:T(8,128)S(1)}, u32[]{:S(2)}, u32[]{:S(2)}) collective-permute-start(f32[24,128]{1,0:T(8,128)S(1)} %shard_map.108.mine), channel_id=1, source_target_pairs={{0,4},{4,0},{1,5},{5,1},{2,6},{6,2},{3,7},{7,3},{8,12},{12,8},{9,1... | collective-permute-start | bytes 36872 | tf_op jit(solution)/shard_map/ppermute | solution.py:336
  65.7 1.1 collective-permute-done.5.partner
  66.9 18.0 %all_to_all.20.pays = f32[16,24,128]{2,1,0:T(8,128)S(1)} all-to-all(f32[16,24,128]{2,1,0:T(8,128)S(1)} %shard_map.109), channel_id=1, replica_groups=mesh['zl'=2,'y'=8,'zh'=4,'core'=2,'sec'=4] {'zh','sec'}, dimensions={0} | all-to-all | bytes 393216 | tf_op jit(solution)/shard_map/all_to_all | solution.py:338
  84.8 0.0 copy-done.2
  84.8 0.0 copy-done.3
  84.8 1.1 shard_map.110
  85.9 23.6 %all_to_all.21.parts = bf16[16,136,128]{2,1,0:T(8,128)(2,1)S(1)} all-to-all(bf16[16,136,128]{2,1,0:T(8,128)(2,1)S(1)} %shard_map.110), channel_id=1, replica_groups=mesh['zl'=2,'y'=8,'zh'=4,'core'=2,'sec'=4] {'zl','y'}, dimensions={0} | all-to-all | bytes 1114112 | tf_op jit(solution)/shard_map/all_to_all | solution.py:350
  109.5 0.9 shard_map.111
  110.4 3.5 %collective-permute-start.6 = (f32[128,128]{1,0:T(8,128)S(1)}, f32[128,128]{1,0:T(8,128)S(1)}, u32[]{:S(2)}, u32[]{:S(2)}) collective-permute-start(f32[128,128]{1,0:T(8,128)S(1)} %get-tuple-element.22), channel_id=1, source_target_pairs={{224,0},{225,1},{226,2},{227,3},{228,4},{229,5},{230,6},{231,7},{4... | collective-permute-start | bytes 196616 | tf_op jit(solution)/shard_map/ppermute | solution.py:358
  113.9 5.7 %collective-permute-done.6 = f32[128,128]{1,0:T(8,128)S(1)} collective-permute-done((f32[128,128]{1,0:T(8,128)S(1)}, f32[128,128]{1,0:T(8,128)S(1)}, u32[]{:S(2)}, u32[]{:S(2)}) %collective-permute-start.6) | collective-permute-done | bytes 65568 | tf_op jit(solution)/shard_map/ppermute | solution.py:358
  119.6 0.6 copy.12
  (6 shorter events, 0.1 us)
Async XLA Ops:
  2.3 23.8 %all-to-all-start = ((bf16[4,128,256]{2,1,0:T(8,128)(2,1)}), bf16[4,128,256]{2,1,0:T(8,128)(2,1)S(1)}, u32[]{:S(2)}, u32[]{:S(2)}) async-start(bf16[4,128,256]{2,1,0:T(8,128)(2,1)} %get-tuple-element.14), calls=%async_computation | async-start | bytes 524288 | tf_op jit(solution)/shard_map/all_to_all | solution.py:313
  12.6 11.5 %collective-permute-start.4 = (bf16[256,128]{1,0:T(8,128)(2,1)}, bf16[256,128]{1,0:T(8,128)(2,1)S(1)}, u32[]{:S(2)}, u32[]{:S(2)}) collective-permute-start(bf16[256,128]{1,0:T(8,128)(2,1)} %get-tuple-element.19), channel_id=1, source_target_pairs={{0,224},{1,225},{2,226},{3,227},{4,228},{5,229},{6,230},{7,231},{8... | collective-permute-start | bytes 196616 | tf_op jit(solution)/shard_map/ppermute | solution.py:303
  24.1 0.7 copy-start.1
  26.1 8.9 %copy-start = (bf16[4,256,256]{2,1,0:T(8,128)(2,1)S(1)}, bf16[4,256,256]{2,1,0:T(8,128)(2,1)}, u32[]{:S(2)}) copy-start(bf16[4,256,256]{2,1,0:T(8,128)(2,1)} %get-tuple-element.13.quarters) | copy-start | bytes 1572868
  26.2 36.3 %all-to-all-start.1 = ((bf16[16,272,128]{2,1,0:T(8,128)(2,1)}), bf16[16,272,128]{2,1,0:T(8,128)(2,1)S(1)}, u32[]{:S(2)}, u32[]{:S(2)}) async-start(bf16[16,272,128]{2,1,0:T(8,128)(2,1)} %shard_map.107), calls=%async_computation.1 | async-start | bytes 2228224 | tf_op jit(solution)/shard_map/all_to_all | solution.py:324
  35.1 15.5 %collective-permute-start = (bf16[768,256]{1,0:T(8,128)(2,1)S(1)}, bf16[768,256]{1,0:T(8,128)(2,1)S(1)}, u32[]{:S(2)}, u32[]{:S(2)}) collective-permute-start(bf16[768,256]{1,0:T(8,128)(2,1)S(1)} %get-tuple-element.16), channel_id=1, source_target_pairs={{0,2},{1,3},{2,0},{3,1},{4,6},{5,7},{6,4},{7,5},{8,10},{9,11},{10,... | collective-permute-start | bytes 1179656 | tf_op jit(solution)/shard_map/ppermute | solution.py:328
  40.1 16.8 %collective-permute-start.1 = (bf16[768,256]{1,0:T(8,128)(2,1)S(1)}, bf16[768,256]{1,0:T(8,128)(2,1)S(1)}, u32[]{:S(2)}, u32[]{:S(2)}) collective-permute-start(bf16[768,256]{1,0:T(8,128)(2,1)S(1)} %get-tuple-element.17), channel_id=1, source_target_pairs={{0,1},{1,2},{2,3},{3,0},{4,5},{5,6},{6,7},{7,4},{8,9},{9,10},{10,1... | collective-permute-start | bytes 1179656 | tf_op jit(solution)/shard_map/ppermute | solution.py:328
  42.6 14.4 %collective-permute-start.2 = (bf16[768,256]{1,0:T(8,128)(2,1)S(1)}, bf16[768,256]{1,0:T(8,128)(2,1)S(1)}, u32[]{:S(2)}, u32[]{:S(2)}) collective-permute-start(bf16[768,256]{1,0:T(8,128)(2,1)S(1)} %get-tuple-element.18), channel_id=1, source_target_pairs={{0,3},{1,0},{2,1},{3,2},{4,7},{5,4},{6,5},{7,6},{8,11},{9,8},{10,9... | collective-permute-start | bytes 1179656 | tf_op jit(solution)/shard_map/ppermute | solution.py:328
  57.0 27.8 %copy-start.2 = (s32[1,256]{1,0:T(1,128)S(1)}, s32[1,256]{1,0:T(1,128)}, u32[]{:S(2)}) copy-start(s32[1,256]{1,0:T(1,128)} %get-tuple-element.21.slots) | copy-start | bytes 3076
  57.0 27.8 %copy-start.3 = (bf16[256]{0:T(256)(128)(2,1)S(1)}, bf16[256]{0:T(256)(128)(2,1)}, u32[]{:S(2)}) copy-start(bf16[256]{0:T(256)(128)(2,1)} %param.11) | copy-start | bytes 1540
  57.0 3.8 %collective-permute-start.3 = (bf16[1024,256]{1,0:T(8,128)(2,1)S(1)}, bf16[1024,256]{1,0:T(8,128)(2,1)S(1)}, u32[]{:S(2)}, u32[]{:S(2)}) collective-permute-start(bf16[1024,256]{1,0:T(8,128)(2,1)S(1)} %pad_maximum_fusion), channel_id=1, source_target_pairs={{0,4},{4,0},{1,5},{5,1},{2,6},{6,2},{3,7},{7,3},{8,12},{12,8},{9,1... | collective-permute-start | bytes 1572872 | tf_op jit(solution)/shard_map/ppermute | solution.py:329
  63.8 3.1 %collective-permute-start.5 = (f32[24,128]{1,0:T(8,128)S(1)}, f32[24,128]{1,0:T(8,128)S(1)}, u32[]{:S(2)}, u32[]{:S(2)}) collective-permute-start(f32[24,128]{1,0:T(8,128)S(1)} %shard_map.108.mine), channel_id=1, source_target_pairs={{0,4},{4,0},{1,5},{5,1},{2,6},{6,2},{3,7},{7,3},{8,12},{12,8},{9,1... | collective-permute-start | bytes 36872 | tf_op jit(solution)/shard_map/ppermute | solution.py:336
  110.4 9.2 %collective-permute-start.6 = (f32[128,128]{1,0:T(8,128)S(1)}, f32[128,128]{1,0:T(8,128)S(1)}, u32[]{:S(2)}, u32[]{:S(2)}) collective-permute-start(f32[128,128]{1,0:T(8,128)S(1)} %get-tuple-element.22), channel_id=1, source_target_pairs={{224,0},{225,1},{226,2},{227,3},{228,4},{229,5},{230,6},{231,7},{4... | collective-permute-start | bytes 196616 | tf_op jit(solution)/shard_map/ppermute | solution.py:358

commit v11 on v10

--- a/solution.py
+++ b/solution.py
@@ -104,7 +104,7 @@
         copy.wait()
 
 
-def terms_kernel(s0, s1, s2, s3, other, weights, pay):
+def terms_kernel(s0, s1, s2, s3, o0, o1, weights, pay):
     shares = (s0, s1, s2, s3)
     zh, core, sec = (lax.axis_index(name) for name in ("zh", "core", "sec"))
     acc = [jnp.zeros((2, 256), F32) for _ in range(4)]
@@ -118,7 +118,9 @@
         for s, share in enumerate(shares):
             key = lax.dot_general(mats[0], share[0:256, :], NT, preferred_element_type=F32)
             key += lax.dot_general(
-                mats[1], other[256 * s : 256 * (s + 1), :], NT, preferred_element_type=F32
+                mats[1],
+                (o0, o1)[s >> 1][256 * (s & 1) : 256 * (s & 1) + 256, :],
+                NT, preferred_element_type=F32
             )
             wide = share[256 + 128 * q : 384 + 128 * q, :].astype(F32)
             acc[s] += jnp.concatenate(
@@ -152,7 +154,7 @@
         out[d] = whole
 
 
-def grads_kernel(pays, s0, s1, s2, s3, other, old_logp, slots, out, change, coefs):
+def grads_kernel(pays, s0, s1, s2, s3, o0, o1, old_logp, slots, out, change, coefs):
     shares = (s0, s1, s2, s3)
     zh, core, sec = (lax.axis_index(name) for name in ("zh", "core", "sec"))
     dp = dp_index()
@@ -202,8 +204,9 @@
             ).astype(BF)
     grads = [
         jnp.dot(change[:, 0:256], s0[0:256, :], preferred_element_type=F32),
-        jnp.dot(change[...], other[...], preferred_element_type=F32),
+        jnp.dot(change[:, 0:512], o0[...], preferred_element_type=F32),
     ]
+    grads[1] += jnp.dot(change[:, 512:1024], o1[...], preferred_element_type=F32)
     for s in range(1, 4):
         grads[0] += jnp.dot(
             change[:, 256 * s : 256 * (s + 1)], shares[s][0:256, :], preferred_element_type=F32
@@ -308,7 +311,6 @@
         inputs=3,
         flops=8 * 256 * 1024 * 2,
         size=1 << 20,
-        vmem_mib=60,
     )(lengths, group_ids, states, reward_head.reshape(8, 128), routes.reshape(1, 256))
     dirs = lax.all_to_all(dir_t, "zh", 0, 0, tiled=True)
     anywhere = pl.BlockSpec(memory_space=pl.ANY)
@@ -326,12 +328,15 @@
         pack_kernel, (shape((768, 256), BF),) * 4, inputs=2, flops=1 << 10, size=3 << 20
     )(quarters, dirs)
     shares = [packs[0]] + [lax.ppermute(packs[n], "sec", ring(STEPS[n])) for n in (1, 2, 3)]
-    other = lax.ppermute(
-        jnp.concatenate([share[0:256] for share in shares], axis=0), "core", [(0, 1), (1, 0)]
-    )
+    others = [
+        lax.ppermute(
+            jnp.concatenate([share[0:256] for share in pair], axis=0), "core", [(0, 1), (1, 0)]
+        )
+        for pair in (shares[0:2], shares[2:4])
+    ]
     pay = call(
-        terms_kernel, shape((24, 128), F32), inputs=6, flops=1 << 30, size=4 << 20
-    )(*shares, other, weights)
+        terms_kernel, shape((24, 128), F32), inputs=7, flops=1 << 30, size=4 << 20
+    )(*shares, *others, weights)
     pays = call(join_kernel, shape((16, 24, 128), F32), inputs=2, flops=1 << 12, size=1 << 18)(
         pay, lax.ppermute(pay, "core", [(0, 1), (1, 0)])
     )
@@ -343,10 +348,10 @@
             pltpu.VMEM((512, 1024), BF),
             pltpu.VMEM((8, 128), F32),
         ],
-        inputs=8,
+        inputs=9,
         flops=1 << 29,
         size=4 << 20,
-    )(pays, *shares, other, old_logp.reshape(2, 128), slots)
+    )(pays, *shares, *others, old_logp.reshape(2, 128), slots)
     parts = lax.all_to_all(parts, DP, 0, 0, tiled=True)
     grad, packed = call(
         finish_kernel,

time: 121 us -> 120 us (level)
  waiting for transfers between devices: 23.3 us -> 18.9 us
  local copies, waits for them, and re-layouts: 1.36 us -> 4.38 us
  starting transfers between devices: 44.5 us -> 46.3 us
  Pallas kernels: 8.65 us -> 7.41 us
    unnamed x9 -> x13, local copies, waits for them, and re-layouts: 1.33 us -> 4.34 us
    ppermute x1, waiting for transfers between devices: 3.27 us -> 0.79 us  [body(): w_here = lax.ppermute(w_t, ALL, TO_HANDLER)]
    ppermute x3, waiting for transfers between devices: 9.77 us -> 7.81 us  [body(): lax.ppermute(packs[n], 'sec', ring(STEPS[n]))]
    ppermute x1 -> x2, starting transfers between devices: 1.92 us -> 3.84 us  [body(): lax.ppermute(jnp.concatenate([share[0:256] for share in pair], axis=0), '...]
    pallas_call x1, Pallas kernels: 2.2 us -> 0.96 us  [body(): call(prepare_kernel, (shape((4, 256, 256), BF), shape((16, 128), BF), sha...]
  transfers between devices with their start and end apart: 9 -> 10, of which waited for: 8 -> 8; matrix products, arithmetic and copies ran while one was open for 0% -> 0% of each run, Pallas kernels for 3% -> 2%
where the time goes in v11:
time: 120 us; the launch traced here: 119 us
  starting transfers between devices  46.3 us (39%)
  blocking collectives  41.1 us (34%)
  waiting for transfers between devices  18.9 us (16%)
  Pallas kernels  7.41 us (6%)
  local copies, waits for them, and re-layouts  4.38 us (4%)
    all_to_all x1, blocking collectives, body(): parts = lax.all_to_all(parts, DP, 0, 0, tiled=True)  23.2 us
    all_to_all x1, blocking collectives, body(): pays = lax.all_to_all(pays, ('zh', 'sec'), 0, 0, tiled=True)  17.9 us
    ppermute x3, starting transfers between devices, body(): lax.ppermute(packs[n], 'sec', ring(STEPS[n]))  12 us
    all_to_all x1, starting transfers between devices, body(): dirs = lax.all_to_all(dir_t, 'zh', 0, 0, tiled=True)  10.3 us
    all_to_all x1, starting transfers between devices, body(): weights = lax.all_to_all(weights, DP, 0, 0, tiled=True)  8.73 us
    ppermute x3, waiting for transfers between devices, body(): lax.ppermute(packs[n], 'sec', ring(STEPS[n]))  7.81 us
    ppermute x1, starting transfers between devices, body(): w_here = lax.ppermute(w_t, ALL, TO_HANDLER)  6.04 us
    ppermute x1, waiting for transfers between devices, body(): return (lax.ppermute(grad, ALL, TO_OWNER), packed.reshape(1, 1, 320))  5.68 us
  transfers between devices with their start and end apart: 10, of which 8 were waited for; matrix products, arithmetic and copies ran while one was open for 0% of the time, Pallas kernels for 2%

profile of v11, /device:TPU:8, one launch (start us, length us, event | category | flops | bytes accessed | tf_op | source)
XLA Modules:
  0.0 118.9 jit_solution(11858577187563455862)
XLA Ops:
  0.6 1.7 %shard_map.105 = (bf16[4,128,256]{2,1,0:T(8,128)(2,1)}, bf16[256,128]{1,0:T(8,128)(2,1)}) custom-call(bf16[256,128]{1,0:T(8,128)(2,1)} %direction.1, bf16[128,128]{1,0:T(8,128)(2,1)} %wp.1, bf16[128,128]{1,0:T(8,128)(2,1)} %wr.1), custom_call_target="tpu_custom_call" | custom-call | flops 65536 | bytes 262144 | tf_op jit(solution)/shard_map/pallas_call | solution.py:298
  2.3 10.3 %all-to-all-start = ((bf16[4,128,256]{2,1,0:T(8,128)(2,1)}), bf16[4,128,256]{2,1,0:T(8,128)(2,1)S(1)}, u32[]{:S(2)}, u32[]{:S(2)}) async-start(bf16[4,128,256]{2,1,0:T(8,128)(2,1)} %get-tuple-element.14), calls=%async_computation | async-start | bytes 524288 | tf_op jit(solution)/shard_map/all_to_all | solution.py:315
  12.6 6.0 %collective-permute-start.5 = (bf16[256,128]{1,0:T(8,128)(2,1)}, bf16[256,128]{1,0:T(8,128)(2,1)S(1)}, u32[]{:S(2)}, u32[]{:S(2)}) collective-permute-start(bf16[256,128]{1,0:T(8,128)(2,1)} %get-tuple-element.19), channel_id=1, source_target_pairs={{0,224},{1,225},{2,226},{3,227},{4,228},{5,229},{6,230},{7,231},{8... | collective-permute-start | bytes 196616 | tf_op jit(solution)/shard_map/ppermute | solution.py:306
  18.7 0.0 copy-start
  18.7 1.0 copy-done
  19.7 0.0 copy-start.1
  19.7 0.7 copy-done.1
  20.4 0.0 copy-start.2
  20.4 0.7 copy-done.2
  21.1 0.0 copy-start.4
  21.1 0.7 copy-done.4
  21.7 0.0 copy-start.5
  21.7 0.7 copy-done.5
  22.4 1.0 shard_map.104
  23.3 0.8 collective-permute-done.5.w
  24.1 1.3 %shard_map.107 = bf16[16,272,128]{2,1,0:T(8,128)(2,1)} custom-call(bf16[256,128]{1,0:T(8,128)(2,1)S(1)} %collective-permute-done.5.w, bf16[16,128]{1,0:T(8,128)(2,1)S(1)} %get-tuple-element.20.extra), custom_call_target="tpu_custom_call" | custom-call | flops 1024 | bytes 1048576 | tf_op jit(solution)/shard_map/pallas_call | solution.py:317
  25.5 0.0 all-to-all-done.dirs
  25.5 8.7 %all-to-all-start.1 = ((bf16[16,272,128]{2,1,0:T(8,128)(2,1)}), bf16[16,272,128]{2,1,0:T(8,128)(2,1)S(1)}, u32[]{:S(2)}, u32[]{:S(2)}) async-start(bf16[16,272,128]{2,1,0:T(8,128)(2,1)} %shard_map.107), calls=%async_computation.1 | async-start | bytes 2228224 | tf_op jit(solution)/shard_map/all_to_all | solution.py:326
  34.2 0.1 shard_map.106
  34.3 4.9 %collective-permute-start = (bf16[768,256]{1,0:T(8,128)(2,1)S(1)}, bf16[768,256]{1,0:T(8,128)(2,1)S(1)}, u32[]{:S(2)}, u32[]{:S(2)}) collective-permute-start(bf16[768,256]{1,0:T(8,128)(2,1)S(1)} %get-tuple-element.16), channel_id=1, source_target_pairs={{0,2},{1,3},{2,0},{3,1},{4,6},{5,7},{6,4},{7,5},{8,10},{9,11},{10,... | collective-permute-start | bytes 1179656 | tf_op jit(solution)/shard_map/ppermute | solution.py:330
  39.2 2.5 %collective-permute-start.1 = (bf16[768,256]{1,0:T(8,128)(2,1)S(1)}, bf16[768,256]{1,0:T(8,128)(2,1)S(1)}, u32[]{:S(2)}, u32[]{:S(2)}) collective-permute-start(bf16[768,256]{1,0:T(8,128)(2,1)S(1)} %get-tuple-element.17), channel_id=1, source_target_pairs={{0,1},{1,2},{2,3},{3,0},{4,5},{5,6},{6,7},{7,4},{8,9},{9,10},{10,1... | collective-permute-start | bytes 1179656 | tf_op jit(solution)/shard_map/ppermute | solution.py:330
  41.7 4.6 %collective-permute-start.2 = (bf16[768,256]{1,0:T(8,128)(2,1)S(1)}, bf16[768,256]{1,0:T(8,128)(2,1)S(1)}, u32[]{:S(2)}, u32[]{:S(2)}) collective-permute-start(bf16[768,256]{1,0:T(8,128)(2,1)S(1)} %get-tuple-element.18), channel_id=1, source_target_pairs={{0,3},{1,0},{2,1},{3,2},{4,7},{5,4},{6,5},{7,6},{8,11},{9,8},{10,9... | collective-permute-start | bytes 1179656 | tf_op jit(solution)/shard_map/ppermute | solution.py:330
  46.3 3.5 %collective-permute-done.s1 = bf16[768,256]{1,0:T(8,128)(2,1)S(1)} collective-permute-done((bf16[768,256]{1,0:T(8,128)(2,1)S(1)}, bf16[768,256]{1,0:T(8,128)(2,1)S(1)}, u32[]{:S(2)}, u32[]{:S(2)}) %collective-permute-start) | collective-permute-done | bytes 393248 | tf_op jit(solution)/shard_map/ppermute | solution.py:330
  49.8 1.9 %collective-permute-start.3 = (bf16[512,256]{1,0:T(8,128)(2,1)S(1)}, bf16[512,256]{1,0:T(8,128)(2,1)S(1)}, u32[]{:S(2)}, u32[]{:S(2)}) collective-permute-start(bf16[512,256]{1,0:T(8,128)(2,1)S(1)} %pad_maximum_fusion), channel_id=1, source_target_pairs={{0,4},{4,0},{1,5},{5,1},{2,6},{6,2},{3,7},{7,3},{8,12},{12,8},{9,1... | collective-permute-start | bytes 786440 | tf_op jit(solution)/shard_map/ppermute | solution.py:332
  51.8 4.3 %collective-permute-done.1.s2 = bf16[768,256]{1,0:T(8,128)(2,1)S(1)} collective-permute-done((bf16[768,256]{1,0:T(8,128)(2,1)S(1)}, bf16[768,256]{1,0:T(8,128)(2,1)S(1)}, u32[]{:S(2)}, u32[]{:S(2)}) %collective-permute-start.1) | collective-permute-done | bytes 393248 | tf_op jit(solution)/shard_map/ppermute | solution.py:330
  56.0 0.1 collective-permute-done.2.s3
  56.2 0.0 copy-start.3
  56.2 1.9 %collective-permute-start.4 = (bf16[512,256]{1,0:T(8,128)(2,1)S(1)}, bf16[512,256]{1,0:T(8,128)(2,1)S(1)}, u32[]{:S(2)}, u32[]{:S(2)}) collective-permute-start(bf16[512,256]{1,0:T(8,128)(2,1)S(1)} %pad_maximum_fusion.1), channel_id=1, source_target_pairs={{0,4},{4,0},{1,5},{5,1},{2,6},{6,2},{3,7},{7,3},{8,12},{12,8},{9,1... | collective-permute-start | bytes 786440 | tf_op jit(solution)/shard_map/ppermute | solution.py:332
  58.1 0.0 collective-permute-done.3.o0
  58.1 1.5 %collective-permute-done.4.o1 = bf16[512,256]{1,0:T(8,128)(2,1)S(1)} collective-permute-done((bf16[512,256]{1,0:T(8,128)(2,1)S(1)}, bf16[512,256]{1,0:T(8,128)(2,1)S(1)}, u32[]{:S(2)}, u32[]{:S(2)}) %collective-permute-start.4) | collective-permute-done | bytes 262176 | tf_op jit(solution)/shard_map/ppermute | solution.py:332
  59.6 2.0 %all-to-all-done.1.weights = bf16[16,272,128]{2,1,0:T(8,128)(2,1)S(1)} async-done(((bf16[16,272,128]{2,1,0:T(8,128)(2,1)}), bf16[16,272,128]{2,1,0:T(8,128)(2,1)S(1)}, u32[]{:S(2)}, u32[]{:S(2)}) %all-to-all-start.1) | async-done | bytes 1114144 | tf_op jit(solution)/shard_map/all_to_all | solution.py:326
  61.6 1.4 %shard_map.108.mine = f32[24,128]{1,0:T(8,128)S(1)} custom-call(bf16[768,256]{1,0:T(8,128)(2,1)S(1)} %get-tuple-element.15.s0, bf16[768,256]{1,0:T(8,128)(2,1)S(1)} %collective-permute-done.s1, bf16[768,256]{1,0:T(8,128)(2,1)S(1)} %collective-permute-done.1.s2, bf16[768,256]{1,0:T(8,128)(2,1)S(1)} %collective-permute-done.2.s3, ...), custom_call_target="tpu_custom_call" | custom-call | flops 1073741824 | bytes 4194304 | tf_op jit(solution)/shard_map/pallas_call | solution.py:337
  63.0 1.9 %collective-permute-start.6 = (f32[24,128]{1,0:T(8,128)S(1)}, f32[24,128]{1,0:T(8,128)S(1)}, u32[]{:S(2)}, u32[]{:S(2)}) collective-permute-start(f32[24,128]{1,0:T(8,128)S(1)} %shard_map.108.mine), channel_id=1, source_target_pairs={{0,4},{4,0},{1,5},{5,1},{2,6},{6,2},{3,7},{7,3},{8,12},{12,8},{9,1... | collective-permute-start | bytes 36872 | tf_op jit(solution)/shard_map/ppermute | solution.py:341
  64.9 1.1 collective-permute-done.6.partner
  66.0 17.9 %all_to_all.20.pays = f32[16,24,128]{2,1,0:T(8,128)S(1)} all-to-all(f32[16,24,128]{2,1,0:T(8,128)S(1)} %shard_map.109), channel_id=1, replica_groups=mesh['zl'=2,'y'=8,'zh'=4,'core'=2,'sec'=4] {'zh','sec'}, dimensions={0} | all-to-all | bytes 393216 | tf_op jit(solution)/shard_map/all_to_all | solution.py:343
  84.0 0.0 copy-done.3
  84.0 1.1 shard_map.110
  85.1 23.2 %all_to_all.21.parts = bf16[16,136,128]{2,1,0:T(8,128)(2,1)S(1)} all-to-all(bf16[16,136,128]{2,1,0:T(8,128)(2,1)S(1)} %shard_map.110), channel_id=1, replica_groups=mesh['zl'=2,'y'=8,'zh'=4,'core'=2,'sec'=4] {'zl','y'}, dimensions={0} | all-to-all | bytes 1114112 | tf_op jit(solution)/shard_map/all_to_all | solution.py:355
  108.3 0.9 shard_map.111
  109.2 3.5 %collective-permute-start.7 = (f32[128,128]{1,0:T(8,128)S(1)}, f32[128,128]{1,0:T(8,128)S(1)}, u32[]{:S(2)}, u32[]{:S(2)}) collective-permute-start(f32[128,128]{1,0:T(8,128)S(1)} %get-tuple-element.22), channel_id=1, source_target_pairs={{224,0},{225,1},{226,2},{227,3},{228,4},{229,5},{230,6},{231,7},{4... | collective-permute-start | bytes 196616 | tf_op jit(solution)/shard_map/ppermute | solution.py:363
  112.6 5.7 %collective-permute-done.7 = f32[128,128]{1,0:T(8,128)S(1)} collective-permute-done((f32[128,128]{1,0:T(8,128)S(1)}, f32[128,128]{1,0:T(8,128)S(1)}, u32[]{:S(2)}, u32[]{:S(2)}) %collective-permute-start.7) | collective-permute-done | bytes 65568 | tf_op jit(solution)/shard_map/ppermute | solution.py:363
  118.3 0.6 copy.12
  (7 shorter events, 0.1 us)
Async XLA Ops:
  2.3 23.1 %all-to-all-start = ((bf16[4,128,256]{2,1,0:T(8,128)(2,1)}), bf16[4,128,256]{2,1,0:T(8,128)(2,1)S(1)}, u32[]{:S(2)}, u32[]{:S(2)}) async-start(bf16[4,128,256]{2,1,0:T(8,128)(2,1)} %get-tuple-element.14), calls=%async_computation | async-start | bytes 524288 | tf_op jit(solution)/shard_map/all_to_all | solution.py:315
  12.6 11.5 %collective-permute-start.5 = (bf16[256,128]{1,0:T(8,128)(2,1)}, bf16[256,128]{1,0:T(8,128)(2,1)S(1)}, u32[]{:S(2)}, u32[]{:S(2)}) collective-permute-start(bf16[256,128]{1,0:T(8,128)(2,1)} %get-tuple-element.19), channel_id=1, source_target_pairs={{0,224},{1,225},{2,226},{3,227},{4,228},{5,229},{6,230},{7,231},{8... | collective-permute-start | bytes 196616 | tf_op jit(solution)/shard_map/ppermute | solution.py:306
  18.7 1.0 copy-start
  19.7 0.7 copy-start.1
  20.4 0.7 copy-start.2
  21.1 0.7 copy-start.4
  21.7 0.7 copy-start.5
  25.5 36.1 %all-to-all-start.1 = ((bf16[16,272,128]{2,1,0:T(8,128)(2,1)}), bf16[16,272,128]{2,1,0:T(8,128)(2,1)S(1)}, u32[]{:S(2)}, u32[]{:S(2)}) async-start(bf16[16,272,128]{2,1,0:T(8,128)(2,1)} %shard_map.107), calls=%async_computation.1 | async-start | bytes 2228224 | tf_op jit(solution)/shard_map/all_to_all | solution.py:326
  34.3 15.5 %collective-permute-start = (bf16[768,256]{1,0:T(8,128)(2,1)S(1)}, bf16[768,256]{1,0:T(8,128)(2,1)S(1)}, u32[]{:S(2)}, u32[]{:S(2)}) collective-permute-start(bf16[768,256]{1,0:T(8,128)(2,1)S(1)} %get-tuple-element.16), channel_id=1, source_target_pairs={{0,2},{1,3},{2,0},{3,1},{4,6},{5,7},{6,4},{7,5},{8,10},{9,11},{10,... | collective-permute-start | bytes 1179656 | tf_op jit(solution)/shard_map/ppermute | solution.py:330
  39.2 16.8 %collective-permute-start.1 = (bf16[768,256]{1,0:T(8,128)(2,1)S(1)}, bf16[768,256]{1,0:T(8,128)(2,1)S(1)}, u32[]{:S(2)}, u32[]{:S(2)}) collective-permute-start(bf16[768,256]{1,0:T(8,128)(2,1)S(1)} %get-tuple-element.17), channel_id=1, source_target_pairs={{0,1},{1,2},{2,3},{3,0},{4,5},{5,6},{6,7},{7,4},{8,9},{9,10},{10,1... | collective-permute-start | bytes 1179656 | tf_op jit(solution)/shard_map/ppermute | solution.py:330
  41.7 14.4 %collective-permute-start.2 = (bf16[768,256]{1,0:T(8,128)(2,1)S(1)}, bf16[768,256]{1,0:T(8,128)(2,1)S(1)}, u32[]{:S(2)}, u32[]{:S(2)}) collective-permute-start(bf16[768,256]{1,0:T(8,128)(2,1)S(1)} %get-tuple-element.18), channel_id=1, source_target_pairs={{0,3},{1,0},{2,1},{3,2},{4,7},{5,4},{6,5},{7,6},{8,11},{9,8},{10,9... | collective-permute-start | bytes 1179656 | tf_op jit(solution)/shard_map/ppermute | solution.py:330
  49.8 8.3 %collective-permute-start.3 = (bf16[512,256]{1,0:T(8,128)(2,1)S(1)}, bf16[512,256]{1,0:T(8,128)(2,1)S(1)}, u32[]{:S(2)}, u32[]{:S(2)}) collective-permute-start(bf16[512,256]{1,0:T(8,128)(2,1)S(1)} %pad_maximum_fusion), channel_id=1, source_target_pairs={{0,4},{4,0},{1,5},{5,1},{2,6},{6,2},{3,7},{7,3},{8,12},{12,8},{9,1... | collective-permute-start | bytes 786440 | tf_op jit(solution)/shard_map/ppermute | solution.py:332
  56.2 27.8 %copy-start.3 = (bf16[256]{0:T(256)(128)(2,1)S(1)}, bf16[256]{0:T(256)(128)(2,1)}, u32[]{:S(2)}) copy-start(bf16[256]{0:T(256)(128)(2,1)} %param.11) | copy-start | bytes 1540
  56.2 3.4 %collective-permute-start.4 = (bf16[512,256]{1,0:T(8,128)(2,1)S(1)}, bf16[512,256]{1,0:T(8,128)(2,1)S(1)}, u32[]{:S(2)}, u32[]{:S(2)}) collective-permute-start(bf16[512,256]{1,0:T(8,128)(2,1)S(1)} %pad_maximum_fusion.1), channel_id=1, source_target_pairs={{0,4},{4,0},{1,5},{5,1},{2,6},{6,2},{3,7},{7,3},{8,12},{12,8},{9,1... | collective-permute-start | bytes 786440 | tf_op jit(solution)/shard_map/ppermute | solution.py:332
  63.0 3.1 %collective-permute-start.6 = (f32[24,128]{1,0:T(8,128)S(1)}, f32[24,128]{1,0:T(8,128)S(1)}, u32[]{:S(2)}, u32[]{:S(2)}) collective-permute-start(f32[24,128]{1,0:T(8,128)S(1)} %shard_map.108.mine), channel_id=1, source_target_pairs={{0,4},{4,0},{1,5},{5,1},{2,6},{6,2},{3,7},{7,3},{8,12},{12,8},{9,1... | collective-permute-start | bytes 36872 | tf_op jit(solution)/shard_map/ppermute | solution.py:341
  109.2 9.2 %collective-permute-start.7 = (f32[128,128]{1,0:T(8,128)S(1)}, f32[128,128]{1,0:T(8,128)S(1)}, u32[]{:S(2)}, u32[]{:S(2)}) collective-permute-start(f32[128,128]{1,0:T(8,128)S(1)} %get-tuple-element.22), channel_id=1, source_target_pairs={{224,0},{225,1},{226,2},{227,3},{228,4},{229,5},{230,6},{231,7},{4... | collective-permute-start | bytes 196616 | tf_op jit(solution)/shard_map/ppermute | solution.py:363

commit v12 on v11

--- a/solution.py
+++ b/solution.py
@@ -43,11 +43,11 @@
 
 
 def turn_kernel(direction, wp, wr, dir_t, w_t):
-    turned = direction[...].astype(F32).T.astype(BF)
+    turned = direction[...].T
     for k in range(4):
         dir_t[k] = turned
-    w_t[0:128, :] = wp[...].astype(F32).T.astype(BF)
-    w_t[128:256, :] = wr[...].astype(F32).T.astype(BF)
+    w_t[0:128, :] = wp[...].T
+    w_t[128:256, :] = wr[...].T
 
 
 def prepare_kernel(lengths, group_ids, states, head, routes, quarters, extra, slots):
@@ -62,18 +62,16 @@
         jnp.broadcast_to(wide_head, (8, 1024)), states[...], NT, preferred_element_type=F32
     )
     lane = lax.broadcasted_iota(jnp.int32, (1, 128), 1)
-    rows = []
+    parts = []
     for q in range(2):
         valid = (lane < lengths[q]).astype(F32)
         part = jnp.sum(score[0:1, 128 * q : 128 * (q + 1)] * valid, axis=1, keepdims=True)
-        rows.extend(split3(part))
-    for values in (group_ids, lengths):
-        for q in range(2):
-            rows.append(jnp.full((1, 1), values[q], jnp.int32).astype(F32))
-    at = lax.broadcasted_iota(jnp.int32, (16, 128), 0)
-    block = jnp.zeros((16, 128), F32)
-    for n, row in enumerate(rows):
-        block = jnp.where(at == n, row, block)
+        numbers = [jnp.full((1, 1), n[q], jnp.int32).astype(F32) for n in (group_ids, lengths)]
+        parts.append([*split3(part), *numbers])
+    at = lax.broadcasted_iota(jnp.int32, (8, 128), 0)
+    block = jnp.zeros((8, 128), F32)
+    for n in range(5):
+        block = jnp.where(at == n, jnp.where(lane < 64, parts[0][n], parts[1][n]), block)
     extra[...] = block.astype(BF)
     target = routes[...]
     choose = (lax.broadcasted_iota(jnp.int32, (16, 256), 0) == target).astype(F32)
@@ -97,7 +95,7 @@
     copies = []
     for k in range(16):
         copies.append(pltpu.make_async_copy(w, out.at[k, 0:256, :], sems.at[k]))
-        copies.append(pltpu.make_async_copy(extra, out.at[k, 256:272, :], sems.at[16 + k]))
+        copies.append(pltpu.make_async_copy(extra, out.at[k, 256:264, :], sems.at[16 + k]))
     for copy in copies:
         copy.start()
     for copy in copies:
@@ -136,15 +134,14 @@
                 pay[pl.ds(8 * p + 4 * q + ((sec - STEPS[s]) & 3), 1), :] = acc[s][
                     p : p + 1, 128 * q : 128 * (q + 1)
                 ]
-    lane = lax.broadcasted_iota(jnp.int32, (16, 128), 1)
-    block = jnp.zeros((16, 128), F32)
+    lane = lax.broadcasted_iota(jnp.int32, (8, 128), 1)
+    block = jnp.zeros((8, 128), F32)
     for i in range(16):
-        block = jnp.where((lane & 15) == i, weights[i, 256:272, :].astype(F32), block)
-    fields = [block[0:1] + block[1:2] + block[2:3], block[3:4] + block[4:5] + block[5:6]]
-    fields.extend(block[n : n + 1] for n in range(6, 10))
-    facts = jnp.zeros((1, 128), F32)
-    for n, field in enumerate(fields):
-        facts = jnp.where((lane[0:1] >> 4) == n, field, facts)
+        block = jnp.where((lane & 15) == i, weights[i, 256:264, :].astype(F32), block)
+    field = (lane[0:1] >> 4) & 3
+    facts = jnp.where(field == 0, block[0:1] + block[1:2] + block[2:3], 0.0)
+    facts = jnp.where(field == 1, block[3:4], facts)
+    facts = jnp.where(field == 2, block[4:5], facts)
     pay[16:24, :] = jnp.broadcast_to(facts, (8, 128))
 
 
@@ -171,10 +168,10 @@
     facts = jnp.concatenate(facts + facts, axis=0)
     lane = lax.broadcasted_iota(jnp.int32, (8, 128), 1)
     at = lax.broadcasted_iota(jnp.int32, (8, 128), 0)
-    facts = jnp.where(at < 4, facts, pltpu.roll(facts, 112, 1))
+    facts = jnp.where(at < 4, facts, pltpu.roll(facts, 64, 1))
     used = lane < 16
-    ids = pltpu.roll(facts, 96, 1) * 0.125
-    lens = jnp.where(used, pltpu.roll(facts, 64, 1) * 0.125, 1.0)
+    ids = pltpu.roll(facts, 112, 1) * 0.125
+    lens = jnp.where(used, pltpu.roll(facts, 96, 1) * 0.125, 1.0)
     reward = facts / jnp.sqrt(lens)
     center = jnp.zeros((8, 128), F32)
     spread = jnp.zeros((8, 128), F32)
@@ -236,12 +233,15 @@
             out[4 * a + k, 128:136, :] = tail
 
 
-def finish_kernel(parts, grad, packed):
-    dp = dp_index()
+def finish_kernel(parts, grad):
     total = parts[0, 0:128, :].astype(F32)
     for i in range(1, 16):
         total = total + parts[i, 0:128, :].astype(F32)
     grad[...] = total.T
+
+
+def pick_kernel(parts, packed):
+    dp = dp_index()
     rows = [
         jnp.sum(parts[i, 128:136, :].astype(F32), axis=0, keepdims=True) for i in range(16)
     ]
@@ -306,7 +306,7 @@
     w_here = lax.ppermute(w_t, ALL, TO_HANDLER)
     quarters, extra, slots = call(
         prepare_kernel,
-        (shape((4, 256, 256), BF), shape((16, 128), BF), shape((1, 256), jnp.int32)),
+        (shape((4, 256, 256), BF), shape((8, 128), BF), shape((1, 256), jnp.int32)),
         smem=2,
         inputs=3,
         flops=8 * 256 * 1024 * 2,
@@ -316,7 +316,7 @@
     anywhere = pl.BlockSpec(memory_space=pl.ANY)
     weights = pl.pallas_call(
         spread_kernel,
-        out_shape=shape((16, 272, 128), BF),
+        out_shape=shape((16, 264, 128), BF),
         in_specs=[anywhere, pl.BlockSpec(memory_space=pltpu.HBM)],
         out_specs=anywhere,
         scratch_shapes=[pltpu.SemaphoreType.DMA((32,))],
@@ -353,13 +353,10 @@
         size=4 << 20,
     )(pays, *shares, *others, old_logp.reshape(2, 128), slots)
     parts = lax.all_to_all(parts, DP, 0, 0, tiled=True)
-    grad, packed = call(
-        finish_kernel,
-        (shape((128, 128), F32), shape((1, 320), F32)),
-        inputs=1,
-        flops=1 << 20,
-        size=1 << 20,
+    grad = call(
+        finish_kernel, shape((128, 128), F32), inputs=1, flops=1 << 20, size=1 << 20
     )(parts)
+    packed = call(pick_kernel, shape((1, 320), F32), inputs=1, flops=1 << 10, size=1 << 16)(parts)
     return lax.ppermute(grad, ALL, TO_OWNER), packed.reshape(1, 1, 320)
 
 

time: 120 us -> 119 us (level)
  waiting for transfers between devices: 18.9 us -> 17.3 us
    pallas_call x3 -> x4, Pallas kernels: 3.16 us -> 3.27 us  [the longest x1 1.3 us: body(): pl.pallas_call(spread_kernel, out_shape=shape((16, 264, 128), BF), in_spe...]
  transfers between devices with their start and end apart: 10 -> 10, of which waited for: 8 -> 8; matrix products, arithmetic and copies ran while one was open for 0% -> 0% of each run, Pallas kernels for 2% -> 3%
where the time goes in v12:
time: 119 us; the launch traced here: 118 us
  starting transfers between devices  46.3 us (39%)
  blocking collectives  41.8 us (35%)
  waiting for transfers between devices  17.3 us (15%)
  Pallas kernels  7.5 us (6%)
  local copies, waits for them, and re-layouts  4.38 us (4%)
    all_to_all x1, blocking collectives, body(): parts = lax.all_to_all(parts, DP, 0, 0, tiled=True)  23.8 us
    all_to_all x1, blocking collectives, body(): pays = lax.all_to_all(pays, ('zh', 'sec'), 0, 0, tiled=True)  18 us
    ppermute x3, starting transfers between devices, body(): lax.ppermute(packs[n], 'sec', ring(STEPS[n]))  12 us
    all_to_all x1, starting transfers between devices, body(): dirs = lax.all_to_all(dir_t, 'zh', 0, 0, tiled=True)  10.3 us
    all_to_all x1, starting transfers between devices, body(): weights = lax.all_to_all(weights, DP, 0, 0, tiled=True)  8.73 us
    ppermute x3, waiting for transfers between devices, body(): lax.ppermute(packs[n], 'sec', ring(STEPS[n]))  7.81 us
    ppermute x1, starting transfers between devices, body(): w_here = lax.ppermute(w_t, ALL, TO_HANDLER)  6.04 us
    ppermute x1, waiting for transfers between devices, body(): return (lax.ppermute(grad, ALL, TO_OWNER), packed.reshape(1, 1, 320))  4.81 us
  transfers between devices with their start and end apart: 10, of which 8 were waited for; matrix products, arithmetic and copies ran while one was open for 0% of the time, Pallas kernels for 3%

profile of v12, /device:TPU:8, one launch (start us, length us, event | category | flops | bytes accessed | tf_op | source)
XLA Modules:
  0.0 118.2 jit_solution(11027567528927301998)
XLA Ops:
  0.6 1.7 %shard_map.105 = (bf16[4,128,256]{2,1,0:T(8,128)(2,1)}, bf16[256,128]{1,0:T(8,128)(2,1)}) custom-call(bf16[256,128]{1,0:T(8,128)(2,1)} %direction.1, bf16[128,128]{1,0:T(8,128)(2,1)} %wp.1, bf16[128,128]{1,0:T(8,128)(2,1)} %wr.1), custom_call_target="tpu_custom_call" | custom-call | flops 65536 | bytes 262144 | tf_op jit(solution)/shard_map/pallas_call | solution.py:298
  2.3 10.3 %all-to-all-start = ((bf16[4,128,256]{2,1,0:T(8,128)(2,1)}), bf16[4,128,256]{2,1,0:T(8,128)(2,1)S(1)}, u32[]{:S(2)}, u32[]{:S(2)}) async-start(bf16[4,128,256]{2,1,0:T(8,128)(2,1)} %get-tuple-element.12), calls=%async_computation | async-start | bytes 524288 | tf_op jit(solution)/shard_map/all_to_all | solution.py:315
  12.6 6.0 %collective-permute-start.5 = (bf16[256,128]{1,0:T(8,128)(2,1)}, bf16[256,128]{1,0:T(8,128)(2,1)S(1)}, u32[]{:S(2)}, u32[]{:S(2)}) collective-permute-start(bf16[256,128]{1,0:T(8,128)(2,1)} %get-tuple-element.17), channel_id=1, source_target_pairs={{0,224},{1,225},{2,226},{3,227},{4,228},{5,229},{6,230},{7,231},{8... | collective-permute-start | bytes 196616 | tf_op jit(solution)/shard_map/ppermute | solution.py:306
  18.6 0.0 copy-start
  18.6 1.0 copy-done
  19.7 0.0 copy-start.1
  19.7 0.7 copy-done.1
  20.4 0.0 copy-start.2
  20.4 0.7 copy-done.2
  21.0 0.0 copy-start.4
  21.0 0.7 copy-done.4
  21.7 0.0 copy-start.5
  21.7 0.7 copy-done.5
  22.3 1.0 shard_map.104
  23.3 0.8 collective-permute-done.5.w
  24.1 1.3 %shard_map.107 = bf16[16,264,128]{2,1,0:T(8,128)(2,1)} custom-call(bf16[256,128]{1,0:T(8,128)(2,1)S(1)} %collective-permute-done.5.w, bf16[8,128]{1,0:T(8,128)(2,1)S(1)} %get-tuple-element.18.extra), custom_call_target="tpu_custom_call" | custom-call | flops 1024 | bytes 1048576 | tf_op jit(solution)/shard_map/pallas_call | solution.py:317
  25.4 0.0 all-to-all-done.dirs
  25.4 8.7 %all-to-all-start.1 = ((bf16[16,264,128]{2,1,0:T(8,128)(2,1)}), bf16[16,264,128]{2,1,0:T(8,128)(2,1)S(1)}, u32[]{:S(2)}, u32[]{:S(2)}) async-start(bf16[16,264,128]{2,1,0:T(8,128)(2,1)} %shard_map.107), calls=%async_computation.1 | async-start | bytes 2162688 | tf_op jit(solution)/shard_map/all_to_all | solution.py:326
  34.1 0.1 shard_map.106
  34.3 4.9 %collective-permute-start = (bf16[768,256]{1,0:T(8,128)(2,1)S(1)}, bf16[768,256]{1,0:T(8,128)(2,1)S(1)}, u32[]{:S(2)}, u32[]{:S(2)}) collective-permute-start(bf16[768,256]{1,0:T(8,128)(2,1)S(1)} %get-tuple-element.14), channel_id=1, source_target_pairs={{0,2},{1,3},{2,0},{3,1},{4,6},{5,7},{6,4},{7,5},{8,10},{9,11},{10,... | collective-permute-start | bytes 1179656 | tf_op jit(solution)/shard_map/ppermute | solution.py:330
  39.2 2.5 %collective-permute-start.1 = (bf16[768,256]{1,0:T(8,128)(2,1)S(1)}, bf16[768,256]{1,0:T(8,128)(2,1)S(1)}, u32[]{:S(2)}, u32[]{:S(2)}) collective-permute-start(bf16[768,256]{1,0:T(8,128)(2,1)S(1)} %get-tuple-element.15), channel_id=1, source_target_pairs={{0,1},{1,2},{2,3},{3,0},{4,5},{5,6},{6,7},{7,4},{8,9},{9,10},{10,1... | collective-permute-start | bytes 1179656 | tf_op jit(solution)/shard_map/ppermute | solution.py:330
  41.7 4.6 %collective-permute-start.2 = (bf16[768,256]{1,0:T(8,128)(2,1)S(1)}, bf16[768,256]{1,0:T(8,128)(2,1)S(1)}, u32[]{:S(2)}, u32[]{:S(2)}) collective-permute-start(bf16[768,256]{1,0:T(8,128)(2,1)S(1)} %get-tuple-element.16), channel_id=1, source_target_pairs={{0,3},{1,0},{2,1},{3,2},{4,7},{5,4},{6,5},{7,6},{8,11},{9,8},{10,9... | collective-permute-start | bytes 1179656 | tf_op jit(solution)/shard_map/ppermute | solution.py:330
  46.3 3.5 %collective-permute-done.s1 = bf16[768,256]{1,0:T(8,128)(2,1)S(1)} collective-permute-done((bf16[768,256]{1,0:T(8,128)(2,1)S(1)}, bf16[768,256]{1,0:T(8,128)(2,1)S(1)}, u32[]{:S(2)}, u32[]{:S(2)}) %collective-permute-start) | collective-permute-done | bytes 393248 | tf_op jit(solution)/shard_map/ppermute | solution.py:330
  49.8 1.9 %collective-permute-start.3 = (bf16[512,256]{1,0:T(8,128)(2,1)S(1)}, bf16[512,256]{1,0:T(8,128)(2,1)S(1)}, u32[]{:S(2)}, u32[]{:S(2)}) collective-permute-start(bf16[512,256]{1,0:T(8,128)(2,1)S(1)} %pad_maximum_fusion), channel_id=1, source_target_pairs={{0,4},{4,0},{1,5},{5,1},{2,6},{6,2},{3,7},{7,3},{8,12},{12,8},{9,1... | collective-permute-start | bytes 786440 | tf_op jit(solution)/shard_map/ppermute | solution.py:332
  51.7 4.3 %collective-permute-done.1.s2 = bf16[768,256]{1,0:T(8,128)(2,1)S(1)} collective-permute-done((bf16[768,256]{1,0:T(8,128)(2,1)S(1)}, bf16[768,256]{1,0:T(8,128)(2,1)S(1)}, u32[]{:S(2)}, u32[]{:S(2)}) %collective-permute-start.1) | collective-permute-done | bytes 393248 | tf_op jit(solution)/shard_map/ppermute | solution.py:330
  56.0 0.1 collective-permute-done.2.s3
  56.1 0.0 copy-start.3
  56.1 1.9 %collective-permute-start.4 = (bf16[512,256]{1,0:T(8,128)(2,1)S(1)}, bf16[512,256]{1,0:T(8,128)(2,1)S(1)}, u32[]{:S(2)}, u32[]{:S(2)}) collective-permute-start(bf16[512,256]{1,0:T(8,128)(2,1)S(1)} %pad_maximum_fusion.1), channel_id=1, source_target_pairs={{0,4},{4,0},{1,5},{5,1},{2,6},{6,2},{3,7},{7,3},{8,12},{12,8},{9,1... | collective-permute-start | bytes 786440 | tf_op jit(solution)/shard_map/ppermute | solution.py:332
  58.1 0.0 collective-permute-done.3.o0
  58.1 1.5 %collective-permute-done.4.o1 = bf16[512,256]{1,0:T(8,128)(2,1)S(1)} collective-permute-done((bf16[512,256]{1,0:T(8,128)(2,1)S(1)}, bf16[512,256]{1,0:T(8,128)(2,1)S(1)}, u32[]{:S(2)}, u32[]{:S(2)}) %collective-permute-start.4) | collective-permute-done | bytes 262176 | tf_op jit(solution)/shard_map/ppermute | solution.py:332
  59.6 1.3 %all-to-all-done.1.weights = bf16[16,264,128]{2,1,0:T(8,128)(2,1)S(1)} async-done(((bf16[16,264,128]{2,1,0:T(8,128)(2,1)}), bf16[16,264,128]{2,1,0:T(8,128)(2,1)S(1)}, u32[]{:S(2)}, u32[]{:S(2)}) %all-to-all-start.1) | async-done | bytes 1081376 | tf_op jit(solution)/shard_map/all_to_all | solution.py:326
  60.8 1.4 %shard_map.108.mine = f32[24,128]{1,0:T(8,128)S(1)} custom-call(bf16[768,256]{1,0:T(8,128)(2,1)S(1)} %get-tuple-element.13.s0, bf16[768,256]{1,0:T(8,128)(2,1)S(1)} %collective-permute-done.s1, bf16[768,256]{1,0:T(8,128)(2,1)S(1)} %collective-permute-done.1.s2, bf16[768,256]{1,0:T(8,128)(2,1)S(1)} %collective-permute-done.2.s3, ...), custom_call_target="tpu_custom_call" | custom-call | flops 1073741824 | bytes 4194304 | tf_op jit(solution)/shard_map/pallas_call | solution.py:337
  62.2 1.9 %collective-permute-start.6 = (f32[24,128]{1,0:T(8,128)S(1)}, f32[24,128]{1,0:T(8,128)S(1)}, u32[]{:S(2)}, u32[]{:S(2)}) collective-permute-start(f32[24,128]{1,0:T(8,128)S(1)} %shard_map.108.mine), channel_id=1, source_target_pairs={{0,4},{4,0},{1,5},{5,1},{2,6},{6,2},{3,7},{7,3},{8,12},{12,8},{9,1... | collective-permute-start | bytes 36872 | tf_op jit(solution)/shard_map/ppermute | solution.py:341
  64.1 1.1 collective-permute-done.6.partner
  65.3 18.0 %all_to_all.20.pays = f32[16,24,128]{2,1,0:T(8,128)S(1)} all-to-all(f32[16,24,128]{2,1,0:T(8,128)S(1)} %shard_map.109), channel_id=1, replica_groups=mesh['zl'=2,'y'=8,'zh'=4,'core'=2,'sec'=4] {'zh','sec'}, dimensions={0} | all-to-all | bytes 393216 | tf_op jit(solution)/shard_map/all_to_all | solution.py:343
  83.3 0.0 copy-done.3
  83.3 1.1 shard_map.110
  84.4 23.8 %all_to_all.21.parts = bf16[16,136,128]{2,1,0:T(8,128)(2,1)S(1)} all-to-all(bf16[16,136,128]{2,1,0:T(8,128)(2,1)S(1)} %shard_map.110), channel_id=1, replica_groups=mesh['zl'=2,'y'=8,'zh'=4,'core'=2,'sec'=4] {'zl','y'}, dimensions={0} | all-to-all | bytes 1114112 | tf_op jit(solution)/shard_map/all_to_all | solution.py:355
  108.2 0.1 shard_map.111
  108.4 3.5 %collective-permute-start.7 = (f32[128,128]{1,0:T(8,128)S(1)}, f32[128,128]{1,0:T(8,128)S(1)}, u32[]{:S(2)}, u32[]{:S(2)}) collective-permute-start(f32[128,128]{1,0:T(8,128)S(1)} %shard_map.111), channel_id=1, source_target_pairs={{224,0},{225,1},{226,2},{227,3},{228,4},{229,5},{230,6},{231,7},{4... | collective-permute-start | bytes 196616 | tf_op jit(solution)/shard_map/ppermute | solution.py:360
  111.9 0.9 shard_map.112
  112.7 4.8 %collective-permute-done.7 = f32[128,128]{1,0:T(8,128)S(1)} collective-permute-done((f32[128,128]{1,0:T(8,128)S(1)}, f32[128,128]{1,0:T(8,128)S(1)}, u32[]{:S(2)}, u32[]{:S(2)}) %collective-permute-start.7) | collective-permute-done | bytes 65568 | tf_op jit(solution)/shard_map/ppermute | solution.py:360
  117.6 0.6 copy.12
  (7 shorter events, 0.1 us)
Async XLA Ops:
  2.3 23.1 %all-to-all-start = ((bf16[4,128,256]{2,1,0:T(8,128)(2,1)}), bf16[4,128,256]{2,1,0:T(8,128)(2,1)S(1)}, u32[]{:S(2)}, u32[]{:S(2)}) async-start(bf16[4,128,256]{2,1,0:T(8,128)(2,1)} %get-tuple-element.12), calls=%async_computation | async-start | bytes 524288 | tf_op jit(solution)/shard_map/all_to_all | solution.py:315
  12.6 11.5 %collective-permute-start.5 = (bf16[256,128]{1,0:T(8,128)(2,1)}, bf16[256,128]{1,0:T(8,128)(2,1)S(1)}, u32[]{:S(2)}, u32[]{:S(2)}) collective-permute-start(bf16[256,128]{1,0:T(8,128)(2,1)} %get-tuple-element.17), channel_id=1, source_target_pairs={{0,224},{1,225},{2,226},{3,227},{4,228},{5,229},{6,230},{7,231},{8... | collective-permute-start | bytes 196616 | tf_op jit(solution)/shard_map/ppermute | solution.py:306
  18.6 1.0 copy-start
  19.7 0.7 copy-start.1
  20.4 0.7 copy-start.2
  21.0 0.7 copy-start.4
  21.7 0.7 copy-start.5
  25.4 35.4 %all-to-all-start.1 = ((bf16[16,264,128]{2,1,0:T(8,128)(2,1)}), bf16[16,264,128]{2,1,0:T(8,128)(2,1)S(1)}, u32[]{:S(2)}, u32[]{:S(2)}) async-start(bf16[16,264,128]{2,1,0:T(8,128)(2,1)} %shard_map.107), calls=%async_computation.1 | async-start | bytes 2162688 | tf_op jit(solution)/shard_map/all_to_all | solution.py:326
  34.3 15.5 %collective-permute-start = (bf16[768,256]{1,0:T(8,128)(2,1)S(1)}, bf16[768,256]{1,0:T(8,128)(2,1)S(1)}, u32[]{:S(2)}, u32[]{:S(2)}) collective-permute-start(bf16[768,256]{1,0:T(8,128)(2,1)S(1)} %get-tuple-element.14), channel_id=1, source_target_pairs={{0,2},{1,3},{2,0},{3,1},{4,6},{5,7},{6,4},{7,5},{8,10},{9,11},{10,... | collective-permute-start | bytes 1179656 | tf_op jit(solution)/shard_map/ppermute | solution.py:330
  39.2 16.8 %collective-permute-start.1 = (bf16[768,256]{1,0:T(8,128)(2,1)S(1)}, bf16[768,256]{1,0:T(8,128)(2,1)S(1)}, u32[]{:S(2)}, u32[]{:S(2)}) collective-permute-start(bf16[768,256]{1,0:T(8,128)(2,1)S(1)} %get-tuple-element.15), channel_id=1, source_target_pairs={{0,1},{1,2},{2,3},{3,0},{4,5},{5,6},{6,7},{7,4},{8,9},{9,10},{10,1... | collective-permute-start | bytes 1179656 | tf_op jit(solution)/shard_map/ppermute | solution.py:330
  41.7 14.4 %collective-permute-start.2 = (bf16[768,256]{1,0:T(8,128)(2,1)S(1)}, bf16[768,256]{1,0:T(8,128)(2,1)S(1)}, u32[]{:S(2)}, u32[]{:S(2)}) collective-permute-start(bf16[768,256]{1,0:T(8,128)(2,1)S(1)} %get-tuple-element.16), channel_id=1, source_target_pairs={{0,3},{1,0},{2,1},{3,2},{4,7},{5,4},{6,5},{7,6},{8,11},{9,8},{10,9... | collective-permute-start | bytes 1179656 | tf_op jit(solution)/shard_map/ppermute | solution.py:330
  49.8 8.3 %collective-permute-start.3 = (bf16[512,256]{1,0:T(8,128)(2,1)S(1)}, bf16[512,256]{1,0:T(8,128)(2,1)S(1)}, u32[]{:S(2)}, u32[]{:S(2)}) collective-permute-start(bf16[512,256]{1,0:T(8,128)(2,1)S(1)} %pad_maximum_fusion), channel_id=1, source_target_pairs={{0,4},{4,0},{1,5},{5,1},{2,6},{6,2},{3,7},{7,3},{8,12},{12,8},{9,1... | collective-permute-start | bytes 786440 | tf_op jit(solution)/shard_map/ppermute | solution.py:332
  56.1 27.2 %copy-start.3 = (bf16[256]{0:T(256)(128)(2,1)S(1)}, bf16[256]{0:T(256)(128)(2,1)}, u32[]{:S(2)}) copy-start(bf16[256]{0:T(256)(128)(2,1)} %param.11) | copy-start | bytes 1540
  56.1 3.4 %collective-permute-start.4 = (bf16[512,256]{1,0:T(8,128)(2,1)S(1)}, bf16[512,256]{1,0:T(8,128)(2,1)S(1)}, u32[]{:S(2)}, u32[]{:S(2)}) collective-permute-start(bf16[512,256]{1,0:T(8,128)(2,1)S(1)} %pad_maximum_fusion.1), channel_id=1, source_target_pairs={{0,4},{4,0},{1,5},{5,1},{2,6},{6,2},{3,7},{7,3},{8,12},{12,8},{9,1... | collective-permute-start | bytes 786440 | tf_op jit(solution)/shard_map/ppermute | solution.py:332
  62.2 3.1 %collective-permute-start.6 = (f32[24,128]{1,0:T(8,128)S(1)}, f32[24,128]{1,0:T(8,128)S(1)}, u32[]{:S(2)}, u32[]{:S(2)}) collective-permute-start(f32[24,128]{1,0:T(8,128)S(1)} %shard_map.108.mine), channel_id=1, source_target_pairs={{0,4},{4,0},{1,5},{5,1},{2,6},{6,2},{3,7},{7,3},{8,12},{12,8},{9,1... | collective-permute-start | bytes 36872 | tf_op jit(solution)/shard_map/ppermute | solution.py:341
  108.4 9.2 %collective-permute-start.7 = (f32[128,128]{1,0:T(8,128)S(1)}, f32[128,128]{1,0:T(8,128)S(1)}, u32[]{:S(2)}, u32[]{:S(2)}) collective-permute-start(f32[128,128]{1,0:T(8,128)S(1)} %shard_map.111), channel_id=1, source_target_pairs={{224,0},{225,1},{226,2},{227,3},{228,4},{229,5},{230,6},{231,7},{4... | collective-permute-start | bytes 196616 | tf_op jit(solution)/shard_map/ppermute | solution.py:360

commit v13 on v12

--- a/solution.py
+++ b/solution.py
@@ -91,11 +91,10 @@
             outs[k][256 + 128 * q : 384 + 128 * q, :] = dirs[q]
 
 
-def spread_kernel(w, extra, out, sems):
-    copies = []
-    for k in range(16):
-        copies.append(pltpu.make_async_copy(w, out.at[k, 0:256, :], sems.at[k]))
-        copies.append(pltpu.make_async_copy(extra, out.at[k, 256:264, :], sems.at[16 + k]))
+def spread_kernel(w, extra, out, block, sems):
+    block[0:256, :] = w[...]
+    block[256:264, :] = extra[...]
+    copies = [pltpu.make_async_copy(block, out.at[k], sems.at[k]) for k in range(16)]
     for copy in copies:
         copy.start()
     for copy in copies:
@@ -317,9 +316,9 @@
     weights = pl.pallas_call(
         spread_kernel,
         out_shape=shape((16, 264, 128), BF),
-        in_specs=[anywhere, pl.BlockSpec(memory_space=pltpu.HBM)],
+        in_specs=[pl.BlockSpec(memory_space=pltpu.VMEM)] * 2,
         out_specs=anywhere,
-        scratch_shapes=[pltpu.SemaphoreType.DMA((32,))],
+        scratch_shapes=[pltpu.VMEM((264, 128), BF), pltpu.SemaphoreType.DMA((16,))],
         cost_estimate=cost(1 << 10, 1 << 20),
         compiler_params=pltpu.CompilerParams(vmem_limit_bytes=16 << 20),
     )(w_here, extra)

time: 119 us -> 119 us (level)
  no operation moved by 1% of the time
where the time goes in v13:
time: 119 us; the launch traced here: 118 us
  starting transfers between devices  46.3 us (39%)
  blocking collectives  41.8 us (35%)
  waiting for transfers between devices  17.3 us (15%)
  Pallas kernels  7.35 us (6%)
  local copies, waits for them, and re-layouts  4.38 us (4%)
    all_to_all x1, blocking collectives, body(): parts = lax.all_to_all(parts, DP, 0, 0, tiled=True)  23.8 us
    all_to_all x1, blocking collectives, body(): pays = lax.all_to_all(pays, ('zh', 'sec'), 0, 0, tiled=True)  18 us
    ppermute x3, starting transfers between devices, body(): lax.ppermute(packs[n], 'sec', ring(STEPS[n]))  12 us
    all_to_all x1, starting transfers between devices, body(): dirs = lax.all_to_all(dir_t, 'zh', 0, 0, tiled=True)  10.3 us
    all_to_all x1, starting transfers between devices, body(): weights = lax.all_to_all(weights, DP, 0, 0, tiled=True)  8.73 us
    ppermute x3, waiting for transfers between devices, body(): lax.ppermute(packs[n], 'sec', ring(STEPS[n]))  7.81 us
    ppermute x1, starting transfers between devices, body(): w_here = lax.ppermute(w_t, ALL, TO_HANDLER)  6.04 us
    ppermute x1, waiting for transfers between devices, body(): return (lax.ppermute(grad, ALL, TO_OWNER), packed.reshape(1, 1, 320))  4.81 us
  transfers between devices with their start and end apart: 10, of which 8 were waited for; matrix products, arithmetic and copies ran while one was open for 0% of the time, Pallas kernels for 3%

profile of v13, /device:TPU:8, one launch (start us, length us, event | category | flops | bytes accessed | tf_op | source)
XLA Modules:
  0.0 118.0 jit_solution(1475002405138881908)
XLA Ops:
  0.6 1.7 %shard_map.105 = (bf16[4,128,256]{2,1,0:T(8,128)(2,1)}, bf16[256,128]{1,0:T(8,128)(2,1)}) custom-call(bf16[256,128]{1,0:T(8,128)(2,1)} %direction.1, bf16[128,128]{1,0:T(8,128)(2,1)} %wp.1, bf16[128,128]{1,0:T(8,128)(2,1)} %wr.1), custom_call_target="tpu_custom_call" | custom-call | flops 65536 | bytes 262144 | tf_op jit(solution)/shard_map/pallas_call | solution.py:297
  2.3 10.3 %all-to-all-start = ((bf16[4,128,256]{2,1,0:T(8,128)(2,1)}), bf16[4,128,256]{2,1,0:T(8,128)(2,1)S(1)}, u32[]{:S(2)}, u32[]{:S(2)}) async-start(bf16[4,128,256]{2,1,0:T(8,128)(2,1)} %get-tuple-element.12), calls=%async_computation | async-start | bytes 524288 | tf_op jit(solution)/shard_map/all_to_all | solution.py:314
  12.6 6.0 %collective-permute-start.5 = (bf16[256,128]{1,0:T(8,128)(2,1)}, bf16[256,128]{1,0:T(8,128)(2,1)S(1)}, u32[]{:S(2)}, u32[]{:S(2)}) collective-permute-start(bf16[256,128]{1,0:T(8,128)(2,1)} %get-tuple-element.17), channel_id=1, source_target_pairs={{0,224},{1,225},{2,226},{3,227},{4,228},{5,229},{6,230},{7,231},{8... | collective-permute-start | bytes 196616 | tf_op jit(solution)/shard_map/ppermute | solution.py:305
  18.6 0.0 copy-start
  18.6 1.0 copy-done
  19.7 0.0 copy-start.1
  19.7 0.7 copy-done.1
  20.4 0.0 copy-start.2
  20.4 0.7 copy-done.2
  21.0 0.0 copy-start.4
  21.0 0.7 copy-done.4
  21.7 0.0 copy-start.5
  21.7 0.7 copy-done.5
  22.3 1.0 shard_map.104
  23.3 0.8 collective-permute-done.5.w
  24.1 1.2 shard_map.107
  25.3 0.0 all-to-all-done.dirs
  25.3 8.7 %all-to-all-start.1 = ((bf16[16,264,128]{2,1,0:T(8,128)(2,1)}), bf16[16,264,128]{2,1,0:T(8,128)(2,1)S(1)}, u32[]{:S(2)}, u32[]{:S(2)}) async-start(bf16[16,264,128]{2,1,0:T(8,128)(2,1)} %shard_map.107), calls=%async_computation.1 | async-start | bytes 2162688 | tf_op jit(solution)/shard_map/all_to_all | solution.py:325
  34.0 0.1 shard_map.106
  34.1 4.9 %collective-permute-start = (bf16[768,256]{1,0:T(8,128)(2,1)S(1)}, bf16[768,256]{1,0:T(8,128)(2,1)S(1)}, u32[]{:S(2)}, u32[]{:S(2)}) collective-permute-start(bf16[768,256]{1,0:T(8,128)(2,1)S(1)} %get-tuple-element.14), channel_id=1, source_target_pairs={{0,2},{1,3},{2,0},{3,1},{4,6},{5,7},{6,4},{7,5},{8,10},{9,11},{10,... | collective-permute-start | bytes 1179656 | tf_op jit(solution)/shard_map/ppermute | solution.py:329
  39.0 2.5 %collective-permute-start.1 = (bf16[768,256]{1,0:T(8,128)(2,1)S(1)}, bf16[768,256]{1,0:T(8,128)(2,1)S(1)}, u32[]{:S(2)}, u32[]{:S(2)}) collective-permute-start(bf16[768,256]{1,0:T(8,128)(2,1)S(1)} %get-tuple-element.15), channel_id=1, source_target_pairs={{0,1},{1,2},{2,3},{3,0},{4,5},{5,6},{6,7},{7,4},{8,9},{9,10},{10,1... | collective-permute-start | bytes 1179656 | tf_op jit(solution)/shard_map/ppermute | solution.py:329
  41.6 4.6 %collective-permute-start.2 = (bf16[768,256]{1,0:T(8,128)(2,1)S(1)}, bf16[768,256]{1,0:T(8,128)(2,1)S(1)}, u32[]{:S(2)}, u32[]{:S(2)}) collective-permute-start(bf16[768,256]{1,0:T(8,128)(2,1)S(1)} %get-tuple-element.16), channel_id=1, source_target_pairs={{0,3},{1,0},{2,1},{3,2},{4,7},{5,4},{6,5},{7,6},{8,11},{9,8},{10,9... | collective-permute-start | bytes 1179656 | tf_op jit(solution)/shard_map/ppermute | solution.py:329
  46.1 3.5 %collective-permute-done.s1 = bf16[768,256]{1,0:T(8,128)(2,1)S(1)} collective-permute-done((bf16[768,256]{1,0:T(8,128)(2,1)S(1)}, bf16[768,256]{1,0:T(8,128)(2,1)S(1)}, u32[]{:S(2)}, u32[]{:S(2)}) %collective-permute-start) | collective-permute-done | bytes 393248 | tf_op jit(solution)/shard_map/ppermute | solution.py:329
  49.6 1.9 %collective-permute-start.3 = (bf16[512,256]{1,0:T(8,128)(2,1)S(1)}, bf16[512,256]{1,0:T(8,128)(2,1)S(1)}, u32[]{:S(2)}, u32[]{:S(2)}) collective-permute-start(bf16[512,256]{1,0:T(8,128)(2,1)S(1)} %pad_maximum_fusion), channel_id=1, source_target_pairs={{0,4},{4,0},{1,5},{5,1},{2,6},{6,2},{3,7},{7,3},{8,12},{12,8},{9,1... | collective-permute-start | bytes 786440 | tf_op jit(solution)/shard_map/ppermute | solution.py:331
  51.6 4.3 %collective-permute-done.1.s2 = bf16[768,256]{1,0:T(8,128)(2,1)S(1)} collective-permute-done((bf16[768,256]{1,0:T(8,128)(2,1)S(1)}, bf16[768,256]{1,0:T(8,128)(2,1)S(1)}, u32[]{:S(2)}, u32[]{:S(2)}) %collective-permute-start.1) | collective-permute-done | bytes 393248 | tf_op jit(solution)/shard_map/ppermute | solution.py:329
  55.9 0.1 collective-permute-done.2.s3
  56.0 0.0 copy-start.3
  56.0 1.9 %collective-permute-start.4 = (bf16[512,256]{1,0:T(8,128)(2,1)S(1)}, bf16[512,256]{1,0:T(8,128)(2,1)S(1)}, u32[]{:S(2)}, u32[]{:S(2)}) collective-permute-start(bf16[512,256]{1,0:T(8,128)(2,1)S(1)} %pad_maximum_fusion.1), channel_id=1, source_target_pairs={{0,4},{4,0},{1,5},{5,1},{2,6},{6,2},{3,7},{7,3},{8,12},{12,8},{9,1... | collective-permute-start | bytes 786440 | tf_op jit(solution)/shard_map/ppermute | solution.py:331
  57.9 0.0 collective-permute-done.3.o0
  57.9 1.5 %collective-permute-done.4.o1 = bf16[512,256]{1,0:T(8,128)(2,1)S(1)} collective-permute-done((bf16[512,256]{1,0:T(8,128)(2,1)S(1)}, bf16[512,256]{1,0:T(8,128)(2,1)S(1)}, u32[]{:S(2)}, u32[]{:S(2)}) %collective-permute-start.4) | collective-permute-done | bytes 262176 | tf_op jit(solution)/shard_map/ppermute | solution.py:331
  59.4 1.3 %all-to-all-done.1.weights = bf16[16,264,128]{2,1,0:T(8,128)(2,1)S(1)} async-done(((bf16[16,264,128]{2,1,0:T(8,128)(2,1)}), bf16[16,264,128]{2,1,0:T(8,128)(2,1)S(1)}, u32[]{:S(2)}, u32[]{:S(2)}) %all-to-all-start.1) | async-done | bytes 1081376 | tf_op jit(solution)/shard_map/all_to_all | solution.py:325
  60.7 1.4 %shard_map.108.mine = f32[24,128]{1,0:T(8,128)S(1)} custom-call(bf16[768,256]{1,0:T(8,128)(2,1)S(1)} %get-tuple-element.13.s0, bf16[768,256]{1,0:T(8,128)(2,1)S(1)} %collective-permute-done.s1, bf16[768,256]{1,0:T(8,128)(2,1)S(1)} %collective-permute-done.1.s2, bf16[768,256]{1,0:T(8,128)(2,1)S(1)} %collective-permute-done.2.s3, ...), custom_call_target="tpu_custom_call" | custom-call | flops 1073741824 | bytes 4194304 | tf_op jit(solution)/shard_map/pallas_call | solution.py:336
  62.1 1.9 %collective-permute-start.6 = (f32[24,128]{1,0:T(8,128)S(1)}, f32[24,128]{1,0:T(8,128)S(1)}, u32[]{:S(2)}, u32[]{:S(2)}) collective-permute-start(f32[24,128]{1,0:T(8,128)S(1)} %shard_map.108.mine), channel_id=1, source_target_pairs={{0,4},{4,0},{1,5},{5,1},{2,6},{6,2},{3,7},{7,3},{8,12},{12,8},{9,1... | collective-permute-start | bytes 36872 | tf_op jit(solution)/shard_map/ppermute | solution.py:340
  64.0 1.1 collective-permute-done.6.partner
  65.2 18.0 %all_to_all.20.pays = f32[16,24,128]{2,1,0:T(8,128)S(1)} all-to-all(f32[16,24,128]{2,1,0:T(8,128)S(1)} %shard_map.109), channel_id=1, replica_groups=mesh['zl'=2,'y'=8,'zh'=4,'core'=2,'sec'=4] {'zh','sec'}, dimensions={0} | all-to-all | bytes 393216 | tf_op jit(solution)/shard_map/all_to_all | solution.py:342
  83.2 0.0 copy-done.3
  83.2 1.1 shard_map.110
  84.3 23.8 %all_to_all.21.parts = bf16[16,136,128]{2,1,0:T(8,128)(2,1)S(1)} all-to-all(bf16[16,136,128]{2,1,0:T(8,128)(2,1)S(1)} %shard_map.110), channel_id=1, replica_groups=mesh['zl'=2,'y'=8,'zh'=4,'core'=2,'sec'=4] {'zl','y'}, dimensions={0} | all-to-all | bytes 1114112 | tf_op jit(solution)/shard_map/all_to_all | solution.py:354
  108.1 0.1 shard_map.111
  108.2 3.5 %collective-permute-start.7 = (f32[128,128]{1,0:T(8,128)S(1)}, f32[128,128]{1,0:T(8,128)S(1)}, u32[]{:S(2)}, u32[]{:S(2)}) collective-permute-start(f32[128,128]{1,0:T(8,128)S(1)} %shard_map.111), channel_id=1, source_target_pairs={{224,0},{225,1},{226,2},{227,3},{228,4},{229,5},{230,6},{231,7},{4... | collective-permute-start | bytes 196616 | tf_op jit(solution)/shard_map/ppermute | solution.py:359
  111.7 0.9 shard_map.112
  112.6 4.8 %collective-permute-done.7 = f32[128,128]{1,0:T(8,128)S(1)} collective-permute-done((f32[128,128]{1,0:T(8,128)S(1)}, f32[128,128]{1,0:T(8,128)S(1)}, u32[]{:S(2)}, u32[]{:S(2)}) %collective-permute-start.7) | collective-permute-done | bytes 65568 | tf_op jit(solution)/shard_map/ppermute | solution.py:359
  117.4 0.6 copy.12
  (7 shorter events, 0.1 us)
Async XLA Ops:
  2.3 23.0 %all-to-all-start = ((bf16[4,128,256]{2,1,0:T(8,128)(2,1)}), bf16[4,128,256]{2,1,0:T(8,128)(2,1)S(1)}, u32[]{:S(2)}, u32[]{:S(2)}) async-start(bf16[4,128,256]{2,1,0:T(8,128)(2,1)} %get-tuple-element.12), calls=%async_computation | async-start | bytes 524288 | tf_op jit(solution)/shard_map/all_to_all | solution.py:314
  12.6 11.5 %collective-permute-start.5 = (bf16[256,128]{1,0:T(8,128)(2,1)}, bf16[256,128]{1,0:T(8,128)(2,1)S(1)}, u32[]{:S(2)}, u32[]{:S(2)}) collective-permute-start(bf16[256,128]{1,0:T(8,128)(2,1)} %get-tuple-element.17), channel_id=1, source_target_pairs={{0,224},{1,225},{2,226},{3,227},{4,228},{5,229},{6,230},{7,231},{8... | collective-permute-start | bytes 196616 | tf_op jit(solution)/shard_map/ppermute | solution.py:305
  18.6 1.0 copy-start
  19.7 0.7 copy-start.1
  20.4 0.7 copy-start.2
  21.0 0.7 copy-start.4
  21.7 0.7 copy-start.5
  25.3 35.4 %all-to-all-start.1 = ((bf16[16,264,128]{2,1,0:T(8,128)(2,1)}), bf16[16,264,128]{2,1,0:T(8,128)(2,1)S(1)}, u32[]{:S(2)}, u32[]{:S(2)}) async-start(bf16[16,264,128]{2,1,0:T(8,128)(2,1)} %shard_map.107), calls=%async_computation.1 | async-start | bytes 2162688 | tf_op jit(solution)/shard_map/all_to_all | solution.py:325
  34.1 15.5 %collective-permute-start = (bf16[768,256]{1,0:T(8,128)(2,1)S(1)}, bf16[768,256]{1,0:T(8,128)(2,1)S(1)}, u32[]{:S(2)}, u32[]{:S(2)}) collective-permute-start(bf16[768,256]{1,0:T(8,128)(2,1)S(1)} %get-tuple-element.14), channel_id=1, source_target_pairs={{0,2},{1,3},{2,0},{3,1},{4,6},{5,7},{6,4},{7,5},{8,10},{9,11},{10,... | collective-permute-start | bytes 1179656 | tf_op jit(solution)/shard_map/ppermute | solution.py:329
  39.0 16.8 %collective-permute-start.1 = (bf16[768,256]{1,0:T(8,128)(2,1)S(1)}, bf16[768,256]{1,0:T(8,128)(2,1)S(1)}, u32[]{:S(2)}, u32[]{:S(2)}) collective-permute-start(bf16[768,256]{1,0:T(8,128)(2,1)S(1)} %get-tuple-element.15), channel_id=1, source_target_pairs={{0,1},{1,2},{2,3},{3,0},{4,5},{5,6},{6,7},{7,4},{8,9},{9,10},{10,1... | collective-permute-start | bytes 1179656 | tf_op jit(solution)/shard_map/ppermute | solution.py:329
  41.6 14.4 %collective-permute-start.2 = (bf16[768,256]{1,0:T(8,128)(2,1)S(1)}, bf16[768,256]{1,0:T(8,128)(2,1)S(1)}, u32[]{:S(2)}, u32[]{:S(2)}) collective-permute-start(bf16[768,256]{1,0:T(8,128)(2,1)S(1)} %get-tuple-element.16), channel_id=1, source_target_pairs={{0,3},{1,0},{2,1},{3,2},{4,7},{5,4},{6,5},{7,6},{8,11},{9,8},{10,9... | collective-permute-start | bytes 1179656 | tf_op jit(solution)/shard_map/ppermute | solution.py:329
  49.6 8.3 %collective-permute-start.3 = (bf16[512,256]{1,0:T(8,128)(2,1)S(1)}, bf16[512,256]{1,0:T(8,128)(2,1)S(1)}, u32[]{:S(2)}, u32[]{:S(2)}) collective-permute-start(bf16[512,256]{1,0:T(8,128)(2,1)S(1)} %pad_maximum_fusion), channel_id=1, source_target_pairs={{0,4},{4,0},{1,5},{5,1},{2,6},{6,2},{3,7},{7,3},{8,12},{12,8},{9,1... | collective-permute-start | bytes 786440 | tf_op jit(solution)/shard_map/ppermute | solution.py:331
  56.0 27.2 %copy-start.3 = (bf16[256]{0:T(256)(128)(2,1)S(1)}, bf16[256]{0:T(256)(128)(2,1)}, u32[]{:S(2)}) copy-start(bf16[256]{0:T(256)(128)(2,1)} %param.11) | copy-start | bytes 1540
  56.0 3.4 %collective-permute-start.4 = (bf16[512,256]{1,0:T(8,128)(2,1)S(1)}, bf16[512,256]{1,0:T(8,128)(2,1)S(1)}, u32[]{:S(2)}, u32[]{:S(2)}) collective-permute-start(bf16[512,256]{1,0:T(8,128)(2,1)S(1)} %pad_maximum_fusion.1), channel_id=1, source_target_pairs={{0,4},{4,0},{1,5},{5,1},{2,6},{6,2},{3,7},{7,3},{8,12},{12,8},{9,1... | collective-permute-start | bytes 786440 | tf_op jit(solution)/shard_map/ppermute | solution.py:331
  62.1 3.1 %collective-permute-start.6 = (f32[24,128]{1,0:T(8,128)S(1)}, f32[24,128]{1,0:T(8,128)S(1)}, u32[]{:S(2)}, u32[]{:S(2)}) collective-permute-start(f32[24,128]{1,0:T(8,128)S(1)} %shard_map.108.mine), channel_id=1, source_target_pairs={{0,4},{4,0},{1,5},{5,1},{2,6},{6,2},{3,7},{7,3},{8,12},{12,8},{9,1... | collective-permute-start | bytes 36872 | tf_op jit(solution)/shard_map/ppermute | solution.py:340
  108.2 9.2 %collective-permute-start.7 = (f32[128,128]{1,0:T(8,128)S(1)}, f32[128,128]{1,0:T(8,128)S(1)}, u32[]{:S(2)}, u32[]{:S(2)}) collective-permute-start(f32[128,128]{1,0:T(8,128)S(1)} %shard_map.111), channel_id=1, source_target_pairs={{224,0},{225,1},{226,2},{227,3},{228,4},{229,5},{230,6},{231,7},{4... | collective-permute-start | bytes 196616 | tf_op jit(solution)/shard_map/ppermute | solution.py:359

commit v14 on v13

--- a/solution.py
+++ b/solution.py
@@ -50,7 +50,7 @@
     w_t[128:256, :] = wr[...].T
 
 
-def prepare_kernel(lengths, group_ids, states, head, routes, quarters, extra, slots):
+def prepare_kernel(lengths, group_ids, states, head, quarters, extra):
     sec = lax.axis_index("sec")
     for k in range(4):
         to = lax.rem(k - sec + 4, 4)
@@ -73,15 +73,6 @@
     for n in range(5):
         block = jnp.where(at == n, jnp.where(lane < 64, parts[0][n], parts[1][n]), block)
     extra[...] = block.astype(BF)
-    target = routes[...]
-    choose = (lax.broadcasted_iota(jnp.int32, (16, 256), 0) == target).astype(F32)
-    before = (
-        lax.broadcasted_iota(jnp.int32, (256, 256), 0)
-        < lax.broadcasted_iota(jnp.int32, (256, 256), 1)
-    ).astype(F32)
-    ranked = jnp.dot(choose.astype(BF), before.astype(BF), preferred_element_type=F32)
-    rank = jnp.sum(choose * ranked, axis=0, keepdims=True)
-    slots[...] = target * SLOT + rank.astype(jnp.int32)
 
 
 def pack_kernel(quarters, dirs, *outs):
@@ -150,7 +141,7 @@
         out[d] = whole
 
 
-def grads_kernel(pays, s0, s1, s2, s3, o0, o1, old_logp, slots, out, change, coefs):
+def grads_kernel(pays, s0, s1, s2, s3, o0, o1, old_logp, routes, out, change, coefs):
     shares = (s0, s1, s2, s3)
     zh, core, sec = (lax.axis_index(name) for name in ("zh", "core", "sec"))
     dp = dp_index()
@@ -224,7 +215,16 @@
     )
     hi, mid, lo = split3(logp)
     rows = jnp.concatenate([hi, mid, lo, jnp.zeros((5, 256), F32)], axis=0).astype(BF)
-    place = (lax.broadcasted_iota(jnp.int32, (16 * SLOT, 256), 0) == slots[...]).astype(F32)
+    target = routes[...]
+    choose = (lax.broadcasted_iota(jnp.int32, (16, 256), 0) == target).astype(F32)
+    before = (
+        lax.broadcasted_iota(jnp.int32, (256, 256), 0)
+        < lax.broadcasted_iota(jnp.int32, (256, 256), 1)
+    ).astype(F32)
+    ranked = jnp.dot(choose.astype(BF), before.astype(BF), preferred_element_type=F32)
+    rank = jnp.sum(choose * ranked, axis=0, keepdims=True)
+    slots = target * SLOT + rank.astype(jnp.int32)
+    place = (lax.broadcasted_iota(jnp.int32, (16 * SLOT, 256), 0) == slots).astype(F32)
     placed = lax.dot_general(rows, place.astype(BF), NT, preferred_element_type=F32)
     for a in range(4):
         tail = placed[:, 128 * a : 128 * (a + 1)].astype(BF)
@@ -303,14 +303,14 @@
         vmem_mib=60,
     )(direction, policy_k, reference_k)
     w_here = lax.ppermute(w_t, ALL, TO_HANDLER)
-    quarters, extra, slots = call(
+    quarters, extra = call(
         prepare_kernel,
-        (shape((4, 256, 256), BF), shape((8, 128), BF), shape((1, 256), jnp.int32)),
+        (shape((4, 256, 256), BF), shape((8, 128), BF)),
         smem=2,
-        inputs=3,
+        inputs=2,
         flops=8 * 256 * 1024 * 2,
         size=1 << 20,
-    )(lengths, group_ids, states, reward_head.reshape(8, 128), routes.reshape(1, 256))
+    )(lengths, group_ids, states, reward_head.reshape(8, 128))
     dirs = lax.all_to_all(dir_t, "zh", 0, 0, tiled=True)
     anywhere = pl.BlockSpec(memory_space=pl.ANY)
     weights = pl.pallas_call(
@@ -350,7 +350,7 @@
         inputs=9,
         flops=1 << 29,
         size=4 << 20,
-    )(pays, *shares, *others, old_logp.reshape(2, 128), slots)
+    )(pays, *shares, *others, old_logp.reshape(2, 128), routes.reshape(1, 256))
     parts = lax.all_to_all(parts, DP, 0, 0, tiled=True)
     grad = call(
         finish_kernel, shape((128, 128), F32), inputs=1, flops=1 << 20, size=1 << 20

time: 119 us -> 119 us (level)
  no operation moved by 1% of the time
where the time goes in v14:
time: 119 us; the launch traced here: 118 us
  starting transfers between devices  46.3 us (39%)
  blocking collectives  41.8 us (35%)
  waiting for transfers between devices  18 us (15%)
  Pallas kernels  7.5 us (6%)
  local copies, waits for them, and re-layouts  3.71 us (3%)
    all_to_all x1, blocking collectives, body(): parts = lax.all_to_all(parts, DP, 0, 0, tiled=True)  23.8 us
    all_to_all x1, blocking collectives, body(): pays = lax.all_to_all(pays, ('zh', 'sec'), 0, 0, tiled=True)  18 us
    ppermute x3, starting transfers between devices, body(): lax.ppermute(packs[n], 'sec', ring(STEPS[n]))  12 us
    all_to_all x1, starting transfers between devices, body(): dirs = lax.all_to_all(dir_t, 'zh', 0, 0, tiled=True)  10.3 us
    all_to_all x1, starting transfers between devices, body(): weights = lax.all_to_all(weights, DP, 0, 0, tiled=True)  8.73 us
    ppermute x3, waiting for transfers between devices, body(): lax.ppermute(packs[n], 'sec', ring(STEPS[n]))  7.81 us
    ppermute x1, starting transfers between devices, body(): w_here = lax.ppermute(w_t, ALL, TO_HANDLER)  6.04 us
    ppermute x1, waiting for transfers between devices, body(): return (lax.ppermute(grad, ALL, TO_OWNER), packed.reshape(1, 1, 320))  4.81 us
  transfers between devices with their start and end apart: 10, of which 8 were waited for; matrix products, arithmetic and copies ran while one was open for 0% of the time, Pallas kernels for 3%

profile of v14, /device:TPU:8, one launch (start us, length us, event | category | flops | bytes accessed | tf_op | source)
XLA Modules:
  0.0 118.2 jit_solution(17646435564298859796)
XLA Ops:
  0.6 1.7 %shard_map.105 = (bf16[4,128,256]{2,1,0:T(8,128)(2,1)}, bf16[256,128]{1,0:T(8,128)(2,1)}) custom-call(bf16[256,128]{1,0:T(8,128)(2,1)} %direction.1, bf16[128,128]{1,0:T(8,128)(2,1)} %wp.1, bf16[128,128]{1,0:T(8,128)(2,1)} %wr.1), custom_call_target="tpu_custom_call" | custom-call | flops 65536 | bytes 262144 | tf_op jit(solution)/shard_map/pallas_call | solution.py:297
  2.3 10.3 %all-to-all-start = ((bf16[4,128,256]{2,1,0:T(8,128)(2,1)}), bf16[4,128,256]{2,1,0:T(8,128)(2,1)S(1)}, u32[]{:S(2)}, u32[]{:S(2)}) async-start(bf16[4,128,256]{2,1,0:T(8,128)(2,1)} %get-tuple-element.11), calls=%async_computation | async-start | bytes 524288 | tf_op jit(solution)/shard_map/all_to_all | solution.py:314
  12.6 6.0 %collective-permute-start.5 = (bf16[256,128]{1,0:T(8,128)(2,1)}, bf16[256,128]{1,0:T(8,128)(2,1)S(1)}, u32[]{:S(2)}, u32[]{:S(2)}) collective-permute-start(bf16[256,128]{1,0:T(8,128)(2,1)} %get-tuple-element.16), channel_id=1, source_target_pairs={{0,224},{1,225},{2,226},{3,227},{4,228},{5,229},{6,230},{7,231},{8... | collective-permute-start | bytes 196616 | tf_op jit(solution)/shard_map/ppermute | solution.py:305
  18.6 0.0 copy-start
  18.6 1.0 copy-done
  19.7 0.0 copy-start.1
  19.7 0.7 copy-done.1
  20.4 0.0 copy-start.4
  20.4 0.7 copy-done.4
  21.0 0.0 copy-start.5
  21.0 0.7 copy-done.5
  21.7 1.0 shard_map.104
  22.6 1.5 %collective-permute-done.5.w = bf16[256,128]{1,0:T(8,128)(2,1)S(1)} collective-permute-done((bf16[256,128]{1,0:T(8,128)(2,1)}, bf16[256,128]{1,0:T(8,128)(2,1)S(1)}, u32[]{:S(2)}, u32[]{:S(2)}) %collective-permute-start.5) | collective-permute-done | bytes 65568 | tf_op jit(solution)/shard_map/ppermute | solution.py:305
  24.1 1.2 shard_map.107
  25.3 0.0 all-to-all-done.dirs
  25.3 8.7 %all-to-all-start.1 = ((bf16[16,264,128]{2,1,0:T(8,128)(2,1)}), bf16[16,264,128]{2,1,0:T(8,128)(2,1)S(1)}, u32[]{:S(2)}, u32[]{:S(2)}) async-start(bf16[16,264,128]{2,1,0:T(8,128)(2,1)} %shard_map.107), calls=%async_computation.1 | async-start | bytes 2162688 | tf_op jit(solution)/shard_map/all_to_all | solution.py:325
  34.0 0.1 shard_map.106
  34.1 4.9 %collective-permute-start = (bf16[768,256]{1,0:T(8,128)(2,1)S(1)}, bf16[768,256]{1,0:T(8,128)(2,1)S(1)}, u32[]{:S(2)}, u32[]{:S(2)}) collective-permute-start(bf16[768,256]{1,0:T(8,128)(2,1)S(1)} %get-tuple-element.13), channel_id=1, source_target_pairs={{0,2},{1,3},{2,0},{3,1},{4,6},{5,7},{6,4},{7,5},{8,10},{9,11},{10,... | collective-permute-start | bytes 1179656 | tf_op jit(solution)/shard_map/ppermute | solution.py:329
  39.0 2.5 %collective-permute-start.1 = (bf16[768,256]{1,0:T(8,128)(2,1)S(1)}, bf16[768,256]{1,0:T(8,128)(2,1)S(1)}, u32[]{:S(2)}, u32[]{:S(2)}) collective-permute-start(bf16[768,256]{1,0:T(8,128)(2,1)S(1)} %get-tuple-element.14), channel_id=1, source_target_pairs={{0,1},{1,2},{2,3},{3,0},{4,5},{5,6},{6,7},{7,4},{8,9},{9,10},{10,1... | collective-permute-start | bytes 1179656 | tf_op jit(solution)/shard_map/ppermute | solution.py:329
  41.6 4.6 %collective-permute-start.2 = (bf16[768,256]{1,0:T(8,128)(2,1)S(1)}, bf16[768,256]{1,0:T(8,128)(2,1)S(1)}, u32[]{:S(2)}, u32[]{:S(2)}) collective-permute-start(bf16[768,256]{1,0:T(8,128)(2,1)S(1)} %get-tuple-element.15), channel_id=1, source_target_pairs={{0,3},{1,0},{2,1},{3,2},{4,7},{5,4},{6,5},{7,6},{8,11},{9,8},{10,9... | collective-permute-start | bytes 1179656 | tf_op jit(solution)/shard_map/ppermute | solution.py:329
  46.1 3.5 %collective-permute-done.s1 = bf16[768,256]{1,0:T(8,128)(2,1)S(1)} collective-permute-done((bf16[768,256]{1,0:T(8,128)(2,1)S(1)}, bf16[768,256]{1,0:T(8,128)(2,1)S(1)}, u32[]{:S(2)}, u32[]{:S(2)}) %collective-permute-start) | collective-permute-done | bytes 393248 | tf_op jit(solution)/shard_map/ppermute | solution.py:329
  49.6 1.9 %collective-permute-start.3 = (bf16[512,256]{1,0:T(8,128)(2,1)S(1)}, bf16[512,256]{1,0:T(8,128)(2,1)S(1)}, u32[]{:S(2)}, u32[]{:S(2)}) collective-permute-start(bf16[512,256]{1,0:T(8,128)(2,1)S(1)} %pad_maximum_fusion), channel_id=1, source_target_pairs={{0,4},{4,0},{1,5},{5,1},{2,6},{6,2},{3,7},{7,3},{8,12},{12,8},{9,1... | collective-permute-start | bytes 786440 | tf_op jit(solution)/shard_map/ppermute | solution.py:331
  51.6 4.3 %collective-permute-done.1.s2 = bf16[768,256]{1,0:T(8,128)(2,1)S(1)} collective-permute-done((bf16[768,256]{1,0:T(8,128)(2,1)S(1)}, bf16[768,256]{1,0:T(8,128)(2,1)S(1)}, u32[]{:S(2)}, u32[]{:S(2)}) %collective-permute-start.1) | collective-permute-done | bytes 393248 | tf_op jit(solution)/shard_map/ppermute | solution.py:329
  55.9 0.1 collective-permute-done.2.s3
  56.0 0.0 copy-start.2
  56.0 0.0 copy-start.3
  56.0 1.9 %collective-permute-start.4 = (bf16[512,256]{1,0:T(8,128)(2,1)S(1)}, bf16[512,256]{1,0:T(8,128)(2,1)S(1)}, u32[]{:S(2)}, u32[]{:S(2)}) collective-permute-start(bf16[512,256]{1,0:T(8,128)(2,1)S(1)} %pad_maximum_fusion.1), channel_id=1, source_target_pairs={{0,4},{4,0},{1,5},{5,1},{2,6},{6,2},{3,7},{7,3},{8,12},{12,8},{9,1... | collective-permute-start | bytes 786440 | tf_op jit(solution)/shard_map/ppermute | solution.py:331
  57.9 0.0 collective-permute-done.3.o0
  57.9 1.5 %collective-permute-done.4.o1 = bf16[512,256]{1,0:T(8,128)(2,1)S(1)} collective-permute-done((bf16[512,256]{1,0:T(8,128)(2,1)S(1)}, bf16[512,256]{1,0:T(8,128)(2,1)S(1)}, u32[]{:S(2)}, u32[]{:S(2)}) %collective-permute-start.4) | collective-permute-done | bytes 262176 | tf_op jit(solution)/shard_map/ppermute | solution.py:331
  59.4 1.3 %all-to-all-done.1.weights = bf16[16,264,128]{2,1,0:T(8,128)(2,1)S(1)} async-done(((bf16[16,264,128]{2,1,0:T(8,128)(2,1)}), bf16[16,264,128]{2,1,0:T(8,128)(2,1)S(1)}, u32[]{:S(2)}, u32[]{:S(2)}) %all-to-all-start.1) | async-done | bytes 1081376 | tf_op jit(solution)/shard_map/all_to_all | solution.py:325
  60.7 1.4 %shard_map.108.mine = f32[24,128]{1,0:T(8,128)S(1)} custom-call(bf16[768,256]{1,0:T(8,128)(2,1)S(1)} %get-tuple-element.12.s0, bf16[768,256]{1,0:T(8,128)(2,1)S(1)} %collective-permute-done.s1, bf16[768,256]{1,0:T(8,128)(2,1)S(1)} %collective-permute-done.1.s2, bf16[768,256]{1,0:T(8,128)(2,1)S(1)} %collective-permute-done.2.s3, ...), custom_call_target="tpu_custom_call" | custom-call | flops 1073741824 | bytes 4194304 | tf_op jit(solution)/shard_map/pallas_call | solution.py:336
  62.1 1.9 %collective-permute-start.6 = (f32[24,128]{1,0:T(8,128)S(1)}, f32[24,128]{1,0:T(8,128)S(1)}, u32[]{:S(2)}, u32[]{:S(2)}) collective-permute-start(f32[24,128]{1,0:T(8,128)S(1)} %shard_map.108.mine), channel_id=1, source_target_pairs={{0,4},{4,0},{1,5},{5,1},{2,6},{6,2},{3,7},{7,3},{8,12},{12,8},{9,1... | collective-permute-start | bytes 36872 | tf_op jit(solution)/shard_map/ppermute | solution.py:340
  64.0 1.1 collective-permute-done.6.partner
  65.1 18.0 %all_to_all.20.pays = f32[16,24,128]{2,1,0:T(8,128)S(1)} all-to-all(f32[16,24,128]{2,1,0:T(8,128)S(1)} %shard_map.109), channel_id=1, replica_groups=mesh['zl'=2,'y'=8,'zh'=4,'core'=2,'sec'=4] {'zh','sec'}, dimensions={0} | all-to-all | bytes 393216 | tf_op jit(solution)/shard_map/all_to_all | solution.py:342
  83.2 0.0 copy-done.2
  83.2 0.0 copy-done.3
  83.2 1.3 %shard_map.110 = bf16[16,136,128]{2,1,0:T(8,128)(2,1)S(1)} custom-call(f32[16,24,128]{2,1,0:T(8,128)S(1)} %all_to_all.20.pays, bf16[768,256]{1,0:T(8,128)(2,1)S(1)} %get-tuple-element.12.s0, bf16[768,256]{1,0:T(8,128)(2,1)S(1)} %collective-permute-done.s1, bf16[768,256]{1,0:T(8,128)(2,1)S(1)} %collective-permute-done.1.s2, ...), custom_call_target="tpu_custom_call" | custom-call | flops 536870912 | bytes 4194304 | tf_op jit(solution)/shard_map/pallas_call | solution.py:343
  84.4 23.8 %all_to_all.21.parts = bf16[16,136,128]{2,1,0:T(8,128)(2,1)S(1)} all-to-all(bf16[16,136,128]{2,1,0:T(8,128)(2,1)S(1)} %shard_map.110), channel_id=1, replica_groups=mesh['zl'=2,'y'=8,'zh'=4,'core'=2,'sec'=4] {'zl','y'}, dimensions={0} | all-to-all | bytes 1114112 | tf_op jit(solution)/shard_map/all_to_all | solution.py:354
  108.3 0.1 shard_map.111
  108.4 3.5 %collective-permute-start.7 = (f32[128,128]{1,0:T(8,128)S(1)}, f32[128,128]{1,0:T(8,128)S(1)}, u32[]{:S(2)}, u32[]{:S(2)}) collective-permute-start(f32[128,128]{1,0:T(8,128)S(1)} %shard_map.111), channel_id=1, source_target_pairs={{224,0},{225,1},{226,2},{227,3},{228,4},{229,5},{230,6},{231,7},{4... | collective-permute-start | bytes 196616 | tf_op jit(solution)/shard_map/ppermute | solution.py:359
  111.9 0.9 shard_map.112
  112.8 4.8 %collective-permute-done.7 = f32[128,128]{1,0:T(8,128)S(1)} collective-permute-done((f32[128,128]{1,0:T(8,128)S(1)}, f32[128,128]{1,0:T(8,128)S(1)}, u32[]{:S(2)}, u32[]{:S(2)}) %collective-permute-start.7) | collective-permute-done | bytes 65568 | tf_op jit(solution)/shard_map/ppermute | solution.py:359
  117.6 0.6 copy.12
  (7 shorter events, 0.1 us)
Async XLA Ops:
  2.3 23.0 %all-to-all-start = ((bf16[4,128,256]{2,1,0:T(8,128)(2,1)}), bf16[4,128,256]{2,1,0:T(8,128)(2,1)S(1)}, u32[]{:S(2)}, u32[]{:S(2)}) async-start(bf16[4,128,256]{2,1,0:T(8,128)(2,1)} %get-tuple-element.11), calls=%async_computation | async-start | bytes 524288 | tf_op jit(solution)/shard_map/all_to_all | solution.py:314
  12.6 11.5 %collective-permute-start.5 = (bf16[256,128]{1,0:T(8,128)(2,1)}, bf16[256,128]{1,0:T(8,128)(2,1)S(1)}, u32[]{:S(2)}, u32[]{:S(2)}) collective-permute-start(bf16[256,128]{1,0:T(8,128)(2,1)} %get-tuple-element.16), channel_id=1, source_target_pairs={{0,224},{1,225},{2,226},{3,227},{4,228},{5,229},{6,230},{7,231},{8... | collective-permute-start | bytes 196616 | tf_op jit(solution)/shard_map/ppermute | solution.py:305
  18.6 1.0 copy-start
  19.7 0.7 copy-start.1
  20.4 0.7 copy-start.4
  21.0 0.7 copy-start.5
  25.3 35.4 %all-to-all-start.1 = ((bf16[16,264,128]{2,1,0:T(8,128)(2,1)}), bf16[16,264,128]{2,1,0:T(8,128)(2,1)S(1)}, u32[]{:S(2)}, u32[]{:S(2)}) async-start(bf16[16,264,128]{2,1,0:T(8,128)(2,1)} %shard_map.107), calls=%async_computation.1 | async-start | bytes 2162688 | tf_op jit(solution)/shard_map/all_to_all | solution.py:325
  34.1 15.5 %collective-permute-start = (bf16[768,256]{1,0:T(8,128)(2,1)S(1)}, bf16[768,256]{1,0:T(8,128)(2,1)S(1)}, u32[]{:S(2)}, u32[]{:S(2)}) collective-permute-start(bf16[768,256]{1,0:T(8,128)(2,1)S(1)} %get-tuple-element.13), channel_id=1, source_target_pairs={{0,2},{1,3},{2,0},{3,1},{4,6},{5,7},{6,4},{7,5},{8,10},{9,11},{10,... | collective-permute-start | bytes 1179656 | tf_op jit(solution)/shard_map/ppermute | solution.py:329
  39.0 16.8 %collective-permute-start.1 = (bf16[768,256]{1,0:T(8,128)(2,1)S(1)}, bf16[768,256]{1,0:T(8,128)(2,1)S(1)}, u32[]{:S(2)}, u32[]{:S(2)}) collective-permute-start(bf16[768,256]{1,0:T(8,128)(2,1)S(1)} %get-tuple-element.14), channel_id=1, source_target_pairs={{0,1},{1,2},{2,3},{3,0},{4,5},{5,6},{6,7},{7,4},{8,9},{9,10},{10,1... | collective-permute-start | bytes 1179656 | tf_op jit(solution)/shard_map/ppermute | solution.py:329
  41.6 14.4 %collective-permute-start.2 = (bf16[768,256]{1,0:T(8,128)(2,1)S(1)}, bf16[768,256]{1,0:T(8,128)(2,1)S(1)}, u32[]{:S(2)}, u32[]{:S(2)}) collective-permute-start(bf16[768,256]{1,0:T(8,128)(2,1)S(1)} %get-tuple-element.15), channel_id=1, source_target_pairs={{0,3},{1,0},{2,1},{3,2},{4,7},{5,4},{6,5},{7,6},{8,11},{9,8},{10,9... | collective-permute-start | bytes 1179656 | tf_op jit(solution)/shard_map/ppermute | solution.py:329
  49.6 8.3 %collective-permute-start.3 = (bf16[512,256]{1,0:T(8,128)(2,1)S(1)}, bf16[512,256]{1,0:T(8,128)(2,1)S(1)}, u32[]{:S(2)}, u32[]{:S(2)}) collective-permute-start(bf16[512,256]{1,0:T(8,128)(2,1)S(1)} %pad_maximum_fusion), channel_id=1, source_target_pairs={{0,4},{4,0},{1,5},{5,1},{2,6},{6,2},{3,7},{7,3},{8,12},{12,8},{9,1... | collective-permute-start | bytes 786440 | tf_op jit(solution)/shard_map/ppermute | solution.py:331
  56.0 27.2 %copy-start.2 = (s32[256,1]{0,1:T(1,128)S(1)}, s32[256,1]{0,1:T(1,128)}, u32[]{:S(2)}) copy-start(s32[256,1]{0,1:T(1,128)} %param.14) | copy-start | bytes 3076
  56.0 27.2 %copy-start.3 = (bf16[256]{0:T(256)(128)(2,1)S(1)}, bf16[256]{0:T(256)(128)(2,1)}, u32[]{:S(2)}) copy-start(bf16[256]{0:T(256)(128)(2,1)} %param.11) | copy-start | bytes 1540
  56.0 3.4 %collective-permute-start.4 = (bf16[512,256]{1,0:T(8,128)(2,1)S(1)}, bf16[512,256]{1,0:T(8,128)(2,1)S(1)}, u32[]{:S(2)}, u32[]{:S(2)}) collective-permute-start(bf16[512,256]{1,0:T(8,128)(2,1)S(1)} %pad_maximum_fusion.1), channel_id=1, source_target_pairs={{0,4},{4,0},{1,5},{5,1},{2,6},{6,2},{3,7},{7,3},{8,12},{12,8},{9,1... | collective-permute-start | bytes 786440 | tf_op jit(solution)/shard_map/ppermute | solution.py:331
  62.1 3.1 %collective-permute-start.6 = (f32[24,128]{1,0:T(8,128)S(1)}, f32[24,128]{1,0:T(8,128)S(1)}, u32[]{:S(2)}, u32[]{:S(2)}) collective-permute-start(f32[24,128]{1,0:T(8,128)S(1)} %shard_map.108.mine), channel_id=1, source_target_pairs={{0,4},{4,0},{1,5},{5,1},{2,6},{6,2},{3,7},{7,3},{8,12},{12,8},{9,1... | collective-permute-start | bytes 36872 | tf_op jit(solution)/shard_map/ppermute | solution.py:340
  108.4 9.2 %collective-permute-start.7 = (f32[128,128]{1,0:T(8,128)S(1)}, f32[128,128]{1,0:T(8,128)S(1)}, u32[]{:S(2)}, u32[]{:S(2)}) collective-permute-start(f32[128,128]{1,0:T(8,128)S(1)} %shard_map.111), channel_id=1, source_target_pairs={{224,0},{225,1},{226,2},{227,3},{228,4},{229,5},{230,6},{231,7},{4... | collective-permute-start | bytes 196616 | tf_op jit(solution)/shard_map/ppermute | solution.py:359

commit v15 on v13

--- a/solution.py
+++ b/solution.py
@@ -11,7 +11,7 @@
 CAP = 20
 SLOT = 32
 
-STEPS = (0, 2, 1, 3)
+STEPS = (0, 2, 3, 1)
 
 kl_weight = 0.4
 var_offset = 0.25

time: 119 us -> 118 us (level)
  waiting for transfers between devices: 17.3 us -> 18.5 us
  starting transfers between devices: 46.3 us -> 45.1 us
    ppermute x3, waiting for transfers between devices: 7.81 us -> 9.36 us  [body(): lax.ppermute(packs[n], 'sec', ring(STEPS[n]))]
    ppermute x3, starting transfers between devices: 12 us -> 10.8 us  [body(): lax.ppermute(packs[n], 'sec', ring(STEPS[n]))]
where the time goes in v15:
time: 118 us
  starting transfers between devices  45.1 us (38%)
  blocking collectives  41.5 us (35%)
  waiting for transfers between devices  18.5 us (16%)
  Pallas kernels  7.35 us (6%)
  local copies, waits for them, and re-layouts  4.38 us (4%)
    all_to_all x1, blocking collectives, body(): parts = lax.all_to_all(parts, DP, 0, 0, tiled=True)  23.5 us
    all_to_all x1, blocking collectives, body(): pays = lax.all_to_all(pays, ('zh', 'sec'), 0, 0, tiled=True)  18 us
    ppermute x3, starting transfers between devices, body(): lax.ppermute(packs[n], 'sec', ring(STEPS[n]))  10.8 us
    all_to_all x1, starting transfers between devices, body(): dirs = lax.all_to_all(dir_t, 'zh', 0, 0, tiled=True)  10.3 us
    ppermute x3, waiting for transfers between devices, body(): lax.ppermute(packs[n], 'sec', ring(STEPS[n]))  9.36 us
    all_to_all x1, starting transfers between devices, body(): weights = lax.all_to_all(weights, DP, 0, 0, tiled=True)  8.73 us
    ppermute x1, starting transfers between devices, body(): w_here = lax.ppermute(w_t, ALL, TO_HANDLER)  6.04 us
    ppermute x1, waiting for transfers between devices, body(): return (lax.ppermute(grad, ALL, TO_OWNER), packed.reshape(1, 1, 320))  4.81 us
  transfers between devices with their start and end apart: 10, of which 8 were waited for; matrix products, arithmetic and copies ran while one was open for 0% of the time, Pallas kernels for 3%

profile of v15, /device:TPU:8, one launch (start us, length us, event | category | flops | bytes accessed | tf_op | source)
XLA Modules:
  0.0 117.7 jit_solution(4891713887080847251)
XLA Ops:
  0.6 1.7 %shard_map.105 = (bf16[4,128,256]{2,1,0:T(8,128)(2,1)}, bf16[256,128]{1,0:T(8,128)(2,1)}) custom-call(bf16[256,128]{1,0:T(8,128)(2,1)} %direction.1, bf16[128,128]{1,0:T(8,128)(2,1)} %wp.1, bf16[128,128]{1,0:T(8,128)(2,1)} %wr.1), custom_call_target="tpu_custom_call" | custom-call | flops 65536 | bytes 262144 | tf_op jit(solution)/shard_map/pallas_call | solution.py:297
  2.3 10.3 %all-to-all-start = ((bf16[4,128,256]{2,1,0:T(8,128)(2,1)}), bf16[4,128,256]{2,1,0:T(8,128)(2,1)S(1)}, u32[]{:S(2)}, u32[]{:S(2)}) async-start(bf16[4,128,256]{2,1,0:T(8,128)(2,1)} %get-tuple-element.12), calls=%async_computation | async-start | bytes 524288 | tf_op jit(solution)/shard_map/all_to_all | solution.py:314
  12.6 6.0 %collective-permute-start.5 = (bf16[256,128]{1,0:T(8,128)(2,1)}, bf16[256,128]{1,0:T(8,128)(2,1)S(1)}, u32[]{:S(2)}, u32[]{:S(2)}) collective-permute-start(bf16[256,128]{1,0:T(8,128)(2,1)} %get-tuple-element.17), channel_id=1, source_target_pairs={{0,224},{1,225},{2,226},{3,227},{4,228},{5,229},{6,230},{7,231},{8... | collective-permute-start | bytes 196616 | tf_op jit(solution)/shard_map/ppermute | solution.py:305
  18.6 0.0 copy-start
  18.6 1.0 copy-done
  19.7 0.0 copy-start.1
  19.7 0.7 copy-done.1
  20.4 0.0 copy-start.2
  20.4 0.7 copy-done.2
  21.0 0.0 copy-start.4
  21.0 0.7 copy-done.4
  21.7 0.0 copy-start.5
  21.7 0.7 copy-done.5
  22.3 1.0 shard_map.104
  23.3 0.8 collective-permute-done.5.w
  24.1 1.2 shard_map.107
  25.3 0.0 all-to-all-done.dirs
  25.3 8.7 %all-to-all-start.1 = ((bf16[16,264,128]{2,1,0:T(8,128)(2,1)}), bf16[16,264,128]{2,1,0:T(8,128)(2,1)S(1)}, u32[]{:S(2)}, u32[]{:S(2)}) async-start(bf16[16,264,128]{2,1,0:T(8,128)(2,1)} %shard_map.107), calls=%async_computation.1 | async-start | bytes 2162688 | tf_op jit(solution)/shard_map/all_to_all | solution.py:325
  34.0 0.1 shard_map.106
  34.1 4.9 %collective-permute-start = (bf16[768,256]{1,0:T(8,128)(2,1)S(1)}, bf16[768,256]{1,0:T(8,128)(2,1)S(1)}, u32[]{:S(2)}, u32[]{:S(2)}) collective-permute-start(bf16[768,256]{1,0:T(8,128)(2,1)S(1)} %get-tuple-element.14), channel_id=1, source_target_pairs={{0,2},{1,3},{2,0},{3,1},{4,6},{5,7},{6,4},{7,5},{8,10},{9,11},{10,... | collective-permute-start | bytes 1179656 | tf_op jit(solution)/shard_map/ppermute | solution.py:329
  39.0 3.0 %collective-permute-start.1 = (bf16[768,256]{1,0:T(8,128)(2,1)S(1)}, bf16[768,256]{1,0:T(8,128)(2,1)S(1)}, u32[]{:S(2)}, u32[]{:S(2)}) collective-permute-start(bf16[768,256]{1,0:T(8,128)(2,1)S(1)} %get-tuple-element.15), channel_id=1, source_target_pairs={{0,3},{1,0},{2,1},{3,2},{4,7},{5,4},{6,5},{7,6},{8,11},{9,8},{10,9... | collective-permute-start | bytes 1179656 | tf_op jit(solution)/shard_map/ppermute | solution.py:329
  42.1 2.8 %collective-permute-start.2 = (bf16[768,256]{1,0:T(8,128)(2,1)S(1)}, bf16[768,256]{1,0:T(8,128)(2,1)S(1)}, u32[]{:S(2)}, u32[]{:S(2)}) collective-permute-start(bf16[768,256]{1,0:T(8,128)(2,1)S(1)} %get-tuple-element.16), channel_id=1, source_target_pairs={{0,1},{1,2},{2,3},{3,0},{4,5},{5,6},{6,7},{7,4},{8,9},{9,10},{10,1... | collective-permute-start | bytes 1179656 | tf_op jit(solution)/shard_map/ppermute | solution.py:329
  44.9 4.6 %collective-permute-done.s1 = bf16[768,256]{1,0:T(8,128)(2,1)S(1)} collective-permute-done((bf16[768,256]{1,0:T(8,128)(2,1)S(1)}, bf16[768,256]{1,0:T(8,128)(2,1)S(1)}, u32[]{:S(2)}, u32[]{:S(2)}) %collective-permute-start) | collective-permute-done | bytes 393248 | tf_op jit(solution)/shard_map/ppermute | solution.py:329
  49.6 1.9 %collective-permute-start.3 = (bf16[512,256]{1,0:T(8,128)(2,1)S(1)}, bf16[512,256]{1,0:T(8,128)(2,1)S(1)}, u32[]{:S(2)}, u32[]{:S(2)}) collective-permute-start(bf16[512,256]{1,0:T(8,128)(2,1)S(1)} %pad_maximum_fusion), channel_id=1, source_target_pairs={{0,4},{4,0},{1,5},{5,1},{2,6},{6,2},{3,7},{7,3},{8,12},{12,8},{9,1... | collective-permute-start | bytes 786440 | tf_op jit(solution)/shard_map/ppermute | solution.py:331
  51.5 4.4 %collective-permute-done.1.s2 = bf16[768,256]{1,0:T(8,128)(2,1)S(1)} collective-permute-done((bf16[768,256]{1,0:T(8,128)(2,1)S(1)}, bf16[768,256]{1,0:T(8,128)(2,1)S(1)}, u32[]{:S(2)}, u32[]{:S(2)}) %collective-permute-start.1) | collective-permute-done | bytes 393248 | tf_op jit(solution)/shard_map/ppermute | solution.py:329
  56.0 0.3 collective-permute-done.2.s3
  56.3 0.0 copy-start.3
  56.3 1.9 %collective-permute-start.4 = (bf16[512,256]{1,0:T(8,128)(2,1)S(1)}, bf16[512,256]{1,0:T(8,128)(2,1)S(1)}, u32[]{:S(2)}, u32[]{:S(2)}) collective-permute-start(bf16[512,256]{1,0:T(8,128)(2,1)S(1)} %pad_maximum_fusion.1), channel_id=1, source_target_pairs={{0,4},{4,0},{1,5},{5,1},{2,6},{6,2},{3,7},{7,3},{8,12},{12,8},{9,1... | collective-permute-start | bytes 786440 | tf_op jit(solution)/shard_map/ppermute | solution.py:331
  58.3 0.0 collective-permute-done.3.o0
  58.3 1.5 %collective-permute-done.4.o1 = bf16[512,256]{1,0:T(8,128)(2,1)S(1)} collective-permute-done((bf16[512,256]{1,0:T(8,128)(2,1)S(1)}, bf16[512,256]{1,0:T(8,128)(2,1)S(1)}, u32[]{:S(2)}, u32[]{:S(2)}) %collective-permute-start.4) | collective-permute-done | bytes 262176 | tf_op jit(solution)/shard_map/ppermute | solution.py:331
  59.8 0.9 all-to-all-done.1.weights
  60.7 1.4 %shard_map.108.mine = f32[24,128]{1,0:T(8,128)S(1)} custom-call(bf16[768,256]{1,0:T(8,128)(2,1)S(1)} %get-tuple-element.13.s0, bf16[768,256]{1,0:T(8,128)(2,1)S(1)} %collective-permute-done.s1, bf16[768,256]{1,0:T(8,128)(2,1)S(1)} %collective-permute-done.1.s2, bf16[768,256]{1,0:T(8,128)(2,1)S(1)} %collective-permute-done.2.s3, ...), custom_call_target="tpu_custom_call" | custom-call | flops 1073741824 | bytes 4194304 | tf_op jit(solution)/shard_map/pallas_call | solution.py:336
  62.1 1.9 %collective-permute-start.6 = (f32[24,128]{1,0:T(8,128)S(1)}, f32[24,128]{1,0:T(8,128)S(1)}, u32[]{:S(2)}, u32[]{:S(2)}) collective-permute-start(f32[24,128]{1,0:T(8,128)S(1)} %shard_map.108.mine), channel_id=1, source_target_pairs={{0,4},{4,0},{1,5},{5,1},{2,6},{6,2},{3,7},{7,3},{8,12},{12,8},{9,1... | collective-permute-start | bytes 36872 | tf_op jit(solution)/shard_map/ppermute | solution.py:340
  64.0 1.1 collective-permute-done.6.partner
  65.2 18.0 %all_to_all.20.pays = f32[16,24,128]{2,1,0:T(8,128)S(1)} all-to-all(f32[16,24,128]{2,1,0:T(8,128)S(1)} %shard_map.109), channel_id=1, replica_groups=mesh['zl'=2,'y'=8,'zh'=4,'core'=2,'sec'=4] {'zh','sec'}, dimensions={0} | all-to-all | bytes 393216 | tf_op jit(solution)/shard_map/all_to_all | solution.py:342
  83.2 0.0 copy-done.3
  83.2 1.1 shard_map.110
  84.3 23.5 %all_to_all.21.parts = bf16[16,136,128]{2,1,0:T(8,128)(2,1)S(1)} all-to-all(bf16[16,136,128]{2,1,0:T(8,128)(2,1)S(1)} %shard_map.110), channel_id=1, replica_groups=mesh['zl'=2,'y'=8,'zh'=4,'core'=2,'sec'=4] {'zl','y'}, dimensions={0} | all-to-all | bytes 1114112 | tf_op jit(solution)/shard_map/all_to_all | solution.py:354
  107.8 0.1 shard_map.111
  108.0 3.5 %collective-permute-start.7 = (f32[128,128]{1,0:T(8,128)S(1)}, f32[128,128]{1,0:T(8,128)S(1)}, u32[]{:S(2)}, u32[]{:S(2)}) collective-permute-start(f32[128,128]{1,0:T(8,128)S(1)} %shard_map.111), channel_id=1, source_target_pairs={{224,0},{225,1},{226,2},{227,3},{228,4},{229,5},{230,6},{231,7},{4... | collective-permute-start | bytes 196616 | tf_op jit(solution)/shard_map/ppermute | solution.py:359
  111.4 0.9 shard_map.112
  112.3 4.8 %collective-permute-done.7 = f32[128,128]{1,0:T(8,128)S(1)} collective-permute-done((f32[128,128]{1,0:T(8,128)S(1)}, f32[128,128]{1,0:T(8,128)S(1)}, u32[]{:S(2)}, u32[]{:S(2)}) %collective-permute-start.7) | collective-permute-done | bytes 65568 | tf_op jit(solution)/shard_map/ppermute | solution.py:359
  117.1 0.6 copy.12
  (7 shorter events, 0.1 us)
Async XLA Ops:
  2.3 23.0 %all-to-all-start = ((bf16[4,128,256]{2,1,0:T(8,128)(2,1)}), bf16[4,128,256]{2,1,0:T(8,128)(2,1)S(1)}, u32[]{:S(2)}, u32[]{:S(2)}) async-start(bf16[4,128,256]{2,1,0:T(8,128)(2,1)} %get-tuple-element.12), calls=%async_computation | async-start | bytes 524288 | tf_op jit(solution)/shard_map/all_to_all | solution.py:314
  12.6 11.5 %collective-permute-start.5 = (bf16[256,128]{1,0:T(8,128)(2,1)}, bf16[256,128]{1,0:T(8,128)(2,1)S(1)}, u32[]{:S(2)}, u32[]{:S(2)}) collective-permute-start(bf16[256,128]{1,0:T(8,128)(2,1)} %get-tuple-element.17), channel_id=1, source_target_pairs={{0,224},{1,225},{2,226},{3,227},{4,228},{5,229},{6,230},{7,231},{8... | collective-permute-start | bytes 196616 | tf_op jit(solution)/shard_map/ppermute | solution.py:305
  18.6 1.0 copy-start
  19.7 0.7 copy-start.1
  20.4 0.7 copy-start.2
  21.0 0.7 copy-start.4
  21.7 0.7 copy-start.5
  25.3 35.4 %all-to-all-start.1 = ((bf16[16,264,128]{2,1,0:T(8,128)(2,1)}), bf16[16,264,128]{2,1,0:T(8,128)(2,1)S(1)}, u32[]{:S(2)}, u32[]{:S(2)}) async-start(bf16[16,264,128]{2,1,0:T(8,128)(2,1)} %shard_map.107), calls=%async_computation.1 | async-start | bytes 2162688 | tf_op jit(solution)/shard_map/all_to_all | solution.py:325
  34.1 15.4 %collective-permute-start = (bf16[768,256]{1,0:T(8,128)(2,1)S(1)}, bf16[768,256]{1,0:T(8,128)(2,1)S(1)}, u32[]{:S(2)}, u32[]{:S(2)}) collective-permute-start(bf16[768,256]{1,0:T(8,128)(2,1)S(1)} %get-tuple-element.14), channel_id=1, source_target_pairs={{0,2},{1,3},{2,0},{3,1},{4,6},{5,7},{6,4},{7,5},{8,10},{9,11},{10,... | collective-permute-start | bytes 1179656 | tf_op jit(solution)/shard_map/ppermute | solution.py:329
  39.0 16.9 %collective-permute-start.1 = (bf16[768,256]{1,0:T(8,128)(2,1)S(1)}, bf16[768,256]{1,0:T(8,128)(2,1)S(1)}, u32[]{:S(2)}, u32[]{:S(2)}) collective-permute-start(bf16[768,256]{1,0:T(8,128)(2,1)S(1)} %get-tuple-element.15), channel_id=1, source_target_pairs={{0,3},{1,0},{2,1},{3,2},{4,7},{5,4},{6,5},{7,6},{8,11},{9,8},{10,9... | collective-permute-start | bytes 1179656 | tf_op jit(solution)/shard_map/ppermute | solution.py:329
  42.1 14.2 %collective-permute-start.2 = (bf16[768,256]{1,0:T(8,128)(2,1)S(1)}, bf16[768,256]{1,0:T(8,128)(2,1)S(1)}, u32[]{:S(2)}, u32[]{:S(2)}) collective-permute-start(bf16[768,256]{1,0:T(8,128)(2,1)S(1)} %get-tuple-element.16), channel_id=1, source_target_pairs={{0,1},{1,2},{2,3},{3,0},{4,5},{5,6},{6,7},{7,4},{8,9},{9,10},{10,1... | collective-permute-start | bytes 1179656 | tf_op jit(solution)/shard_map/ppermute | solution.py:329
  49.6 8.7 %collective-permute-start.3 = (bf16[512,256]{1,0:T(8,128)(2,1)S(1)}, bf16[512,256]{1,0:T(8,128)(2,1)S(1)}, u32[]{:S(2)}, u32[]{:S(2)}) collective-permute-start(bf16[512,256]{1,0:T(8,128)(2,1)S(1)} %pad_maximum_fusion), channel_id=1, source_target_pairs={{0,4},{4,0},{1,5},{5,1},{2,6},{6,2},{3,7},{7,3},{8,12},{12,8},{9,1... | collective-permute-start | bytes 786440 | tf_op jit(solution)/shard_map/ppermute | solution.py:331
  56.3 26.9 %copy-start.3 = (bf16[256]{0:T(256)(128)(2,1)S(1)}, bf16[256]{0:T(256)(128)(2,1)}, u32[]{:S(2)}) copy-start(bf16[256]{0:T(256)(128)(2,1)} %param.11) | copy-start | bytes 1540
  56.3 3.4 %collective-permute-start.4 = (bf16[512,256]{1,0:T(8,128)(2,1)S(1)}, bf16[512,256]{1,0:T(8,128)(2,1)S(1)}, u32[]{:S(2)}, u32[]{:S(2)}) collective-permute-start(bf16[512,256]{1,0:T(8,128)(2,1)S(1)} %pad_maximum_fusion.1), channel_id=1, source_target_pairs={{0,4},{4,0},{1,5},{5,1},{2,6},{6,2},{3,7},{7,3},{8,12},{12,8},{9,1... | collective-permute-start | bytes 786440 | tf_op jit(solution)/shard_map/ppermute | solution.py:331
  62.1 3.1 %collective-permute-start.6 = (f32[24,128]{1,0:T(8,128)S(1)}, f32[24,128]{1,0:T(8,128)S(1)}, u32[]{:S(2)}, u32[]{:S(2)}) collective-permute-start(f32[24,128]{1,0:T(8,128)S(1)} %shard_map.108.mine), channel_id=1, source_target_pairs={{0,4},{4,0},{1,5},{5,1},{2,6},{6,2},{3,7},{7,3},{8,12},{12,8},{9,1... | collective-permute-start | bytes 36872 | tf_op jit(solution)/shard_map/ppermute | solution.py:340
  108.0 9.2 %collective-permute-start.7 = (f32[128,128]{1,0:T(8,128)S(1)}, f32[128,128]{1,0:T(8,128)S(1)}, u32[]{:S(2)}, u32[]{:S(2)}) collective-permute-start(f32[128,128]{1,0:T(8,128)S(1)} %shard_map.111), channel_id=1, source_target_pairs={{224,0},{225,1},{226,2},{227,3},{228,4},{229,5},{230,6},{231,7},{4... | collective-permute-start | bytes 196616 | tf_op jit(solution)/shard_map/ppermute | solution.py:359
